TPU v7x, 32 devices: a whole 2x2x4 slice. The times are simulated.
32 devices in a mesh: ctx: 8 (over z, x), wa: 4 (over y, core).
Axes of the slice: x: 2, y: 2, z: 4, core: 2. Of those that a mesh axis runs over, the one named last changes fastest.
Arguments:
- tokens: bfloat16 [4, 1024, 960], P('wa', 'ctx'), may hold values from -6 to 6
- cotangent: bfloat16 [4, 1024, 960], P('wa', 'ctx'), may hold values from -6 to 6
- segment_ids: int32 [4, 1024], P('wa'), may hold values from 0 to 7, never falling along the last dimension, each value on 1 to 512 neighbouring positions
- block_order: int32 [4, 8], P('wa'), may hold values from 0 to 7, each once within a row
- gain_attn: float32 [960], P('wa'), may hold values from 0.5 to 1.5
- w_query: float32 [960, 960], P('wa'), may hold values from -0.1875 to 0.1875
- key_projection: float32 [960, 320], P('wa'), may hold values from -0.1875 to 0.1875
- value_projection: float32 [960, 320], P('wa'), may hold values from -0.1875 to 0.1875
- w_out: float32 [960, 960], P('wa'), may hold values from -0.75 to 0.75
- gain_mlp: float32 [960], P('wa'), may hold values from 0.5 to 1.5
- w_gate: float32 [960, 2560], P('wa'), may hold values from -0.1875 to 0.1875
- w_up: float32 [960, 2560], P('wa'), may hold values from -0.1875 to 0.1875
- w_down: float32 [2560, 960], P('wa'), may hold values from -0.125 to 0.125
Outputs:
- output: bfloat16 [4, 1024, 960], P('wa', 'ctx')
- input_grad: bfloat16 [4, 1024, 960], P('wa', 'ctx')
- grad_gain_attn: float32 [960], P('wa')
- grad_query: float32 [960, 960], P('wa')
- grad_key: float32 [960, 320], P('wa')
- grad_value: float32 [960, 320], P('wa')
- grad_out: float32 [960, 960], P('wa')
- grad_gain_mlp: float32 [960], P('wa')
- grad_gate: float32 [960, 2560], P('wa')
- grad_up: float32 [960, 2560], P('wa')
- grad_down: float32 [2560, 960], P('wa')
Inputs may be any that keep to these rules, and one draw needn't show every extreme that they name: `segment_ids`: in each group ids never fall along the given order; each of the 8 sequences has 1 to 512 tokens, and one has exactly 512. `block_order`: each row names every block of its group once.
All inputs are finite; a program needn't handle non-finite values.
Results may differ from a plain program's by a relative error of at most 0.023.
Values may be sent and summed in bfloat16 or wider, within the bound.
No kernel may reach another device: no remote copies, remote signals or barrier semaphores. Data moves between devices by JAX's collectives and lax.ppermute only.
A program may use at most 256 MiB of HBM per device.

v0:
```python
from functools import reduce

import jax
import jax.numpy as jnp
from jax import lax
from jax.sharding import PartitionSpec as P

QUERY_HEADS = 15
KEY_VALUE_HEADS = 5
HEAD_SIZE = 64
SEQS = 8
REPEATS = 2


epsilon = 1e-05
masked_score = -1e30
rope_base = 10000.0


def as_sent(shard):

    def short(part):
        return part.astype(jnp.bfloat16) if part.dtype == jnp.float32 else part

    return jax.tree.map(short, shard)


def token_layout(segment_row, order_row):
    key_count = segment_row.shape[0]
    count_of_blocks = order_row.shape[0]
    block_size = key_count // count_of_blocks
    dealt_index = jnp.arange(key_count, dtype=jnp.int32)
    which_block = dealt_index // block_size
    block_labels = jnp.arange(count_of_blocks, dtype=jnp.int32)
    anchor = jnp.sum(
        jnp.where(which_block[:, None] == block_labels[None, :], order_row[None, :], 0), axis=1
    )
    natural = anchor * block_size + dealt_index % block_size
    labels = jnp.arange(SEQS, dtype=jnp.int32)
    segment_sizes = jnp.sum((segment_row[None, :] == labels[:, None]).astype(jnp.int32), axis=1)
    segment_start = jnp.cumsum(segment_sizes) - segment_sizes
    inside = (segment_start[None, :] <= natural[:, None]).astype(jnp.int32)
    segment_of = jnp.sum(inside, axis=1) - 1
    start_of = jnp.max(jnp.where(inside > 0, segment_start[None, :], 0), axis=1)
    return (natural, segment_of, natural - start_of)


def rope_tables(positions, head_size):
    half_size = head_size // 2
    frequency = rope_base ** (-jnp.arange(half_size, dtype=jnp.float32) * 2.0 / head_size)
    angles = positions.astype(jnp.float32)[:, None] * frequency[None, :]
    cosine_table = jnp.concatenate([jnp.cos(angles), jnp.cos(angles)], axis=1)
    sine_values = jnp.concatenate([jnp.sin(angles), jnp.sin(angles)], axis=1)
    return (cosine_table[:, None, :], sine_values[:, None, :])


def rotate_heads(value_rows, cosine_table, sine_values):
    half_size = value_rows.shape[-1] // 2
    turned = jnp.concatenate([-value_rows[..., half_size:], value_rows[..., :half_size]], axis=-1)
    return value_rows * cosine_table + turned * sine_values


def inverse_rotation(grads, cosine_table, sine_values):
    half_size = grads.shape[-1] // 2
    scaled = grads * sine_values
    turned = jnp.concatenate([scaled[..., half_size:], -scaled[..., :half_size]], axis=-1)
    return grads * cosine_table + turned


def matrix_product(left, right):
    return jnp.dot(left, right, preferred_element_type=jnp.float32)


def times_transposed(left, right):
    return lax.dot_general(
        left, right, (((1,), (1,)), ((), ())), preferred_element_type=jnp.float32
    )


def weight_grad(inputs, grads):
    return lax.dot_general(
        inputs, grads, (((0,), (0,)), ((), ())), preferred_element_type=jnp.float32
    )


def norm_forward(hidden, gain):
    ratio = lax.rsqrt(jnp.mean(hidden * hidden, axis=-1, keepdims=True) + epsilon)
    return (hidden * ratio * gain, ratio)


def norm_backward(grads, hidden, ratio, gain):
    scaled = hidden * ratio
    gain_grad = jnp.sum(grads * scaled, axis=0)
    inner = grads * gain
    hidden_grad = ratio * (inner - scaled * jnp.mean(inner * scaled, axis=-1, keepdims=True))
    return (hidden_grad, gain_grad)


def masks_for(query_nat, query_seg, nat_block, seg_block):
    return (seg_block[None, :] == query_seg[:, None]) & (nat_block[None, :] <= query_nat[:, None])


def block_scores(queries, key_block, allowed, score_scale):
    raw = jnp.einsum("tkgd,skd->kgts", queries, key_block, preferred_element_type=jnp.float32)
    return jnp.where(allowed[None, None], raw * score_scale, masked_score)


def attend_forward(
    queries, blocks_of_keys, blocks_of_values, nat_blocks, seg_blocks, query_nat, query_seg
):
    number_of_tokens, heads_kv, tokens_per_group, head_size = queries.shape
    score_scale = head_size ** (-0.5)
    start_state = (
        jnp.full((heads_kv, tokens_per_group, number_of_tokens), masked_score, jnp.float32),
        jnp.zeros((heads_kv, tokens_per_group, number_of_tokens), jnp.float32),
    )

    def first_pass(state, inputs):
        key_block, nat_block, seg_block = inputs
        allowed = masks_for(query_nat, query_seg, nat_block, seg_block)
        scores = block_scores(queries, key_block, allowed, score_scale)
        largest = jnp.maximum(state[0], jnp.max(scores, axis=-1))
        weights = jnp.where(allowed[None, None], jnp.exp(scores - largest[..., None]), 0.0)
        return ((largest, state[1] * jnp.exp(state[0] - largest) + jnp.sum(weights, axis=-1)), None)

    (largest, total), ignored = lax.scan(
        first_pass, start_state, (blocks_of_keys, nat_blocks, seg_blocks)
    )
    log_total = largest + jnp.log(total)

    def second_pass(summed, inputs):
        key_block, value_block, nat_block, seg_block = inputs
        allowed = masks_for(query_nat, query_seg, nat_block, seg_block)
        scores = block_scores(queries, key_block, allowed, score_scale)
        weights = jnp.where(
            allowed[None, None], jnp.exp(scores - log_total[..., None]), 0.0
        ).astype(jnp.bfloat16)
        return (
            summed
            + jnp.einsum(
                "kgts,skd->tkgd", weights, value_block, preferred_element_type=jnp.float32
            ),
            None,
        )

    start_sum = jnp.zeros(queries.shape, jnp.float32)
    attended, ignored = lax.scan(
        second_pass, start_sum, (blocks_of_keys, blocks_of_values, nat_blocks, seg_blocks)
    )
    return (log_total, attended)


def attend_backward(
    queries,
    blocks_of_keys,
    blocks_of_values,
    nat_blocks,
    seg_blocks,
    query_nat,
    query_seg,
    log_total,
    attended,
    out_grad,
):
    head_size = queries.shape[-1]
    score_scale = head_size ** (-0.5)
    row_dots = jnp.einsum("tkgd,tkgd->kgt", out_grad.astype(jnp.float32), attended)

    def backward_step(query_sum, inputs):
        key_block, value_block, nat_block, seg_block = inputs
        allowed = masks_for(query_nat, query_seg, nat_block, seg_block)
        scores = block_scores(queries, key_block, allowed, score_scale)
        weights = jnp.where(allowed[None, None], jnp.exp(scores - log_total[..., None]), 0.0)
        weight_grads = jnp.einsum(
            "tkgd,skd->kgts", out_grad, value_block, preferred_element_type=jnp.float32
        )
        score_grad = (weights * (weight_grads - row_dots[..., None]) * score_scale).astype(
            jnp.bfloat16
        )
        query_part = query_sum + jnp.einsum(
            "kgts,skd->tkgd", score_grad, key_block, preferred_element_type=jnp.float32
        )
        key_part = jnp.einsum(
            "kgts,tkgd->skd", score_grad, queries, preferred_element_type=jnp.float32
        )
        value_part = jnp.einsum(
            "kgts,tkgd->skd",
            weights.astype(jnp.bfloat16),
            out_grad,
            preferred_element_type=jnp.float32,
        )
        return (query_part, (key_part, value_part))

    start_sum = jnp.zeros(queries.shape, jnp.float32)
    query_grad, (key_grads, value_grads) = lax.scan(
        backward_step, start_sum, (blocks_of_keys, blocks_of_values, nat_blocks, seg_blocks)
    )
    return (query_grad, key_grads, value_grads)


def forward_layer(hidden, weights, context):
    (
        attn_gain,
        query_weight,
        key_matrix,
        value_matrix,
        out_weight,
        mlp_gain,
        gate_weight,
        up_weight,
        down_weight,
    ) = weights
    cosine_table, sine_values, query_nat, query_seg, nat_blocks, seg_blocks = context
    number_of_tokens = hidden.shape[0]
    normed_pre, first_ratio = norm_forward(hidden, attn_gain)
    normalized_rows = normed_pre.astype(jnp.bfloat16)
    query_lin = matrix_product(normalized_rows, query_weight).reshape(
        number_of_tokens, QUERY_HEADS, HEAD_SIZE
    )
    queries = (
        rotate_heads(query_lin, cosine_table, sine_values)
        .astype(jnp.bfloat16)
        .reshape(number_of_tokens, KEY_VALUE_HEADS, QUERY_HEADS // KEY_VALUE_HEADS, HEAD_SIZE)
    )
    key_projected = matrix_product(normalized_rows, key_matrix).reshape(
        number_of_tokens, KEY_VALUE_HEADS, HEAD_SIZE
    )
    keys = (
        rotate_heads(key_projected, cosine_table, sine_values)
        .astype(jnp.bfloat16)
        .reshape(number_of_tokens, KEY_VALUE_HEADS * HEAD_SIZE)
    )
    value_rows = matrix_product(normalized_rows, value_matrix).astype(jnp.bfloat16)
    every_key, every_value = (
        lax.all_gather(keys, "ctx", axis=0, tiled=True),
        lax.all_gather(value_rows, "ctx", axis=0, tiled=True),
    )
    count_of_blocks = nat_blocks.shape[0]
    blocks_of_keys = every_key.reshape(count_of_blocks, -1, KEY_VALUE_HEADS, HEAD_SIZE)
    blocks_of_values = every_value.reshape(count_of_blocks, -1, KEY_VALUE_HEADS, HEAD_SIZE)
    log_total, attended = attend_forward(
        queries, blocks_of_keys, blocks_of_values, nat_blocks, seg_blocks, query_nat, query_seg
    )
    attended_low = attended.reshape(number_of_tokens, QUERY_HEADS * HEAD_SIZE).astype(jnp.bfloat16)
    middle = hidden + matrix_product(attended_low, out_weight)
    normed_mid_pre, second_ratio = norm_forward(middle, mlp_gain)
    normed_mid = normed_mid_pre.astype(jnp.bfloat16)
    gate_lin = matrix_product(normed_mid, gate_weight)
    up_lin = matrix_product(normed_mid, up_weight)
    mixed = (jax.nn.silu(gate_lin) * up_lin).astype(jnp.bfloat16)
    result = middle + matrix_product(mixed, down_weight)
    kept = (
        hidden,
        first_ratio,
        normalized_rows,
        queries,
        blocks_of_keys,
        blocks_of_values,
        log_total,
        attended,
        attended_low,
        middle,
        second_ratio,
        normed_mid,
        gate_lin,
        up_lin,
        mixed,
    )
    return (result, kept)


def sum_key_grads(key_grads, value_grads):
    key_value_width = KEY_VALUE_HEADS * HEAD_SIZE
    key_flat = key_grads.reshape(-1, key_value_width)
    value_flat = value_grads.reshape(-1, key_value_width)
    joined = jnp.concatenate([key_flat, value_flat], axis=1)
    summed = lax.psum_scatter(joined, "ctx", scatter_dimension=0, tiled=True)
    return (summed[:, :key_value_width], summed[:, key_value_width:])


def backward_layer(incoming, kept, weights, context):
    (
        attn_gain,
        query_weight,
        key_matrix,
        value_matrix,
        out_weight,
        mlp_gain,
        gate_weight,
        up_weight,
        down_weight,
    ) = weights
    cosine_table, sine_values, query_nat, query_seg, nat_blocks, seg_blocks = context
    (
        hidden,
        first_ratio,
        normalized_rows,
        queries,
        blocks_of_keys,
        blocks_of_values,
        log_total,
        attended,
        attended_low,
        middle,
        second_ratio,
        normed_mid,
        gate_lin,
        up_lin,
        mixed,
    ) = kept
    number_of_tokens = hidden.shape[0]
    down_in = incoming.astype(jnp.bfloat16)
    mixed_grad = times_transposed(down_in, down_weight)
    down_w_grad = weight_grad(mixed, down_in)
    gate_sig = jax.nn.sigmoid(gate_lin)
    gate_low = (mixed_grad * up_lin * gate_sig * (1.0 + gate_lin * (1.0 - gate_sig))).astype(
        jnp.bfloat16
    )
    up_low = (mixed_grad * gate_lin * gate_sig).astype(jnp.bfloat16)
    mid_normed_grad = times_transposed(gate_low, gate_weight) + times_transposed(up_low, up_weight)
    gate_w_grad = weight_grad(normed_mid, gate_low)
    up_w_grad = weight_grad(normed_mid, up_low)
    mid_part, mlp_gain_grad = norm_backward(mid_normed_grad, middle, second_ratio, mlp_gain)
    middle_grad = incoming + mid_part
    out_in = middle_grad.astype(jnp.bfloat16)
    attended_grad = (
        times_transposed(out_in, out_weight)
        .astype(jnp.bfloat16)
        .reshape(number_of_tokens, KEY_VALUE_HEADS, QUERY_HEADS // KEY_VALUE_HEADS, HEAD_SIZE)
    )
    out_w_grad = weight_grad(attended_low, out_in)
    query_grad, key_grads, value_grads = attend_backward(
        queries,
        blocks_of_keys,
        blocks_of_values,
        nat_blocks,
        seg_blocks,
        query_nat,
        query_seg,
        log_total,
        attended,
        attended_grad,
    )
    summed_keys, value_sum = sum_key_grads(key_grads, value_grads)
    query_lin_grad = (
        inverse_rotation(
            query_grad.reshape(number_of_tokens, QUERY_HEADS, HEAD_SIZE), cosine_table, sine_values
        )
        .reshape(number_of_tokens, QUERY_HEADS * HEAD_SIZE)
        .astype(jnp.bfloat16)
    )
    key_lin_grad = (
        inverse_rotation(
            summed_keys.reshape(number_of_tokens, KEY_VALUE_HEADS, HEAD_SIZE),
            cosine_table,
            sine_values,
        )
        .reshape(number_of_tokens, KEY_VALUE_HEADS * HEAD_SIZE)
        .astype(jnp.bfloat16)
    )
    value_lin_grad = value_sum.astype(jnp.bfloat16)
    normed_grad = (
        times_transposed(query_lin_grad, query_weight)
        + times_transposed(key_lin_grad, key_matrix)
        + times_transposed(value_lin_grad, value_matrix)
    )
    query_w_grad = weight_grad(normalized_rows, query_lin_grad)
    key_w_grad = weight_grad(normalized_rows, key_lin_grad)
    value_w_grad = weight_grad(normalized_rows, value_lin_grad)
    first_part, attn_gain_grad = norm_backward(normed_grad, hidden, first_ratio, attn_gain)
    layer_grads = (
        attn_gain_grad,
        query_w_grad,
        key_w_grad,
        value_w_grad,
        out_w_grad,
        mlp_gain_grad,
        gate_w_grad,
        up_w_grad,
        down_w_grad,
    )
    return (middle_grad + first_part, layer_grads)


def add_trees(first_tree, second_tree):
    return jax.tree.map(jnp.add, first_tree, second_tree)


def body(
    tokens,
    cotangent,
    segment_ids,
    block_order,
    gain_attn,
    w_query,
    key_projection,
    value_projection,
    w_out,
    gain_mlp,
    w_gate,
    w_up,
    w_down,
):
    hidden = tokens[0].astype(jnp.float32)
    number_of_tokens = hidden.shape[0]
    natural, segment_of, positions = token_layout(segment_ids[0], block_order[0])
    key_count = natural.shape[0]
    key_block = min(1024, key_count)
    first_row = lax.axis_index("ctx") * number_of_tokens
    query_nat = lax.dynamic_slice_in_dim(natural, first_row, number_of_tokens)
    query_seg = lax.dynamic_slice_in_dim(segment_of, first_row, number_of_tokens)
    query_pos = lax.dynamic_slice_in_dim(positions, first_row, number_of_tokens)
    cosine_table, sine_values = rope_tables(query_pos, HEAD_SIZE)
    nat_blocks = natural.reshape(key_count // key_block, key_block)
    seg_blocks = segment_of.reshape(key_count // key_block, key_block)
    context = (cosine_table, sine_values, query_nat, query_seg, nat_blocks, seg_blocks)
    gathered = (
        lax.all_gather(gain_attn.astype(jnp.bfloat16), "wa", axis=0, tiled=True),
        lax.all_gather(w_query.astype(jnp.bfloat16), "wa", axis=0, tiled=True),
        lax.all_gather(key_projection.astype(jnp.bfloat16), "wa", axis=0, tiled=True),
        lax.all_gather(value_projection.astype(jnp.bfloat16), "wa", axis=0, tiled=True),
        lax.all_gather(w_out.astype(jnp.bfloat16), "wa", axis=0, tiled=True),
        lax.all_gather(gain_mlp.astype(jnp.bfloat16), "wa", axis=0, tiled=True),
        lax.all_gather(w_gate.astype(jnp.bfloat16), "wa", axis=0, tiled=True),
        lax.all_gather(w_up.astype(jnp.bfloat16), "wa", axis=0, tiled=True),
        lax.all_gather(w_down.astype(jnp.bfloat16), "wa", axis=0, tiled=True),
    )
    weights = (
        gathered[0].astype(jnp.float32),
        gathered[1],
        gathered[2],
        gathered[3],
        gathered[4],
        gathered[5].astype(jnp.float32),
        gathered[6],
        gathered[7],
        gathered[8],
    )
    kept_layers = []
    for repeat_index in range(REPEATS):
        hidden, kept = forward_layer(hidden, weights, context)
        kept_layers.append(kept)
    output = hidden.astype(jnp.bfloat16)[None]
    grad_now = cotangent[0].astype(jnp.float32)
    local_list = []
    for kept in reversed(kept_layers):
        grad_now, layer_grads = backward_layer(grad_now, kept, weights, context)
        local_list.append(layer_grads)
    local_sum = reduce(add_trees, local_list)
    shares = jax.tree.map(
        lambda part: part.astype(jnp.float32),
        lax.psum_scatter(as_sent(local_sum), "wa", scatter_dimension=0, tiled=True),
    )
    totals = lax.psum(shares, "ctx")
    return (output, grad_now.astype(jnp.bfloat16)[None]) + tuple(totals)


def solution(mesh):
    return jax.shard_map(
        body,
        mesh=mesh,
        in_specs=(
            P("wa", "ctx", None),
            P("wa", "ctx", None),
            P("wa", None),
            P("wa", None),
            P("wa"),
            P("wa", None),
            P("wa", None),
            P("wa", None),
            P("wa", None),
            P("wa"),
            P("wa", None),
            P("wa", None),
            P("wa", None),
        ),
        out_specs=(
            P("wa", "ctx", None),
            P("wa", "ctx", None),
            P("wa"),
            P("wa", None),
            P("wa", None),
            P("wa", None),
            P("wa", None),
            P("wa"),
            P("wa", None),
            P("wa", None),
            P("wa", None),
        ),
        check_vma=False,
    )
```

profile of v0, /device:TPU:0, one launch (start us, length us, event | category | flops | bytes accessed | tf_op | source)
XLA Modules:
  0.0 1109.8 jit_solution(4447544085348025021)
XLA Ops:
  21.1 13.1 %all-gather = bf16[4,240,320]{1,2,0:T(8,128)(2,1)S(1)} all-gather(bf16[1,240,320]{1,2,0:T(8,128)(2,1)S(1)} %convert_bitcast_fusion.2), channel_id=1, replica_groups=mesh['ctx'=8,'wa'=4] {'wa'}, dimensions={0}, use_global_device_ids=true | all-gather | bytes 768000 | tf_op jit(solution)/shard_map/all_gather | solution.py:421
  34.2 8.1 all-gather.1
  44.2 7.6 all-reduce.6
  56.3 29.0 %all_gather.43 = bf16[1024,320]{0,1:T(8,128)(2,1)S(1)} all-gather(bf16[128,320]{0,1:T(8,128)(2,1)S(1)} %bitcast.389), channel_id=1, replica_groups=mesh['ctx'=8,'wa'=4] {'ctx'}, dimensions={0}, use_global_device_ids=true | all-gather | bytes 737280 | tf_op jit(solution)/shard_map/all_gather | solution.py:235
  85.3 28.5 %all_gather.41 = bf16[1024,320]{0,1:T(8,128)(2,1)} all-gather(bf16[128,320]{0,1:T(8,128)(2,1)S(1)} %convolution_convert_fusion.3), channel_id=1, replica_groups=mesh['ctx'=8,'wa'=4] {'ctx'}, dimensions={0}, use_global_device_ids=true | all-gather | bytes 737280 | tf_op jit(solution)/shard_map/all_gather | solution.py:236
  113.8 4.1 copy.57
  130.9 3.4 fusion.101
  134.4 8.9 all-gather.14.cloned.1.call-done
  143.2 4.7 multiply_convert_fusion.5
  147.9 35.3 %all-gather.16.cloned.1.call-done = bf16[2560,960]{0,1:T(8,128)(2,1)} async-done(((bf16[640,960]{0,1:T(8,128)(2,1)}), bf16[2560,960]{0,1:T(8,128)(2,1)}) %all-gather.16.cloned.1.call-update) | async-done | bytes 4915216 | tf_op jit(solution)/shard_map/all_gather | solution.py:426
  183.2 4.2 multiply_reduce_fusion.7
  189.8 28.3 %all_gather.51 = bf16[1024,320]{0,1:T(8,128)(2,1)S(1)} all-gather(bf16[128,320]{0,1:T(8,128)(2,1)S(1)} %fusion.55), channel_id=1, replica_groups=mesh['ctx'=8,'wa'=4] {'ctx'}, dimensions={0}, use_global_device_ids=true | all-gather | bytes 737280 | tf_op jit(solution)/shard_map/all_gather | solution.py:235
  218.0 28.7 %all_gather.50 = bf16[1024,320]{0,1:T(8,128)(2,1)S(1)} all-gather(bf16[128,320]{0,1:T(8,128)(2,1)S(1)} %convolution_convert_fusion.2), channel_id=1, replica_groups=mesh['ctx'=8,'wa'=4] {'ctx'}, dimensions={0}, use_global_device_ids=true | all-gather | bytes 737280 | tf_op jit(solution)/shard_map/all_gather | solution.py:236
  265.4 3.3 fusion.5
  273.9 3.0 fusion.106
  277.9 63.4 %reduce-scatter.16.cloned.1.call-done = f32[128,640]{0,1:T(8,128)} async-done(((f32[1024,640]{0,1:T(8,128)}), f32[128,640]{0,1:T(8,128)}) %reduce-scatter.16.cloned.1.call-update) | async-done | bytes 327696 | tf_op jit(solution)/shard_map/reduce_scatter | solution.py:277
  348.7 3.9 multiply_convert_fusion
  359.8 3.3 fusion.2
  383.8 54.4 %reduce-scatter.18.cloned.1.call-done = f32[128,640]{0,1:T(8,128)} async-done(((f32[1024,640]{0,1:T(8,128)}), f32[128,640]{0,1:T(8,128)}) %reduce-scatter.18.cloned.1.call-update) | async-done | bytes 327696 | tf_op jit(solution)/shard_map/reduce_scatter | solution.py:277
  452.9 3.6 add_convert_fusion
  456.5 8.0 copy.100
  467.4 3.6 add_convert_fusion.1
  474.0 3.6 add_convert_fusion.2
  478.4 5.2 fusion.15
  484.4 20.4 %reduce-scatter.20.cloned.1.call-done = bf16[240,960]{1,0:T(8,128)(2,1)} async-done(((bf16[960,960]{1,0:T(8,128)(2,1)}), bf16[240,960]{1,0:T(8,128)(2,1)}) %reduce-scatter.20.cloned.1.call-update) | async-done | bytes 460816 | tf_op jit(solution)/shard_map/reduce_scatter | solution.py:452
  508.6 5.8 all-reduce.5
  515.4 15.4 %reduce-scatter.30.cloned.1.call-done = bf16[240,320]{1,0:T(8,128)(2,1)} async-done(((bf16[960,320]{1,0:T(8,128)(2,1)}), bf16[240,320]{1,0:T(8,128)(2,1)}) %reduce-scatter.30.cloned.1.call-update) | async-done | bytes 153616
  531.8 25.3 %reduce-scatter.28.cloned.1.call-done = bf16[240,320]{1,0:T(8,128)(2,1)} async-done(((bf16[960,320]{1,0:T(8,128)(2,1)}), bf16[240,320]{1,0:T(8,128)(2,1)}) %reduce-scatter.28.cloned.1.call-update) | async-done | bytes 153616
  558.1 52.8 %reduce-scatter.32.cloned.1.call-done = bf16[640,960]{1,0:T(8,128)(2,1)} async-done(((bf16[2560,960]{1,0:T(8,128)(2,1)}), bf16[640,960]{1,0:T(8,128)(2,1)}) %reduce-scatter.32.cloned.1.call-update) | async-done | bytes 1228816
  613.0 49.9 %reduce-scatter.26.cloned.1.call-done = bf16[240,2560]{1,0:T(8,128)(2,1)} async-done(((bf16[960,2560]{1,0:T(8,128)(2,1)}), bf16[240,2560]{1,0:T(8,128)(2,1)}) %reduce-scatter.26.cloned.1.call-update) | async-done | bytes 1228816 | tf_op jit(solution)/shard_map/reduce_scatter | solution.py:452
  662.9 51.7 %reduce-scatter.24.cloned.1.call-done = bf16[240,2560]{1,0:T(8,128)(2,1)} async-done(((bf16[960,2560]{1,0:T(8,128)(2,1)}), bf16[240,2560]{1,0:T(8,128)(2,1)}) %reduce-scatter.24.cloned.1.call-update) | async-done | bytes 1228816 | tf_op jit(solution)/shard_map/reduce_scatter | solution.py:452
  714.6 388.3 %all-reduce.8 = (f32[240]{0:T(256)}, f32[240,960]{1,0:T(8,128)}, f32[240,320]{0,1:T(8,128)}, f32[240,320]{0,1:T(8,128)}, f32[240,960]{1,0:T(8,128)}, /*index=5*/...) all-reduce(f32[240]{0:T(256)S(1)} %get-tuple-element.280, ...), channel_id=1, replica_groups=mesh['ctx'=8,'wa'=4] {'ctx'}, use_global_device_ids=true, to_apply=%region_22.23 | all-reduce | flops 2458080 | bytes 14749440 | tf_op jit(solution)/shard_map/psum | solution.py:454
  (355 shorter events, 124.0 us)
Async XLA Ops:
  7.2 106.6 %all-gather.8.cloned.1.call-start = ((), (), s32[]{:S(2)}) async-start(), calls=%async_computation.9 | async-start | bytes 2457600 | tf_op jit(solution)/shard_map/all_gather | solution.py:419
  9.3 118.5 %all-gather.10.cloned.1.call-start = ((), (), s32[]{:S(2)}) async-start(), calls=%async_computation.10 | async-start | bytes 2457600 | tf_op jit(solution)/shard_map/all_gather | solution.py:422
  11.4 119.5 %all-gather.12.cloned.1.call-start = ((), (), s32[]{:S(2)}) async-start(), calls=%async_computation.11 | async-start | bytes 6144000 | tf_op jit(solution)/shard_map/all_gather | solution.py:424
  14.4 128.8 %all-gather.14.cloned.1.call-start = ((), (), s32[]{:S(2)}) async-start(), calls=%async_computation.12 | async-start | bytes 6144000 | tf_op jit(solution)/shard_map/all_gather | solution.py:425
  17.4 25.1 %copy-start.74 = (f32[240]{0:T(256)S(1)}, f32[240]{0:T(256)}, u32[]{:S(2)}) copy-start(f32[240]{0:T(256)} %param.17) | copy-start | bytes 2884
  17.4 25.1 %copy-start.75 = (f32[240]{0:T(256)S(1)}, f32[240]{0:T(256)}, u32[]{:S(2)}) copy-start(f32[240]{0:T(256)} %param.22) | copy-start | bytes 2884
  17.4 25.1 %copy-start.72 = (u32[32]{0:T(128)S(1)}, u32[32]{0:T(128)}, u32[]{:S(2)}) copy-start(u32[32]{0:T(128)} %constant.184) | copy-start | bytes 388
  17.4 165.8 %all-gather.16.cloned.1.call-start = ((), (), s32[]{:S(2)}) async-start(), calls=%async_computation.13 | async-start | bytes 6144000 | tf_op jit(solution)/shard_map/all_gather | solution.py:426
  20.4 34.4 %copy-start.7 = (bf16[1,128,960]{1,2,0:T(8,128)(2,1)S(1)}, bf16[1,128,960]{1,2,0:T(8,128)(2,1)}, u32[]{:S(2)}) copy-start(bf16[1,128,960]{1,2,0:T(8,128)(2,1)} %param.13) | copy-start | bytes 737284
  20.4 320.8 %reduce-scatter.16.cloned.1.call-start = ((), (), s32[]{:S(2)}) async-start(), calls=%async_computation.14 | async-start | bytes 2949120 | tf_op jit(solution)/shard_map/reduce_scatter | solution.py:277
  51.8 66.1 %copy-start.50 = (f32[960]{0:T(1024)}, f32[960]{0:T(1024)S(1)}, u32[]{:S(2)}) copy-start(f32[960]{0:T(1024)S(1)} %convert_element_type.251) | copy-start | bytes 11524
  53.5 64.4 %copy-start.13 = (bf16[960,320]{0,1:T(8,128)(2,1)}, bf16[960,320]{0,1:T(8,128)(2,1)S(1)}, u32[]{:S(2)}) copy-start(bf16[960,320]{0,1:T(8,128)(2,1)S(1)} %reshape.399) | copy-start | bytes 1843204
  54.9 63.0 %copy-start.60 = (f32[128]{0:T(128)}, f32[128]{0:T(128)S(1)}, u32[]{:S(2)}) copy-start(f32[128]{0:T(128)S(1)} %add_rsqrt_fusion.3) | copy-start | bytes 1540
  85.3 36.4 %copy-start.25 = (bf16[1024,320]{0,1:T(8,128)(2,1)}, bf16[1024,320]{0,1:T(8,128)(2,1)S(1)}, u32[]{:S(2)}) copy-start(bf16[1024,320]{0,1:T(8,128)(2,1)S(1)} %all_gather.43) | copy-start | bytes 1966084
  130.3 52.9 %copy-start.8 = (f32[128,960]{0,1:T(8,128)}, f32[128,960]{0,1:T(8,128)S(1)}, u32[]{:S(2)}) copy-start(f32[128,960]{0,1:T(8,128)S(1)} %get-tuple-element.264) | copy-start | bytes 1474564
  130.9 16.9 %copy-start.17 = (bf16[128,960]{0,1:T(8,128)(2,1)}, bf16[128,960]{0,1:T(8,128)(2,1)S(1)}, u32[]{:S(2)}) copy-start(bf16[128,960]{0,1:T(8,128)(2,1)S(1)} %multiply_convert_fusion.8) | copy-start | bytes 737284
  134.3 13.5 %copy-start.29 = (f32[128,2560]{1,0:T(8,128)}, f32[128,2560]{1,0:T(8,128)S(1)}, u32[]{:S(2)}) copy-start(f32[128,2560]{1,0:T(8,128)S(1)} %fusion.101) | copy-start | bytes 3932164
  187.4 64.8 %copy-start.10 = (f32[128,960]{0,1:T(8,128)}, f32[128,960]{0,1:T(8,128)S(1)}, u32[]{:S(2)}) copy-start(f32[128,960]{0,1:T(8,128)S(1)} %get-tuple-element.268) | copy-start | bytes 1474564
  188.0 60.1 %copy-start.12 = (bf16[128,960]{0,1:T(8,128)(2,1)}, bf16[128,960]{0,1:T(8,128)(2,1)S(1)}, u32[]{:S(2)}) copy-start(bf16[128,960]{0,1:T(8,128)(2,1)S(1)} %multiply_convert_fusion.7) | copy-start | bytes 737284
  218.0 30.1 %copy-start.26 = (bf16[1024,320]{0,1:T(8,128)(2,1)}, bf16[1024,320]{0,1:T(8,128)(2,1)S(1)}, u32[]{:S(2)}) copy-start(bf16[1024,320]{0,1:T(8,128)(2,1)S(1)} %all_gather.51) | copy-start | bytes 1966084
  273.9 164.4 %reduce-scatter.18.cloned.1.call-start = ((), (), s32[]{:S(2)}) async-start(), calls=%async_computation.15 | async-start | bytes 2949120 | tf_op jit(solution)/shard_map/reduce_scatter | solution.py:277
  345.7 8.4 slice-start.2
  368.1 116.3 %reduce-scatter.22.cloned.1.call-start = ((), (), s32[]{:S(2)}) async-start(), calls=%async_computation.17 | async-start | bytes 2457600 | tf_op jit(solution)/shard_map/reduce_scatter | solution.py:452
  373.2 131.6 %reduce-scatter.20.cloned.1.call-start = ((), (), s32[]{:S(2)}) async-start(), calls=%async_computation.16 | async-start | bytes 2457600 | tf_op jit(solution)/shard_map/reduce_scatter | solution.py:452
  381.3 61.9 %copy-start.47 = (bf16[128,320]{0,1:T(8,128)(2,1)S(1)}, bf16[128,320]{0,1:T(8,128)(2,1)}, u32[]{:S(2)}) copy-start(bf16[128,320]{0,1:T(8,128)(2,1)} %copy-done.46) | copy-start | bytes 245764
  381.3 149.4 %reduce-scatter.30.cloned.1.call-start = ((), (), s32[]{:S(2)}) async-start(), calls=%async_computation.21 | async-start | bytes 921600
  443.2 113.9 %reduce-scatter.28.cloned.1.call-start = ((), (), s32[]{:S(2)}) async-start(), calls=%async_computation.20 | async-start | bytes 921600
  450.1 160.8 %reduce-scatter.32.cloned.1.call-start = ((), (), s32[]{:S(2)}) async-start(), calls=%async_computation.22 | async-start | bytes 6553600
  464.6 198.3 %reduce-scatter.26.cloned.1.call-start = ((), (), s32[]{:S(2)}) async-start(), calls=%async_computation.19 | async-start | bytes 6144000 | tf_op jit(solution)/shard_map/reduce_scatter | solution.py:452
  471.0 243.6 %reduce-scatter.24.cloned.1.call-start = ((), (), s32[]{:S(2)}) async-start(), calls=%async_computation.18 | async-start | bytes 6144000 | tf_op jit(solution)/shard_map/reduce_scatter | solution.py:452
  483.6 25.0 %copy-start.63 = (f32[960]{0:T(1024)S(1)}, f32[960]{0:T(1024)}, u32[]{:S(2)}) copy-start(f32[960]{0:T(1024)} %get-tuple-element.157) | copy-start | bytes 11524
  483.6 30.9 %copy-start.22 = (f32[128,960]{0,1:T(8,128)S(1)}, f32[128,960]{0,1:T(8,128)}, u32[]{:S(2)}) copy-start(f32[128,960]{0,1:T(8,128)} %copy-done.20) | copy-start | bytes 1474564
  (70 other events, 262.1 us)
Sparse Core Ops, SparseCore 0:
  10.1 28.0 all-gather.7
  39.8 21.9 all-gather.9
  63.9 38.6 all-gather.11
  104.6 38.5 all-gather.13
  144.6 38.5 all-gather.15
  274.0 67.2 reduce-scatter.15
  368.2 69.9 reduce-scatter.17
  441.4 29.4 reduce-scatter.21
  474.2 30.6 reduce-scatter.19
  507.8 22.9 reduce-scatter.29
  534.1 22.9 reduce-scatter.27
  559.5 51.3 reduce-scatter.31
  613.6 49.1 reduce-scatter.25
  665.3 49.1 reduce-scatter.23
where the time goes:
time: 1120 us; the launch traced here: 1110 us
  blocking collectives  537 us (48%)
  waiting for transfers between devices  378 us (34%)
  matrix products  112 us (10%)
  local copies, waits for them, and re-layouts  34.8 us (3%)
  other arithmetic  29.4 us (3%)
  between operations  17.2 us (2%)
    psum x1, blocking collectives, body(): totals = lax.psum(shares, 'ctx')  388 us
    reduce_scatter x4, waiting for transfers between devices, body(): lax.psum_scatter(as_sent(local_sum), 'wa', scatter_dimension=0, tiled=True)  122 us
    reduce_scatter x2, waiting for transfers between devices, sum_key_grads(): summed = lax.psum_scatter(joined, 'ctx', scatter_dimension=0, tiled=True)  118 us
    unnamed x17, waiting for transfers between devices  93.7 us
    all_gather x2, blocking collectives, forward_layer(): lax.all_gather(keys, 'ctx', axis=0, tiled=True)  57.3 us
    all_gather x2, blocking collectives, forward_layer(): lax.all_gather(value_rows, 'ctx', axis=0, tiled=True)  57.2 us
    dot_general x14, matrix products, weight_grad(): lax.dot_general(inputs, grads, (((0,), (0,)), ((), ())), preferred_elemen...  35.5 us
    all_gather x1, waiting for transfers between devices, body(): lax.all_gather(w_down.astype(jnp.bfloat16), 'wa', axis=0, tiled=True)  35.3 us
  transfers between devices with their start and end apart: 14, of which 10 were waited for; matrix products, arithmetic and copies ran while one was open for 10% of the time, Pallas kernels for 0%

commit v1 on v0

v1 whole, which is shorter than its diff:
```python
import jax
import jax.numpy as jnp
from jax import lax
from jax.sharding import PartitionSpec as P

QUERY_HEADS = 15
KEY_VALUE_HEADS = 5
HEAD_SIZE = 64
SEQS = 8
REPEATS = 2
WA = 4

epsilon = 1e-05
masked_score = -1e30
rope_base = 10000.0
bf16 = jnp.bfloat16
f32 = jnp.float32


def swap(x, mask):
    return lax.ppermute(x, "wa", [(i, i ^ mask) for i in range(WA)])


def ring_order(n):
    return [i for i in range(0, n, 2)] + [i for i in range(n - 1, 0, -2)]


def ring_shift(x, n, step):
    order = ring_order(n)
    return lax.ppermute(x, "ctx", [(order[i], order[(i + step) % n]) for i in range(n)])


def ring_position(r, n):
    return jnp.where(r % 2 == 0, r // 2, n - 1 - r // 2)


def ring_device(p, n):
    return jnp.where(p < n // 2, 2 * p, 2 * (n - 1 - p) + 1)


def ring_gather(x, n):
    half = n // 2
    rows = x.shape[0] // 2
    ahead = [x]
    behind = [x]
    for _ in range(half - 1):
        ahead.append(ring_shift(ahead[-1], n, 1))
        behind.append(ring_shift(behind[-1], n, -1))
    far = jnp.concatenate(
        [ring_shift(ahead[-1][:rows], n, 1), ring_shift(behind[-1][rows:], n, -1)], axis=0
    )
    return ahead + [far] + behind[:0:-1]


def add_low(x, y):
    return (x.astype(f32) + y.astype(f32)).astype(bf16)


def ring_scatter(piece, n):
    half = n // 2
    far = piece(half)
    rows = far.shape[0] // 2
    go = ring_shift(far[:rows], n, 1)
    back = ring_shift(far[rows:], n, -1)
    own = piece(half + 1)
    go = jnp.concatenate([add_low(own[:rows], go), own[rows:]], axis=0)
    own = piece(half - 1)
    back = jnp.concatenate([own[:rows], add_low(own[rows:], back)], axis=0)
    for k in range(half - 2, 0, -1):
        go = add_low(ring_shift(go, n, 1), piece(n - k))
        back = add_low(ring_shift(back, n, -1), piece(k))
    go = ring_shift(go, n, 1)
    back = ring_shift(back, n, -1)
    return piece(0).astype(f32) + go.astype(f32) + back.astype(f32)


def ring_all_reduce(pieces, n, position):
    def piece(k):
        return lax.dynamic_index_in_dim(pieces, (position - k) % n, 0, keepdims=False)

    mine = ring_scatter(piece, n).astype(bf16)
    gathered = ring_gather(mine, n)
    out = jnp.zeros(pieces.shape, bf16)
    for k in range(n):
        out = lax.dynamic_update_index_in_dim(out, gathered[k], (position - k) % n, 0)
    return out


def cut(x, n):
    if x.shape[0] % (2 * n) == 0:
        return x.reshape(n, x.shape[0] // n, x.shape[1])
    return x.reshape(n, -1)


def all_sum(x, n):
    for mask in (1, 2):
        x = x + swap(x, mask)
    step = 1
    while step < n:
        x = x + lax.ppermute(x, "ctx", [(i, i ^ step) for i in range(n)])
        step *= 2
    return x


def everyone(x):
    side = swap(x, 1)
    across = swap(x, 2)
    return jnp.concatenate([x, side, across, swap(across, 1)], axis=0)


def own_slices(x, w):
    rows, width = x.shape
    parts = x.reshape(rows, WA, width // WA).transpose(1, 0, 2)

    def of(mask):
        part = lax.dynamic_index_in_dim(parts, w ^ mask, 0, keepdims=False)
        return swap(part, mask) if mask else part

    return jnp.concatenate([of(m) for m in range(WA)], axis=0)


def whole_rows(x, w):
    across = swap(x, 2)
    parts = jnp.stack([x, swap(x, 1), across, swap(across, 1)])
    return jnp.concatenate(
        [lax.dynamic_index_in_dim(parts, w ^ j, 0, keepdims=False) for j in range(WA)], axis=0
    )


def in_order(first, second, flag):
    return jnp.stack([jnp.where(flag, second, first), jnp.where(flag, first, second)])


def token_layout(segment_row, order_row, blocks):
    key_count = segment_row.shape[0]
    count_of_blocks = order_row.shape[0]
    block_size = key_count // count_of_blocks
    labels = jnp.arange(count_of_blocks, dtype=jnp.int32)
    anchor = jnp.sum(jnp.where(blocks[:, None] == labels[None, :], order_row[None, :], 0), axis=1)
    natural = (
        anchor[:, None] * block_size + jnp.arange(block_size, dtype=jnp.int32)[None, :]
    ).reshape(-1)
    labels = jnp.arange(SEQS, dtype=jnp.int32)
    segment_sizes = jnp.sum((segment_row[None, :] == labels[:, None]).astype(jnp.int32), axis=1)
    segment_start = jnp.cumsum(segment_sizes) - segment_sizes
    inside = (segment_start[None, :] <= natural[:, None]).astype(jnp.int32)
    segment_of = jnp.sum(inside, axis=1) - 1
    start_of = jnp.max(jnp.where(inside > 0, segment_start[None, :], 0), axis=1)
    return (natural, segment_of, natural - start_of)


def rope_tables(positions, head_size):
    half_size = head_size // 2
    frequency = rope_base ** (-jnp.arange(half_size, dtype=jnp.float32) * 2.0 / head_size)
    angles = positions.astype(jnp.float32)[:, None] * frequency[None, :]
    cosine_table = jnp.concatenate([jnp.cos(angles), jnp.cos(angles)], axis=1)
    sine_values = jnp.concatenate([jnp.sin(angles), jnp.sin(angles)], axis=1)
    return (cosine_table[:, None, :], sine_values[:, None, :])


def rotate_heads(value_rows, cosine_table, sine_values):
    half_size = value_rows.shape[-1] // 2
    turned = jnp.concatenate([-value_rows[..., half_size:], value_rows[..., :half_size]], axis=-1)
    return value_rows * cosine_table + turned * sine_values


def inverse_rotation(grads, cosine_table, sine_values):
    half_size = grads.shape[-1] // 2
    scaled = grads * sine_values
    turned = jnp.concatenate([scaled[..., half_size:], -scaled[..., :half_size]], axis=-1)
    return grads * cosine_table + turned


def matrix_product(left, right):
    return jnp.dot(left, right, preferred_element_type=jnp.float32)


def times_transposed(left, right):
    return lax.dot_general(
        left, right, (((1,), (1,)), ((), ())), preferred_element_type=jnp.float32
    )


def weight_grad(inputs, grads):
    return lax.dot_general(
        inputs, grads, (((0,), (0,)), ((), ())), preferred_element_type=jnp.float32
    )


def norm_forward(hidden, gain):
    ratio = lax.rsqrt(jnp.mean(hidden * hidden, axis=-1, keepdims=True) + epsilon)
    return (hidden * ratio * gain, ratio)


def norm_backward(grads, hidden, ratio, gain):
    scaled = hidden * ratio
    gain_grad = jnp.sum(grads * scaled, axis=0)
    inner = grads * gain
    hidden_grad = ratio * (inner - scaled * jnp.mean(inner * scaled, axis=-1, keepdims=True))
    return (hidden_grad, gain_grad)


def masks_for(query_nat, query_seg, nat_block, seg_block):
    return (seg_block[None, :] == query_seg[:, None]) & (nat_block[None, :] <= query_nat[:, None])


def block_scores(queries, key_block, allowed, score_scale):
    raw = jnp.einsum("tkgd,skd->kgts", queries, key_block, preferred_element_type=jnp.float32)
    return jnp.where(allowed[None, None], raw * score_scale, masked_score)


def attend_forward(
    queries, blocks_of_keys, blocks_of_values, nat_blocks, seg_blocks, query_nat, query_seg
):
    number_of_tokens, heads_kv, tokens_per_group, head_size = queries.shape
    score_scale = head_size ** (-0.5)
    start_state = (
        jnp.full((heads_kv, tokens_per_group, number_of_tokens), masked_score, jnp.float32),
        jnp.zeros((heads_kv, tokens_per_group, number_of_tokens), jnp.float32),
    )

    def first_pass(state, inputs):
        key_block, nat_block, seg_block = inputs
        allowed = masks_for(query_nat, query_seg, nat_block, seg_block)
        scores = block_scores(queries, key_block, allowed, score_scale)
        largest = jnp.maximum(state[0], jnp.max(scores, axis=-1))
        weights = jnp.where(allowed[None, None], jnp.exp(scores - largest[..., None]), 0.0)
        return ((largest, state[1] * jnp.exp(state[0] - largest) + jnp.sum(weights, axis=-1)), None)

    (largest, total), ignored = lax.scan(
        first_pass, start_state, (blocks_of_keys, nat_blocks, seg_blocks)
    )
    log_total = largest + jnp.log(total)

    def second_pass(summed, inputs):
        key_block, value_block, nat_block, seg_block = inputs
        allowed = masks_for(query_nat, query_seg, nat_block, seg_block)
        scores = block_scores(queries, key_block, allowed, score_scale)
        weights = jnp.where(
            allowed[None, None], jnp.exp(scores - log_total[..., None]), 0.0
        ).astype(jnp.bfloat16)
        return (
            summed
            + jnp.einsum(
                "kgts,skd->tkgd", weights, value_block, preferred_element_type=jnp.float32
            ),
            None,
        )

    start_sum = jnp.zeros(queries.shape, jnp.float32)
    attended, ignored = lax.scan(
        second_pass, start_sum, (blocks_of_keys, blocks_of_values, nat_blocks, seg_blocks)
    )
    return (log_total, attended)


def attend_backward(
    queries,
    blocks_of_keys,
    blocks_of_values,
    nat_blocks,
    seg_blocks,
    query_nat,
    query_seg,
    log_total,
    attended,
    out_grad,
):
    head_size = queries.shape[-1]
    score_scale = head_size ** (-0.5)
    row_dots = jnp.einsum("tkgd,tkgd->kgt", out_grad.astype(jnp.float32), attended)

    def backward_step(query_sum, inputs):
        key_block, value_block, nat_block, seg_block = inputs
        allowed = masks_for(query_nat, query_seg, nat_block, seg_block)
        scores = block_scores(queries, key_block, allowed, score_scale)
        weights = jnp.where(allowed[None, None], jnp.exp(scores - log_total[..., None]), 0.0)
        weight_grads = jnp.einsum(
            "tkgd,skd->kgts", out_grad, value_block, preferred_element_type=jnp.float32
        )
        score_grad = (weights * (weight_grads - row_dots[..., None]) * score_scale).astype(
            jnp.bfloat16
        )
        query_part = query_sum + jnp.einsum(
            "kgts,skd->tkgd", score_grad, key_block, preferred_element_type=jnp.float32
        )
        key_part = jnp.einsum(
            "kgts,tkgd->skd", score_grad, queries, preferred_element_type=jnp.float32
        )
        value_part = jnp.einsum(
            "kgts,tkgd->skd",
            weights.astype(jnp.bfloat16),
            out_grad,
            preferred_element_type=jnp.float32,
        )
        return (query_part, (key_part, value_part))

    start_sum = jnp.zeros(queries.shape, jnp.float32)
    query_grad, (key_grads, value_grads) = lax.scan(
        backward_step, start_sum, (blocks_of_keys, blocks_of_values, nat_blocks, seg_blocks)
    )
    return (query_grad, key_grads, value_grads)


def forward_layer(hidden, weights, context):
    gain_attn, w_qkv, w_out, gain_mlp, w_gate, w_up, w_down = weights
    cosine, sine, query_nat, query_seg, nat_blocks, seg_blocks, w, n = context
    tokens = hidden.shape[0]
    kv_width = KEY_VALUE_HEADS * HEAD_SIZE
    q_width = QUERY_HEADS * HEAD_SIZE
    normed_pre, first_ratio = norm_forward(hidden, gain_attn)
    normed = normed_pre.astype(bf16)
    qkv = matrix_product(normed, w_qkv)
    turned = rotate_heads(
        qkv[:, : q_width + kv_width].reshape(tokens, -1, HEAD_SIZE), cosine, sine
    ).astype(bf16)
    queries = turned[:, :QUERY_HEADS].reshape(
        tokens, KEY_VALUE_HEADS, QUERY_HEADS // KEY_VALUE_HEADS, HEAD_SIZE
    )
    pair = jnp.concatenate(
        [turned[:, QUERY_HEADS:].reshape(tokens, kv_width), qkv[:, q_width + kv_width :].astype(bf16)],
        axis=1,
    )
    every = jnp.stack(ring_gather(pair, n))
    count = nat_blocks.shape[0]
    blocks_of_keys = every[:, :, :kv_width].reshape(count, -1, KEY_VALUE_HEADS, HEAD_SIZE)
    blocks_of_values = every[:, :, kv_width:].reshape(count, -1, KEY_VALUE_HEADS, HEAD_SIZE)
    log_total, attended = attend_forward(
        queries, blocks_of_keys, blocks_of_values, nat_blocks, seg_blocks, query_nat, query_seg
    )
    attended_low = attended.reshape(tokens, q_width).astype(bf16)
    middle = hidden + matrix_product(attended_low, w_out)
    normed_mid_pre, second_ratio = norm_forward(middle, gain_mlp)
    normed_mid = normed_mid_pre.astype(bf16)
    both = jnp.concatenate([normed_mid, swap(normed_mid, 1)], axis=0)
    gate_lin = matrix_product(both, w_gate)
    up_lin = matrix_product(both, w_up)
    mixed = (jax.nn.silu(gate_lin) * up_lin).astype(bf16)
    partial = matrix_product(mixed, w_down)
    result = middle + partial[:tokens] + swap(partial[tokens:], 1)
    quarter = mixed.shape[1] // 2
    halves = mixed.reshape(2 * tokens, 2, quarter)
    mine = jnp.where(w < 2, halves[:, 0], halves[:, 1])
    other = jnp.where(w < 2, halves[:, 1], halves[:, 0])
    mixed_all = jnp.concatenate([mine, swap(other, 2)], axis=0)
    kept = dict(
        hidden=hidden,
        first_ratio=first_ratio,
        queries=queries,
        keys=blocks_of_keys,
        values=blocks_of_values,
        log_total=log_total,
        attended=attended,
        middle=middle,
        second_ratio=second_ratio,
        gate_lin=gate_lin,
        up_lin=up_lin,
        normed_slices=own_slices(normed, w),
        attended_slices=own_slices(attended_low, w),
        mid_slices=own_slices(normed_mid, w),
        mixed_all=mixed_all,
    )
    return (result, kept)


def flip(x):
    rows = x.shape[0] // 2
    return jnp.concatenate([x[rows:], x[:rows]], axis=0)


def backward_layer(incoming, kept, weights, context):
    gain_attn, w_qkv, w_out, gain_mlp, w_gate, w_up, w_down = weights
    cosine, sine, query_nat, query_seg, nat_blocks, seg_blocks, w, n = context
    tokens = incoming.shape[0]
    kv_width = KEY_VALUE_HEADS * HEAD_SIZE
    q_width = QUERY_HEADS * HEAD_SIZE
    low = incoming.astype(bf16)
    side = swap(low, 1)
    across = swap(low, 2)
    both = jnp.concatenate([low, side], axis=0)
    mixed_grad = times_transposed(both, w_down)
    gate_lin = kept["gate_lin"]
    up_lin = kept["up_lin"]
    gate_sig = jax.nn.sigmoid(gate_lin)
    gate_low = (mixed_grad * up_lin * gate_sig * (1.0 + gate_lin * (1.0 - gate_sig))).astype(bf16)
    up_low = (mixed_grad * gate_lin * gate_sig).astype(bf16)
    partial = times_transposed(gate_low, w_gate) + times_transposed(up_low, w_up)
    mid_normed_grad = partial[:tokens] + swap(partial[tokens:], 1)
    mid_part, gain_mlp_grad = norm_backward(
        mid_normed_grad, kept["middle"], kept["second_ratio"], gain_mlp
    )
    middle_grad = incoming + mid_part
    low_all = jnp.concatenate([both, across, swap(across, 1)], axis=0)
    down_grad = weight_grad(kept["mixed_all"], low_all)
    pair = jnp.concatenate([gate_low, up_low], axis=1)
    pair_far = swap(pair, 2)
    mine_cols = jnp.concatenate([pair, pair_far], axis=0)
    other_cols = jnp.concatenate([flip(swap(pair, 1)), flip(swap(pair_far, 1))], axis=0)
    mine_grad = weight_grad(kept["mid_slices"], mine_cols)
    other_grad = weight_grad(kept["mid_slices"], other_cols)

    out_in = middle_grad.astype(bf16)
    attended_grad = (
        times_transposed(out_in, w_out)
        .astype(bf16)
        .reshape(tokens, KEY_VALUE_HEADS, QUERY_HEADS // KEY_VALUE_HEADS, HEAD_SIZE)
    )
    out_grad = weight_grad(kept["attended_slices"], everyone(out_in))
    query_grad, key_grads, value_grads = attend_backward(
        kept["queries"],
        kept["keys"],
        kept["values"],
        nat_blocks,
        seg_blocks,
        query_nat,
        query_seg,
        kept["log_total"],
        kept["attended"],
        attended_grad,
    )
    joined = jnp.concatenate(
        [
            key_grads.reshape(n, tokens, kv_width).astype(bf16),
            value_grads.reshape(n, tokens, kv_width).astype(bf16),
        ],
        axis=2,
    )
    summed = ring_scatter(lambda k: joined[k], n)
    heads = jnp.concatenate(
        [
            query_grad.reshape(tokens, QUERY_HEADS, HEAD_SIZE),
            summed[:, :kv_width].reshape(tokens, KEY_VALUE_HEADS, HEAD_SIZE),
        ],
        axis=1,
    )
    lin_grad = jnp.concatenate(
        [
            inverse_rotation(heads, cosine, sine).reshape(tokens, q_width + kv_width).astype(bf16),
            summed[:, kv_width:].astype(bf16),
        ],
        axis=1,
    )
    normed_grad = times_transposed(lin_grad, w_qkv)
    qkv_grad = weight_grad(kept["normed_slices"], everyone(lin_grad))
    first_part, gain_attn_grad = norm_backward(
        normed_grad, kept["hidden"], kept["first_ratio"], gain_attn
    )
    gains = jnp.stack([gain_attn_grad, gain_mlp_grad])
    return (
        middle_grad + first_part,
        (gains, qkv_grad, out_grad, mine_grad, other_grad, down_grad),
    )


def body(
    tokens,
    cotangent,
    segment_ids,
    block_order,
    gain_attn,
    w_query,
    key_projection,
    value_projection,
    w_out,
    gain_mlp,
    w_gate,
    w_up,
    w_down,
):
    n = block_order.shape[1]
    w = lax.axis_index("wa")
    core = w % 2
    row = w // 2
    position = ring_position(lax.axis_index("ctx"), n)
    blocks = ring_device((position - jnp.arange(n, dtype=jnp.int32)) % n, n)
    natural, segment_of, positions = token_layout(segment_ids[0], block_order[0], blocks)
    count = tokens.shape[1]
    cosine, sine = rope_tables(positions[:count], HEAD_SIZE)
    key_block = min(1024, natural.shape[0])
    context = (
        cosine,
        sine,
        natural[:count],
        segment_of[:count],
        natural.reshape(-1, key_block),
        segment_of.reshape(-1, key_block),
        w,
        n,
    )

    gains = jnp.stack([gain_attn, gain_mlp]).astype(bf16)
    gains = whole_rows(gains.T, w).T.astype(f32)
    qkv = jnp.concatenate([w_query, key_projection, value_projection], axis=1).astype(bf16)
    qkv_whole = whole_rows(qkv, w)
    out_whole = whole_rows(w_out.astype(bf16), w)

    rows, ff = w_gate.shape
    quarter = ff // WA
    gate_up = (
        jnp.stack([w_gate, w_up]).astype(bf16).reshape(2, rows, 2, 2, quarter).transpose(0, 2, 3, 1, 4)
    )
    keep = lax.dynamic_index_in_dim(gate_up, core, 2, keepdims=False)
    give = lax.dynamic_index_in_dim(gate_up, 1 - core, 2, keepdims=False)
    chip = in_order(keep, swap(give, 1), core == 1)
    everything = in_order(chip, swap(chip, 2), row == 1)
    everything = everything.transpose(2, 0, 1, 4, 3, 5).reshape(2, WA * rows, 2 * quarter)
    down = w_down.astype(bf16)
    down_half = in_order(down, swap(down, 2), row == 1).reshape(2 * quarter, -1)
    weights = (gains[0], qkv_whole, out_whole, gains[1], everything[0], everything[1], down_half)

    hidden = tokens[0].astype(f32)
    kept_layers = []
    for repeat_index in range(REPEATS):
        hidden, kept = forward_layer(hidden, weights, context)
        kept_layers.append(kept)
    output = hidden.astype(bf16)[None]
    grad_now = cotangent[0].astype(f32)
    totals = None
    for kept in reversed(kept_layers):
        grad_now, grads = backward_layer(grad_now, kept, weights, context)
        totals = grads if totals is None else jax.tree.map(jnp.add, totals, grads)
    input_grad = grad_now.astype(bf16)[None]

    gain_sum, qkv_grad, out_grad, mine_grad, other_grad, down_grad = totals
    gain_sum = lax.dynamic_slice_in_dim(all_sum(gain_sum, n), w * rows, rows, 1)

    def reduced(x):
        return ring_all_reduce(cut(x.astype(bf16), n), n, position).reshape(x.shape).astype(f32)

    down_total = reduced(down_grad)
    both_grad = jnp.stack([mine_grad, other_grad], axis=1).reshape(rows, n, -1)
    both_total = (
        ring_all_reduce(both_grad.transpose(1, 0, 2).astype(bf16), n, position)
        .transpose(1, 0, 2)
        .reshape(rows, 2, 2, 2, quarter)
    )
    mine_total = both_total[:, 0]
    other_total = both_total[:, 1]
    low_cols = jnp.where(core == 0, mine_total, other_total)
    high_cols = jnp.where(core == 0, other_total, mine_total)
    gate_up_total = jnp.stack([low_cols, high_cols], axis=3).reshape(rows, 2, ff).astype(f32)
    out_total = reduced(out_grad)
    qkv_total = reduced(qkv_grad)
    q_width = w_query.shape[1]
    kv_width = key_projection.shape[1]
    return (
        output,
        input_grad,
        gain_sum[0],
        qkv_total[:, :q_width],
        qkv_total[:, q_width : q_width + kv_width],
        qkv_total[:, q_width + kv_width :],
        out_total,
        gain_sum[1],
        gate_up_total[:, 0],
        gate_up_total[:, 1],
        down_total,
    )


def solution(mesh):
    rows = P("wa", None)
    return jax.shard_map(
        body,
        mesh=mesh,
        in_specs=(
            P("wa", "ctx", None),
            P("wa", "ctx", None),
            rows,
            rows,
            P("wa"),
            rows,
            rows,
            rows,
            rows,
            P("wa"),
            rows,
            rows,
            rows,
        ),
        out_specs=(
            P("wa", "ctx", None),
            P("wa", "ctx", None),
            P("wa"),
            rows,
            rows,
            rows,
            rows,
            P("wa"),
            rows,
            rows,
            rows,
        ),
        check_vma=False,
    )
```

time: 1120 us -> 703 us (0.63)
  blocking collectives: 537 us -> 0 us
  starting transfers between devices: 1.05 us -> 139 us
  waiting for transfers between devices: 378 us -> 245 us
  local copies, waits for them, and re-layouts: 34.8 us -> 152 us
  other arithmetic: 29.4 us -> 69.7 us
  matrix products: 112 us -> 81.9 us
  between operations: 17.2 us -> 4.44 us
    psum x1 -> x0, blocking collectives: 388 us -> none  [body(): totals = lax.psum(shares, 'ctx')]
    ppermute x0 -> x163, waiting for transfers between devices: none -> 245 us  [the longest x96 151 us: ring_shift(): lax.ppermute(x, 'ctx', [(order[i], order[(i + step) % n]) for i in range(...]
    reduce_scatter x6 -> x0, waiting for transfers between devices: 240 us -> none  [the longest x4 122 us: body(): lax.psum_scatter(as_sent(local_sum), 'wa', scatter_dimension=0, tiled=True)]
    ppermute x0 -> x163, starting transfers between devices: none -> 139 us  [the longest x96 94.7 us: ring_shift(): lax.ppermute(x, 'ctx', [(order[i], order[(i + step) % n]) for i in range(...]
    all_gather x6 -> x0, blocking collectives: 136 us -> none  [the longest x2 57.3 us: forward_layer(): lax.all_gather(keys, 'ctx', axis=0, tiled=True)]
    unnamed x17 -> x0, waiting for transfers between devices: 93.7 us -> none
    all_gather x5 -> x0, waiting for transfers between devices: 44.2 us -> none  [the longest x1 35.3 us: body(): lax.all_gather(w_down.astype(jnp.bfloat16), 'wa', axis=0, tiled=True)]
    slice x2 -> x54, local copies, waits for them, and re-layouts: 1.95 us -> 40.4 us  [the longest x4 6.08 us: flip(): return jnp.concatenate([x[rows:], x[:rows]], axis=0)]
  transfers between devices with their start and end apart: 14 -> 163, of which waited for: 10 -> 76; matrix products, arithmetic and copies ran while one was open for 10% -> 39% of each run, Pallas kernels for 0% -> 0%
where the time goes in v1:
time: 703 us; the launch traced here: 692 us
  waiting for transfers between devices  245 us (35%)
  local copies, waits for them, and re-layouts  152 us (22%)
  starting transfers between devices  139 us (20%)
  matrix products  81.9 us (12%)
  other arithmetic  69.7 us (10%)
    ppermute x96, waiting for transfers between devices, ring_shift(): lax.ppermute(x, 'ctx', [(order[i], order[(i + step) % n]) for i in range(...  151 us
    ppermute x96, starting transfers between devices, ring_shift(): lax.ppermute(x, 'ctx', [(order[i], order[(i + step) % n]) for i in range(...  94.7 us
    ppermute x64, waiting for transfers between devices, swap(): return lax.ppermute(x, 'wa', [(i, i ^ mask) for i in range(WA)])  87.7 us
    ppermute x64, starting transfers between devices, swap(): return lax.ppermute(x, 'wa', [(i, i ^ mask) for i in range(WA)])  40.2 us
    dot_general x10, matrix products, weight_grad(): lax.dot_general(inputs, grads, (((0,), (0,)), ((), ())), preferred_elemen...  21.4 us
    unnamed x355, local copies, waits for them, and re-layouts  18.6 us
  transfers between devices with their start and end apart: 163, of which 76 were waited for; matrix products, arithmetic and copies ran while one was open for 39% of the time, Pallas kernels for 0%

profile of v1, /device:TPU:0, one launch (start us, length us, event | category | flops | bytes accessed | tf_op | source)
XLA Modules:
  0.0 692.5 jit_solution(11877693033721106294)
XLA Ops:
  24.4 3.9 stack.207
  31.6 7.3 %dynamic-slice_bitcast_fusion = (bf16[2,2,1,240,640]{4,2,1,3,0:T(2,128)(2,1)}, bf16[2,2,1,240,640]{4,2,1,3,0:T(2,128)(2,1)}) fusion(bf16[2,240,2,2,640]{4,3,2,1,0:T(2,128)(2,1)S(1)} %constant_dynamic-update-slice_fusion, s32[]{:T(128)S(6)} %select_n.494, s32[]{:T(128)S(6)} %select_n.493), kind=kLoop, calls=%fused_computation.64 | loop fusion | bytes 4915208 | tf_op jit(solution)/shard_map/jit(dynamic_index_in_dim)/dynamic_slice | solution.py:502
  56.7 27.2 %collective-permute-done.142 = bf16[128,960]{0,1:T(8,128)(2,1)} collective-permute-done((bf16[128,960]{0,1:T(8,128)(2,1)}, bf16[128,960]{0,1:T(8,128)(2,1)}, u32[]{:S(2)}, u32[]{:S(2)}) %collective-permute-start.142) | collective-permute-done | bytes 245792 | tf_op jit(solution)/shard_map/ppermute | solution.py:21
  92.1 4.9 pad_maximum_fusion.1
  107.4 3.6 collective-permute-done.7
  113.1 5.0 collective-permute-done.12
  128.4 5.7 fusion.8
  137.6 5.3 select_reduce_fusion.1
  143.1 4.1 bitcast_convert_fusion.2
  182.6 3.8 collective-permute-done.23
  188.4 5.0 collective-permute-done.28
  213.3 6.2 bitcast_convert_fusion.1
  225.7 3.6 multiply_convert_fusion.2
  289.2 4.6 collective-permute-done.145
  346.7 4.8 collective-permute-done.48
  375.8 14.1 %collective-permute-done.95 = bf16[128,960]{0,1:T(8,128)(2,1)S(1)} collective-permute-done((bf16[128,960]{0,1:T(8,128)(2,1)S(1)}, bf16[128,960]{0,1:T(8,128)(2,1)S(1)}, u32[]{:S(2)}, u32[]{:S(2)}) %collective-permute-start.95) | collective-permute-done | bytes 245792 | tf_op jit(solution)/shard_map/ppermute | solution.py:21
  440.0 3.9 collective-permute-done.56
  444.3 4.7 collective-permute-done.104
  453.7 3.4 collective-permute-done.157
  469.2 22.9 %collective-permute-done.119 = bf16[128,240]{0,1:T(8,128)(2,1)S(1)} collective-permute-done((bf16[128,240]{0,1:T(8,128)(2,1)S(1)}, bf16[128,240]{0,1:T(8,128)(2,1)S(1)}, u32[]{:S(2)}, u32[]{:S(2)}) %collective-permute-start.119) | collective-permute-done | bytes 61472 | tf_op jit(solution)/shard_map/ppermute | solution.py:21
  510.5 11.9 %collective-permute-done.67 = bf16[128,1600]{0,1:T(8,128)(2,1)} collective-permute-done((bf16[128,1600]{0,1:T(8,128)(2,1)}, bf16[128,1600]{0,1:T(8,128)(2,1)}, u32[]{:S(2)}, u32[]{:S(2)}) %collective-permute-start.67) | collective-permute-done | bytes 409632 | tf_op jit(solution)/shard_map/ppermute | solution.py:21
  589.2 4.0 copy.291
  593.1 5.5 convert_element_type.939
  598.7 5.0 constant_dynamic-slice_fusion.7
  606.0 4.7 collective-permute-done.125
  613.0 7.3 %collective-permute-done.126 = bf16[240,640]{1,0:T(8,128)(2,1)S(1)} collective-permute-done((bf16[240,640]{1,0:T(8,128)(2,1)S(1)}, bf16[240,640]{1,0:T(8,128)(2,1)S(1)}, u32[]{:S(2)}, u32[]{:S(2)}) %collective-permute-start.126) | collective-permute-done | bytes 307232 | tf_op jit(solution)/shard_map/ppermute | solution.py:30
  623.5 6.0 collective-permute-done.127
  631.8 6.9 %collective-permute-done.128 = bf16[240,640]{1,0:T(8,128)(2,1)S(1)} collective-permute-done((bf16[240,640]{1,0:T(8,128)(2,1)S(1)}, bf16[240,640]{1,0:T(8,128)(2,1)S(1)}, u32[]{:S(2)}, u32[]{:S(2)}) %collective-permute-start.128) | collective-permute-done | bytes 307232 | tf_op jit(solution)/shard_map/ppermute | solution.py:30
  642.8 4.9 collective-permute-done.133
  673.5 6.0 copy.297
  679.6 7.5 %reshape.743 = f32[240,2,2560]{2,0,1:T(8,128)} reshape(f32[240,2,2,2,640]{4,3,2,0,1:T(2,128)} %copy.297) | data formatting | bytes 9830400 | tf_op jit(solution)/shard_map/convert_element_type | solution.py:541
  687.0 5.0 slice_bitcast_fusion
  (973 shorter events, 469.4 us)
Async XLA Ops:
  2.1 44.0 %collective-permute-start.1 = (bf16[240,2]{0,1:T(2,128)(2,1)S(1)}, bf16[240,2]{0,1:T(2,128)(2,1)S(1)}, u32[]{:S(2)}, u32[]{:S(2)}) collective-permute-start(bf16[240,2]{0,1:T(2,128)(2,1)S(1)} %fusion.327), channel_id=1, source_target_pairs={{0,2},{1,3},{2,0},{3,1},{4,6},{5,7},{6,4},{7,5},{8,10},{9,11},{10,... | collective-permute-start | bytes 2888 | tf_op jit(solution)/shard_map/ppermute | solution.py:21
  5.1 43.5 %collective-permute-start = (bf16[240,2]{0,1:T(2,128)(2,1)S(1)}, bf16[240,2]{0,1:T(2,128)(2,1)S(1)}, u32[]{:S(2)}, u32[]{:S(2)}) collective-permute-start(bf16[240,2]{0,1:T(2,128)(2,1)S(1)} %fusion.327), channel_id=1, source_target_pairs={{0,1},{1,0},{2,3},{3,2},{4,5},{5,4},{6,7},{7,6},{8,9},{9,8},{10,11... | collective-permute-start | bytes 2888 | tf_op jit(solution)/shard_map/ppermute | solution.py:21
  7.2 42.4 %collective-permute-start.15 = (bf16[240,960]{1,0:T(8,128)(2,1)}, bf16[240,960]{1,0:T(8,128)(2,1)}, u32[]{:S(2)}, u32[]{:S(2)}) collective-permute-start(bf16[240,960]{1,0:T(8,128)(2,1)} %convert_element_type.773), channel_id=1, source_target_pairs={{0,2},{1,3},{2,0},{3,1},{4,6},{5,7},{6,4},{7,5},{8,10},{9,11},{10,... | collective-permute-start | bytes 1382408 | tf_op jit(solution)/shard_map/ppermute | solution.py:21
  7.3 43.4 %collective-permute-start.14 = (bf16[240,960]{1,0:T(8,128)(2,1)}, bf16[240,960]{1,0:T(8,128)(2,1)}, u32[]{:S(2)}, u32[]{:S(2)}) collective-permute-start(bf16[240,960]{1,0:T(8,128)(2,1)} %convert_element_type.773), channel_id=1, source_target_pairs={{0,1},{1,0},{2,3},{3,2},{4,5},{5,4},{6,7},{7,6},{8,9},{9,8},{10,11... | collective-permute-start | bytes 1382408 | tf_op jit(solution)/shard_map/ppermute | solution.py:21
  12.7 71.1 %collective-permute-start.4 = (bf16[240,1600]{1,0:T(8,128)(2,1)}, bf16[240,1600]{1,0:T(8,128)(2,1)}, u32[]{:S(2)}, u32[]{:S(2)}) collective-permute-start(bf16[240,1600]{1,0:T(8,128)(2,1)} %concatenate.206), channel_id=1, source_target_pairs={{0,2},{1,3},{2,0},{3,1},{4,6},{5,7},{6,4},{7,5},{8,10},{9,11},{10,... | collective-permute-start | bytes 2304008 | tf_op jit(solution)/shard_map/ppermute | solution.py:21
  48.6 35.7 %collective-permute-start.18 = (bf16[2,2,240,640]{3,2,1,0:T(8,128)(2,1)}, bf16[2,2,240,640]{3,2,1,0:T(8,128)(2,1)}, u32[]{:S(2)}, u32[]{:S(2)}) collective-permute-start(bf16[2,2,240,640]{3,2,1,0:T(8,128)(2,1)} %bitcast.821), channel_id=1, source_target_pairs={{0,1},{1,0},{2,3},{3,2},{4,5},{5,4},{6,7},{7,6},{8,9},{9,8},{10,11... | collective-permute-start | bytes 3686408 | tf_op jit(solution)/shard_map/ppermute | solution.py:21
  49.2 39.1 %collective-permute-start.20 = (bf16[640,960]{0,1:T(8,128)(2,1)}, bf16[640,960]{0,1:T(8,128)(2,1)}, u32[]{:S(2)}, u32[]{:S(2)}) collective-permute-start(bf16[640,960]{0,1:T(8,128)(2,1)} %convert_element_type.776), channel_id=1, source_target_pairs={{0,2},{1,3},{2,0},{3,1},{4,6},{5,7},{6,4},{7,5},{8,10},{9,11},{10,... | collective-permute-start | bytes 3686408 | tf_op jit(solution)/shard_map/ppermute | solution.py:21
  50.8 39.4 %collective-permute-start.3 = (bf16[240,1600]{1,0:T(8,128)(2,1)}, bf16[240,1600]{1,0:T(8,128)(2,1)S(1)}, u32[]{:S(2)}, u32[]{:S(2)}) collective-permute-start(bf16[240,1600]{1,0:T(8,128)(2,1)} %concatenate.206), channel_id=1, source_target_pairs={{0,1},{1,0},{2,3},{3,2},{4,5},{5,4},{6,7},{7,6},{8,9},{9,8},{10,11... | collective-permute-start | bytes 2304008 | tf_op jit(solution)/shard_map/ppermute | solution.py:21
  52.8 31.0 %collective-permute-start.142 = (bf16[128,960]{0,1:T(8,128)(2,1)}, bf16[128,960]{0,1:T(8,128)(2,1)}, u32[]{:S(2)}, u32[]{:S(2)}) collective-permute-start(bf16[128,960]{0,1:T(8,128)(2,1)} %bitcast.85), channel_id=1, source_target_pairs={{0,2},{1,3},{2,0},{3,1},{4,6},{5,7},{6,4},{7,5},{8,10},{9,11},{10,... | collective-permute-start | bytes 737288 | tf_op jit(solution)/shard_map/ppermute | solution.py:21
  83.8 141.0 %collective-permute-start.32 = (bf16[128,960]{0,1:T(8,128)(2,1)}, bf16[128,960]{0,1:T(8,128)(2,1)}, u32[]{:S(2)}, u32[]{:S(2)}) collective-permute-start(bf16[128,960]{0,1:T(8,128)(2,1)} %bitcast.85), channel_id=1, source_target_pairs={{0,1},{1,0},{2,3},{3,2},{4,5},{5,4},{6,7},{7,6},{8,9},{9,8},{10,11... | collective-permute-start | bytes 737288 | tf_op jit(solution)/shard_map/ppermute | solution.py:21
  83.8 219.2 %collective-permute-start.143 = (bf16[128,960]{0,1:T(8,128)(2,1)}, bf16[128,960]{0,1:T(8,128)(2,1)}, u32[]{:S(2)}, u32[]{:S(2)}) collective-permute-start(bf16[128,960]{0,1:T(8,128)(2,1)} %collective-permute-done.142), channel_id=1, source_target_pairs={{0,1},{1,0},{2,3},{3,2},{4,5},{5,4},{6,7},{7,6},{8,9},{9,8},{10,11... | collective-permute-start | bytes 737288 | tf_op jit(solution)/shard_map/ppermute | solution.py:21
  88.3 60.8 %collective-permute-start.19 = (bf16[2,2,2,240,640]{4,3,2,1,0:T(8,128)(2,1)}, bf16[2,2,2,240,640]{4,3,2,1,0:T(8,128)(2,1)}, u32[]{:S(2)}, u32[]{:S(2)}) collective-permute-start(bf16[2,2,2,240,640]{4,3,2,1,0:T(8,128)(2,1)} %pad_maximum_fusion.2), channel_id=1, source_target_pairs={{0,2},{1,3},{2,0},{3,1},{4,6},{5,7},{6,4},{7,5},{8,10},{9,11},{10,... | collective-permute-start | bytes 7372808 | tf_op jit(solution)/shard_map/ppermute | solution.py:21
  176.9 121.6 %collective-permute-start.144 = (bf16[256,640]{1,0:T(8,128)(2,1)}, bf16[256,640]{1,0:T(8,128)(2,1)}, u32[]{:S(2)}, u32[]{:S(2)}) collective-permute-start(bf16[256,640]{1,0:T(8,128)(2,1)} %get-tuple-element.340), channel_id=1, source_target_pairs={{0,2},{1,3},{2,0},{3,1},{4,6},{5,7},{6,4},{7,5},{8,10},{9,11},{10,... | collective-permute-start | bytes 983048 | tf_op jit(solution)/shard_map/ppermute | solution.py:21
  298.6 64.1 %collective-permute-start.91 = (bf16[128,240]{0,1:T(8,128)(2,1)}, bf16[128,240]{0,1:T(8,128)(2,1)}, u32[]{:S(2)}, u32[]{:S(2)}) collective-permute-start(bf16[128,240]{0,1:T(8,128)(2,1)} %get-tuple-element.425), channel_id=1, source_target_pairs={{0,1},{1,0},{2,3},{3,2},{4,5},{5,4},{6,7},{7,6},{8,9},{9,8},{10,11... | collective-permute-start | bytes 184328 | tf_op jit(solution)/shard_map/ppermute | solution.py:21
  298.6 66.6 %collective-permute-start.92 = (bf16[128,240]{0,1:T(8,128)(2,1)}, bf16[128,240]{0,1:T(8,128)(2,1)}, u32[]{:S(2)}, u32[]{:S(2)}) collective-permute-start(bf16[128,240]{0,1:T(8,128)(2,1)} %get-tuple-element.424), channel_id=1, source_target_pairs={{0,2},{1,3},{2,0},{3,1},{4,6},{5,7},{6,4},{7,5},{8,10},{9,11},{10,... | collective-permute-start | bytes 184328 | tf_op jit(solution)/shard_map/ppermute | solution.py:21
  303.0 21.3 %collective-permute-start.43 = (f32[128,960]{0,1:T(8,128)}, f32[128,960]{0,1:T(8,128)}, u32[]{:S(2)}, u32[]{:S(2)}) collective-permute-start(f32[128,960]{0,1:T(8,128)} %slice.655), channel_id=1, source_target_pairs={{0,1},{1,0},{2,3},{3,2},{4,5},{5,4},{6,7},{7,6},{8,9},{9,8},{10,11... | collective-permute-start | bytes 1474568 | tf_op jit(solution)/shard_map/ppermute | solution.py:21
  321.6 48.0 %collective-permute-start.93 = (bf16[128,240]{0,1:T(8,128)(2,1)S(1)}, bf16[128,240]{0,1:T(8,128)(2,1)S(1)}, u32[]{:S(2)}, u32[]{:S(2)}) collective-permute-start(bf16[128,240]{0,1:T(8,128)(2,1)S(1)} %copy-done.133), channel_id=1, source_target_pairs={{0,3},{1,2},{2,1},{3,0},{4,7},{5,6},{6,5},{7,4},{8,11},{9,10},{10,... | collective-permute-start | bytes 184328 | tf_op jit(solution)/shard_map/ppermute | solution.py:21
  322.3 30.0 %collective-permute-start.149 = (bf16[80,960]{1,0:T(8,128)(2,1)S(1)}, bf16[80,960]{1,0:T(8,128)(2,1)S(1)}, u32[]{:S(2)}, u32[]{:S(2)}) collective-permute-start(bf16[80,960]{1,0:T(8,128)(2,1)S(1)} %get-tuple-element.329), channel_id=1, source_target_pairs={{0,8},{8,16},{16,24},{24,28},{28,20},{20,12},{12,4},{4,0},{1,9},{9... | collective-permute-start | bytes 460808 | tf_op jit(solution)/shard_map/ppermute | solution.py:30
  352.3 48.3 %collective-permute-start.116 = (bf16[256,2560]{1,0:T(8,128)(2,1)}, bf16[256,2560]{1,0:T(8,128)(2,1)}, u32[]{:S(2)}, u32[]{:S(2)}) collective-permute-start(bf16[256,2560]{1,0:T(8,128)(2,1)} %pad_maximum_fusion.6), channel_id=1, source_target_pairs={{0,2},{1,3},{2,0},{3,1},{4,6},{5,7},{6,4},{7,5},{8,10},{9,11},{10,... | collective-permute-start | bytes 3932168 | tf_op jit(solution)/shard_map/ppermute | solution.py:21
  362.7 27.2 %collective-permute-start.95 = (bf16[128,960]{0,1:T(8,128)(2,1)S(1)}, bf16[128,960]{0,1:T(8,128)(2,1)S(1)}, u32[]{:S(2)}, u32[]{:S(2)}) collective-permute-start(bf16[128,960]{0,1:T(8,128)(2,1)S(1)} %get-tuple-element.282), channel_id=1, source_target_pairs={{0,2},{1,3},{2,0},{3,1},{4,6},{5,7},{6,4},{7,5},{8,10},{9,11},{10,... | collective-permute-start | bytes 737288 | tf_op jit(solution)/shard_map/ppermute | solution.py:21
  370.5 22.9 %collective-permute-start.89 = (bf16[128,960]{0,1:T(8,128)(2,1)S(1)}, bf16[128,960]{0,1:T(8,128)(2,1)S(1)}, u32[]{:S(2)}, u32[]{:S(2)}) collective-permute-start(bf16[128,960]{0,1:T(8,128)(2,1)S(1)} %copy-done.107), channel_id=1, source_target_pairs={{0,2},{1,3},{2,0},{3,1},{4,6},{5,7},{6,4},{7,5},{8,10},{9,11},{10,... | collective-permute-start | bytes 737288 | tf_op jit(solution)/shard_map/ppermute | solution.py:21
  400.6 105.7 %collective-permute-start.63 = (bf16[128,240]{0,1:T(8,128)(2,1)}, bf16[128,240]{0,1:T(8,128)(2,1)}, u32[]{:S(2)}, u32[]{:S(2)}) collective-permute-start(bf16[128,240]{0,1:T(8,128)(2,1)} %get-tuple-element.433), channel_id=1, source_target_pairs={{0,1},{1,0},{2,3},{3,2},{4,5},{5,4},{6,7},{7,6},{8,9},{9,8},{10,11... | collective-permute-start | bytes 184328 | tf_op jit(solution)/shard_map/ppermute | solution.py:21
  400.6 62.3 %collective-permute-start.122 = (bf16[256,2560]{1,0:T(8,128)(2,1)}, bf16[256,2560]{1,0:T(8,128)(2,1)}, u32[]{:S(2)}, u32[]{:S(2)}) collective-permute-start(bf16[256,2560]{1,0:T(8,128)(2,1)} %collective-permute-done.116), channel_id=1, source_target_pairs={{0,1},{1,0},{2,3},{3,2},{4,5},{5,4},{6,7},{7,6},{8,9},{9,8},{10,11... | collective-permute-start | bytes 3932168 | tf_op jit(solution)/shard_map/ppermute | solution.py:21
  444.0 22.0 %collective-permute-start.123 = (bf16[256,2560]{1,0:T(8,128)(2,1)S(1)}, bf16[256,2560]{1,0:T(8,128)(2,1)S(1)}, u32[]{:S(2)}, u32[]{:S(2)}) collective-permute-start(bf16[256,2560]{1,0:T(8,128)(2,1)S(1)} %copy-done.62), channel_id=1, source_target_pairs={{0,1},{1,0},{2,3},{3,2},{4,5},{5,4},{6,7},{7,6},{8,9},{9,8},{10,11... | collective-permute-start | bytes 3932168 | tf_op jit(solution)/shard_map/ppermute | solution.py:21
  462.9 30.5 %collective-permute-start.120 = (bf16[256,2560]{1,0:T(8,128)(2,1)S(1)}, bf16[256,2560]{1,0:T(8,128)(2,1)}, u32[]{:S(2)}, u32[]{:S(2)}) collective-permute-start(bf16[256,2560]{1,0:T(8,128)(2,1)S(1)} %copy-done.62), channel_id=1, source_target_pairs={{0,2},{1,3},{2,0},{3,1},{4,6},{5,7},{6,4},{7,5},{8,10},{9,11},{10,... | collective-permute-start | bytes 3932168 | tf_op jit(solution)/shard_map/ppermute | solution.py:21
  466.1 26.1 %collective-permute-start.119 = (bf16[128,240]{0,1:T(8,128)(2,1)S(1)}, bf16[128,240]{0,1:T(8,128)(2,1)S(1)}, u32[]{:S(2)}, u32[]{:S(2)}) collective-permute-start(bf16[128,240]{0,1:T(8,128)(2,1)S(1)} %copy-done.126), channel_id=1, source_target_pairs={{0,3},{1,2},{2,1},{3,0},{4,7},{5,6},{6,5},{7,4},{8,11},{9,10},{10,... | collective-permute-start | bytes 184328 | tf_op jit(solution)/shard_map/ppermute | solution.py:21
  467.2 39.1 %collective-permute-start.64 = (bf16[128,240]{0,1:T(8,128)(2,1)S(1)}, bf16[128,240]{0,1:T(8,128)(2,1)S(1)}, u32[]{:S(2)}, u32[]{:S(2)}) collective-permute-start(bf16[128,240]{0,1:T(8,128)(2,1)S(1)} %copy-done.122), channel_id=1, source_target_pairs={{0,2},{1,3},{2,0},{3,1},{4,6},{5,7},{6,4},{7,5},{8,10},{9,11},{10,... | collective-permute-start | bytes 184328 | tf_op jit(solution)/shard_map/ppermute | solution.py:21
  468.7 28.6 %collective-permute-start.113 = (bf16[128,240]{0,1:T(8,128)(2,1)S(1)}, bf16[128,240]{0,1:T(8,128)(2,1)S(1)}, u32[]{:S(2)}, u32[]{:S(2)}) collective-permute-start(bf16[128,240]{0,1:T(8,128)(2,1)S(1)} %copy-done.131), channel_id=1, source_target_pairs={{0,1},{1,0},{2,3},{3,2},{4,5},{5,4},{6,7},{7,6},{8,9},{9,8},{10,11... | collective-permute-start | bytes 184328 | tf_op jit(solution)/shard_map/ppermute | solution.py:21
  506.3 23.9 %collective-permute-start.66 = (bf16[128,1600]{0,1:T(8,128)(2,1)}, bf16[128,1600]{0,1:T(8,128)(2,1)}, u32[]{:S(2)}, u32[]{:S(2)}) collective-permute-start(bf16[128,1600]{0,1:T(8,128)(2,1)} %pad_maximum_fusion.13), channel_id=1, source_target_pairs={{0,1},{1,0},{2,3},{3,2},{4,5},{5,4},{6,7},{7,6},{8,9},{9,8},{10,11... | collective-permute-start | bytes 1228808 | tf_op jit(solution)/shard_map/ppermute | solution.py:21
  533.7 51.5 %collective-permute-start.124 = (bf16[256,2560]{1,0:T(8,128)(2,1)}, bf16[256,2560]{1,0:T(8,128)(2,1)S(1)}, u32[]{:S(2)}, u32[]{:S(2)}) collective-permute-start(bf16[256,2560]{1,0:T(8,128)(2,1)} %collective-permute-done.120), channel_id=1, source_target_pairs={{0,1},{1,0},{2,3},{3,2},{4,5},{5,4},{6,7},{7,6},{8,9},{9,8},{10,11... | collective-permute-start | bytes 3932168 | tf_op jit(solution)/shard_map/ppermute | solution.py:21
  582.6 40.0 %collective-permute-start.80 = (bf16[15,1600]{1,0:T(8,128)(2,1)}, bf16[15,1600]{1,0:T(8,128)(2,1)}, u32[]{:S(2)}, u32[]{:S(2)}) collective-permute-start(bf16[15,1600]{1,0:T(8,128)(2,1)} %slice.672), channel_id=1, source_target_pairs={{0,8},{8,16},{16,24},{24,28},{28,20},{20,12},{12,4},{4,0},{1,9},{9... | collective-permute-start | bytes 144008 | tf_op jit(solution)/shard_map/ppermute | solution.py:30
  583.4 39.2 %collective-permute-start.84 = (bf16[15,1600]{1,0:T(8,128)(2,1)}, bf16[15,1600]{1,0:T(8,128)(2,1)}, u32[]{:S(2)}, u32[]{:S(2)}) collective-permute-start(bf16[15,1600]{1,0:T(8,128)(2,1)} %slice.673), channel_id=1, source_target_pairs={{0,4},{8,0},{16,8},{24,16},{28,24},{20,28},{12,20},{4,12},{1,5},{9... | collective-permute-start | bytes 144008 | tf_op jit(solution)/shard_map/ppermute | solution.py:30
  (292 other events, 2332.1 us)

commit v2 on v1

v2 whole, which is shorter than its diff:
```python
import functools

import jax
import jax.numpy as jnp
from jax import lax
from jax.experimental import pallas as pl
from jax.experimental.pallas import tpu as pltpu
from jax.sharding import PartitionSpec as P

QH = 15
KVH = 5
GQ = QH // KVH
HS = 64
SEQS = 8
REPEATS = 2
WA = 4
BLK = 128
D = 960
SL = D // WA
KV = KVH * HS
QKV = 2 * KV + D
FFQ = 640
R3 = GQ * BLK

epsilon = 1e-05
masked_score = -1e30
rope_base = 10000.0
bf16 = jnp.bfloat16
f32 = jnp.float32
i32 = jnp.int32
MB = 1 << 20


def swap(x, mask):
    return lax.ppermute(x, "wa", [(i, i ^ mask) for i in range(WA)])


def side_swap(x, n):
    return lax.ppermute(x, "ctx", [(i, i ^ 1) for i in range(n)])


def ring_order(n):
    return [i for i in range(0, n, 2)] + [i for i in range(n - 1, 0, -2)]


def ring_shift(x, n, step):
    order = ring_order(n)
    return lax.ppermute(x, "ctx", [(order[i], order[(i + step) % n]) for i in range(n)])


def ring_position(r, n):
    return jnp.where(r % 2 == 0, r // 2, n - 1 - r // 2)


def ring_device(p, n):
    return jnp.where(p < n // 2, 2 * p, 2 * (n - 1 - p) + 1)


def ring_gather(x, n):
    half = n // 2
    rows = x.shape[0] // 2
    ahead = [x]
    behind = [x]
    for _ in range(half - 1):
        ahead.append(ring_shift(ahead[-1], n, 1))
        behind.append(ring_shift(behind[-1], n, -1))
    far = jnp.concatenate(
        [ring_shift(ahead[-1][:rows], n, 1), ring_shift(behind[-1][rows:], n, -1)], axis=0
    )
    return ahead + [far] + behind[:0:-1]


def add_low(x, y):
    return (x.astype(f32) + y.astype(f32)).astype(bf16)


def ring_scatter(piece, n):
    half = n // 2
    far = piece(half)
    rows = far.shape[0] // 2
    go = ring_shift(far[:rows], n, 1)
    back = ring_shift(far[rows:], n, -1)
    own = piece(half + 1)
    go = jnp.concatenate([add_low(own[:rows], go), own[rows:]], axis=0)
    own = piece(half - 1)
    back = jnp.concatenate([own[:rows], add_low(own[rows:], back)], axis=0)
    for k in range(half - 2, 0, -1):
        go = add_low(ring_shift(go, n, 1), piece(n - k))
        back = add_low(ring_shift(back, n, -1), piece(k))
    go = ring_shift(go, n, 1)
    back = ring_shift(back, n, -1)
    return piece(0), go, back


def ring_sum(pieces, n, position):
    def piece(k):
        return lax.dynamic_index_in_dim(pieces, (position - k) % n, 0, keepdims=False)

    own, go, back = ring_scatter(piece, n)
    mine = (own.astype(f32) + go.astype(f32) + back.astype(f32)).astype(bf16)
    return ring_gather(mine, n)


def placed(gathered, n, position):
    out = jnp.zeros((n,) + gathered[0].shape, bf16)
    for k in range(n):
        out = lax.dynamic_update_index_in_dim(out, gathered[k], (position - k) % n, 0)
    return out


def all_sum(x, n):
    for mask in (1, 2):
        x = x + swap(x, mask)
    step = 1
    while step < n:
        x = x + lax.ppermute(x, "ctx", [(i, i ^ step) for i in range(n)])
        step *= 2
    return x


def everyone(x):
    side = swap(x, 1)
    across = swap(x, 2)
    return [x, side, across, swap(across, 1)]


def own_slices(chunks, w):
    out = []
    for mask in range(WA):
        part = jnp.stack(
            [lax.dynamic_index_in_dim(c, w ^ mask, 0, keepdims=False) for c in chunks]
        )
        out.append(swap(part, mask) if mask else part)
    return out


VMEM = pl.BlockSpec(memory_space=pltpu.VMEM)
SMEM = pl.BlockSpec(memory_space=pltpu.SMEM)


def call(body, name, n_scalar, ins, outs, scratch=(), flops=0, limit=40):
    size = sum(x.size * x.dtype.itemsize for x in list(ins) + list(outs))
    return pl.pallas_call(
        body,
        name=name,
        in_specs=[SMEM] * n_scalar + [VMEM] * (len(ins) - n_scalar),
        out_specs=[VMEM] * len(outs),
        out_shape=list(outs),
        scratch_shapes=list(scratch),
        cost_estimate=pl.CostEstimate(flops=flops, transcendentals=0, bytes_accessed=size),
        compiler_params=pltpu.CompilerParams(vmem_limit_bytes=limit * MB),
    )(*ins)


def shape(dims, dtype):
    return jax.ShapeDtypeStruct(dims, dtype)


def mm(a, b):
    return jnp.dot(a, b, preferred_element_type=f32)


def nt(a, b):
    return lax.dot_general(a, b, (((1,), (1,)), ((), ())), preferred_element_type=f32)


def tn(a, b):
    return lax.dot_general(a, b, (((0,), (0,)), ((), ())), preferred_element_type=f32)


def turn(u):
    lane = lax.broadcasted_iota(i32, u.shape, 1) % HS
    return jnp.where(lane < HS // 2, -pltpu.roll(u, 128 - HS // 2, 1), pltpu.roll(u, HS // 2, 1))


def turn_back(u):
    lane = lax.broadcasted_iota(i32, u.shape, 1) % HS
    return jnp.where(lane < HS // 2, pltpu.roll(u, 128 - HS // 2, 1), -pltpu.roll(u, HS // 2, 1))


def rope(u, cos, sin):
    return u * cos + turn(u) * sin


def rope_back(u, cos, sin):
    return u * cos + turn_back(u * sin)


def head_only(tables):
    cos, sin = tables
    lane = lax.broadcasted_iota(i32, cos.shape, 1)
    return jnp.where(lane < HS, cos, 1.0), jnp.where(lane < HS, sin, 0.0)


def project_body(n_in, sc, *refs):
    xs = refs[:n_in]
    gain, cos_ref, sin_ref, p0, p1, p2, p3 = refs[n_in : n_in + 7]
    x_ref, a4, q3, kv, acc_ref = refs[n_in + 7 :]
    x = xs[0][...].astype(f32)
    for r in xs[1:]:
        x = x + r[...]
    x_ref[...] = x
    ratio = lax.rsqrt(jnp.mean(x * x, axis=1, keepdims=True) + epsilon)
    a = (x * ratio * gain[...]).astype(bf16)
    for j in range(WA):
        a4[j] = a[:, SL * j : SL * (j + 1)]
    acc = None
    for m, p in enumerate((p0, p1, p2, p3)):
        part = mm(a4[sc[0] ^ m], p[...])
        acc = part if acc is None else acc + part
    acc_ref[:, :QKV] = acc
    cos, sin = cos_ref[...], sin_ref[...]
    edge = head_only((cos, sin))
    for i in range(2):
        kv[:, 128 * i : 128 * (i + 1)] = rope(acc_ref[:, 128 * i : 128 * (i + 1)], cos, sin).astype(bf16)
    kv[:, 256:384] = rope(acc_ref[:, 256:384], *edge).astype(bf16)
    kv[:, 384:640] = acc_ref[:, 384:640].astype(bf16)
    for i in range(8):
        lo = 2 * KV + 128 * i
        u = rope(acc_ref[:, lo : lo + 128], cos, sin).astype(bf16) * bf16(0.125)
        for j in range(2):
            h = 2 * i + j
            if h < QH:
                q3[h // GQ, BLK * (h % GQ) : BLK * (h % GQ + 1), :] = u[:, HS * j : HS * (j + 1)]


def project(scal, xs, gain, tables, parts):
    return call(
        functools.partial(project_body, len(xs)),
        "project",
        1,
        [scal, *xs, gain, *tables, *parts],
        [
            shape((BLK, D), f32),
            shape((WA, BLK, SL), bf16),
            shape((KVH, R3, HS), bf16),
            shape((BLK, 2 * KV), bf16),
        ],
        [pltpu.VMEM((BLK, QKV + 64), f32)],
        flops=2 * BLK * D * QKV,
    )


def list_blocks(sched, lst, n):
    def step(k, count):
        first = sched[k] * BLK
        seen = (sched[k] <= sched[0]) & (first + BLK > sched[n])

        @pl.when(seen)
        def _():
            lst[count] = k

        return count + seen.astype(i32)

    return lax.fori_loop(0, n, step, jnp.int32(0))


def block_bias(sched, qinfo, k):
    key = sched[k] * BLK + lax.broadcasted_iota(i32, (BLK, R3), 0)
    ok = (key <= qinfo[0:1, :]) & (key >= qinfo[1:2, :])
    return jnp.where(ok, 0.0, masked_score).astype(f32)


def attend_body(n, sc, sched, qinfo, q3, kv, x, gain, p0, p1, p2, p3, *refs):
    ol4, o_t, lse, m_ref, b_ref, b4, lst, s_scr, bias, o_scr = refs
    count = list_blocks(sched, lst, n)

    @pl.loop(0, count)
    def _(i):
        bias[i] = block_bias(sched, qinfo, lst[i])

    for h in range(KVH):
        q = q3[h]

        def first(i, top):
            keys = kv[lst[i], :, HS * h : HS * (h + 1)]
            s = nt(keys, q) + bias[i]
            s_scr[i] = s
            return jnp.maximum(top, jnp.max(s.reshape(BLK // 8, 8, R3), axis=0))

        top = lax.fori_loop(0, count, first, jnp.full((8, R3), masked_score, f32))
        top = jnp.max(top, axis=0, keepdims=True)

        def second(i, state):
            total, out = state
            p = jnp.exp(s_scr[i] - top)
            total = total + jnp.sum(p.reshape(BLK // 8, 8, R3), axis=0)
            values = kv[lst[i], :, KV + HS * h : KV + HS * (h + 1)]
            return total, out + tn(values, p.astype(bf16))

        total, out = lax.fori_loop(
            0, count, second, (jnp.zeros((8, R3), f32), jnp.zeros((HS, R3), f32))
        )
        total = jnp.sum(total, axis=0, keepdims=True)
        out = out * (1.0 / total)
        o_t[h] = out
        lse[h : h + 1, :] = top + jnp.log(total)
        rows = out.T
        for g in range(GQ):
            j = GQ * h + g
            o_scr[:, HS * j : HS * (j + 1)] = rows[BLK * g : BLK * (g + 1), :]
    low = o_scr[...].astype(bf16)
    for j in range(WA):
        ol4[j] = low[:, SL * j : SL * (j + 1)]
    m = x[...]
    for k, p in enumerate((p0, p1, p2, p3)):
        m = m + mm(ol4[sc[0] ^ k], p[...])
    m_ref[...] = m
    ratio = lax.rsqrt(jnp.mean(m * m, axis=1, keepdims=True) + epsilon)
    b = (m * ratio * gain[...]).astype(bf16)
    b_ref[...] = b
    for j in range(WA):
        b4[j] = b[:, SL * j : SL * (j + 1)]


def attend(scal, sched, qinfo, q3, kv, x, gain, parts):
    n = kv.shape[0]
    return call(
        functools.partial(attend_body, n),
        "attend",
        2,
        [scal, sched, qinfo, q3, kv, x, gain, *parts],
        [
            shape((WA, BLK, SL), bf16),
            shape((KVH, HS, R3), f32),
            shape((8, R3), f32),
            shape((BLK, D), f32),
            shape((BLK, D), bf16),
            shape((WA, BLK, SL), bf16),
        ],
        [
            pltpu.SMEM((n,), i32),
            pltpu.VMEM((n, BLK, R3), f32),
            pltpu.VMEM((n, BLK, R3), f32),
            pltpu.VMEM((BLK, D), f32),
        ],
        flops=2 * BLK * D * D + 4 * BLK * D * 6 * BLK,
        limit=24 if n <= 8 else 60,
    )


def hidden_units(sc, chunk_of, keep, core, y_mine, y_other, which, j, is_mine):
    pass


def mlp_body(sc, b_own, b_side, keep, core, ym, yo, d_own, d_far, *refs):
    z_ref, gu_ref, y_own, y_side, bs = refs
    w = sc[0]
    for half, b in enumerate((b_own, b_side)):
        for j in range(WA):
            bs[j, BLK * half : BLK * (half + 1), :] = b[:, SL * j : SL * (j + 1)]
    for t, far in ((sc[1], ym), (1 - sc[1], yo)):
        lin = []
        for gu in range(2):
            acc = mm(bs[w], keep[gu, t]) + mm(bs[w ^ 1], core[gu, t])
            acc = acc + mm(bs[w ^ 2], far[gu, 0]) + mm(bs[w ^ 3], far[gu, 1])
            gu_ref[gu, t] = acc
            lin.append(acc)
        gate, up = lin
        z_ref[t] = (gate / (1.0 + jnp.exp(-gate)) * up).astype(bf16)
    row = sc[2]
    out = mm(z_ref[row], d_own[...]) + mm(z_ref[1 - row], d_far[...])
    y_own[...] = out[:BLK]
    y_side[...] = out[BLK:]


def mlp(scal, b_own, b_side, wts):
    return call(
        mlp_body,
        "mlp",
        1,
        [scal, b_own, b_side, *wts],
        [
            shape((2, 2 * BLK, FFQ), bf16),
            shape((2, 2, 2 * BLK, FFQ), f32),
            shape((BLK, D), f32),
            shape((BLK, D), f32),
        ],
        [pltpu.VMEM((WA, 2 * BLK, SL), bf16)],
        flops=2 * 2 * BLK * 3 * D * 2 * FFQ,
        limit=56,
    )


def mlp_back_body(sc, l_own, l_side, gu_ref, keep, core, ym, yo, d_own, d_far, *refs):
    pair, db_own, db_side, low, acc = refs
    w, row = sc[0], sc[2]
    low[:BLK] = l_own[...]
    low[BLK:] = l_side[...]
    for first, (t, far) in enumerate(((sc[1], ym), (1 - sc[1], yo))):
        ds = []
        dz = jnp.where(t == row, nt(low[...], d_own[...]), nt(low[...], d_far[...]))
        gate, up = gu_ref[0, t], gu_ref[1, t]
        sig = 1.0 / (1.0 + jnp.exp(-gate))
        dg = (dz * up * sig * (1.0 + gate * (1.0 - sig))).astype(bf16)
        du = (dz * gate * sig).astype(bf16)
        lo = pl.multiple_of(t * FFQ, 128)
        pair[:, pl.ds(lo, FFQ)] = dg
        lo = pl.multiple_of(t * FFQ + 2 * FFQ, 128)
        pair[:, pl.ds(lo, FFQ)] = du
        for j, p in ((w, keep.at[0, t]), (w ^ 1, core.at[0, t]), (w ^ 2, far.at[0, 0]), (w ^ 3, far.at[0, 1])):
            part = nt(dg, p[...])
            acc[j] = part if first == 0 else acc[j] + part
        for j, p in ((w, keep.at[1, t]), (w ^ 1, core.at[1, t]), (w ^ 2, far.at[1, 0]), (w ^ 3, far.at[1, 1])):
            acc[j] = acc[j] + nt(du, p[...])
    for j in range(WA):
        db_own[:, SL * j : SL * (j + 1)] = acc[j, :BLK, :]
        db_side[:, SL * j : SL * (j + 1)] = acc[j, BLK:, :]


def mlp_back(scal, l_own, l_side, gu, wts):
    return call(
        mlp_back_body,
        "mlp_back",
        1,
        [scal, l_own, l_side, gu, *wts],
        [shape((2 * BLK, 4 * FFQ), bf16), shape((BLK, D), f32), shape((BLK, D), f32)],
        [pltpu.VMEM((2 * BLK, D), bf16), pltpu.VMEM((WA, 2 * BLK, SL), f32)],
        flops=2 * 2 * BLK * 3 * D * 2 * FFQ,
        limit=56,
    )


def norm_back(grads, hidden, gain):
    ratio = lax.rsqrt(jnp.mean(hidden * hidden, axis=1, keepdims=True) + epsilon)
    scaled = hidden * ratio
    gain_grad = jnp.sum(grads * scaled, axis=0, keepdims=True)
    inner = grads * gain
    out = ratio * (inner - scaled * jnp.mean(inner * scaled, axis=1, keepdims=True))
    return out, gain_grad


def attend_back_body(n, sc, sched, qinfo, dy, db_own, db_got, m, gain, p0, p1, p2, p3, q3, kv, o_t, lse, cos_ref, sin_ref, *refs):
    dm_ref, dml_ref, gg, dq_ref, dkv_ref, lst, do3, d_scr, dq_scr = refs
    count = list_blocks(sched, lst, n)
    part, gain_grad = norm_back(db_own[...] + db_got[...], m[...], gain[...])
    gg[...] = gain_grad
    dm = dy[...].astype(f32) + part
    dm_ref[...] = dm
    dml = dm.astype(bf16)
    dml_ref[...] = dml
    for k, p in enumerate((p0, p1, p2, p3)):
        d_scr[sc[0] ^ k] = nt(dml, p[...]).astype(bf16).astype(f32)
    whole = jnp.concatenate([d_scr[j] for j in range(WA)], axis=1)
    for j in range(QH):
        do3[j // GQ, BLK * (j % GQ) : BLK * (j % GQ + 1), :] = whole[:, HS * j : HS * (j + 1)].astype(bf16)

    @pl.loop(1, n)
    def _(k):
        seen = (sched[k] <= sched[0]) & (sched[k] * BLK + BLK > sched[n])

        @pl.when(jnp.logical_not(seen))
        def _():
            dkv_ref[k] = jnp.zeros((BLK, 2 * KV), bf16)

    for h in range(KVH):
        q = q3[h]
        do = do3[h]
        delta = jnp.sum(do.astype(f32).T * o_t[h], axis=0, keepdims=True)
        log_total = lse[h : h + 1, :]

        def step(i, dq):
            k = lst[i]
            keys = kv[k, :, HS * h : HS * (h + 1)]
            values = kv[k, :, KV + HS * h : KV + HS * (h + 1)]
            s = nt(keys, q) + block_bias(sched, qinfo, k)
            p = jnp.exp(s - log_total)
            ds = (p * (nt(values, do) - delta)).astype(bf16)
            dkv_ref[k, :, HS * h : HS * (h + 1)] = mm(ds, q).astype(bf16)
            dkv_ref[k, :, KV + HS * h : KV + HS * (h + 1)] = mm(p.astype(bf16), do).astype(bf16)
            return dq + tn(keys, ds)

        dq = lax.fori_loop(0, count, step, jnp.zeros((HS, R3), f32))
        rows = (dq * 0.125).T
        for g in range(GQ):
            j = GQ * h + g
            dq_scr[:, HS * j : HS * (j + 1)] = rows[BLK * g : BLK * (g + 1), :]
    cos, sin = cos_ref[...], sin_ref[...]
    for i in range(8):
        u = rope_back(dq_scr[:, 128 * i : 128 * (i + 1)], cos, sin).astype(bf16)
        if i < 7:
            dq_ref[:, 128 * i : 128 * (i + 1)] = u
        else:
            dq_ref[:, 128 * i :] = u[:, :HS]


def attend_back(scal, sched, qinfo, dy, db_own, db_got, m, gain, parts, q3, kv, o_t, lse, tables):
    n = kv.shape[0]
    return call(
        functools.partial(attend_back_body, n),
        "attend_back",
        2,
        [scal, sched, qinfo, dy, db_own, db_got, m, gain, *parts, q3, kv, o_t, lse, *tables],
        [
            shape((BLK, D), f32),
            shape((BLK, D), bf16),
            shape((1, D), f32),
            shape((BLK, D), bf16),
            shape((n, BLK, 2 * KV), bf16),
        ],
        [
            pltpu.SMEM((n,), i32),
            pltpu.VMEM((KVH, R3, HS), bf16),
            pltpu.VMEM((WA, BLK, SL), f32),
            pltpu.VMEM((BLK, D + 64), f32),
        ],
        flops=2 * BLK * D * D + 10 * BLK * D * 6 * BLK,
        limit=24 if n <= 8 else 60,
    )


def query_back_body(sc, dq, p0, p1, p2, p3, da):
    for k, p in enumerate((p0, p1, p2, p3)):
        da[sc[0] ^ k] = nt(dq[...], p[:, 2 * KV :])


def query_back(scal, dq, parts):
    return call(
        query_back_body,
        "query_back",
        1,
        [scal, dq, *parts],
        [shape((WA, BLK, SL), f32)],
        flops=2 * BLK * D * D,
    )[0]


def project_back_body(sc, own, go, back, cos_ref, sin_ref, da, p0, p1, p2, p3, x, dm, gain, *refs):
    dkv_ref, dx_ref, dxl_ref, gg, d4 = refs
    total = own[...].astype(f32) + go[...].astype(f32) + back[...].astype(f32)
    cos, sin = cos_ref[...], sin_ref[...]
    edge = head_only((cos, sin))
    for i in range(2):
        dkv_ref[:, 128 * i : 128 * (i + 1)] = rope_back(total[:, 128 * i : 128 * (i + 1)], cos, sin).astype(bf16)
    dkv_ref[:, 256:384] = rope_back(total[:, 256:384], *edge).astype(bf16)
    dkv_ref[:, 384:] = total[:, 384:].astype(bf16)
    for k, p in enumerate((p0, p1, p2, p3)):
        d4[sc[0] ^ k] = da[sc[0] ^ k] + nt(dkv_ref[...], p[:, : 2 * KV])
    grads = jnp.concatenate([d4[j] for j in range(WA)], axis=1)
    part, gain_grad = norm_back(grads, x[...], gain[...])
    gg[...] = gain_grad
    dx = dm[...] + part
    dx_ref[...] = dx
    dxl_ref[...] = dx.astype(bf16)


def project_back(scal, addends, tables, da, parts, x, dm, gain):
    return call(
        project_back_body,
        "project_back",
        1,
        [scal, *addends, *tables, da, *parts, x, dm, gain],
        [
            shape((BLK, 2 * KV), bf16),
            shape((BLK, D), f32),
            shape((BLK, D), bf16),
            shape((1, D), f32),
        ],
        [pltpu.VMEM((WA, BLK, SL), f32)],
        flops=2 * BLK * D * 2 * KV,
    )


def grad_rows_body(kind, n_low, has_prev, *refs):
    slices = refs[:WA]
    lows = refs[WA : WA + n_low]
    per = n_low // WA
    rest = refs[WA + n_low :]
    out = rest[-1]
    lo = 0
    for t in range(per):
        acc = None
        for m in range(WA):
            part = tn(slices[m][kind], lows[per * m + t][...])
            acc = part if acc is None else acc + part
        width = acc.shape[1]
        if has_prev:
            acc = acc + rest[0][:, lo : lo + width]
            out[:SL, lo : lo + width] = acc.astype(bf16)
        else:
            out[:, lo : lo + width] = acc
        lo += width
    if has_prev:
        out[SL:, :] = jnp.zeros((256 - SL, lo), bf16)


def grad_rows(kind, slices, lows, prev):
    flat = [x for group in lows for x in group]
    cols = sum(x.shape[1] for x in lows[0])
    has_prev = prev is not None
    return call(
        functools.partial(grad_rows_body, kind, len(flat), has_prev),
        "grad_rows",
        0,
        [*slices, *flat] + ([prev] if has_prev else []),
        [shape((256, cols), bf16) if has_prev else shape((SL, cols), f32)],
        flops=2 * WA * BLK * SL * cols,
    )[0]


def grad_gate_body(kind, has_prev, s0, s1, s2, s3, own, side, far, diag, *refs):
    out = refs[-1]
    slices = (s0, s1, s2, s3)
    for t in range(8):
        near, off = (own, far) if t < 4 else (side, diag)
        flip = 0 if t < 4 else 1
        lo = FFQ * (t % 4)
        acc = None
        for m in range(WA):
            src = near if m < 2 else off
            r = BLK * ((m % 2) ^ flip)
            part = tn(slices[m][kind], src[r : r + BLK, lo : lo + FFQ])
            acc = part if acc is None else acc + part
        if has_prev:
            acc = acc + refs[0][t]
        out[t] = acc.astype(out.dtype)


def grad_gate(kind, slices, pairs, prev):
    has_prev = prev is not None
    return call(
        functools.partial(grad_gate_body, kind, has_prev),
        "grad_gate",
        0,
        [*slices, *pairs] + ([prev] if has_prev else []),
        [shape((8, SL, FFQ), bf16 if has_prev else f32)],
        flops=2 * WA * BLK * SL * 8 * FFQ,
        limit=48,
    )[0]


def grad_down_body(has_prev, sc, z, z_far, l0, l1, l2, l3, *refs):
    out = refs[-1]
    acc = tn(z[sc[2], :BLK], l0[...]) + tn(z[sc[2], BLK:], l1[...])
    acc = acc + tn(z_far[:BLK], l2[...]) + tn(z_far[BLK:], l3[...])
    if has_prev:
        acc = acc + refs[0][...]
    out[...] = acc.astype(out.dtype)


def grad_down(scal, z, z_far, lows, prev):
    has_prev = prev is not None
    return call(
        functools.partial(grad_down_body, has_prev),
        "grad_down",
        1,
        [scal, z, z_far, *lows] + ([prev] if has_prev else []),
        [shape((FFQ, D), bf16 if has_prev else f32)],
        flops=2 * WA * BLK * FFQ * D,
        limit=32,
    )[0]


def finish_gate_body(n, sc, *refs):
    gate, up = refs[n], refs[n + 1]
    position, core = sc[3], sc[4]
    for k in range(n):
        p = (position - k + n) % n
        low = jnp.where(p < 4, core, 1 - core)
        lo = pl.multiple_of(FFQ * (2 * (p % 2) + low), 128)
        is_up = (p // 2) % 2

        @pl.when(is_up == 0)
        def _():
            gate[:, pl.ds(lo, FFQ)] = refs[k][...].astype(f32)

        @pl.when(is_up == 1)
        def _():
            up[:, pl.ds(lo, FFQ)] = refs[k][...].astype(f32)


def finish_gate(scal, gathered):
    return call(
        functools.partial(finish_gate_body, len(gathered)),
        "finish_gate",
        1,
        [scal, *gathered],
        [shape((SL, 4 * FFQ), f32)] * 2,
    )


def finish_rows_body(n, widths, sc, *refs):
    outs = refs[n:]
    for k in range(n):
        p = (sc[3] - k + n) % n
        rows = refs[k].shape[0]
        tail = SL - rows * (n - 1)
        first = pl.multiple_of(p * rows, 8)

        @pl.when(p < n - 1)
        def _():
            lo = 0
            for out, width in zip(outs, widths):
                out[pl.ds(first, rows), :] = refs[k][:, lo : lo + width].astype(f32)
                lo += width

        @pl.when(p == n - 1)
        def _():
            lo = 0
            for out, width in zip(outs, widths):
                out[rows * (n - 1) :, :] = refs[k][:tail, lo : lo + width].astype(f32)
                lo += width


def finish_rows(scal, gathered, widths):
    return call(
        functools.partial(finish_rows_body, len(gathered), tuple(widths)),
        "finish_rows",
        1,
        [scal, *gathered],
        [shape((SL, width), f32) for width in widths],
    )


def token_layout(segment_row, order_row, block_size):
    labels = jnp.arange(SEQS, dtype=i32)
    segment_sizes = jnp.sum((segment_row[None, :] == labels[:, None]).astype(i32), axis=1)
    segment_start = jnp.cumsum(segment_sizes) - segment_sizes
    return segment_start


def body(
    tokens,
    cotangent,
    segment_ids,
    block_order,
    gain_attn,
    w_query,
    key_projection,
    value_projection,
    w_out,
    gain_mlp,
    w_gate,
    w_up,
    w_down,
):
    n = block_order.shape[1]
    w = lax.axis_index("wa")
    r = lax.axis_index("ctx")
    core = w % 2
    row = w // 2
    position = ring_position(r, n)
    x_side = r % 2
    scal = jnp.stack([w, x_side, row, position, core]).astype(i32)

    qkv_own = jnp.concatenate([key_projection, value_projection, w_query], axis=1).astype(bf16)
    gains_own = jnp.stack([gain_attn, gain_mlp])
    qkv_across = swap(qkv_own, 2)
    qkv_side = swap(qkv_own, 1)
    qkv_parts = [qkv_own, qkv_side, qkv_across, swap(qkv_across, 1)]
    gains_parts = jnp.stack(everyone(gains_own.astype(bf16)))
    gains = jnp.concatenate(
        [lax.dynamic_index_in_dim(gains_parts, w ^ j, 0, keepdims=False) for j in range(WA)], axis=1
    ).astype(f32)
    gain_a, gain_m = gains[0:1], gains[1:2]

    blocks = ring_device((position - jnp.arange(n, dtype=i32)) % n, n)
    labels = jnp.arange(n, dtype=i32)
    order_row = block_order[0]
    anchors = jnp.sum(jnp.where(blocks[:, None] == labels[None, :], order_row[None, :], 0), axis=1)
    natural = anchors[0] * BLK + jnp.arange(BLK, dtype=i32)
    seg_labels = jnp.arange(SEQS, dtype=i32)
    sizes = jnp.sum((segment_ids[0][None, :] == seg_labels[:, None]).astype(i32), axis=1)
    before = (seg_labels[None, :] < seg_labels[:, None]).astype(i32)
    starts = jnp.sum(before * sizes[None, :], axis=1)
    start_of = jnp.max(jnp.where(starts[None, :] <= natural[:, None], starts[None, :], 0), axis=1)
    sched = jnp.concatenate([anchors, start_of[:1]]).astype(i32)
    qinfo = jnp.pad(
        jnp.stack([jnp.tile(natural, GQ), jnp.tile(start_of, GQ)]), ((0, 6), (0, 0))
    ).astype(i32)
    frequency = rope_base ** (-jnp.arange(HS // 2, dtype=f32) * 2.0 / HS)
    angles = (natural - start_of).astype(f32)[:, None] * frequency[None, :]
    tables = (jnp.tile(jnp.cos(angles), (1, 4)), jnp.tile(jnp.sin(angles), (1, 4)))

    out_parts = everyone(w_out.astype(bf16))
    gate_up = jnp.stack([w_gate, w_up]).astype(bf16).reshape(2, SL, 2, 2, FFQ).transpose(3, 0, 2, 1, 4)
    keep = lax.dynamic_index_in_dim(gate_up, core, 0, keepdims=False)
    core_part = swap(lax.dynamic_index_in_dim(gate_up, 1 - core, 0, keepdims=False), 1)
    give = jnp.stack(
        [
            lax.dynamic_index_in_dim(keep, x_side, 1, keepdims=False),
            lax.dynamic_index_in_dim(core_part, x_side, 1, keepdims=False),
        ],
        axis=1,
    )
    y_mine = swap(give, 2)
    y_other = side_swap(y_mine, n)
    down_own = w_down.astype(bf16)
    down_far = swap(down_own, 2)
    ff_parts = [keep, core_part, y_mine, y_other, down_own, down_far]

    xs = [tokens[0]]
    kept = []
    for repeat_index in range(REPEATS):
        x, a4, q3, kv = project(scal, xs, gain_a, tables, qkv_parts)
        every = jnp.stack(ring_gather(kv, n))
        ol4, o_t, lse, m, b, b4 = attend(scal, sched, qinfo, q3, every, x, gain_m, out_parts)
        z, gu, y_own, y_side = mlp(scal, b, swap(b, 1), ff_parts)
        xs = [m, y_own, swap(y_side, 1)]
        slices = own_slices([a4, ol4, b4], w)
        z_far = swap(lax.dynamic_index_in_dim(z, 1 - row, 0, keepdims=False), 2)
        kept.append((x, q3, every, o_t, lse, m, gu, z, z_far, slices))
    output = (xs[0] + xs[1] + xs[2]).astype(bf16)[None]

    dy = cotangent[0]
    low = cotangent[0]
    prev = [None] * 4
    gain_sums = []
    for x, q3, every, o_t, lse, m, gu, z, z_far, slices in reversed(kept):
        low_side = swap(low, 1)
        pair, db_own, db_side = mlp_back(scal, low, low_side, gu, ff_parts)
        db_got = swap(db_side, 1)
        low_far = swap(low, 2)
        lows = [low, low_side, low_far, swap(low_far, 1)]
        down_grad = grad_down(scal, z, z_far, lows, prev[0])
        pair_far = swap(pair, 2)
        pairs = [pair, swap(pair, 1), pair_far, swap(pair_far, 1)]
        gate_grad = grad_gate(2, slices, pairs, prev[1])
        dm, dml, gain_m_grad, dq, dkv = attend_back(
            scal, sched, qinfo, dy, db_own, db_got, m, gain_m, out_parts, q3, every, o_t, lse, tables
        )
        addends = ring_scatter(lambda k: dkv[k], n)
        da = query_back(scal, dq, qkv_parts)
        dkv0, dx, low, gain_a_grad = project_back(
            scal, addends, tables, da, qkv_parts, x, dm, gain_a
        )
        dy = dx
        out_grad = grad_rows(1, slices, [[t] for t in everyone(dml)], prev[2])
        dqs = everyone(dq)
        dkvs = everyone(dkv0)
        qkv_grad = grad_rows(0, slices, [[dkvs[i], dqs[i]] for i in range(WA)], prev[3])
        prev = [down_grad, gate_grad, out_grad, qkv_grad]
        gain_sums.append(jnp.concatenate([gain_a_grad, gain_m_grad], axis=0))
    input_grad = low[None]
    down_grad, gate_grad, out_grad, qkv_grad = prev

    gain_sum = lax.dynamic_slice_in_dim(all_sum(gain_sums[0] + gain_sums[1], n), w * SL, SL, 1)
    down_total = placed(
        ring_sum(down_grad.reshape(n, FFQ // n, D), n, position), n, position
    ).reshape(FFQ, D).astype(f32)
    gate_all = ring_sum(gate_grad.reshape(n, SL * 8 // n, FFQ), n, position)
    out_all = ring_sum(out_grad.reshape(n, 256 // n, D), n, position)
    qkv_all = ring_sum(qkv_grad.reshape(n, 256 // n, QKV), n, position)
    if n == 8:
        gate_total, up_total = finish_gate(scal, gate_all)
        (out_total,) = finish_rows(scal, out_all, [D])
        key_total, value_total, query_total = finish_rows(scal, qkv_all, [KV, KV, D])
    else:
        whole = placed(gate_all, n, position).reshape(2, 2, 2, SL, FFQ)
        low_half = jnp.where(core == 0, whole[0], whole[1])
        high_half = jnp.where(core == 0, whole[1], whole[0])
        gate_up_total = (
            jnp.stack([low_half, high_half], axis=2).transpose(0, 3, 1, 2, 4).reshape(2, SL, -1).astype(f32)
        )
        gate_total, up_total = gate_up_total[0], gate_up_total[1]
        out_total = placed(out_all, n, position).reshape(256, D)[:SL].astype(f32)
        qkv_total = placed(qkv_all, n, position).reshape(256, QKV)[:SL].astype(f32)
        key_total, value_total, query_total = (
            qkv_total[:, :KV],
            qkv_total[:, KV : 2 * KV],
            qkv_total[:, 2 * KV :],
        )
    return (
        output,
        input_grad,
        gain_sum[0],
        query_total,
        key_total,
        value_total,
        out_total,
        gain_sum[1],
        gate_total,
        up_total,
        down_total,
    )


def solution(mesh):
    rows = P("wa", None)
    flat = P("wa")
    act = P("wa", "ctx", None)
    return jax.shard_map(
        body,
        mesh=mesh,
        in_specs=(act, act, rows, rows, flat, rows, rows, rows, rows, flat, rows, rows, rows),
        out_specs=(act, act, flat, rows, rows, rows, rows, flat, rows, rows, rows),
        check_vma=False,
    )
```

time: 703 us -> 594 us (0.84)
  Pallas kernels: 0 us -> 143 us
  matrix products: 81.9 us -> 0 us
  local copies, waits for them, and re-layouts: 152 us -> 85.9 us
  waiting for transfers between devices: 245 us -> 194 us
  other arithmetic: 69.7 us -> 28.1 us
    pallas_call x0 -> x25, Pallas kernels: none -> 143 us  [call(): pl.pallas_call(body, name=name, in_specs=[SMEM] * n_scalar + [VMEM] * (le...]
    dot_general x42 -> x0, matrix products: 81.9 us -> none  [the longest x10 21.4 us: weight_grad(): lax.dot_general(inputs, grads, (((0,), (0,)), ((), ())), preferred_elemen...]
    ppermute x96, waiting for transfers between devices: 151 us -> 104 us  [ring_shift(): lax.ppermute(x, 'ctx', [(order[i], order[(i + step) % n]) for i in range(...]
    slice x38 -> x1, local copies, waits for them, and re-layouts: 33.3 us -> 0.01 us  [body(): gain_a, gain_m = (gains[0:1], gains[1:2])]
    unnamed x355 -> x325, local copies, waits for them, and re-layouts: 18.6 us -> 48.3 us
    convert_element_type x6 -> x1, local copies, waits for them, and re-layouts: 25.1 us -> 2.39 us  [body(): down_own = w_down.astype(bf16)]
    squeeze x14 -> x6, local copies, waits for them, and re-layouts: 20.1 us -> 3.47 us  [the longest x1 3.36 us: body(): lax.dynamic_index_in_dim(gate_up, 1 - core, 0, keepdims=False)]
    ppermute x64 -> x58, starting transfers between devices: 40.2 us -> 27.1 us  [swap(): return lax.ppermute(x, 'wa', [(i, i ^ mask) for i in range(WA)])]
  transfers between devices with their start and end apart: 163 -> 158, of which waited for: 76 -> 57; matrix products, arithmetic and copies ran while one was open for 39% -> 13% of each run, Pallas kernels for 0% -> 22%
where the time goes in v2:
time: 594 us; the launch traced here: 586 us
  waiting for transfers between devices  194 us (33%)
  Pallas kernels  143 us (24%)
  starting transfers between devices  132 us (22%)
  local copies, waits for them, and re-layouts  85.9 us (14%)
  other arithmetic  28.1 us (5%)
    pallas_call x25, Pallas kernels, call(): pl.pallas_call(body, name=name, in_specs=[SMEM] * n_scalar + [VMEM] * (le...  143 us
    ppermute x96, waiting for transfers between devices, ring_shift(): lax.ppermute(x, 'ctx', [(order[i], order[(i + step) % n]) for i in range(...  104 us
    ppermute x96, starting transfers between devices, ring_shift(): lax.ppermute(x, 'ctx', [(order[i], order[(i + step) % n]) for i in range(...  101 us
    ppermute x58, waiting for transfers between devices, swap(): return lax.ppermute(x, 'wa', [(i, i ^ mask) for i in range(WA)])  84.2 us
    unnamed x325, local copies, waits for them, and re-layouts  48.3 us
    ppermute x58, starting transfers between devices, swap(): return lax.ppermute(x, 'wa', [(i, i ^ mask) for i in range(WA)])  27.1 us
  transfers between devices with their start and end apart: 158, of which 57 were waited for; matrix products, arithmetic and copies ran while one was open for 13% of the time, Pallas kernels for 22%

profile of v2, /device:TPU:0, one launch (start us, length us, event | category | flops | bytes accessed | tf_op | source)
XLA Modules:
  0.0 585.6 jit_solution(10448410038286562102)
XLA Ops:
  11.4 3.9 stack.194
  19.1 3.9 stack.195
  25.4 3.4 dynamic-slice_bitcast_fusion
  51.4 3.7 collective-permute-done.6
  62.6 5.1 collective-permute-done.12
  69.8 37.1 %collective-permute-done.19.ym = bf16[2,2,240,640]{3,2,1,0:T(8,128)(2,1)} collective-permute-done((bf16[2,2,240,640]{3,2,1,0:T(8,128)(2,1)S(1)}, bf16[2,2,240,640]{3,2,1,0:T(8,128)(2,1)}, u32[]{:S(2)}, u32[]{:S(2)}) %collective-permute-start.19) | collective-permute-done | bytes 1228832 | tf_op jit(solution)/shard_map/ppermute | solution.py:35
  111.4 14.5 %attend.2 = (bf16[4,128,240]{2,1,0:T(8,128)(2,1)S(1)}, f32[5,64,384]{2,1,0:T(8,128)S(1)}, f32[8,384]{1,0:T(8,128)S(1)}, f32[128,960]{1,0:T(8,128)S(1)}, bf16[128...) custom-call(s32[5]{0:T(128)S(1)} %stack.173.sc, s32[9]{0:T(128)S(1)} %pad_add_fusion.1.sched, ...), custom_call_target="tpu_custom_call" | custom-call | flops 613416960 | bytes 5639992 | tf_op jit(solution)/shard_map/attend/pallas_call | solution.py:143
  132.0 4.1 collective-permute-done.20.yo
  136.1 8.1 %mlp.2 = (bf16[2,256,640]{2,1,0:T(8,128)(2,1)}, f32[2,2,256,640]{3,2,1,0:T(8,128)}, f32[128,960]{1,0:T(8,128)}, f32[128,960]{1,0:T(8,128)}) custom-call(s32[5]{0:T(128)} %copy-done.99, bf16[128,960]{1,0:T(8,128)(2,1)} %copy-done.86, bf16[128,960]{1,0:T(8,128)(2,1)} %collective-permute-done.17.b_side, bf16[2,2,240,640]{3,2,1,0:T(8,128)(2,1)} %get-tuple-element.191.keep, ...), custom_call_target="tpu_custom_call" | custom-call | flops 1887436800 | bytes 12124180 | tf_op jit(solution)/shard_map/mlp/pallas_call | solution.py:143
  154.5 4.3 collective-permute-done.23
  160.9 3.5 collective-permute-done.24
  166.4 4.8 collective-permute-done.29
  176.5 15.5 %attend.3 = (bf16[4,128,240]{2,1,0:T(8,128)(2,1)S(1)}, f32[5,64,384]{2,1,0:T(8,128)S(1)}, f32[8,384]{1,0:T(8,128)S(1)}, f32[128,960]{1,0:T(8,128)S(1)}, bf16[128...) custom-call(s32[5]{0:T(128)S(1)} %copy-done.100, s32[9]{0:T(128)S(1)} %pad_add_fusion.1.sched, s32[8,384]{1,0:T(8,128)S(1)} %pad.4.qinfo, ...), custom_call_target="tpu_custom_call" | custom-call | flops 613416960 | bytes 5639992 | tf_op jit(solution)/shard_map/attend/pallas_call | solution.py:143
  197.9 8.1 %mlp.3 = (bf16[2,256,640]{2,1,0:T(8,128)(2,1)}, f32[2,2,256,640]{3,2,1,0:T(8,128)}, f32[128,960]{1,0:T(8,128)}, f32[128,960]{1,0:T(8,128)}) custom-call(s32[5]{0:T(128)} %copy-done.99, bf16[128,960]{1,0:T(8,128)(2,1)} %get-tuple-element.78.b_own, bf16[128,960]{1,0:T(8,128)(2,1)} %collective-permute-done.31.b_side, ...), custom_call_target="tpu_custom_call" | custom-call | flops 1887436800 | bytes 12124180 | tf_op jit(solution)/shard_map/mlp/pallas_call | solution.py:143
  206.0 9.4 %mlp_back.2 = (bf16[256,2560]{1,0:T(8,128)(2,1)}, f32[128,960]{1,0:T(8,128)}, f32[128,960]{1,0:T(8,128)}) custom-call(s32[5]{0:T(128)} %copy-done.99, bf16[128,960]{1,0:T(8,128)(2,1)} %bitcast.310, bf16[128,960]{1,0:T(8,128)(2,1)} %collective-permute-done.33.l_side.l1, f32[2,2,256,640]{3,2,1,0:T(8,128)} %get-tuple-element.81.gu_ref, ...), custom_call_target="tpu_custom_call" | custom-call | flops 1887436800 | bytes 12779540 | tf_op jit(solution)/shard_map/mlp_back/pallas_call | solution.py:143
  221.5 16.2 %attend_back.2 = (f32[128,960]{1,0:T(8,128)S(1)}, bf16[128,960]{1,0:T(8,128)(2,1)}, f32[1,960]{1,0:T(1,128)S(1)}, bf16[128,960]{1,0:T(8,128)(2,1)S(1)}, bf16[8,128,640]{2,1,0:T(8,128)(2,1)S(1)}) custom-call(s32[5]{0:T(128)S(1)} %copy-done.101, s32[9]{0:T(128)S(1)} %pad_add_fusion.1.sched, s32[8,384]{1,0:T(8,128)S(1)} %pad.4.qinfo, ...), custom_call_target="tpu_custom_call" | custom-call | flops 1179648000 | bytes 8068664 | tf_op jit(solution)/shard_map/attend_back/pallas_call | solution.py:143
  246.3 3.8 collective-permute-done.40
  272.2 5.5 collective-permute-done.139.z_far
  284.6 9.3 %mlp_back.3 = (bf16[256,2560]{1,0:T(8,128)(2,1)}, f32[128,960]{1,0:T(8,128)}, f32[128,960]{1,0:T(8,128)}) custom-call(s32[5]{0:T(128)} %copy-done.99, bf16[128,960]{1,0:T(8,128)(2,1)} %copy-done.60, bf16[128,960]{1,0:T(8,128)(2,1)} %copy-done.62, f32[2,2,256,640]{3,2,1,0:T(8,128)} %get-tuple-element.91.gu_ref, ...), custom_call_target="tpu_custom_call" | custom-call | flops 1887436800 | bytes 12779540 | tf_op jit(solution)/shard_map/mlp_back/pallas_call | solution.py:143
  311.9 16.9 %attend_back.3 = (f32[128,960]{1,0:T(8,128)S(1)}, bf16[128,960]{1,0:T(8,128)(2,1)S(1)}, f32[1,960]{1,0:T(1,128)S(1)}, bf16[128,960]{1,0:T(8,128)(2,1)}, bf16[8,128,640]{2,1,0:T(8,128)(2,1)S(1)}) custom-call(s32[5]{0:T(128)S(1)} %copy-done.102, s32[9]{0:T(128)S(1)} %pad_add_fusion.1.sched, s32[8,384]{1,0:T(8,128)S(1)} %pad.4.qinfo, ...), custom_call_target="tpu_custom_call" | custom-call | flops 1179648000 | bytes 8314424 | tf_op jit(solution)/shard_map/attend_back/pallas_call | solution.py:143
  357.8 3.4 collective-permute-done.73.refs_9_
  376.7 25.8 %collective-permute-done.72.refs_8_ = bf16[128,640]{1,0:T(8,128)(2,1)S(1)} collective-permute-done((bf16[128,640]{1,0:T(8,128)(2,1)S(1)}, bf16[128,640]{1,0:T(8,128)(2,1)S(1)}, u32[]{:S(2)}, u32[]{:S(2)}) %collective-permute-start.72) | collective-permute-done | bytes 163872 | tf_op jit(solution)/shard_map/ppermute | solution.py:35
  405.1 3.6 collective-permute-done.145
  454.4 4.9 collective-permute-done.63.refs_8_
  464.2 7.2 %grad_gate.2.refs_0_ = f32[8,240,640]{2,1,0:T(8,128)} custom-call(bf16[3,128,240]{2,1,0:T(8,128)(2,1)S(1)} %copy-done.19, bf16[3,128,240]{2,1,0:T(8,128)(2,1)S(1)} %copy-done.43, bf16[3,128,240]{2,1,0:T(8,128)(2,1)S(1)} %copy-done.46, bf16[3,128,240]{2,1,0:T(8,128)(2,1)S(1)} %copy-done.49, bf16[256,2560]{1,0:T(8,128)(2,1)S(1)} %copy-done.54, ...), custom_call_target="tpu_custom_call" | custom-call | flops 1258291200 | bytes 10895360 | tf_op jit(solution)/shard_map/grad_gate/pallas_call | solution.py:143
  481.9 7.9 %grad_gate.3 = bf16[8,240,640]{2,1,0:T(8,128)(2,1)} custom-call(bf16[3,128,240]{2,1,0:T(8,128)(2,1)S(1)} %pad_maximum_fusion.4.refs_0_.s0, bf16[3,128,240]{2,1,0:T(8,128)(2,1)S(1)} %copy-done.36, bf16[3,128,240]{2,1,0:T(8,128)(2,1)S(1)} %copy-done.38, bf16[3,128,240]{2,1,0:T(8,128)(2,1)S(1)} %copy-done.40, bf16[256,2560]{1,0:T(8,128)(2,1)} %get-tuple-element.117.own, ...), custom_call_target="tpu_custom_call" | custom-call | flops 1258291200 | bytes 13352960 | tf_op jit(solution)/shard_map/grad_gate/pallas_call | solution.py:143
  501.4 5.1 collective-permute-done.121
  513.0 3.9 collective-permute-done.122
  524.0 6.8 %collective-permute-done.127 = bf16[240,640]{1,0:T(8,128)(2,1)S(1)} collective-permute-done((bf16[240,640]{1,0:T(8,128)(2,1)S(1)}, bf16[240,640]{1,0:T(8,128)(2,1)S(1)}, u32[]{:S(2)}, u32[]{:S(2)}) %collective-permute-start.127) | collective-permute-done | bytes 307232 | tf_op jit(solution)/shard_map/ppermute | solution.py:48
  538.4 7.3 %collective-permute-done.88.refs_7_ = bf16[32,1600]{1,0:T(8,128)(2,1)S(1)} collective-permute-done((bf16[32,1600]{1,0:T(8,128)(2,1)S(1)}, bf16[32,1600]{1,0:T(8,128)(2,1)S(1)}, u32[]{:S(2)}, u32[]{:S(2)}) %collective-permute-start.88) | collective-permute-done | bytes 102432 | tf_op jit(solution)/shard_map/ppermute | solution.py:48
  554.1 3.3 collective-permute-done.108.refs_3_
  581.8 3.3 finish_gate.1
  (775 shorter events, 318.6 us)
Async XLA Ops:
  2.1 38.0 %collective-permute-start.1 = (bf16[2,240]{1,0:T(2,128)(2,1)S(1)}, bf16[2,240]{1,0:T(2,128)(2,1)S(1)}, u32[]{:S(2)}, u32[]{:S(2)}) collective-permute-start(bf16[2,240]{1,0:T(2,128)(2,1)S(1)} %pad_maximum_fusion.25), channel_id=1, source_target_pairs={{0,2},{1,3},{2,0},{3,1},{4,6},{5,7},{6,4},{7,5},{8,10},{9,11},{10,... | collective-permute-start | bytes 2888 | tf_op jit(solution)/shard_map/ppermute | solution.py:35
  5.2 39.9 %collective-permute-start = (bf16[2,240]{1,0:T(2,128)(2,1)S(1)}, bf16[2,240]{1,0:T(2,128)(2,1)S(1)}, u32[]{:S(2)}, u32[]{:S(2)}) collective-permute-start(bf16[2,240]{1,0:T(2,128)(2,1)S(1)} %pad_maximum_fusion.25), channel_id=1, source_target_pairs={{0,1},{1,0},{2,3},{3,2},{4,5},{5,4},{6,7},{7,6},{8,9},{9,8},{10,11... | collective-permute-start | bytes 2888 | tf_op jit(solution)/shard_map/ppermute | solution.py:35
  7.9 39.5 %collective-permute-start.3 = (bf16[240,1600]{1,0:T(8,128)(2,1)S(1)}, bf16[240,1600]{1,0:T(8,128)(2,1)S(1)}, u32[]{:S(2)}, u32[]{:S(2)}) collective-permute-start(bf16[240,1600]{1,0:T(8,128)(2,1)S(1)} %concatenate.82.refs_4_.refs_6_.p0), channel_id=1, source_target_pairs={{0,1},{1,0},{2,3},{3,2},{4,5},{5,4},{6,7},{7,6},{8,9},{9,8},{10,11... | collective-permute-start | bytes 2304008 | tf_op jit(solution)/shard_map/ppermute | solution.py:35
  8.5 33.6 %collective-permute-start.4 = (bf16[240,1600]{1,0:T(8,128)(2,1)S(1)}, bf16[240,1600]{1,0:T(8,128)(2,1)S(1)}, u32[]{:S(2)}, u32[]{:S(2)}) collective-permute-start(bf16[240,1600]{1,0:T(8,128)(2,1)S(1)} %concatenate.82.refs_4_.refs_6_.p0), channel_id=1, source_target_pairs={{0,2},{1,3},{2,0},{3,1},{4,6},{5,7},{6,4},{7,5},{8,10},{9,11},{10,... | collective-permute-start | bytes 2304008 | tf_op jit(solution)/shard_map/ppermute | solution.py:35
  40.1 68.6 %collective-permute-start.15 = (bf16[240,960]{1,0:T(8,128)(2,1)}, bf16[240,960]{1,0:T(8,128)(2,1)S(1)}, u32[]{:S(2)}, u32[]{:S(2)}) collective-permute-start(bf16[240,960]{1,0:T(8,128)(2,1)} %convert_element_type.535.p0), channel_id=1, source_target_pairs={{0,2},{1,3},{2,0},{3,1},{4,6},{5,7},{6,4},{7,5},{8,10},{9,11},{10,... | collective-permute-start | bytes 1382408 | tf_op jit(solution)/shard_map/ppermute | solution.py:35
  45.2 84.3 %collective-permute-start.21 = (bf16[640,960]{0,1:T(8,128)(2,1)S(1)}, bf16[640,960]{0,1:T(8,128)(2,1)}, u32[]{:S(2)}, u32[]{:S(2)}) collective-permute-start(bf16[640,960]{0,1:T(8,128)(2,1)S(1)} %copy-done.131), channel_id=1, source_target_pairs={{0,2},{1,3},{2,0},{3,1},{4,6},{5,7},{6,4},{7,5},{8,10},{9,11},{10,... | collective-permute-start | bytes 3686408 | tf_op jit(solution)/shard_map/ppermute | solution.py:35
  45.4 61.6 %collective-permute-start.19 = (bf16[2,2,240,640]{3,2,1,0:T(8,128)(2,1)S(1)}, bf16[2,2,240,640]{3,2,1,0:T(8,128)(2,1)}, u32[]{:S(2)}, u32[]{:S(2)}) collective-permute-start(bf16[2,2,240,640]{3,2,1,0:T(8,128)(2,1)S(1)} %pad_maximum_fusion), channel_id=1, source_target_pairs={{0,2},{1,3},{2,0},{3,1},{4,6},{5,7},{6,4},{7,5},{8,10},{9,11},{10,... | collective-permute-start | bytes 3686408 | tf_op jit(solution)/shard_map/ppermute | solution.py:35
  67.7 41.1 %collective-permute-start.13 = (bf16[64,640]{1,0:T(8,128)(2,1)S(1)}, bf16[64,640]{1,0:T(8,128)(2,1)S(1)}, u32[]{:S(2)}, u32[]{:S(2)}) collective-permute-start(bf16[64,640]{1,0:T(8,128)(2,1)S(1)} %slice.384), channel_id=1, source_target_pairs={{0,4},{8,0},{16,8},{24,16},{28,24},{20,28},{12,20},{4,12},{1,5},{9... | collective-permute-start | bytes 245768 | tf_op jit(solution)/shard_map/ppermute | solution.py:48
  68.2 41.1 %collective-permute-start.9 = (bf16[64,640]{1,0:T(8,128)(2,1)S(1)}, bf16[64,640]{1,0:T(8,128)(2,1)S(1)}, u32[]{:S(2)}, u32[]{:S(2)}) collective-permute-start(bf16[64,640]{1,0:T(8,128)(2,1)S(1)} %slice.383), channel_id=1, source_target_pairs={{0,8},{8,16},{16,24},{24,28},{28,20},{20,12},{12,4},{4,0},{1,9},{9... | collective-permute-start | bytes 245768 | tf_op jit(solution)/shard_map/ppermute | solution.py:48
  107.0 29.1 %collective-permute-start.20 = (bf16[2,2,240,640]{3,2,1,0:T(8,128)(2,1)}, bf16[2,2,240,640]{3,2,1,0:T(8,128)(2,1)}, u32[]{:S(2)}, u32[]{:S(2)}) collective-permute-start(bf16[2,2,240,640]{3,2,1,0:T(8,128)(2,1)} %collective-permute-done.19.ym), channel_id=1, source_target_pairs={{0,4},{4,0},{8,12},{12,8},{16,20},{20,16},{24,28},{28,24},{1,5},{5... | collective-permute-start | bytes 3686408 | tf_op jit(solution)/shard_map/ppermute | solution.py:39
  145.3 50.9 %collective-permute-start.140 = (bf16[128,960]{1,0:T(8,128)(2,1)S(1)}, bf16[128,960]{1,0:T(8,128)(2,1)}, u32[]{:S(2)}, u32[]{:S(2)}) collective-permute-start(bf16[128,960]{1,0:T(8,128)(2,1)S(1)} %bitcast.308), channel_id=1, source_target_pairs={{0,2},{1,3},{2,0},{3,1},{4,6},{5,7},{6,4},{7,5},{8,10},{9,11},{10,... | collective-permute-start | bytes 737288 | tf_op jit(solution)/shard_map/ppermute | solution.py:35
  196.2 72.4 %collective-permute-start.141 = (bf16[128,960]{1,0:T(8,128)(2,1)}, bf16[128,960]{1,0:T(8,128)(2,1)S(1)}, u32[]{:S(2)}, u32[]{:S(2)}) collective-permute-start(bf16[128,960]{1,0:T(8,128)(2,1)} %collective-permute-done.140.l2), channel_id=1, source_target_pairs={{0,1},{1,0},{2,3},{3,2},{4,5},{5,4},{6,7},{7,6},{8,9},{9,8},{10,11... | collective-permute-start | bytes 737288 | tf_op jit(solution)/shard_map/ppermute | solution.py:35
  245.5 35.7 %collective-permute-start.136 = (bf16[256,640]{1,0:T(8,128)(2,1)S(1)}, bf16[256,640]{1,0:T(8,128)(2,1)S(1)}, u32[]{:S(2)}, u32[]{:S(2)}) collective-permute-start(bf16[256,640]{1,0:T(8,128)(2,1)S(1)} %dynamic-slice_bitcast_fusion.4), channel_id=1, source_target_pairs={{0,2},{1,3},{2,0},{3,1},{4,6},{5,7},{6,4},{7,5},{8,10},{9,11},{10,... | collective-permute-start | bytes 983048 | tf_op jit(solution)/shard_map/ppermute | solution.py:35
  268.6 25.3 %collective-permute-start.96 = (bf16[128,960]{1,0:T(8,128)(2,1)}, bf16[128,960]{1,0:T(8,128)(2,1)}, u32[]{:S(2)}, u32[]{:S(2)}) collective-permute-start(bf16[128,960]{1,0:T(8,128)(2,1)} %get-tuple-element.116.refs_4_), channel_id=1, source_target_pairs={{0,2},{1,3},{2,0},{3,1},{4,6},{5,7},{6,4},{7,5},{8,10},{9,11},{10,... | collective-permute-start | bytes 737288 | tf_op jit(solution)/shard_map/ppermute | solution.py:35
  271.5 22.7 %collective-permute-start.138 = (bf16[128,960]{1,0:T(8,128)(2,1)}, bf16[128,960]{1,0:T(8,128)(2,1)}, u32[]{:S(2)}, u32[]{:S(2)}) collective-permute-start(bf16[128,960]{1,0:T(8,128)(2,1)} %collective-permute-done.137.l2), channel_id=1, source_target_pairs={{0,1},{1,0},{2,3},{3,2},{4,5},{5,4},{6,7},{7,6},{8,9},{9,8},{10,11... | collective-permute-start | bytes 737288 | tf_op jit(solution)/shard_map/ppermute | solution.py:35
  277.7 23.4 %collective-permute-start.67 = (bf16[3,128,240]{2,1,0:T(8,128)(2,1)}, bf16[3,128,240]{2,1,0:T(8,128)(2,1)S(1)}, u32[]{:S(2)}, u32[]{:S(2)}) collective-permute-start(bf16[3,128,240]{2,1,0:T(8,128)(2,1)} %pad_maximum_fusion.9), channel_id=1, source_target_pairs={{0,1},{1,0},{2,3},{3,2},{4,5},{5,4},{6,7},{7,6},{8,9},{9,8},{10,11... | collective-permute-start | bytes 552968 | tf_op jit(solution)/shard_map/ppermute | solution.py:35
  282.0 19.5 %collective-permute-start.68 = (bf16[3,128,240]{2,1,0:T(8,128)(2,1)}, bf16[3,128,240]{2,1,0:T(8,128)(2,1)S(1)}, u32[]{:S(2)}, u32[]{:S(2)}) collective-permute-start(bf16[3,128,240]{2,1,0:T(8,128)(2,1)} %pad_maximum_fusion.10), channel_id=1, source_target_pairs={{0,2},{1,3},{2,0},{3,1},{4,6},{5,7},{6,4},{7,5},{8,10},{9,11},{10,... | collective-permute-start | bytes 552968 | tf_op jit(solution)/shard_map/ppermute | solution.py:35
  283.4 20.3 %collective-permute-start.69 = (bf16[3,128,240]{2,1,0:T(8,128)(2,1)}, bf16[3,128,240]{2,1,0:T(8,128)(2,1)S(1)}, u32[]{:S(2)}, u32[]{:S(2)}) collective-permute-start(bf16[3,128,240]{2,1,0:T(8,128)(2,1)} %pad_maximum_fusion.11), channel_id=1, source_target_pairs={{0,3},{1,2},{2,1},{3,0},{4,7},{5,6},{6,5},{7,4},{8,11},{9,10},{10,... | collective-permute-start | bytes 552968 | tf_op jit(solution)/shard_map/ppermute | solution.py:35
  305.1 41.3 %collective-permute-start.58 = (bf16[3,128,240]{2,1,0:T(8,128)(2,1)S(1)}, bf16[3,128,240]{2,1,0:T(8,128)(2,1)S(1)}, u32[]{:S(2)}, u32[]{:S(2)}) collective-permute-start(bf16[3,128,240]{2,1,0:T(8,128)(2,1)S(1)} %copy-done.140), channel_id=1, source_target_pairs={{0,1},{1,0},{2,3},{3,2},{4,5},{5,4},{6,7},{7,6},{8,9},{9,8},{10,11... | collective-permute-start | bytes 552968 | tf_op jit(solution)/shard_map/ppermute | solution.py:35
  305.2 43.2 %collective-permute-start.59 = (bf16[3,128,240]{2,1,0:T(8,128)(2,1)S(1)}, bf16[3,128,240]{2,1,0:T(8,128)(2,1)S(1)}, u32[]{:S(2)}, u32[]{:S(2)}) collective-permute-start(bf16[3,128,240]{2,1,0:T(8,128)(2,1)S(1)} %copy-done.139), channel_id=1, source_target_pairs={{0,2},{1,3},{2,0},{3,1},{4,6},{5,7},{6,4},{7,5},{8,10},{9,11},{10,... | collective-permute-start | bytes 552968 | tf_op jit(solution)/shard_map/ppermute | solution.py:35
  310.6 41.9 %collective-permute-start.60 = (bf16[3,128,240]{2,1,0:T(8,128)(2,1)S(1)}, bf16[3,128,240]{2,1,0:T(8,128)(2,1)S(1)}, u32[]{:S(2)}, u32[]{:S(2)}) collective-permute-start(bf16[3,128,240]{2,1,0:T(8,128)(2,1)S(1)} %copy-done.141), channel_id=1, source_target_pairs={{0,3},{1,2},{2,1},{3,0},{4,7},{5,6},{6,5},{7,4},{8,11},{9,10},{10,... | collective-permute-start | bytes 552968 | tf_op jit(solution)/shard_map/ppermute | solution.py:35
  367.7 47.0 %collective-permute-start.117 = (bf16[256,2560]{1,0:T(8,128)(2,1)S(1)}, bf16[256,2560]{1,0:T(8,128)(2,1)S(1)}, u32[]{:S(2)}, u32[]{:S(2)}) collective-permute-start(bf16[256,2560]{1,0:T(8,128)(2,1)S(1)} %copy-done.53), channel_id=1, source_target_pairs={{0,1},{1,0},{2,3},{3,2},{4,5},{5,4},{6,7},{7,6},{8,9},{9,8},{10,11... | collective-permute-start | bytes 3932168 | tf_op jit(solution)/shard_map/ppermute | solution.py:35
  367.8 48.6 %collective-permute-start.118 = (bf16[256,2560]{1,0:T(8,128)(2,1)S(1)}, bf16[256,2560]{1,0:T(8,128)(2,1)}, u32[]{:S(2)}, u32[]{:S(2)}) collective-permute-start(bf16[256,2560]{1,0:T(8,128)(2,1)S(1)} %copy-done.53), channel_id=1, source_target_pairs={{0,2},{1,3},{2,0},{3,1},{4,6},{5,7},{6,4},{7,5},{8,10},{9,11},{10,... | collective-permute-start | bytes 3932168 | tf_op jit(solution)/shard_map/ppermute | solution.py:35
  371.8 30.6 %collective-permute-start.72 = (bf16[128,640]{1,0:T(8,128)(2,1)S(1)}, bf16[128,640]{1,0:T(8,128)(2,1)S(1)}, u32[]{:S(2)}, u32[]{:S(2)}) collective-permute-start(bf16[128,640]{1,0:T(8,128)(2,1)S(1)} %copy-done.104), channel_id=1, source_target_pairs={{0,2},{1,3},{2,0},{3,1},{4,6},{5,7},{6,4},{7,5},{8,10},{9,11},{10,... | collective-permute-start | bytes 491528 | tf_op jit(solution)/shard_map/ppermute | solution.py:35
  373.5 29.2 %collective-permute-start.149 = (bf16[80,960]{1,0:T(8,128)(2,1)S(1)}, bf16[80,960]{1,0:T(8,128)(2,1)S(1)}, u32[]{:S(2)}, u32[]{:S(2)}) collective-permute-start(bf16[80,960]{1,0:T(8,128)(2,1)S(1)} %get-tuple-element.193), channel_id=1, source_target_pairs={{0,4},{8,0},{16,8},{24,16},{28,24},{20,28},{12,20},{4,12},{1,5},{9... | collective-permute-start | bytes 460808 | tf_op jit(solution)/shard_map/ppermute | solution.py:48
  376.0 27.6 %collective-permute-start.54 = (f32[2,960]{1,0:T(2,128)S(1)}, f32[2,960]{1,0:T(2,128)S(1)}, u32[]{:S(2)}, u32[]{:S(2)}) collective-permute-start(f32[2,960]{1,0:T(2,128)S(1)} %fusion.57), channel_id=1, source_target_pairs={{0,2},{1,3},{2,0},{3,1},{4,6},{5,7},{6,4},{7,5},{8,10},{9,11},{10,... | collective-permute-start | bytes 23048 | tf_op jit(solution)/shard_map/ppermute | solution.py:35
  402.4 44.2 %collective-permute-start.115 = (bf16[256,2560]{1,0:T(8,128)(2,1)}, bf16[256,2560]{1,0:T(8,128)(2,1)}, u32[]{:S(2)}, u32[]{:S(2)}) collective-permute-start(bf16[256,2560]{1,0:T(8,128)(2,1)} %get-tuple-element.117.own), channel_id=1, source_target_pairs={{0,2},{1,3},{2,0},{3,1},{4,6},{5,7},{6,4},{7,5},{8,10},{9,11},{10,... | collective-permute-start | bytes 3932168 | tf_op jit(solution)/shard_map/ppermute | solution.py:35
  433.4 26.9 %collective-permute-start.119 = (bf16[256,2560]{1,0:T(8,128)(2,1)}, bf16[256,2560]{1,0:T(8,128)(2,1)}, u32[]{:S(2)}, u32[]{:S(2)}) collective-permute-start(bf16[256,2560]{1,0:T(8,128)(2,1)} %collective-permute-done.118.far), channel_id=1, source_target_pairs={{0,1},{1,0},{2,3},{3,2},{4,5},{5,4},{6,7},{7,6},{8,9},{9,8},{10,11... | collective-permute-start | bytes 3932168 | tf_op jit(solution)/shard_map/ppermute | solution.py:35
  443.7 37.3 %collective-permute-start.114 = (bf16[256,2560]{1,0:T(8,128)(2,1)}, bf16[256,2560]{1,0:T(8,128)(2,1)S(1)}, u32[]{:S(2)}, u32[]{:S(2)}) collective-permute-start(bf16[256,2560]{1,0:T(8,128)(2,1)} %get-tuple-element.117.own), channel_id=1, source_target_pairs={{0,1},{1,0},{2,3},{3,2},{4,5},{5,4},{6,7},{7,6},{8,9},{9,8},{10,11... | collective-permute-start | bytes 3932168 | tf_op jit(solution)/shard_map/ppermute | solution.py:35
  446.7 35.2 %collective-permute-start.116 = (bf16[256,2560]{1,0:T(8,128)(2,1)}, bf16[256,2560]{1,0:T(8,128)(2,1)S(1)}, u32[]{:S(2)}, u32[]{:S(2)}) collective-permute-start(bf16[256,2560]{1,0:T(8,128)(2,1)} %collective-permute-done.115.far), channel_id=1, source_target_pairs={{0,1},{1,0},{2,3},{3,2},{4,5},{5,4},{6,7},{7,6},{8,9},{9,8},{10,11... | collective-permute-start | bytes 3932168 | tf_op jit(solution)/shard_map/ppermute | solution.py:35
  475.7 62.0 %collective-permute-start.107 = (bf16[32,960]{1,0:T(8,128)(2,1)S(1)}, bf16[32,960]{1,0:T(8,128)(2,1)S(1)}, u32[]{:S(2)}, u32[]{:S(2)}) collective-permute-start(bf16[32,960]{1,0:T(8,128)(2,1)S(1)} %collective-permute-done.106.refs_1_), channel_id=1, source_target_pairs={{0,8},{8,16},{16,24},{24,28},{28,20},{20,12},{12,4},{4,0},{1,9},{9... | collective-permute-start | bytes 184328 | tf_op jit(solution)/shard_map/ppermute | solution.py:48
  476.8 59.6 %collective-permute-start.111 = (bf16[32,960]{1,0:T(8,128)(2,1)S(1)}, bf16[32,960]{1,0:T(8,128)(2,1)S(1)}, u32[]{:S(2)}, u32[]{:S(2)}) collective-permute-start(bf16[32,960]{1,0:T(8,128)(2,1)S(1)} %collective-permute-done.110.refs_7_), channel_id=1, source_target_pairs={{0,4},{8,0},{16,8},{24,16},{28,24},{20,28},{12,20},{4,12},{1,5},{9... | collective-permute-start | bytes 184328 | tf_op jit(solution)/shard_map/ppermute | solution.py:48
  (277 other events, 2765.1 us)

commit v3 on v2

v3 whole, which is shorter than its diff:
```python
import functools

import jax
import jax.numpy as jnp
from jax import lax
from jax.experimental import pallas as pl
from jax.experimental.pallas import tpu as pltpu
from jax.sharding import PartitionSpec as P

QH = 15
KVH = 5
GQ = QH // KVH
HS = 64
SEQS = 8
REPEATS = 2
WA = 4
BLK = 128
D = 960
SL = D // WA
KV = KVH * HS
QKV = 2 * KV + D
FFQ = 640
R3 = GQ * BLK

epsilon = 1e-05
masked_score = -1e30
rope_base = 10000.0
bf16 = jnp.bfloat16
f32 = jnp.float32
i32 = jnp.int32
MB = 1 << 20


def swap(x, mask):
    return lax.ppermute(x, "wa", [(i, i ^ mask) for i in range(WA)])


def side_swap(x, n):
    return lax.ppermute(x, "ctx", [(i, i ^ 1) for i in range(n)])


def ring_order(n):
    return [i for i in range(0, n, 2)] + [i for i in range(n - 1, 0, -2)]


def ring_shift(x, n, step):
    order = ring_order(n)
    return lax.ppermute(x, "ctx", [(order[i], order[(i + step) % n]) for i in range(n)])


def ring_position(r, n):
    return jnp.where(r % 2 == 0, r // 2, n - 1 - r // 2) if n == 8 else r


def ring_device(p, n):
    return jnp.where(p < n // 2, 2 * p, 2 * (n - 1 - p) + 1) if n == 8 else p


def after(x, *others):
    return lax.optimization_barrier((x,) + others)[0]


def bar(*xs):
    return lax.optimization_barrier(xs)


def by_distance(x, n, position):
    return jnp.take(x, (position - jnp.arange(n, dtype=i32)) % n, axis=0)


def ring_gather(x, n, position):
    if n != 8:
        return by_distance(lax.all_gather(x, "ctx"), n, position)
    half = n // 2
    rows = x.shape[0] // 2
    ahead = [x]
    behind = [x]
    for _ in range(half - 1):
        ahead.append(ring_shift(ahead[-1], n, 1))
        behind.append(ring_shift(behind[-1], n, -1))
    far = jnp.concatenate(
        [ring_shift(ahead[-1][:rows], n, 1), ring_shift(behind[-1][rows:], n, -1)], axis=0
    )
    return ahead + [far] + behind[:0:-1]


def add_low(x, y):
    return (x.astype(f32) + y.astype(f32)).astype(bf16)


def ring_far(piece, n):
    far = piece(n // 2)
    rows = far.shape[0] // 2
    return ring_shift(far[:rows], n, 1), ring_shift(far[rows:], n, -1)


def ring_near(piece, n, k, go, back):
    ahead, behind = piece(n - k), piece(k)
    if go.shape != ahead.shape:
        rows = go.shape[0]
        go = jnp.concatenate([add_low(ahead[:rows], go), ahead[rows:]], axis=0)
        back = jnp.concatenate([behind[:rows], add_low(behind[rows:], back)], axis=0)
    else:
        go, back = add_low(ahead, go), add_low(behind, back)
    return ring_shift(go, n, 1), ring_shift(back, n, -1)


def ring_scatter(piece, n):
    go, back = ring_far(piece, n)
    for k in range(n // 2 - 1, 0, -1):
        go, back = ring_near(piece, n, k, go, back)
    return piece(0), go, back


def total_low(own, go, back):
    return (own.astype(f32) + go.astype(f32) + back.astype(f32)).astype(bf16)


def at_position(pieces, n, position):
    return lambda k: lax.dynamic_index_in_dim(pieces, (position - k) % n, 0, keepdims=False)


def ring_sum(pieces, n, position):
    if n != 8:
        mine = lax.psum_scatter(pieces, "ctx", scatter_dimension=0, tiled=False)
    else:
        mine = total_low(*ring_scatter(at_position(pieces, n, position), n))
    return ring_gather(mine, n, position)


def rows_home(mine, w):
    out = []
    for mask in range(WA):
        block = lax.dynamic_index_in_dim(mine, w ^ mask, 0, keepdims=False)
        out.append(swap(block, mask) if mask else block)
    return jnp.stack(out)


def placed(gathered, n, position):
    if n != 8:
        return by_distance(gathered, n, position)
    out = jnp.zeros((n,) + gathered[0].shape, bf16)
    for k in range(n):
        out = lax.dynamic_update_index_in_dim(out, gathered[k], (position - k) % n, 0)
    return out


def all_sum(x, n):
    for mask in (1, 2):
        x = x + swap(x, mask)
    step = 1
    while step < n:
        x = x + lax.ppermute(x, "ctx", [(i, i ^ step) for i in range(n)])
        step *= 2
    return x


def everyone(x):
    side = swap(x, 1)
    across = swap(x, 2)
    return [x, side, across, swap(across, 1)]


VMEM = pl.BlockSpec(memory_space=pltpu.VMEM)
SMEM = pl.BlockSpec(memory_space=pltpu.SMEM)


def call(body, name, n_scalar, ins, outs, scratch=(), us=2.0, limit=10, spec=VMEM):
    return pl.pallas_call(
        body,
        name=name,
        in_specs=[SMEM] * n_scalar + [spec] * (len(ins) - n_scalar),
        out_specs=[VMEM] * len(outs),
        out_shape=list(outs),
        scratch_shapes=list(scratch),
        cost_estimate=pl.CostEstimate(flops=int(us * 1.15e9), transcendentals=0, bytes_accessed=1 << 16),
        compiler_params=pltpu.CompilerParams(vmem_limit_bytes=limit * MB),
    )(*ins)


def shape(dims, dtype):
    return jax.ShapeDtypeStruct(dims, dtype)


def mm(a, b):
    return jnp.dot(a, b, preferred_element_type=f32)


def nt(a, b):
    return lax.dot_general(a, b, (((1,), (1,)), ((), ())), preferred_element_type=f32)


def tn(a, b):
    return lax.dot_general(a, b, (((0,), (0,)), ((), ())), preferred_element_type=f32)


def turn(u):
    lane = lax.broadcasted_iota(i32, u.shape, 1) % HS
    return jnp.where(lane < HS // 2, -pltpu.roll(u, 128 - HS // 2, 1), pltpu.roll(u, HS // 2, 1))


def turn_back(u):
    lane = lax.broadcasted_iota(i32, u.shape, 1) % HS
    return jnp.where(lane < HS // 2, pltpu.roll(u, 128 - HS // 2, 1), -pltpu.roll(u, HS // 2, 1))


def rope(u, cos, sin):
    return u * cos + turn(u) * sin


def rope_back(u, cos, sin):
    return u * cos + turn_back(u * sin)


def pack_qkv_body(wq, wk, wv, gains, out):
    out[:SL, :KV] = wk[...].astype(bf16)
    out[:SL, KV : 2 * KV] = wv[...].astype(bf16)
    out[:SL, 2 * KV :] = wq[...].astype(bf16)
    out[SL:, :] = jnp.zeros((8, QKV), bf16)
    out[SL:, :SL] = gains[...].astype(bf16)


def pack_rest_body(sc, w_out, w_gate, w_up, w_down, out_ref, keep, give, down):
    core = sc[4]
    out_ref[...] = w_out[...].astype(bf16)
    down[...] = w_down[...].astype(bf16)
    for gu, src in enumerate((w_gate, w_up)):
        for t in range(2):
            lo = pl.multiple_of(FFQ * (2 * t + core), 128)
            keep[gu, t] = src[:, pl.ds(lo, FFQ)].astype(bf16)
            lo = pl.multiple_of(FFQ * (2 * t + 1 - core), 128)
            give[gu, t] = src[:, pl.ds(lo, FFQ)].astype(bf16)


def pack_qkv(wq, wk, wv, gains):
    ins = [wq, wk, wv, gains]
    return call(pack_qkv_body, "pack_qkv", 0, ins, [shape((SL + 8, QKV), bf16)], us=1.5)[0]


def pack_rest(scal, w_out, w_gate, w_up, w_down):
    quarters = shape((2, 2, SL, FFQ), bf16)
    return call(
        pack_rest_body,
        "pack_rest",
        1,
        [scal, w_out, w_gate, w_up, w_down],
        [shape((SL, D), bf16), quarters, quarters, shape((FFQ, D), bf16)],
        limit=16,
        us=4,
    )


def head_only(tables):
    cos, sin = tables
    lane = lax.broadcasted_iota(i32, cos.shape, 1)
    return jnp.where(lane < HS, cos, 1.0), jnp.where(lane < HS, sin, 0.0)


def project_body(n_in, sc, *refs):
    xs = refs[:n_in]
    cos_ref, sin_ref, p0, p1, p2, p3 = refs[n_in : n_in + 6]
    x_ref, a4, q3, kv, acc_ref, x4 = refs[n_in + 6 :]
    x = xs[0][...].astype(f32)
    for r in xs[1:]:
        x = x + r[...]
    x_ref[...] = x
    ratio = lax.rsqrt(jnp.mean(x * x, axis=1, keepdims=True) + epsilon)
    x = x * ratio
    for j in range(WA):
        x4[j] = x[:, SL * j : SL * (j + 1)]
    acc = None
    for m, p in enumerate((p0, p1, p2, p3)):
        j = sc[0] ^ m
        a = (x4[j] * p[SL : SL + 1, :SL].astype(f32)).astype(bf16)
        a4[j] = a
        part = mm(a, p[:SL, :])
        acc = part if acc is None else acc + part
    acc_ref[:, :QKV] = acc
    cos, sin = cos_ref[...], sin_ref[...]
    edge = head_only((cos, sin))
    for i in range(2):
        kv[:, 128 * i : 128 * (i + 1)] = rope(acc_ref[:, 128 * i : 128 * (i + 1)], cos, sin).astype(bf16)
    kv[:, 256:384] = rope(acc_ref[:, 256:384], *edge).astype(bf16)
    kv[:, 384:640] = acc_ref[:, 384:640].astype(bf16)
    for i in range(8):
        lo = 2 * KV + 128 * i
        u = rope(acc_ref[:, lo : lo + 128], cos, sin).astype(bf16) * bf16(0.125)
        for j in range(2):
            h = 2 * i + j
            if h < QH:
                q3[h // GQ, BLK * (h % GQ) : BLK * (h % GQ + 1), :] = u[:, HS * j : HS * (j + 1)]


def project(scal, xs, tables, parts):
    return call(
        functools.partial(project_body, len(xs)),
        "project",
        1,
        [scal, *xs, *tables, *parts],
        [
            shape((BLK, D), f32),
            shape((WA, BLK, SL), bf16),
            shape((KVH, R3, HS), bf16),
            shape((BLK, 2 * KV), bf16),
        ],
        [pltpu.VMEM((BLK, QKV + 64), f32), pltpu.VMEM((WA, BLK, SL), f32)],
        us=2.5,
    )


def list_blocks(sched, lst, n):
    def step(k, count):
        first = sched[k] * BLK
        seen = (sched[k] <= sched[0]) & (first + BLK > sched[n])

        @pl.when(seen)
        def _():
            lst[count] = k

        return count + seen.astype(i32)

    return lax.fori_loop(0, n, step, jnp.int32(0))


def block_bias(sched, qinfo, k):
    key = sched[k] * BLK + lax.broadcasted_iota(i32, (BLK, R3), 0)
    ok = (key <= qinfo[0:1, :]) & (key >= qinfo[1:2, :])
    return jnp.where(ok, 0.0, masked_score).astype(f32)


def attend_body(n, sc, sched, qinfo, q3, kv, x, a4, gain, p0, p1, p2, p3, *refs):
    sl = refs[:WA]
    o_t, lse, m_ref, b_ref, lst, o_scr, ol4 = refs[WA:]
    count = list_blocks(sched, lst, n)
    o_t[...] = jnp.zeros(o_t.shape, f32)

    def step(i, state):
        k = lst[i]
        bias = block_bias(sched, qinfo, k)
        out = []
        for h in range(KVH):
            top, total = state[h]
            s = nt(kv[k, :, HS * h : HS * (h + 1)], q3[h]) + bias
            new = jnp.maximum(top, jnp.max(s, axis=0, keepdims=True))
            p = jnp.exp(s - new)
            fix = jnp.exp(top - new)
            values = kv[k, :, KV + HS * h : KV + HS * (h + 1)]
            o_t[h] = o_t[h] * fix + tn(values, p.astype(bf16))
            out.append((new, total * fix + jnp.sum(p, axis=0, keepdims=True)))
        return tuple(out)

    start = tuple(
        (jnp.full((1, R3), masked_score, f32), jnp.zeros((1, R3), f32)) for _ in range(KVH)
    )
    state = lax.fori_loop(0, count, step, start)
    for h in range(KVH):
        top, total = state[h]
        out = o_t[h] * (1.0 / total)
        o_t[h] = out
        lse[h : h + 1, :] = top + jnp.log(total)
        rows = out.T
        for g in range(GQ):
            j = GQ * h + g
            o_scr[:, HS * j : HS * (j + 1)] = rows[BLK * g : BLK * (g + 1), :]
    low = o_scr[...].astype(bf16)
    for j in range(WA):
        ol4[j] = low[:, SL * j : SL * (j + 1)]
    m = x[...]
    for k, p in enumerate((p0, p1, p2, p3)):
        j = sc[0] ^ k
        sl[k][0] = a4[j]
        sl[k][1] = ol4[j]
        m = m + mm(ol4[j], p[...])
    m_ref[...] = m
    ratio = lax.rsqrt(jnp.mean(m * m, axis=1, keepdims=True) + epsilon)
    b = (m * ratio * gain[...]).astype(bf16)
    b_ref[...] = b


def attend(scal, sched, qinfo, q3, kv, x, a4, gain, parts):
    n = kv.shape[0]
    return call(
        functools.partial(attend_body, n),
        "attend",
        2,
        [scal, sched, qinfo, q3, kv, x, a4, gain, *parts],
        [
            *[shape((2, BLK, SL), bf16)] * WA,
            shape((KVH, HS, R3), f32),
            shape((8, R3), f32),
            shape((BLK, D), f32),
            shape((BLK, D), bf16),
        ],
        [
            pltpu.SMEM((n,), i32),
            pltpu.VMEM((BLK, D), f32),
            pltpu.VMEM((WA, BLK, SL), bf16),
        ],
        limit=8,
        us=10,
    )


def mlp_body(sc, b_own, b_side, keep, core, gm, um, go, uo, d_own, d_far, *refs):
    z_keep, z_give, gu_ref, y_own, y_side, bs, z_ref = refs
    w = sc[0]
    for half, b in enumerate((b_own, b_side)):
        for j in range(WA):
            bs[j, BLK * half : BLK * (half + 1), :] = b[:, SL * j : SL * (j + 1)]
    for t, fars in ((sc[1], (gm, um)), (1 - sc[1], (go, uo))):
        lin = []
        for gu in range(2):
            acc = mm(bs[w], keep[gu, t]) + mm(bs[w ^ 1], core[gu, t])
            acc = acc + mm(bs[w ^ 2], fars[gu][0]) + mm(bs[w ^ 3], fars[gu][1])
            gu_ref[gu, t] = acc
            lin.append(acc)
        gate, up = lin
        z_ref[t] = (gate / (1.0 + jnp.exp(-gate)) * up).astype(bf16)
    row = sc[2]
    out = mm(z_ref[row], d_own[...]) + mm(z_ref[1 - row], d_far[...])
    y_own[...] = out[:BLK]
    y_side[...] = out[BLK:]
    z_keep[...] = z_ref[row]
    z_give[...] = z_ref[1 - row]


def mlp(scal, b_own, b_side, wts):
    return call(
        mlp_body,
        "mlp",
        1,
        [scal, b_own, b_side, *wts],
        [
            shape((2 * BLK, FFQ), bf16),
            shape((2 * BLK, FFQ), bf16),
            shape((2, 2, 2 * BLK, FFQ), f32),
            shape((BLK, D), f32),
            shape((BLK, D), f32),
        ],
        [pltpu.VMEM((WA, 2 * BLK, SL), bf16), pltpu.VMEM((2, 2 * BLK, FFQ), bf16)],
        limit=12,
        us=5.5,
    )


def mlp_back_body(sc, l_own, l_side, gu_ref, keep, core, gm, um, go, uo, d_own, d_far, *refs):
    keep_ref, give_ref, db_own, db_side, low, acc = refs
    w, row = sc[0], sc[2]
    low[:BLK] = l_own[...]
    low[BLK:] = l_side[...]
    for first, (t, fg, fu) in enumerate(((sc[1], gm, um), (1 - sc[1], go, uo))):
        dz = jnp.where(t == row, nt(low[...], d_own[...]), nt(low[...], d_far[...]))
        gate, up = gu_ref[0, t], gu_ref[1, t]
        sig = 1.0 / (1.0 + jnp.exp(-gate))
        dg = (dz * up * sig * (1.0 + gate * (1.0 - sig))).astype(bf16)
        du = (dz * gate * sig).astype(bf16)

        @pl.when(t == row)
        def _():
            keep_ref[0] = dg
            keep_ref[1] = du

        @pl.when(t != row)
        def _():
            give_ref[0] = dg
            give_ref[1] = du

        for j, p in ((w, keep.at[0, t]), (w ^ 1, core.at[0, t]), (w ^ 2, fg.at[0]), (w ^ 3, fg.at[1])):
            part = nt(dg, p[...])
            acc[j] = part if first == 0 else acc[j] + part
        for j, p in ((w, keep.at[1, t]), (w ^ 1, core.at[1, t]), (w ^ 2, fu.at[0]), (w ^ 3, fu.at[1])):
            acc[j] = acc[j] + nt(du, p[...])
    for j in range(WA):
        db_own[:, SL * j : SL * (j + 1)] = acc[j, :BLK, :]
        db_side[:, SL * j : SL * (j + 1)] = acc[j, BLK:, :]


def mlp_back(scal, l_own, l_side, gu, wts):
    return call(
        mlp_back_body,
        "mlp_back",
        1,
        [scal, l_own, l_side, gu, *wts],
        [
            shape((2, 2 * BLK, FFQ), bf16),
            shape((2, 2 * BLK, FFQ), bf16),
            shape((BLK, D), f32),
            shape((BLK, D), f32),
        ],
        [pltpu.VMEM((2 * BLK, D), bf16), pltpu.VMEM((WA, 2 * BLK, SL), f32)],
        limit=12,
        us=6.7,
    )


def norm_back(grads, hidden, gain):
    ratio = lax.rsqrt(jnp.mean(hidden * hidden, axis=1, keepdims=True) + epsilon)
    scaled = hidden * ratio
    gain_grad = jnp.sum(grads * scaled, axis=0, keepdims=True)
    inner = grads * gain
    out = ratio * (inner - scaled * jnp.mean(inner * scaled, axis=1, keepdims=True))
    return out, gain_grad


def attend_back_body(n, sc, sched, qinfo, dy, db_own, db_got, m, gain, p0, p1, p2, p3, q3, kv, o_t, lse, cos_ref, sin_ref, *refs):
    dm_ref, dml_ref, gg, dq_ref, dkv_ref, lst, do3, d_scr, dq_scr, dq_t = refs
    count = list_blocks(sched, lst, n)
    part, gain_grad = norm_back(db_own[...] + db_got[...], m[...], gain[...])
    gg[...] = gain_grad
    dm = dy[...].astype(f32) + part
    dm_ref[...] = dm
    dml = dm.astype(bf16)
    dml_ref[...] = dml
    for k, p in enumerate((p0, p1, p2, p3)):
        d_scr[sc[0] ^ k] = nt(dml, p[...]).astype(bf16).astype(f32)
    whole = jnp.concatenate([d_scr[j] for j in range(WA)], axis=1)
    for j in range(QH):
        do3[j // GQ, BLK * (j % GQ) : BLK * (j % GQ + 1), :] = whole[:, HS * j : HS * (j + 1)].astype(bf16)

    @pl.loop(1, n)
    def _(k):
        seen = (sched[k] <= sched[0]) & (sched[k] * BLK + BLK > sched[n])

        @pl.when(jnp.logical_not(seen))
        def _():
            dkv_ref[k] = jnp.zeros((BLK, 2 * KV), bf16)

    deltas = [
        jnp.sum(do3[h].astype(f32).T * o_t[h], axis=0, keepdims=True) for h in range(KVH)
    ]
    dq_t[...] = jnp.zeros(dq_t.shape, f32)

    @pl.loop(0, count)
    def _(i):
        k = lst[i]
        bias = block_bias(sched, qinfo, k)
        for h in range(KVH):
            keys = kv[k, :, HS * h : HS * (h + 1)]
            values = kv[k, :, KV + HS * h : KV + HS * (h + 1)]
            s = nt(keys, q3[h]) + bias
            p = jnp.exp(s - lse[h : h + 1, :])
            ds = (p * (nt(values, do3[h]) - deltas[h])).astype(bf16)
            dkv_ref[k, :, HS * h : HS * (h + 1)] = mm(ds, q3[h]).astype(bf16)
            dkv_ref[k, :, KV + HS * h : KV + HS * (h + 1)] = mm(p.astype(bf16), do3[h]).astype(bf16)
            dq_t[h] = dq_t[h] + tn(keys, ds)

    for h in range(KVH):
        rows = (dq_t[h] * 0.125).T
        for g in range(GQ):
            j = GQ * h + g
            dq_scr[:, HS * j : HS * (j + 1)] = rows[BLK * g : BLK * (g + 1), :]
    cos, sin = cos_ref[...], sin_ref[...]
    for i in range(8):
        u = rope_back(dq_scr[:, 128 * i : 128 * (i + 1)], cos, sin).astype(bf16)
        if i < 7:
            dq_ref[:, 128 * i : 128 * (i + 1)] = u
        else:
            dq_ref[:, 128 * i :] = u[:, :HS]


def attend_back(scal, sched, qinfo, dy, db_own, db_got, m, gain, parts, q3, kv, o_t, lse, tables):
    n = kv.shape[0]
    return call(
        functools.partial(attend_back_body, n),
        "attend_back",
        2,
        [scal, sched, qinfo, dy, db_own, db_got, m, gain, *parts, q3, kv, o_t, lse, *tables],
        [
            shape((BLK, D), f32),
            shape((BLK, D), bf16),
            shape((1, D), f32),
            shape((BLK, D), bf16),
            shape((n, BLK, 2 * KV), bf16),
        ],
        [
            pltpu.SMEM((n,), i32),
            pltpu.VMEM((KVH, R3, HS), bf16),
            pltpu.VMEM((WA, BLK, SL), f32),
            pltpu.VMEM((BLK, D + 64), f32),
            pltpu.VMEM((KVH, HS, R3), f32),
        ],
        limit=8,
        us=12,
    )


def query_back_body(sc, dq, p0, p1, p2, p3, da):
    for k, p in enumerate((p0, p1, p2, p3)):
        da[sc[0] ^ k] = nt(dq[...], p[:SL, 2 * KV :])


def query_back(scal, dq, parts):
    return call(
        query_back_body,
        "query_back",
        1,
        [scal, dq, *parts],
        [shape((WA, BLK, SL), f32)],
        us=2,
    )[0]


def project_back_body(sc, own, go, back, cos_ref, sin_ref, da, p0, p1, p2, p3, x, dm, gain, *refs):
    dkv_ref, dx_ref, dxl_ref, gg, d4 = refs
    total = own[...].astype(f32) + go[...].astype(f32) + back[...].astype(f32)
    cos, sin = cos_ref[...], sin_ref[...]
    edge = head_only((cos, sin))
    for i in range(2):
        dkv_ref[:, 128 * i : 128 * (i + 1)] = rope_back(total[:, 128 * i : 128 * (i + 1)], cos, sin).astype(bf16)
    dkv_ref[:, 256:384] = rope_back(total[:, 256:384], *edge).astype(bf16)
    dkv_ref[:, 384:] = total[:, 384:].astype(bf16)
    for k, p in enumerate((p0, p1, p2, p3)):
        d4[sc[0] ^ k] = da[sc[0] ^ k] + nt(dkv_ref[...], p[:SL, : 2 * KV])
    grads = jnp.concatenate([d4[j] for j in range(WA)], axis=1)
    part, gain_grad = norm_back(grads, x[...], gain[...])
    gg[...] = gain_grad
    dx = dm[...] + part
    dx_ref[...] = dx
    dxl_ref[...] = dx.astype(bf16)


def project_back(scal, addends, tables, da, parts, x, dm, gain):
    return call(
        project_back_body,
        "project_back",
        1,
        [scal, *addends, *tables, da, *parts, x, dm, gain],
        [
            shape((BLK, 2 * KV), bf16),
            shape((BLK, D), f32),
            shape((BLK, D), bf16),
            shape((1, D), f32),
        ],
        [pltpu.VMEM((WA, BLK, SL), f32)],
        us=2.5,
    )


def fetched(refs, bufs, sem):
    copies = [pltpu.make_async_copy(r, b, sem.at[i]) for i, (r, b) in enumerate(zip(refs, bufs))]
    for c in copies:
        c.start()
    for c in copies:
        c.wait()


def call_fetched(body, name, scal, ins, outs, us, limit, scratch=()):
    count = len(ins)

    def whole(sc, *refs):
        sources, results = refs[:count], refs[count : count + len(outs)]
        bufs = refs[count + len(outs) : 2 * count + len(outs)]
        sem, rest = refs[2 * count + len(outs)], refs[2 * count + len(outs) + 1 :]
        fetched(sources, bufs, sem)
        body(sc, *bufs, *results, *rest)

    bufs = [pltpu.VMEM(x.shape, x.dtype) for x in ins]
    return call(
        whole,
        name,
        1,
        [scal, *ins],
        outs,
        bufs + [pltpu.SemaphoreType.DMA((count,)), *scratch],
        us=us,
        limit=limit,
        spec=pl.BlockSpec(memory_space=pl.ANY),
    )


def grad_rows_body(has_prev, sc, *refs):
    out = refs[-1]
    slices = refs[:WA]
    lo = 0
    for t, kind in enumerate((0, 0, 1)):
        lows = refs[WA * (t + 1) : WA * (t + 2)]
        acc = None
        for sl, low in zip(slices, lows):
            part = tn(sl[kind], low[...])
            acc = part if acc is None else acc + part
        width = acc.shape[1]
        if has_prev:
            acc = acc + refs[4 * WA][:, lo : lo + width]
            out[:SL, lo : lo + width] = acc.astype(bf16)
        else:
            out[:, lo : lo + width] = acc
        lo += width
    if has_prev:
        out[SL:, :] = jnp.zeros((256 - SL, lo), bf16)


def grad_rows(scal, slices, dkvs, dqs, dms, prev):
    has_prev = prev is not None
    cols = QKV + D
    return call_fetched(
        functools.partial(grad_rows_body, has_prev),
        "grad_rows",
        scal,
        [*slices, *dkvs, *dqs, *dms] + ([prev] if has_prev else []),
        [shape((256, cols), bf16) if has_prev else shape((SL, cols), f32)],
        us=4,
        limit=20,
    )[0]


def grad_ff_body(has_prev, sc, b0, b1, b2, b3, keep, got, *refs):
    out, bt = refs[-2:]
    for m, b in enumerate((b0, b1, b2, b3)):
        bt[:, BLK * m : BLK * (m + 1)] = b[...].astype(f32).T.astype(bf16)
    for gu in range(2):
        for j in range(WA):
            lhs = bt[SL * j : SL * (j + 1), :]
            acc = mm(lhs[:, : 2 * BLK], keep[gu]) + mm(lhs[:, 2 * BLK :], got[gu])
            for i in range(4):
                rows = min(64, SL - 64 * i)
                part = acc[64 * i : 64 * i + rows]
                if has_prev:
                    part = part + refs[0][4 * gu + i, j, :rows]
                out[4 * gu + i, j, :rows] = part.astype(out.dtype)
                if rows < 64:
                    out[4 * gu + i, j, rows:] = jnp.zeros((64 - rows, FFQ), out.dtype)


def grad_ff(scal, bs, keep, got, prev):
    has_prev = prev is not None
    return call_fetched(
        functools.partial(grad_ff_body, has_prev),
        "grad_ff",
        scal,
        [*bs, keep, got] + ([prev] if has_prev else []),
        [shape((8, WA, 64, FFQ), bf16 if has_prev else f32)],
        us=5,
        limit=24,
        scratch=[pltpu.VMEM((D, WA * BLK), bf16)],
    )[0]


def grad_down_body(has_prev, sc, z, zg, l0, l1, l2, l3, *refs):
    out = refs[-1]
    acc = tn(z[:BLK], l0[...]) + tn(z[BLK:], l1[...])
    acc = acc + tn(zg[:BLK], l2[...]) + tn(zg[BLK:], l3[...])
    if has_prev:
        acc = acc + refs[0][...]
    out[...] = acc.astype(out.dtype)


def grad_down(scal, z, z_got, lows, prev):
    has_prev = prev is not None
    return call_fetched(
        functools.partial(grad_down_body, has_prev),
        "grad_down",
        scal,
        [z, z_got, *lows] + ([prev] if has_prev else []),
        [shape((FFQ, D), bf16 if has_prev else f32)],
        us=3,
        limit=16,
    )[0]


def finish_ff_body(n, sc, *refs):
    gate, up = refs[n:]
    position, w = sc[3], sc[0]
    for k in range(n):
        p = (position - k + n) % n
        first = pl.multiple_of(64 * (p % 4), 8)
        for gu, out in enumerate((gate, up)):
            for rows in (64, SL - 192):

                @pl.when((p // 4 == gu) & ((p % 4 < 3) == (rows == 64)))
                def _():
                    for m in range(WA):
                        lo = pl.multiple_of(FFQ * (w ^ m), 128)
                        out[pl.ds(first, rows), pl.ds(lo, FFQ)] = refs[k][m, :rows].astype(f32)


def finish_ff(scal, gathered):
    return call(
        functools.partial(finish_ff_body, len(gathered)),
        "finish_ff",
        1,
        [scal, *gathered],
        [shape((SL, 4 * FFQ), f32)] * 2,
        us=4,
        limit=12,
    )


def finish_down_body(n, sc, *refs):
    out = refs[n]
    for k in range(n):
        p = (sc[3] - k + n) % n
        rows = refs[k].shape[0]
        out[pl.ds(pl.multiple_of(p * rows, 8), rows), :] = refs[k][...].astype(f32)


def finish_down(scal, gathered):
    return call(
        functools.partial(finish_down_body, len(gathered)),
        "finish_down",
        1,
        [scal, *gathered],
        [shape((FFQ, D), f32)],
        us=2.5,
    )[0]


def finish_rows_body(n, widths, sc, *refs):
    outs = refs[n:]
    for k in range(n):
        p = (sc[3] - k + n) % n
        rows = refs[k].shape[0]
        tail = SL - rows * (n - 1)
        first = pl.multiple_of(p * rows, 8)

        @pl.when(p < n - 1)
        def _():
            lo = 0
            for out, width in zip(outs, widths):
                out[pl.ds(first, rows), :] = refs[k][:, lo : lo + width].astype(f32)
                lo += width

        @pl.when(p == n - 1)
        def _():
            lo = 0
            for out, width in zip(outs, widths):
                out[rows * (n - 1) :, :] = refs[k][:tail, lo : lo + width].astype(f32)
                lo += width


def finish_rows(scal, gathered, widths):
    return call(
        functools.partial(finish_rows_body, len(gathered), tuple(widths)),
        "finish_rows",
        1,
        [scal, *gathered],
        [shape((SL, width), f32) for width in widths],
        us=2.5,
    )


def body(
    tokens,
    cotangent,
    segment_ids,
    block_order,
    gain_attn,
    w_query,
    key_projection,
    value_projection,
    w_out,
    gain_mlp,
    w_gate,
    w_up,
    w_down,
):
    n = block_order.shape[1]
    w = lax.axis_index("wa")
    r = lax.axis_index("ctx")
    core = w % 2
    row = w // 2
    position = ring_position(r, n)
    x_side = r % 2
    scal = jnp.stack([w, x_side, row, position, core]).astype(i32)

    blocks = ring_device((position - jnp.arange(n, dtype=i32)) % n, n)
    labels = jnp.arange(n, dtype=i32)
    order_row = block_order[0]
    anchors = jnp.sum(jnp.where(blocks[:, None] == labels[None, :], order_row[None, :], 0), axis=1)
    natural = anchors[0] * BLK + jnp.arange(BLK, dtype=i32)
    seg_labels = jnp.arange(SEQS, dtype=i32)
    sizes = jnp.sum((segment_ids[0][None, :] == seg_labels[:, None]).astype(i32), axis=1)
    before = (seg_labels[None, :] < seg_labels[:, None]).astype(i32)
    starts = jnp.sum(before * sizes[None, :], axis=1)
    start_of = jnp.max(jnp.where(starts[None, :] <= natural[:, None], starts[None, :], 0), axis=1)
    sched = jnp.concatenate([anchors, start_of[:1]]).astype(i32)
    qinfo = jnp.pad(
        jnp.stack([jnp.tile(natural, GQ), jnp.tile(start_of, GQ)]), ((0, 6), (0, 0))
    ).astype(i32)
    frequency = rope_base ** (-jnp.arange(HS // 2, dtype=f32) * 2.0 / HS)
    angles = (natural - start_of).astype(f32)[:, None] * frequency[None, :]
    tables = (jnp.tile(jnp.cos(angles), (1, 4)), jnp.tile(jnp.sin(angles), (1, 4)))

    gains_own = jnp.pad(jnp.stack([gain_attn, gain_mlp]), ((0, 6), (0, 0)))
    qkv_own = pack_qkv(w_query, key_projection, value_projection, gains_own)
    qkv_across = swap(qkv_own, 2)
    qkv_side = swap(qkv_own, 1)
    out_own, keep, give, down_own = pack_rest(scal, after(w_out, qkv_own), w_gate, w_up, w_down)
    core_part = swap(give, 1)

    def y_half(gu):
        return jnp.stack(
            [
                lax.dynamic_index_in_dim(keep[gu], x_side, 0, keepdims=False),
                lax.dynamic_index_in_dim(core_part[gu], x_side, 0, keepdims=False),
            ]
        )

    gate_half, up_half = y_half(0), y_half(1)
    down_half = lax.dynamic_slice_in_dim(down_own, x_side * (FFQ // 2), FFQ // 2, 0)
    qkv_across, qkv_side, core_part, out_own, gate_half, up_half, down_half = bar(
        qkv_across, qkv_side, core_part, out_own, gate_half, up_half, down_half
    )
    qkv_parts = [qkv_own, qkv_side, qkv_across, swap(qkv_across, 1)]
    gains_parts = jnp.stack([p[SL : SL + 2, :SL] for p in qkv_parts])
    gains = jnp.concatenate(
        [lax.dynamic_index_in_dim(gains_parts, w ^ j, 0, keepdims=False) for j in range(WA)], axis=1
    ).astype(f32)
    gain_a, gain_m = gains[0:1], gains[1:2]

    def ring_keys(kv, extras):
        if n != 8:
            done = [e() for e in extras]
            return ring_gather(kv, n, position), done
        rows = BLK // 2
        ahead, behind, done = [kv], [kv], []
        for step in range(4):
            more = extras[step]()
            if step < 3:
                f, b = ring_shift(ahead[-1], n, 1), ring_shift(behind[-1], n, -1)
            else:
                f = ring_shift(ahead[-1][:rows], n, 1)
                b = ring_shift(behind[-1][rows:], n, -1)
            f, b, *more = bar(f, b, *more)
            ahead.append(f)
            behind.append(b)
            done.append(more)
        far = jnp.concatenate([ahead[4], behind[4]], axis=0)
        return jnp.stack(ahead[:4] + [far] + behind[3:0:-1]), done

    def nothing():
        return []

    out_across = swap(out_own, 2)
    gate_mine = swap(gate_half, 2)
    x, a4, q3, kv = project(scal, [tokens[0]], tables, qkv_parts)
    held = {}

    def step1():
        return [out_across]

    def step2():
        held["up_mine"] = swap(after(up_half, kv), 2)
        return [swap(out_across, 1), swap(out_own, 1), gate_mine]

    def step3():
        held["gate_other"] = side_swap(gate_mine, n)
        return []

    def step4():
        return [held["up_mine"], held["gate_other"]]

    every, more = ring_keys(kv, [step1, step2, step3, step4])
    out_across, (out_diag, out_side, gate_mine), (up_mine, gate_other) = more[0][0], more[1], more[3]
    out_parts = [out_own, out_side, out_across, out_diag]
    up_other = side_swap(up_mine, n)
    down_mine = swap(after(down_half, every), 2)
    *sl, o_t, lse, m, b = attend(scal, sched, qinfo, q3, every, x, a4, gain_m, out_parts)
    m, b, up_other, down_mine = bar(m, b, up_other, down_mine)
    b_side = swap(b, 1)
    down_other = side_swap(down_mine, n)
    down_far = jnp.concatenate(
        [
            jnp.where(x_side == 0, down_mine, down_other),
            jnp.where(x_side == 0, down_other, down_mine),
        ],
        axis=0,
    )
    ff_parts = [keep, core_part, gate_mine, up_mine, gate_other, up_other, down_own, down_far]
    b_far = swap(b, 2)
    z, z_give, gu, y_own, y_side = mlp(scal, b, b_side, ff_parts)
    y_own, y_side, b_far, z_give = bar(y_own, y_side, b_far, z_give)
    kept0 = [x, q3, every, o_t, lse, m, gu, z]

    y_got = swap(y_side, 1)
    z_got0 = swap(z_give, 2)
    x, a4, q3, kv = project(scal, [m, y_own, y_got], tables, qkv_parts)
    top = cotangent[0]
    b0, sl0 = b, sl

    def step1():
        return [z_got0, swap(b_far, 1)]

    def step2():
        return [swap(sl0[1], 1), swap(sl0[2], 2)]

    def step3():
        return [swap(sl0[3], 3), swap(after(top, kv), 2)]

    def step4():
        return [swap(top, 1)]

    every, more = ring_keys(kv, [step1, step2, step3, step4])
    (z_got0, b_diag), (s1, s2), (s3, top_far), (top_side,) = more
    kept0 += [z_got0, [b0, b_side, b_far, b_diag], [sl0[0], s1, s2, s3]]
    top_diag = swap(top_far, 1)
    *sl, o_t, lse, m, b = attend(scal, sched, qinfo, q3, every, x, a4, gain_m, out_parts)
    m, b, top_diag = bar(m, b, top_diag)
    b_side = swap(b, 1)
    b_far = swap(b, 2)
    z, z_give, gu, y_own, y_side = mlp(scal, b, b_side, ff_parts)
    y_own, y_side, b_far, z_give, z = bar(y_own, y_side, b_far, z_give, z)
    kept1 = [x, q3, every, o_t, lse, m, gu, z]

    x, q3, every, o_t, lse, m, gu, z = kept1
    y_got = swap(y_side, 1)
    z_got = swap(z_give, 2)
    b_diag = swap(b_far, 1)
    keep_d, give_d, db_own, db_side = mlp_back(scal, after(top, y_side), top_side, gu, ff_parts)
    db_own, db_side, give_d, z_got, b_diag, y_got = bar(
        db_own, db_side, give_d, z_got, b_diag, y_got
    )
    output = (m + y_own + y_got).astype(bf16)[None]
    db_got = swap(db_side, 1)
    got_d = swap(give_d, 2)
    dm, dml, gain_m_1, dq, dkv = attend_back(
        scal, sched, qinfo, top, db_own, db_got, m, gain_m, out_parts, q3, every, o_t, lse, tables
    )
    dkv, dq, dml, got_d = bar(dkv, dq, dml, got_d)

    def spread(dkv, extras):
        if n != 8:
            done = [e() for e in extras]
            total = lax.psum_scatter(
                by_distance(dkv, n, position), "ctx", scatter_dimension=0, tiled=False
            )
            return (total, jnp.zeros_like(total), jnp.zeros_like(total)), done
        done = []
        go = back = None
        for step in range(4):
            more = extras[step]()
            if step == 0:
                go, back = ring_far(lambda k: dkv[k], n)
            else:
                go, back = ring_near(lambda k: dkv[k], n, 4 - step, go, back)
            go, back, *more = bar(go, back, *more)
            done.append(more)
        return (dkv[0], go, back), done

    lows = [top, top_side, top_far, top_diag]

    def step1():
        return [swap(sl[1], 1), swap(sl[2], 2), grad_down(scal, z, z_got, lows, None)]

    def step2():
        return [swap(sl[3], 3), swap(dq, 2), query_back(scal, after(dq, dkv), qkv_parts)]

    def step3():
        bs = [b, b_side, b_far, b_diag]
        return [swap(after(dml, dq), 2), grad_ff(scal, bs, keep_d, got_d, None)]

    def step4():
        return [swap(dq, 1), swap(dml, 1)]


    addends, more = spread(dkv, [step1, step2, step3, step4])
    (s1, s2, down_1), (s3, dq_far, da), (dml_far, ff_1), (dq_side, dml_side) = more
    dq_diag = swap(dq_far, 1)
    dml_diag = swap(dml_far, 1)
    dkv0, dx, low, gain_a_1 = project_back(scal, addends, tables, da, qkv_parts, x, dm, gain_a)
    dx, low, dkv0, dq_diag, dml_diag = bar(dx, low, dkv0, dq_diag, dml_diag)
    slices_1 = [sl[0], s1, s2, s3]
    dqs_1 = [dq, dq_side, dq_far, dq_diag]
    dmls_1 = [dml, dml_side, dml_far, dml_diag]

    x, q3, every, o_t, lse, m, gu, z, z_got, bs, slices = kept0
    low_side = swap(low, 1)
    low_far = swap(low, 2)
    keep_d, give_d, db_own, db_side = mlp_back(scal, low, low_side, gu, ff_parts)
    db_own, db_side, give_d, low_far = bar(db_own, db_side, give_d, low_far)
    db_got = swap(db_side, 1)
    low_diag = swap(low_far, 1)
    dkv_side, dkv_far = swap(dkv0, 1), swap(dkv0, 2)
    down_grad = grad_down(scal, z, z_got, [low, low_side, low_far, low_diag], down_1)
    db_got, down_grad = bar(db_got, down_grad)
    down_piece = at_position(down_grad.reshape(n, FFQ // n, D), n, position)
    got_d = swap(give_d, 2)
    down_go = down_back = None
    if n == 8:
        down_go, down_back = ring_far(down_piece, n)
    dm, dml, gain_m_0, dq, dkv = attend_back(
        scal, sched, qinfo, dx, db_own, db_got, m, gain_m, out_parts, q3, every, o_t, lse, tables
    )
    dkv, dq, dml, got_d, dkv_side, dkv_far = bar(dkv, dq, dml, got_d, dkv_side, dkv_far)

    def ff_piece_of(ff):
        sub = n // 8
        pieces = ff.reshape(8, WA, sub, 64 // sub, FFQ).transpose(0, 2, 1, 3, 4)
        return pieces.reshape(n, WA, 64 // sub, FFQ)

    def down_step(k):
        nonlocal down_go, down_back
        if n != 8:
            return []
        down_go, down_back = ring_near(down_piece, n, k, down_go, down_back)
        return [down_go, down_back]

    def keep_down(pair):
        nonlocal down_go, down_back
        if n == 8:
            down_go, down_back = pair

    def step1():
        ff = grad_ff(scal, bs, keep_d, got_d, ff_1)
        return [ff, swap(dq, 2)] + down_step(3)

    def step2():
        return [swap(after(dml, dq), 2), query_back(scal, dq, qkv_parts)] + down_step(2)

    def step3():
        dkvs = [dkv0, dkv_side, dkv_far, swap(dkv_far, 1)]
        return [grad_rows(scal, slices_1, dkvs, dqs_1, dmls_1, None)] + down_step(1)

    def step4():
        return [swap(dq, 1), swap(dml, 1)]

    addends, more = spread(dkv, [step1, step2, step3, step4])
    (ff_grad, dq_far, *_), (dml_far, da, *_), (rows_1, *_), (dq_side, dml_side) = more
    dqs = [dq, dq_side, dq_far, swap(dq_far, 1)]
    dmls = [dml, dml_side, dml_far, swap(dml_far, 1)]
    dkv0, dx, low, gain_a_0 = project_back(scal, addends, tables, da, qkv_parts, x, dm, gain_a)
    input_grad = low[None]

    gain_sum = jnp.concatenate([gain_a_0 + gain_a_1, gain_m_0 + gain_m_1], axis=0)
    gain_sum = lax.dynamic_slice_in_dim(all_sum(gain_sum, n), w * SL, SL, 1)
    ff_pieces = ff_piece_of(ff_grad)
    if n == 8:
        down_all = ring_gather(total_low(down_piece(0), down_go, down_back), n, position)
        ff_mine = total_low(*ring_scatter(at_position(ff_pieces, n, position), n))
    else:
        down_all = ring_sum(down_grad.reshape(n, FFQ // n, D), n, position)
        ff_mine = lax.psum_scatter(ff_pieces, "ctx", scatter_dimension=0, tiled=False)
    ff_all = ring_gather(rows_home(ff_mine, w), n, position)
    rows_grad = grad_rows(scal, slices, everyone(dkv0), dqs, dmls, rows_1)
    rows_all = ring_sum(rows_grad.reshape(n, 256 // n, QKV + D), n, position)
    if n == 8:
        down_total = finish_down(scal, down_all)
        gate_total, up_total = finish_ff(scal, ff_all)
        key_total, value_total, query_total, out_total = finish_rows(scal, rows_all, [KV, KV, D, D])
    else:
        sub = n // 8
        whole = placed(ff_all, n, position).reshape(2, 4, sub, WA, 64 // sub, FFQ)
        whole = whole.transpose(0, 3, 1, 2, 4, 5).reshape(2, WA, 256, FFQ)[:, :, :SL]
        whole = jnp.take(whole, w ^ jnp.arange(WA, dtype=i32), axis=1).transpose(0, 2, 1, 3)
        gate_total, up_total = whole.reshape(2, SL, -1).astype(f32)
        down_total = placed(down_all, n, position).reshape(FFQ, D).astype(f32)
        rows_total = placed(rows_all, n, position).reshape(256, QKV + D)[:SL].astype(f32)
        key_total, value_total, query_total, out_total = (
            rows_total[:, :KV],
            rows_total[:, KV : 2 * KV],
            rows_total[:, 2 * KV : QKV],
            rows_total[:, QKV:],
        )
    return (
        output,
        input_grad,
        gain_sum[0],
        query_total,
        key_total,
        value_total,
        out_total,
        gain_sum[1],
        gate_total,
        up_total,
        down_total,
    )


def solution(mesh):
    rows = P("wa", None)
    flat = P("wa")
    act = P("wa", "ctx", None)
    return jax.shard_map(
        body,
        mesh=mesh,
        in_specs=(act, act, rows, rows, flat, rows, rows, rows, rows, flat, rows, rows, rows),
        out_specs=(act, act, flat, rows, rows, rows, rows, flat, rows, rows, rows),
        check_vma=False,
    )
```

time: 594 us -> 486 us (0.82)
  Pallas kernels: 143 us -> 91.8 us
  other arithmetic: 28.1 us -> 5.21 us
  local copies, waits for them, and re-layouts: 85.9 us -> 69.3 us
  waiting for transfers between devices: 194 us -> 178 us
    pallas_call x25, Pallas kernels: 143 us -> 91.8 us  [call(): pl.pallas_call(body, name=name, in_specs=[SMEM] * n_scalar + [spec] * (le...]
    ppermute x58 -> x59, waiting for transfers between devices: 84.2 us -> 45.6 us  [swap(): return lax.ppermute(x, 'wa', [(i, i ^ mask) for i in range(WA)])]
    ppermute x96 -> x80, waiting for transfers between devices: 104 us -> 119 us  [ring_shift(): lax.ppermute(x, 'ctx', [(order[i], order[(i + step) % n]) for i in range(...]
    another operation x18 -> x5, other arithmetic: 14.1 us -> 1.03 us  [the longest x2 0.96 us: y_half(): jnp.stack([lax.dynamic_index_in_dim(keep[gu], x_side, 0, keepdims=False),...]
    another operation x11 -> x6, local copies, waits for them, and re-layouts: 10.6 us -> 0.06 us  [the longest x2 0.05 us: ring_keys(): return (jnp.stack(ahead[:4] + [far] + behind[3:0:-1]), done)]
    ppermute x96 -> x80, starting transfers between devices: 101 us -> 91.7 us  [ring_shift(): lax.ppermute(x, 'ctx', [(order[i], order[(i + step) % n]) for i in range(...]
    ppermute x1 -> x3, waiting for transfers between devices: 4.09 us -> 13.1 us  [side_swap(): return lax.ppermute(x, 'ctx', [(i, i ^ 1) for i in range(n)])]
    unnamed x325 -> x326, local copies, waits for them, and re-layouts: 48.3 us -> 56.6 us
  transfers between devices with their start and end apart: 158 -> 145, of which waited for: 57 -> 54; matrix products, arithmetic and copies ran while one was open for 13% -> 6% of each run, Pallas kernels for 22% -> 18%
where the time goes in v3:
time: 486 us; the launch traced here: 478 us
  waiting for transfers between devices  178 us (37%)
  starting transfers between devices  131 us (27%)
  Pallas kernels  91.8 us (19%)
  local copies, waits for them, and re-layouts  69.3 us (14%)
  other arithmetic  5.21 us (1%)
    ppermute x80, waiting for transfers between devices, ring_shift(): lax.ppermute(x, 'ctx', [(order[i], order[(i + step) % n]) for i in range(...  119 us
    pallas_call x25, Pallas kernels, call(): pl.pallas_call(body, name=name, in_specs=[SMEM] * n_scalar + [spec] * (le...  91.8 us
    ppermute x80, starting transfers between devices, ring_shift(): lax.ppermute(x, 'ctx', [(order[i], order[(i + step) % n]) for i in range(...  91.7 us
    unnamed x326, local copies, waits for them, and re-layouts  56.6 us
    ppermute x59, waiting for transfers between devices, swap(): return lax.ppermute(x, 'wa', [(i, i ^ mask) for i in range(WA)])  45.6 us
    ppermute x59, starting transfers between devices, swap(): return lax.ppermute(x, 'wa', [(i, i ^ mask) for i in range(WA)])  31.6 us
    ppermute x3, waiting for transfers between devices, side_swap(): return lax.ppermute(x, 'ctx', [(i, i ^ 1) for i in range(n)])  13.1 us
  transfers between devices with their start and end apart: 145, of which 54 were waited for; matrix products, arithmetic and copies ran while one was open for 6% of the time, Pallas kernels for 18%

profile of v3, /device:TPU:0, one launch (start us, length us, event | category | flops | bytes accessed | tf_op | source)
XLA Modules:
  0.0 478.0 jit_solution(1125067911684430726)
XLA Ops:
  33.1 19.9 %collective-permute-done.6.p2 = bf16[240,960]{1,0:T(8,128)(2,1)} collective-permute-done((bf16[240,960]{1,0:T(8,128)(2,1)}, bf16[240,960]{1,0:T(8,128)(2,1)}, u32[]{:S(2)}, u32[]{:S(2)}) %collective-permute-start.6) | collective-permute-done | bytes 460832 | tf_op jit(solution)/shard_map/ppermute | solution.py:35
  61.8 11.2 %collective-permute-done.4 = bf16[128,640]{1,0:T(8,128)(2,1)S(1)} collective-permute-done((bf16[128,640]{1,0:T(8,128)(2,1)S(1)}, bf16[128,640]{1,0:T(8,128)(2,1)S(1)}, u32[]{:S(2)}, u32[]{:S(2)}) %collective-permute-start.4) | collective-permute-done | bytes 163872 | tf_op jit(solution)/shard_map/ppermute | solution.py:48
  76.9 3.5 collective-permute-done.7
  82.5 3.3 collective-permute-done.12
  96.3 5.6 %attend.2 = (bf16[2,128,240]{2,1,0:T(8,128)(2,1)S(1)}, bf16[2,128,240]{2,1,0:T(8,128)(2,1)S(1)}, bf16[2,128,240]{2,1,0:T(8,128)(2,1)S(1)}, bf16[2,128,240]{2,1,0...) custom-call(s32[5]{0:T(128)S(1)} %stack.127.sc, ...), custom_call_target="tpu_custom_call" | custom-call | flops 11500000256 | bytes 65536 | tf_op jit(solution)/shard_map/attend/pallas_call | solution.py:169
  109.8 10.6 %collective-permute-done.21 = bf16[320,960]{1,0:T(8,128)(2,1)S(1)} collective-permute-done((bf16[320,960]{1,0:T(8,128)(2,1)S(1)}, bf16[320,960]{1,0:T(8,128)(2,1)S(1)}, u32[]{:S(2)}, u32[]{:S(2)}) %collective-permute-start.21) | collective-permute-done | bytes 614432 | tf_op jit(solution)/shard_map/ppermute | solution.py:39
  122.5 6.0 %mlp.2 = (bf16[256,640]{1,0:T(8,128)(2,1)S(1)}, bf16[256,640]{1,0:T(8,128)(2,1)S(1)}, f32[2,2,256,640]{3,2,1,0:T(8,128)S(1)}, f32[128,960]{1,0:T(8,128)S(1)}, f32[128,960]{1,0:T(8,128)}) custom-call(s32[5]{0:T(128)S(1)} %stack.127.sc, bf16[128,960]{1,0:T(8,128)(2,1)S(1)} %get-tuple-element.232.b_own.refs_0_, ...), custom_call_target="tpu_custom_call" | custom-call | flops 6325000192 | bytes 65536 | tf_op jit(solution)/shard_map/mlp/pallas_call | solution.py:169
  159.2 3.2 collective-permute-done.32
  170.6 6.0 %attend.3 = (bf16[2,128,240]{2,1,0:T(8,128)(2,1)S(1)}, bf16[2,128,240]{2,1,0:T(8,128)(2,1)S(1)}, bf16[2,128,240]{2,1,0:T(8,128)(2,1)S(1)}, bf16[2,128,240]{2,1,0...) custom-call(s32[5]{0:T(128)S(1)} %stack.127.sc, ...), custom_call_target="tpu_custom_call" | custom-call | flops 11500000256 | bytes 65536 | tf_op jit(solution)/shard_map/attend/pallas_call | solution.py:169
  178.3 5.1 %mlp.3 = (bf16[256,640]{1,0:T(8,128)(2,1)S(1)}, bf16[256,640]{1,0:T(8,128)(2,1)S(1)}, f32[2,2,256,640]{3,2,1,0:T(8,128)S(1)}, f32[128,960]{1,0:T(8,128)S(1)}, f32[128,960]{1,0:T(8,128)S(1)}) custom-call(s32[5]{0:T(128)S(1)} %stack.127.sc, bf16[128,960]{1,0:T(8,128)(2,1)S(1)} %get-tuple-element.265.b_own.refs_0_, ...), custom_call_target="tpu_custom_call" | custom-call | flops 6325000192 | bytes 65536 | tf_op jit(solution)/shard_map/mlp/pallas_call | solution.py:169
  186.0 6.0 %mlp_back.2 = (bf16[2,256,640]{2,1,0:T(8,128)(2,1)S(1)}, bf16[2,256,640]{2,1,0:T(8,128)(2,1)S(1)}, f32[128,960]{1,0:T(8,128)S(1)}, f32[128,960]{1,0:T(8,128)S(1)}) custom-call(s32[5]{0:T(128)S(1)} %stack.127.sc, bf16[128,960]{1,0:T(8,128)(2,1)S(1)} %bitcast.271, bf16[128,960]{1,0:T(8,128)(2,1)S(1)} %collective-permute-done.38.l_side.refs_3_, ...), custom_call_target="tpu_custom_call" | custom-call | flops 7704999936 | bytes 65536 | tf_op jit(solution)/shard_map/mlp_back/pallas_call | solution.py:169
  192.0 3.6 collective-permute-done.42.refs_1_
  199.0 7.1 %attend_back.2 = (f32[128,960]{1,0:T(8,128)S(1)}, bf16[128,960]{1,0:T(8,128)(2,1)S(1)}, f32[1,960]{1,0:T(1,128)S(1)}, bf16[128,960]{1,0:T(8,128)(2,1)S(1)}, bf16[8,128,640]{2,1,0:T(8,128)(2,1)S(1)}) custom-call(s32[5]{0:T(128)S(1)} %stack.127.sc, s32[9]{0:T(128)S(1)} %pad_add_fusion.1.sched, s32[8,384]{1,0:T(8,128)S(1)} %pad.8.qinfo, ...), custom_call_target="tpu_custom_call" | custom-call | flops 13799999488 | bytes 65536 | tf_op jit(solution)/shard_map/attend_back/pallas_call | solution.py:169
  206.1 13.1 %collective-permute-done.46.refs_5_ = bf16[2,256,640]{2,1,0:T(8,128)(2,1)S(1)} collective-permute-done((bf16[2,256,640]{2,1,0:T(8,128)(2,1)S(1)}, bf16[2,256,640]{2,1,0:T(8,128)(2,1)S(1)}, u32[]{:S(2)}, u32[]{:S(2)}) %collective-permute-start.46) | collective-permute-done | bytes 655392 | tf_op jit(solution)/shard_map/ppermute | solution.py:35
  253.2 7.0 %mlp_back.3 = (bf16[2,256,640]{2,1,0:T(8,128)(2,1)S(1)}, bf16[2,256,640]{2,1,0:T(8,128)(2,1)S(1)}, f32[128,960]{1,0:T(8,128)S(1)}, f32[128,960]{1,0:T(8,128)}) custom-call(s32[5]{0:T(128)S(1)} %stack.127.sc, bf16[128,960]{1,0:T(8,128)(2,1)S(1)} %get-tuple-element.319.l_own.refs_2_, bf16[128,960]{1,0:T(8,128)(2,1)S(1)} %collective-permute-done.64.l_side.refs_3_, ...), custom_call_target="tpu_custom_call" | custom-call | flops 7704999936 | bytes 65536 | tf_op jit(solution)/shard_map/mlp_back/pallas_call | solution.py:169
  271.0 3.7 grad_down.3
  277.0 7.3 %attend_back.3 = (f32[128,960]{1,0:T(8,128)S(1)}, bf16[128,960]{1,0:T(8,128)(2,1)S(1)}, f32[1,960]{1,0:T(1,128)S(1)}, bf16[128,960]{1,0:T(8,128)(2,1)S(1)}, bf16[8,128,640]{2,1,0:T(8,128)(2,1)S(1)}) custom-call(s32[5]{0:T(128)S(1)} %stack.127.sc, s32[9]{0:T(128)S(1)} %pad_add_fusion.1.sched, s32[8,384]{1,0:T(8,128)S(1)} %pad.8.qinfo, ...), custom_call_target="tpu_custom_call" | custom-call | flops 13799999488 | bytes 65536 | tf_op jit(solution)/shard_map/attend_back/pallas_call | solution.py:169
  286.7 3.2 collective-permute-start.73
  290.5 3.5 grad_ff.3
  299.1 4.1 grad_rows.2.refs_16_
  306.2 3.8 collective-permute-done.81
  313.6 3.4 collective-permute-done.78
  353.8 4.4 grad_rows.3
  367.9 11.8 %collective-permute-done.103 = bf16[32,2560]{1,0:T(8,128)(2,1)S(1)} collective-permute-done((bf16[32,2560]{1,0:T(8,128)(2,1)S(1)}, bf16[32,2560]{1,0:T(8,128)(2,1)S(1)}, u32[]{:S(2)}, u32[]{:S(2)}) %collective-permute-start.103) | collective-permute-done | bytes 163872 | tf_op jit(solution)/shard_map/ppermute | solution.py:48
  383.1 4.4 collective-permute-done.107
  390.1 6.3 %collective-permute-done.124 = bf16[4,64,640]{2,1,0:T(8,128)(2,1)S(1)} collective-permute-done((bf16[4,64,640]{2,1,0:T(8,128)(2,1)S(1)}, bf16[4,64,640]{2,1,0:T(8,128)(2,1)S(1)}, u32[]{:S(2)}, u32[]{:S(2)}) %collective-permute-start.124) | collective-permute-done | bytes 327712 | tf_op jit(solution)/shard_map/ppermute | solution.py:48
  398.9 4.5 collective-permute-done.108
  405.7 5.6 %collective-permute-done.125 = bf16[4,64,640]{2,1,0:T(8,128)(2,1)S(1)} collective-permute-done((bf16[4,64,640]{2,1,0:T(8,128)(2,1)S(1)}, bf16[4,64,640]{2,1,0:T(8,128)(2,1)S(1)}, u32[]{:S(2)}, u32[]{:S(2)}) %collective-permute-start.125) | collective-permute-done | bytes 327712 | tf_op jit(solution)/shard_map/ppermute | solution.py:48
  413.5 3.2 collective-permute-done.109
  435.3 4.5 collective-permute-done.129.refs_1_
  456.2 7.0 %collective-permute-done.135.refs_5_ = bf16[4,64,640]{2,1,0:T(8,128)(2,1)S(1)} collective-permute-done((bf16[4,64,640]{2,1,0:T(8,128)(2,1)}, bf16[4,64,640]{2,1,0:T(8,128)(2,1)S(1)}, u32[]{:S(2)}, u32[]{:S(2)}) %collective-permute-start.135) | collective-permute-done | bytes 327712 | tf_op jit(solution)/shard_map/ppermute | solution.py:48
  473.5 4.1 finish_ff.1
  (716 shorter events, 278.3 us)
Async XLA Ops:
  4.6 21.5 %collective-permute-start = (bf16[248,1600]{0,1:T(8,128)(2,1)}, bf16[248,1600]{0,1:T(8,128)(2,1)}, u32[]{:S(2)}, u32[]{:S(2)}) collective-permute-start(bf16[248,1600]{0,1:T(8,128)(2,1)} %copy.104), channel_id=1, source_target_pairs={{0,2},{1,3},{2,0},{3,1},{4,6},{5,7},{6,4},{7,5},{8,10},{9,11},{10,... | collective-permute-start | bytes 2380808 | tf_op jit(solution)/shard_map/ppermute | solution.py:35
  7.6 18.6 %collective-permute-start.1 = (bf16[248,1600]{0,1:T(8,128)(2,1)}, bf16[248,1600]{0,1:T(8,128)(2,1)}, u32[]{:S(2)}, u32[]{:S(2)}) collective-permute-start(bf16[248,1600]{0,1:T(8,128)(2,1)} %copy.104), channel_id=1, source_target_pairs={{0,1},{1,0},{2,3},{3,2},{4,5},{5,4},{6,7},{7,6},{8,9},{9,8},{10,11... | collective-permute-start | bytes 2380808 | tf_op jit(solution)/shard_map/ppermute | solution.py:35
  26.1 28.6 %collective-permute-start.3 = (bf16[248,1600]{0,1:T(8,128)(2,1)}, bf16[248,1600]{0,1:T(8,128)(2,1)}, u32[]{:S(2)}, u32[]{:S(2)}) collective-permute-start(bf16[248,1600]{0,1:T(8,128)(2,1)} %collective-permute-done), channel_id=1, source_target_pairs={{0,1},{1,0},{2,3},{3,2},{4,5},{5,4},{6,7},{7,6},{8,9},{9,8},{10,11... | collective-permute-start | bytes 2380808 | tf_op jit(solution)/shard_map/ppermute | solution.py:35
  26.2 26.9 %collective-permute-start.11 = (bf16[2,240,640]{2,1,0:T(8,128)(2,1)S(1)}, bf16[2,240,640]{2,1,0:T(8,128)(2,1)}, u32[]{:S(2)}, u32[]{:S(2)}) collective-permute-start(bf16[2,240,640]{2,1,0:T(8,128)(2,1)S(1)} %pad_maximum_fusion.1), channel_id=1, source_target_pairs={{0,2},{1,3},{2,0},{3,1},{4,6},{5,7},{6,4},{7,5},{8,10},{9,11},{10,... | collective-permute-start | bytes 1843208 | tf_op jit(solution)/shard_map/ppermute | solution.py:35
  28.0 25.1 %collective-permute-start.6 = (bf16[240,960]{1,0:T(8,128)(2,1)}, bf16[240,960]{1,0:T(8,128)(2,1)}, u32[]{:S(2)}, u32[]{:S(2)}) collective-permute-start(bf16[240,960]{1,0:T(8,128)(2,1)} %get-tuple-element.209.p0), channel_id=1, source_target_pairs={{0,2},{1,3},{2,0},{3,1},{4,6},{5,7},{6,4},{7,5},{8,10},{9,11},{10,... | collective-permute-start | bytes 1382408 | tf_op jit(solution)/shard_map/ppermute | solution.py:35
  31.1 43.7 %collective-permute-start.10 = (bf16[240,960]{1,0:T(8,128)(2,1)}, bf16[240,960]{1,0:T(8,128)(2,1)}, u32[]{:S(2)}, u32[]{:S(2)}) collective-permute-start(bf16[240,960]{1,0:T(8,128)(2,1)} %get-tuple-element.209.p0), channel_id=1, source_target_pairs={{0,1},{1,0},{2,3},{3,2},{4,5},{5,4},{6,7},{7,6},{8,9},{9,8},{10,11... | collective-permute-start | bytes 1382408 | tf_op jit(solution)/shard_map/ppermute | solution.py:35
  53.1 23.8 %collective-permute-start.9 = (bf16[240,960]{1,0:T(8,128)(2,1)}, bf16[240,960]{1,0:T(8,128)(2,1)}, u32[]{:S(2)}, u32[]{:S(2)}) collective-permute-start(bf16[240,960]{1,0:T(8,128)(2,1)} %collective-permute-done.6.p2), channel_id=1, source_target_pairs={{0,1},{1,0},{2,3},{3,2},{4,5},{5,4},{6,7},{7,6},{8,9},{9,8},{10,11... | collective-permute-start | bytes 1382408 | tf_op jit(solution)/shard_map/ppermute | solution.py:35
  53.1 37.0 %collective-permute-start.17 = (bf16[2,240,640]{2,1,0:T(8,128)(2,1)}, bf16[2,240,640]{2,1,0:T(8,128)(2,1)}, u32[]{:S(2)}, u32[]{:S(2)}) collective-permute-start(bf16[2,240,640]{2,1,0:T(8,128)(2,1)} %collective-permute-done.11.gm), channel_id=1, source_target_pairs={{0,4},{4,0},{8,12},{12,8},{16,20},{20,16},{24,28},{28,24},{1,5},{5... | collective-permute-start | bytes 1843208 | tf_op jit(solution)/shard_map/ppermute | solution.py:39
  73.1 21.4 %collective-permute-start.16 = (bf16[2,240,640]{2,1,0:T(8,128)(2,1)S(1)}, bf16[2,240,640]{2,1,0:T(8,128)(2,1)S(1)}, u32[]{:S(2)}, u32[]{:S(2)}) collective-permute-start(bf16[2,240,640]{2,1,0:T(8,128)(2,1)S(1)} %copy-done.141), channel_id=1, source_target_pairs={{0,2},{1,3},{2,0},{3,1},{4,6},{5,7},{6,4},{7,5},{8,10},{9,11},{10,... | collective-permute-start | bytes 1843208 | tf_op jit(solution)/shard_map/ppermute | solution.py:35
  109.0 23.3 %collective-permute-start.22 = (bf16[128,960]{1,0:T(8,128)(2,1)S(1)}, bf16[128,960]{1,0:T(8,128)(2,1)}, u32[]{:S(2)}, u32[]{:S(2)}) collective-permute-start(bf16[128,960]{1,0:T(8,128)(2,1)S(1)} %get-tuple-element.232.b_own.refs_0_), channel_id=1, source_target_pairs={{0,2},{1,3},{2,0},{3,1},{4,6},{5,7},{6,4},{7,5},{8,10},{9,11},{10,... | collective-permute-start | bytes 737288 | tf_op jit(solution)/shard_map/ppermute | solution.py:35
  134.1 19.1 %collective-permute-start.30 = (bf16[2,128,240]{2,1,0:T(8,128)(2,1)}, bf16[2,128,240]{2,1,0:T(8,128)(2,1)S(1)}, u32[]{:S(2)}, u32[]{:S(2)}) collective-permute-start(bf16[2,128,240]{2,1,0:T(8,128)(2,1)} %copy-done.109), channel_id=1, source_target_pairs={{0,1},{1,0},{2,3},{3,2},{4,5},{5,4},{6,7},{7,6},{8,9},{9,8},{10,11... | collective-permute-start | bytes 368648 | tf_op jit(solution)/shard_map/ppermute | solution.py:35
  196.4 28.9 %collective-permute-start.49 = (bf16[2,128,240]{2,1,0:T(8,128)(2,1)S(1)}, bf16[2,128,240]{2,1,0:T(8,128)(2,1)S(1)}, u32[]{:S(2)}, u32[]{:S(2)}) collective-permute-start(bf16[2,128,240]{2,1,0:T(8,128)(2,1)S(1)} %get-tuple-element.290), channel_id=1, source_target_pairs={{0,1},{1,0},{2,3},{3,2},{4,5},{5,4},{6,7},{7,6},{8,9},{9,8},{10,11... | collective-permute-start | bytes 368648 | tf_op jit(solution)/shard_map/ppermute | solution.py:35
  196.9 30.2 %collective-permute-start.50 = (bf16[2,128,240]{2,1,0:T(8,128)(2,1)S(1)}, bf16[2,128,240]{2,1,0:T(8,128)(2,1)S(1)}, u32[]{:S(2)}, u32[]{:S(2)}) collective-permute-start(bf16[2,128,240]{2,1,0:T(8,128)(2,1)S(1)} %get-tuple-element.291), channel_id=1, source_target_pairs={{0,2},{1,3},{2,0},{3,1},{4,6},{5,7},{6,4},{7,5},{8,10},{9,11},{10,... | collective-permute-start | bytes 368648 | tf_op jit(solution)/shard_map/ppermute | solution.py:35
  197.2 34.1 %collective-permute-start.53 = (bf16[2,128,240]{2,1,0:T(8,128)(2,1)S(1)}, bf16[2,128,240]{2,1,0:T(8,128)(2,1)S(1)}, u32[]{:S(2)}, u32[]{:S(2)}) collective-permute-start(bf16[2,128,240]{2,1,0:T(8,128)(2,1)S(1)} %get-tuple-element.297), channel_id=1, source_target_pairs={{0,3},{1,2},{2,1},{3,0},{4,7},{5,6},{6,5},{7,4},{8,11},{9,10},{10,... | collective-permute-start | bytes 368648 | tf_op jit(solution)/shard_map/ppermute | solution.py:35
  198.2 20.9 %collective-permute-start.46 = (bf16[2,256,640]{2,1,0:T(8,128)(2,1)S(1)}, bf16[2,256,640]{2,1,0:T(8,128)(2,1)S(1)}, u32[]{:S(2)}, u32[]{:S(2)}) collective-permute-start(bf16[2,256,640]{2,1,0:T(8,128)(2,1)S(1)} %get-tuple-element.288), channel_id=1, source_target_pairs={{0,2},{1,3},{2,0},{3,1},{4,6},{5,7},{6,4},{7,5},{8,10},{9,11},{10,... | collective-permute-start | bytes 1966088 | tf_op jit(solution)/shard_map/ppermute | solution.py:35
  227.7 17.0 %collective-permute-start.60 = (bf16[128,960]{1,0:T(8,128)(2,1)S(1)}, bf16[128,960]{1,0:T(8,128)(2,1)S(1)}, u32[]{:S(2)}, u32[]{:S(2)}) collective-permute-start(bf16[128,960]{1,0:T(8,128)(2,1)S(1)} %get-tuple-element.299.dq.refs_8_), channel_id=1, source_target_pairs={{0,1},{1,0},{2,3},{3,2},{4,5},{5,4},{6,7},{7,6},{8,9},{9,8},{10,11... | collective-permute-start | bytes 737288 | tf_op jit(solution)/shard_map/ppermute | solution.py:35
  263.2 23.5 %collective-permute-start.69 = (bf16[128,640]{1,0:T(8,128)(2,1)}, bf16[128,640]{1,0:T(8,128)(2,1)S(1)}, u32[]{:S(2)}, u32[]{:S(2)}) collective-permute-start(bf16[128,640]{1,0:T(8,128)(2,1)} %copy-done.77), channel_id=1, source_target_pairs={{0,1},{1,0},{2,3},{3,2},{4,5},{5,4},{6,7},{7,6},{8,9},{9,8},{10,11... | collective-permute-start | bytes 491528 | tf_op jit(solution)/shard_map/ppermute | solution.py:35
  263.3 23.3 %collective-permute-start.70 = (bf16[128,640]{1,0:T(8,128)(2,1)}, bf16[128,640]{1,0:T(8,128)(2,1)S(1)}, u32[]{:S(2)}, u32[]{:S(2)}) collective-permute-start(bf16[128,640]{1,0:T(8,128)(2,1)} %copy-done.77), channel_id=1, source_target_pairs={{0,2},{1,3},{2,0},{3,1},{4,6},{5,7},{6,4},{7,5},{8,10},{9,11},{10,... | collective-permute-start | bytes 491528 | tf_op jit(solution)/shard_map/ppermute | solution.py:35
  263.9 22.7 %collective-permute-start.68 = (bf16[2,256,640]{2,1,0:T(8,128)(2,1)}, bf16[2,256,640]{2,1,0:T(8,128)(2,1)S(1)}, u32[]{:S(2)}, u32[]{:S(2)}) collective-permute-start(bf16[2,256,640]{2,1,0:T(8,128)(2,1)} %copy-done.41), channel_id=1, source_target_pairs={{0,2},{1,3},{2,0},{3,1},{4,6},{5,7},{6,4},{7,5},{8,10},{9,11},{10,... | collective-permute-start | bytes 1966088 | tf_op jit(solution)/shard_map/ppermute | solution.py:35
  286.7 18.6 %collective-permute-start.73 = (bf16[128,960]{1,0:T(8,128)(2,1)S(1)}, bf16[128,960]{1,0:T(8,128)(2,1)S(1)}, u32[]{:S(2)}, u32[]{:S(2)}) collective-permute-start(bf16[128,960]{1,0:T(8,128)(2,1)S(1)} %get-tuple-element.343.dq.refs_8_), channel_id=1, source_target_pairs={{0,2},{1,3},{2,0},{3,1},{4,6},{5,7},{6,4},{7,5},{8,10},{9,11},{10,... | collective-permute-start | bytes 737288 | tf_op jit(solution)/shard_map/ppermute | solution.py:35
  289.9 45.5 %collective-permute-start.90 = (bf16[128,960]{1,0:T(8,128)(2,1)S(1)}, bf16[128,960]{1,0:T(8,128)(2,1)S(1)}, u32[]{:S(2)}, u32[]{:S(2)}) collective-permute-start(bf16[128,960]{1,0:T(8,128)(2,1)S(1)} %get-tuple-element.343.dq.refs_8_), channel_id=1, source_target_pairs={{0,1},{1,0},{2,3},{3,2},{4,5},{5,4},{6,7},{7,6},{8,9},{9,8},{10,11... | collective-permute-start | bytes 737288 | tf_op jit(solution)/shard_map/ppermute | solution.py:35
  289.9 45.6 %collective-permute-start.91 = (bf16[128,960]{1,0:T(8,128)(2,1)S(1)}, bf16[128,960]{1,0:T(8,128)(2,1)S(1)}, u32[]{:S(2)}, u32[]{:S(2)}) collective-permute-start(bf16[128,960]{1,0:T(8,128)(2,1)S(1)} %get-tuple-element.348.refs_12_), channel_id=1, source_target_pairs={{0,1},{1,0},{2,3},{3,2},{4,5},{5,4},{6,7},{7,6},{8,9},{9,8},{10,11... | collective-permute-start | bytes 737288 | tf_op jit(solution)/shard_map/ppermute | solution.py:35
  318.9 24.9 %collective-permute-start.100 = (bf16[128,960]{1,0:T(8,128)(2,1)S(1)}, bf16[128,960]{1,0:T(8,128)(2,1)S(1)}, u32[]{:S(2)}, u32[]{:S(2)}) collective-permute-start(bf16[128,960]{1,0:T(8,128)(2,1)S(1)} %collective-permute-done.73.refs_10_), channel_id=1, source_target_pairs={{0,1},{1,0},{2,3},{3,2},{4,5},{5,4},{6,7},{7,6},{8,9},{9,8},{10,11... | collective-permute-start | bytes 737288 | tf_op jit(solution)/shard_map/ppermute | solution.py:35
  335.5 15.2 %collective-permute-start.101 = (bf16[128,960]{1,0:T(8,128)(2,1)S(1)}, bf16[128,960]{1,0:T(8,128)(2,1)S(1)}, u32[]{:S(2)}, u32[]{:S(2)}) collective-permute-start(bf16[128,960]{1,0:T(8,128)(2,1)S(1)} %collective-permute-done.80.refs_14_), channel_id=1, source_target_pairs={{0,1},{1,0},{2,3},{3,2},{4,5},{5,4},{6,7},{7,6},{8,9},{9,8},{10,11... | collective-permute-start | bytes 737288 | tf_op jit(solution)/shard_map/ppermute | solution.py:35
  350.7 14.0 %collective-permute-start.142 = (bf16[80,960]{1,0:T(8,128)(2,1)S(1)}, bf16[80,960]{1,0:T(8,128)(2,1)S(1)}, u32[]{:S(2)}, u32[]{:S(2)}) collective-permute-start(bf16[80,960]{1,0:T(8,128)(2,1)S(1)} %collective-permute-done.141.refs_7_), channel_id=1, source_target_pairs={{0,4},{8,0},{16,8},{24,16},{28,24},{20,28},{12,20},{4,12},{1,5},{9... | collective-permute-start | bytes 460808 | tf_op jit(solution)/shard_map/ppermute | solution.py:48
  362.7 17.3 %collective-permute-start.123 = (bf16[4,64,640]{2,1,0:T(8,128)(2,1)S(1)}, bf16[4,64,640]{2,1,0:T(8,128)(2,1)S(1)}, u32[]{:S(2)}, u32[]{:S(2)}) collective-permute-start(bf16[4,64,640]{2,1,0:T(8,128)(2,1)S(1)} %pad_maximum_fusion.4), channel_id=1, source_target_pairs={{0,4},{8,0},{16,8},{24,16},{28,24},{20,28},{12,20},{4,12},{1,5},{9... | collective-permute-start | bytes 983048 | tf_op jit(solution)/shard_map/ppermute | solution.py:48
  364.7 63.1 %collective-permute-start.139 = (bf16[80,960]{1,0:T(8,128)(2,1)S(1)}, bf16[80,960]{1,0:T(8,128)(2,1)S(1)}, u32[]{:S(2)}, u32[]{:S(2)}) collective-permute-start(bf16[80,960]{1,0:T(8,128)(2,1)S(1)} %collective-permute-done.138.refs_2_), channel_id=1, source_target_pairs={{0,8},{8,16},{16,24},{24,28},{28,20},{20,12},{12,4},{4,0},{1,9},{9... | collective-permute-start | bytes 460808 | tf_op jit(solution)/shard_map/ppermute | solution.py:48
  364.7 53.0 %collective-permute-start.143 = (bf16[80,960]{1,0:T(8,128)(2,1)S(1)}, bf16[80,960]{1,0:T(8,128)(2,1)S(1)}, u32[]{:S(2)}, u32[]{:S(2)}) collective-permute-start(bf16[80,960]{1,0:T(8,128)(2,1)S(1)} %collective-permute-done.142.refs_6_), channel_id=1, source_target_pairs={{0,4},{8,0},{16,8},{24,16},{28,24},{20,28},{12,20},{4,12},{1,5},{9... | collective-permute-start | bytes 460808 | tf_op jit(solution)/shard_map/ppermute | solution.py:48
  366.8 16.2 %collective-permute-start.120 = (bf16[4,64,640]{2,1,0:T(8,128)(2,1)S(1)}, bf16[4,64,640]{2,1,0:T(8,128)(2,1)S(1)}, u32[]{:S(2)}, u32[]{:S(2)}) collective-permute-start(bf16[4,64,640]{2,1,0:T(8,128)(2,1)S(1)} %fusion.2), channel_id=1, source_target_pairs={{0,8},{8,16},{16,24},{24,28},{28,20},{20,12},{12,4},{4,0},{1,9},{9... | collective-permute-start | bytes 983048 | tf_op jit(solution)/shard_map/ppermute | solution.py:48
  379.7 37.9 %collective-permute-start.95 = (f32[2,960]{1,0:T(2,128)S(1)}, f32[2,960]{1,0:T(2,128)S(1)}, u32[]{:S(2)}, u32[]{:S(2)}) collective-permute-start(f32[2,960]{1,0:T(2,128)S(1)} %add.354), channel_id=1, source_target_pairs={{0,8},{4,12},{8,0},{12,4},{16,24},{20,28},{24,16},{28,20},{1,9},{5... | collective-permute-start | bytes 23048 | tf_op jit(solution)/shard_map/ppermute | solution.py:153
  390.0 15.6 %collective-permute-start.121 = (bf16[4,64,640]{2,1,0:T(8,128)(2,1)S(1)}, bf16[4,64,640]{2,1,0:T(8,128)(2,1)S(1)}, u32[]{:S(2)}, u32[]{:S(2)}) collective-permute-start(bf16[4,64,640]{2,1,0:T(8,128)(2,1)S(1)} %get-tuple-element.433), channel_id=1, source_target_pairs={{0,8},{8,16},{16,24},{24,28},{28,20},{20,12},{12,4},{4,0},{1,9},{9... | collective-permute-start | bytes 983048 | tf_op jit(solution)/shard_map/ppermute | solution.py:48
  439.9 14.7 %collective-permute-start.134 = (bf16[4,64,640]{2,1,0:T(8,128)(2,1)}, bf16[4,64,640]{2,1,0:T(8,128)(2,1)}, u32[]{:S(2)}, u32[]{:S(2)}) collective-permute-start(bf16[4,64,640]{2,1,0:T(8,128)(2,1)} %collective-permute-done.133.refs_7_), channel_id=1, source_target_pairs={{0,4},{8,0},{16,8},{24,16},{28,24},{20,28},{12,20},{4,12},{1,5},{9... | collective-permute-start | bytes 983048 | tf_op jit(solution)/shard_map/ppermute | solution.py:48
  (264 other events, 2077.8 us)

commit v4 on v3

--- a/solution.py
+++ b/solution.py
@@ -21,6 +21,7 @@
 QKV = 2 * KV + D
 FFQ = 640
 R3 = GQ * BLK
+QKVP = 1664
 
 epsilon = 1e-05
 masked_score = -1e30
@@ -145,16 +146,6 @@
     return out
 
 
-def all_sum(x, n):
-    for mask in (1, 2):
-        x = x + swap(x, mask)
-    step = 1
-    while step < n:
-        x = x + lax.ppermute(x, "ctx", [(i, i ^ step) for i in range(n)])
-        step *= 2
-    return x
-
-
 def everyone(x):
     side = swap(x, 1)
     across = swap(x, 2)
@@ -165,12 +156,15 @@
 SMEM = pl.BlockSpec(memory_space=pltpu.SMEM)
 
 
-def call(body, name, n_scalar, ins, outs, scratch=(), us=2.0, limit=10, spec=VMEM):
+HBM = pl.BlockSpec(memory_space=pltpu.HBM)
+
+
+def call(body, name, n_scalar, ins, outs, scratch=(), us=2.0, limit=10, specs=None, out_specs=None):
     return pl.pallas_call(
         body,
         name=name,
-        in_specs=[SMEM] * n_scalar + [spec] * (len(ins) - n_scalar),
-        out_specs=[VMEM] * len(outs),
+        in_specs=[SMEM] * n_scalar + (specs or [VMEM] * (len(ins) - n_scalar)),
+        out_specs=out_specs or [VMEM] * len(outs),
         out_shape=list(outs),
         scratch_shapes=list(scratch),
         cost_estimate=pl.CostEstimate(flops=int(us * 1.15e9), transcendentals=0, bytes_accessed=1 << 16),
@@ -178,6 +172,45 @@
     )(*ins)
 
 
+def fetched(refs, bufs, sem):
+    copies = [pltpu.make_async_copy(r, b, sem.at[i]) for i, (r, b) in enumerate(zip(refs, bufs))]
+    for c in copies:
+        c.start()
+    for c in copies:
+        c.wait()
+
+
+def call_fetched(body, name, scal, ins, outs, us, limit, scratch=(), far=None, far_out=False):
+    count, n_out = len(ins), len(outs)
+    far = [True] * count if far is None else far
+
+    def whole(sc, *refs):
+        sources, results = refs[:count], refs[count : count + n_out]
+        bufs = refs[count + n_out : 2 * count + n_out]
+        sem, rest = refs[2 * count + n_out], refs[2 * count + n_out + 1 :]
+        fetched(sources, bufs, sem)
+        if not far_out:
+            body(sc, *bufs, *results, *rest)
+            return
+        body(sc, *bufs, *rest)
+        fetched(rest[:n_out], results, sem)
+
+    bufs = [pltpu.VMEM(x.shape, x.dtype) for x in ins]
+    held = [pltpu.VMEM(x.shape, x.dtype) for x in outs] if far_out else []
+    return call(
+        whole,
+        name,
+        1,
+        [scal, *ins],
+        outs,
+        bufs + [pltpu.SemaphoreType.DMA((max(count, n_out),)), *held, *scratch],
+        us=us,
+        limit=limit,
+        specs=[HBM if f else pl.BlockSpec(memory_space=pl.ANY) for f in far],
+        out_specs=[HBM] * n_out if far_out else None,
+    )
+
+
 def shape(dims, dtype):
     return jax.ShapeDtypeStruct(dims, dtype)
 
@@ -212,18 +245,25 @@
     return u * cos + turn_back(u * sin)
 
 
-def pack_qkv_body(wq, wk, wv, gains, out):
-    out[:SL, :KV] = wk[...].astype(bf16)
-    out[:SL, KV : 2 * KV] = wv[...].astype(bf16)
-    out[:SL, 2 * KV :] = wq[...].astype(bf16)
-    out[SL:, :] = jnp.zeros((8, QKV), bf16)
+def pack_qkv_body(sc, wq, wk, wv, gains, out):
+    out[:SL, :KV] = wk[...].T.astype(bf16)
+    out[:SL, KV : 2 * KV] = wv[...].T.astype(bf16)
+    out[:SL, 2 * KV : QKV] = wq[...].astype(bf16)
+    out[:SL, QKV:] = jnp.zeros((SL, QKVP - QKV), bf16)
+    out[SL:, :] = jnp.zeros((8, QKVP), bf16)
     out[SL:, :SL] = gains[...].astype(bf16)
+
+
+def pack_qkv(scal, wq, wk, wv, gains):
+    ins = [wq, wk.T, wv.T, gains]
+    outs = [shape((SL + 8, QKVP), bf16)]
+    return call_fetched(pack_qkv_body, "pack_qkv", scal, ins, outs, us=3, limit=8)[0]
 
 
 def pack_rest_body(sc, w_out, w_gate, w_up, w_down, out_ref, keep, give, down):
     core = sc[4]
     out_ref[...] = w_out[...].astype(bf16)
-    down[...] = w_down[...].astype(bf16)
+    down[...] = w_down[...].T.astype(bf16)
     for gu, src in enumerate((w_gate, w_up)):
         for t in range(2):
             lo = pl.multiple_of(FFQ * (2 * t + core), 128)
@@ -232,22 +272,11 @@
             give[gu, t] = src[:, pl.ds(lo, FFQ)].astype(bf16)
 
 
-def pack_qkv(wq, wk, wv, gains):
-    ins = [wq, wk, wv, gains]
-    return call(pack_qkv_body, "pack_qkv", 0, ins, [shape((SL + 8, QKV), bf16)], us=1.5)[0]
-
-
 def pack_rest(scal, w_out, w_gate, w_up, w_down):
     quarters = shape((2, 2, SL, FFQ), bf16)
-    return call(
-        pack_rest_body,
-        "pack_rest",
-        1,
-        [scal, w_out, w_gate, w_up, w_down],
-        [shape((SL, D), bf16), quarters, quarters, shape((FFQ, D), bf16)],
-        limit=16,
-        us=4,
-    )
+    outs = [shape((SL, D), bf16), quarters, quarters, shape((FFQ, D), bf16)]
+    ins = [w_out, w_gate, w_up, w_down.T]
+    return call_fetched(pack_rest_body, "pack_rest", scal, ins, outs, us=6, limit=24)
 
 
 def head_only(tables):
@@ -258,8 +287,11 @@
 
 def project_body(n_in, sc, *refs):
     xs = refs[:n_in]
-    cos_ref, sin_ref, p0, p1, p2, p3 = refs[n_in : n_in + 6]
-    x_ref, a4, q3, kv, acc_ref, x4 = refs[n_in + 6 :]
+    cos_ref, sin_ref, *parts = refs[n_in : n_in + 6]
+    x_ref, a4, q3, kv, gains, acc_ref, x4, g4, buf, sem = refs[n_in + 6 :]
+    copies = [pltpu.make_async_copy(p, buf.at[m], sem.at[m]) for m, p in enumerate(parts)]
+    for c in copies:
+        c.start()
     x = xs[0][...].astype(f32)
     for r in xs[1:]:
         x = x + r[...]
@@ -269,13 +301,17 @@
     for j in range(WA):
         x4[j] = x[:, SL * j : SL * (j + 1)]
     acc = None
-    for m, p in enumerate((p0, p1, p2, p3)):
+    for m in range(WA):
+        copies[m].wait()
         j = sc[0] ^ m
-        a = (x4[j] * p[SL : SL + 1, :SL].astype(f32)).astype(bf16)
+        gain = buf[m, SL:, :SL].astype(f32)
+        g4[j] = gain
+        a = (x4[j] * gain[:1]).astype(bf16)
         a4[j] = a
-        part = mm(a, p[:SL, :])
+        part = mm(a, buf[m, :SL, :])
         acc = part if acc is None else acc + part
-    acc_ref[:, :QKV] = acc
+    gains[...] = jnp.concatenate([g4[j] for j in range(WA)], axis=1)
+    acc_ref[...] = acc
     cos, sin = cos_ref[...], sin_ref[...]
     edge = head_only((cos, sin))
     for i in range(2):
@@ -302,9 +338,18 @@
             shape((WA, BLK, SL), bf16),
             shape((KVH, R3, HS), bf16),
             shape((BLK, 2 * KV), bf16),
+            shape((8, D), f32),
         ],
-        [pltpu.VMEM((BLK, QKV + 64), f32), pltpu.VMEM((WA, BLK, SL), f32)],
-        us=2.5,
+        [
+            pltpu.VMEM((BLK, QKVP), f32),
+            pltpu.VMEM((WA, BLK, SL), f32),
+            pltpu.VMEM((WA, 8, SL), f32),
+            pltpu.VMEM((WA, SL + 8, QKVP), bf16),
+            pltpu.SemaphoreType.DMA((WA,)),
+        ],
+        us=3,
+        limit=16,
+        specs=[VMEM] * (len(xs) + 2) + [HBM] * WA,
     )
 
 
@@ -402,7 +447,8 @@
 
 
 def mlp_body(sc, b_own, b_side, keep, core, gm, um, go, uo, d_own, d_far, *refs):
-    z_keep, z_give, gu_ref, y_own, y_side, bs, z_ref = refs
+    z_hbm, z_give, gu_hbm, y_own, y_side, bs, z_ref, gu_ref, sem = refs
+    copies = []
     w = sc[0]
     for half, b in enumerate((b_own, b_side)):
         for j in range(WA):
@@ -414,14 +460,21 @@
             acc = acc + mm(bs[w ^ 2], fars[gu][0]) + mm(bs[w ^ 3], fars[gu][1])
             gu_ref[gu, t] = acc
             lin.append(acc)
+        for gu in range(2):
+            c = pltpu.make_async_copy(gu_ref.at[gu, t], gu_hbm.at[gu, t], sem.at[len(copies)])
+            c.start()
+            copies.append(c)
         gate, up = lin
         z_ref[t] = (gate / (1.0 + jnp.exp(-gate)) * up).astype(bf16)
     row = sc[2]
+    copies.append(pltpu.make_async_copy(z_ref.at[row], z_hbm, sem.at[4]))
+    copies[4].start()
     out = mm(z_ref[row], d_own[...]) + mm(z_ref[1 - row], d_far[...])
     y_own[...] = out[:BLK]
     y_side[...] = out[BLK:]
-    z_keep[...] = z_ref[row]
     z_give[...] = z_ref[1 - row]
+    for c in copies:
+        c.wait()
 
 
 def mlp(scal, b_own, b_side, wts):
@@ -437,19 +490,33 @@
             shape((BLK, D), f32),
             shape((BLK, D), f32),
         ],
-        [pltpu.VMEM((WA, 2 * BLK, SL), bf16), pltpu.VMEM((2, 2 * BLK, FFQ), bf16)],
+        [
+            pltpu.VMEM((WA, 2 * BLK, SL), bf16),
+            pltpu.VMEM((2, 2 * BLK, FFQ), bf16),
+            pltpu.VMEM((2, 2, 2 * BLK, FFQ), f32),
+            pltpu.SemaphoreType.DMA((5,)),
+        ],
+        out_specs=[HBM, VMEM, HBM, VMEM, VMEM],
         limit=12,
         us=5.5,
     )
 
 
-def mlp_back_body(sc, l_own, l_side, gu_ref, keep, core, gm, um, go, uo, d_own, d_far, *refs):
-    keep_ref, give_ref, db_own, db_side, low, acc = refs
+def mlp_back_body(sc, l_own, l_side, gu_hbm, keep, core, gm, um, go, uo, d_own, d_far, *refs):
+    keep_ref, give_ref, db_own, db_side, low, acc, gu_ref, sem = refs
+    copies = [
+        [pltpu.make_async_copy(gu_hbm.at[gu, t], gu_ref.at[gu, t], sem.at[2 * i + gu]) for gu in range(2)]
+        for i, t in enumerate((sc[1], 1 - sc[1]))
+    ]
+    for c in copies[0] + copies[1]:
+        c.start()
     w, row = sc[0], sc[2]
     low[:BLK] = l_own[...]
     low[BLK:] = l_side[...]
     for first, (t, fg, fu) in enumerate(((sc[1], gm, um), (1 - sc[1], go, uo))):
         dz = jnp.where(t == row, nt(low[...], d_own[...]), nt(low[...], d_far[...]))
+        for c in copies[first]:
+            c.wait()
         gate, up = gu_ref[0, t], gu_ref[1, t]
         sig = 1.0 / (1.0 + jnp.exp(-gate))
         dg = (dz * up * sig * (1.0 + gate * (1.0 - sig))).astype(bf16)
@@ -487,7 +554,13 @@
             shape((BLK, D), f32),
             shape((BLK, D), f32),
         ],
-        [pltpu.VMEM((2 * BLK, D), bf16), pltpu.VMEM((WA, 2 * BLK, SL), f32)],
+        [
+            pltpu.VMEM((2 * BLK, D), bf16),
+            pltpu.VMEM((WA, 2 * BLK, SL), f32),
+            pltpu.VMEM((2, 2, 2 * BLK, FFQ), f32),
+            pltpu.SemaphoreType.DMA((4,)),
+        ],
+        specs=[VMEM, VMEM, HBM] + [VMEM] * 8,
         limit=12,
         us=6.7,
     )
@@ -584,9 +657,15 @@
     )
 
 
-def query_back_body(sc, dq, p0, p1, p2, p3, da):
-    for k, p in enumerate((p0, p1, p2, p3)):
-        da[sc[0] ^ k] = nt(dq[...], p[:SL, 2 * KV :])
+def query_back_body(sc, dq, p0, p1, p2, p3, da, buf, sem):
+    copies = [
+        pltpu.make_async_copy(p, buf.at[m], sem.at[m]) for m, p in enumerate((p0, p1, p2, p3))
+    ]
+    for c in copies:
+        c.start()
+    for k, c in enumerate(copies):
+        c.wait()
+        da[sc[0] ^ k] = nt(dq[...], buf[k, :SL, 2 * KV : QKV])
 
 
 def query_back(scal, dq, parts):
@@ -596,75 +675,55 @@
         1,
         [scal, dq, *parts],
         [shape((WA, BLK, SL), f32)],
+        [pltpu.VMEM((WA, SL + 8, QKVP), bf16), pltpu.SemaphoreType.DMA((WA,))],
+        specs=[VMEM] + [HBM] * WA,
         us=2,
     )[0]
 
 
-def project_back_body(sc, own, go, back, cos_ref, sin_ref, da, p0, p1, p2, p3, x, dm, gain, *refs):
-    dkv_ref, dx_ref, dxl_ref, gg, d4 = refs
+def project_back_body(sc, own, go, back, cos_ref, sin_ref, da, x, dm, gain, gain_m, p0, p1, p2, p3, *refs):
+    dkv_ref, dx_ref, dxl_ref, d4, buf, sem = refs
+    copies = [
+        pltpu.make_async_copy(p.at[:, pl.ds(0, 2 * KV)], buf.at[m], sem.at[m])
+        for m, p in enumerate((p0, p1, p2, p3))
+    ]
+    for c in copies:
+        c.start()
     total = own[...].astype(f32) + go[...].astype(f32) + back[...].astype(f32)
     cos, sin = cos_ref[...], sin_ref[...]
     edge = head_only((cos, sin))
     for i in range(2):
-        dkv_ref[:, 128 * i : 128 * (i + 1)] = rope_back(total[:, 128 * i : 128 * (i + 1)], cos, sin).astype(bf16)
-    dkv_ref[:, 256:384] = rope_back(total[:, 256:384], *edge).astype(bf16)
-    dkv_ref[:, 384:] = total[:, 384:].astype(bf16)
-    for k, p in enumerate((p0, p1, p2, p3)):
-        d4[sc[0] ^ k] = da[sc[0] ^ k] + nt(dkv_ref[...], p[:SL, : 2 * KV])
+        dkv_ref[:BLK, 128 * i : 128 * (i + 1)] = rope_back(total[:, 128 * i : 128 * (i + 1)], cos, sin).astype(bf16)
+    dkv_ref[:BLK, 256:384] = rope_back(total[:, 256:384], *edge).astype(bf16)
+    dkv_ref[:BLK, 384:] = total[:, 384:].astype(bf16)
+    for k, c in enumerate(copies):
+        c.wait()
+        d4[sc[0] ^ k] = da[sc[0] ^ k] + nt(dkv_ref[:BLK, :], buf[k, :SL, :])
     grads = jnp.concatenate([d4[j] for j in range(WA)], axis=1)
     part, gain_grad = norm_back(grads, x[...], gain[...])
-    gg[...] = gain_grad
+    dkv_ref[BLK:, :] = jnp.zeros((8, 2 * KV), bf16)
+    for i, g in enumerate((gain_grad, gain_m[...])):
+        dkv_ref[BLK + 2 * i : BLK + 2 * i + 1, :] = g[:, : 2 * KV].astype(bf16)
+        dkv_ref[BLK + 2 * i + 1 : BLK + 2 * i + 2, : D - 2 * KV] = g[:, 2 * KV :].astype(bf16)
     dx = dm[...] + part
     dx_ref[...] = dx
     dxl_ref[...] = dx.astype(bf16)
 
 
-def project_back(scal, addends, tables, da, parts, x, dm, gain):
+def project_back(scal, addends, tables, da, parts, x, dm, gain, gain_m_grad):
     return call(
         project_back_body,
         "project_back",
         1,
-        [scal, *addends, *tables, da, *parts, x, dm, gain],
+        [scal, *addends, *tables, da, x, dm, gain, gain_m_grad, *parts],
+        [shape((BLK + 8, 2 * KV), bf16), shape((BLK, D), f32), shape((BLK, D), bf16)],
         [
-            shape((BLK, 2 * KV), bf16),
-            shape((BLK, D), f32),
-            shape((BLK, D), bf16),
-            shape((1, D), f32),
+            pltpu.VMEM((WA, BLK, SL), f32),
+            pltpu.VMEM((WA, SL + 8, 2 * KV), bf16),
+            pltpu.SemaphoreType.DMA((WA,)),
         ],
-        [pltpu.VMEM((WA, BLK, SL), f32)],
         us=2.5,
-    )
-
-
-def fetched(refs, bufs, sem):
-    copies = [pltpu.make_async_copy(r, b, sem.at[i]) for i, (r, b) in enumerate(zip(refs, bufs))]
-    for c in copies:
-        c.start()
-    for c in copies:
-        c.wait()
-
-
-def call_fetched(body, name, scal, ins, outs, us, limit, scratch=()):
-    count = len(ins)
-
-    def whole(sc, *refs):
-        sources, results = refs[:count], refs[count : count + len(outs)]
-        bufs = refs[count + len(outs) : 2 * count + len(outs)]
-        sem, rest = refs[2 * count + len(outs)], refs[2 * count + len(outs) + 1 :]
-        fetched(sources, bufs, sem)
-        body(sc, *bufs, *results, *rest)
-
-    bufs = [pltpu.VMEM(x.shape, x.dtype) for x in ins]
-    return call(
-        whole,
-        name,
-        1,
-        [scal, *ins],
-        outs,
-        bufs + [pltpu.SemaphoreType.DMA((count,)), *scratch],
-        us=us,
-        limit=limit,
-        spec=pl.BlockSpec(memory_space=pl.ANY),
+        specs=[VMEM] * 10 + [HBM] * WA,
     )
 
 
@@ -676,20 +735,31 @@
         lows = refs[WA * (t + 1) : WA * (t + 2)]
         acc = None
         for sl, low in zip(slices, lows):
-            part = tn(sl[kind], low[...])
+            part = tn(sl[kind], low[:BLK])
             acc = part if acc is None else acc + part
         width = acc.shape[1]
         if has_prev:
-            acc = acc + refs[4 * WA][:, lo : lo + width]
+            acc = acc + refs[4 * WA][:SL, lo : lo + width]
             out[:SL, lo : lo + width] = acc.astype(bf16)
         else:
-            out[:, lo : lo + width] = acc
+            out[:SL, lo : lo + width] = acc
         lo += width
+    gains = sum(low[BLK:, :].astype(f32) for low in refs[WA : 2 * WA])
+    rest = D - 2 * KV
+    whole = jnp.concatenate(
+        [
+            jnp.concatenate([gains[2 * i : 2 * i + 1], gains[2 * i + 1 : 2 * i + 2, :rest]], axis=1)
+            for i in range(2)
+        ],
+        axis=0,
+    )
     if has_prev:
-        out[SL:, :] = jnp.zeros((256 - SL, lo), bf16)
-
-
-def grad_rows(scal, slices, dkvs, dqs, dms, prev):
+        whole = whole + refs[4 * WA][SL : SL + 2, :D]
+    out[SL:, :] = jnp.zeros((256 - SL, lo), out.dtype)
+    out[SL : SL + 2, :D] = whole.astype(out.dtype)
+
+
+def grad_rows(scal, slices, dkvs, dqs, dms, prev, far=None):
     has_prev = prev is not None
     cols = QKV + D
     return call_fetched(
@@ -697,9 +767,11 @@
         "grad_rows",
         scal,
         [*slices, *dkvs, *dqs, *dms] + ([prev] if has_prev else []),
-        [shape((256, cols), bf16) if has_prev else shape((SL, cols), f32)],
+        [shape((256, cols), bf16 if has_prev else f32)],
         us=4,
-        limit=20,
+        limit=24,
+        far=far,
+        far_out=not has_prev,
     )[0]
 
 
@@ -730,8 +802,10 @@
         [*bs, keep, got] + ([prev] if has_prev else []),
         [shape((8, WA, 64, FFQ), bf16 if has_prev else f32)],
         us=5,
-        limit=24,
+        limit=32,
         scratch=[pltpu.VMEM((D, WA * BLK), bf16)],
+        far=[False] * 6 + [True] * has_prev,
+        far_out=not has_prev,
     )[0]
 
 
@@ -753,7 +827,9 @@
         [z, z_got, *lows] + ([prev] if has_prev else []),
         [shape((FFQ, D), bf16 if has_prev else f32)],
         us=3,
-        limit=16,
+        limit=20,
+        far=[True, True] + [False] * 4 + [True] * has_prev,
+        far_out=not has_prev,
     )[0]
 
 
@@ -774,14 +850,15 @@
 
 
 def finish_ff(scal, gathered):
-    return call(
+    return call_fetched(
         functools.partial(finish_ff_body, len(gathered)),
         "finish_ff",
-        1,
-        [scal, *gathered],
+        scal,
+        list(gathered),
         [shape((SL, 4 * FFQ), f32)] * 2,
         us=4,
-        limit=12,
+        limit=20,
+        far=[False] * len(gathered),
     )
 
 
@@ -794,18 +871,20 @@
 
 
 def finish_down(scal, gathered):
-    return call(
+    return call_fetched(
         functools.partial(finish_down_body, len(gathered)),
         "finish_down",
-        1,
-        [scal, *gathered],
+        scal,
+        list(gathered),
         [shape((FFQ, D), f32)],
         us=2.5,
+        limit=20,
+        far=[False] * len(gathered),
     )[0]
 
 
 def finish_rows_body(n, widths, sc, *refs):
-    outs = refs[n:]
+    *outs, gains = refs[n:]
     for k in range(n):
         p = (sc[3] - k + n) % n
         rows = refs[k].shape[0]
@@ -825,16 +904,19 @@
             for out, width in zip(outs, widths):
                 out[rows * (n - 1) :, :] = refs[k][:tail, lo : lo + width].astype(f32)
                 lo += width
+            gains[...] = refs[k][tail : tail + 8, :D].astype(f32)
 
 
 def finish_rows(scal, gathered, widths):
-    return call(
+    return call_fetched(
         functools.partial(finish_rows_body, len(gathered), tuple(widths)),
         "finish_rows",
-        1,
-        [scal, *gathered],
-        [shape((SL, width), f32) for width in widths],
+        scal,
+        list(gathered),
+        [shape((SL, width), f32) for width in widths] + [shape((8, D), f32)],
         us=2.5,
+        limit=20,
+        far=[False] * len(gathered),
     )
 
 
@@ -881,7 +963,7 @@
     tables = (jnp.tile(jnp.cos(angles), (1, 4)), jnp.tile(jnp.sin(angles), (1, 4)))
 
     gains_own = jnp.pad(jnp.stack([gain_attn, gain_mlp]), ((0, 6), (0, 0)))
-    qkv_own = pack_qkv(w_query, key_projection, value_projection, gains_own)
+    qkv_own = pack_qkv(scal, w_query, key_projection, value_projection, gains_own)
     qkv_across = swap(qkv_own, 2)
     qkv_side = swap(qkv_own, 1)
     out_own, keep, give, down_own = pack_rest(scal, after(w_out, qkv_own), w_gate, w_up, w_down)
@@ -897,62 +979,76 @@
 
     gate_half, up_half = y_half(0), y_half(1)
     down_half = lax.dynamic_slice_in_dim(down_own, x_side * (FFQ // 2), FFQ // 2, 0)
-    qkv_across, qkv_side, core_part, out_own, gate_half, up_half, down_half = bar(
-        qkv_across, qkv_side, core_part, out_own, gate_half, up_half, down_half
-    )
+    top = cotangent[0]
+    first = tokens[0]
+    cos, sin = tables
+    (qkv_across, qkv_side, core_part, out_own, gate_half, up_half, down_half, top, first, cos, sin,
+     sched, qinfo) = bar(
+        qkv_across, qkv_side, core_part, out_own, gate_half, up_half, down_half, top, first, cos, sin,
+        sched, qinfo)
+    tables = (cos, sin)
     qkv_parts = [qkv_own, qkv_side, qkv_across, swap(qkv_across, 1)]
-    gains_parts = jnp.stack([p[SL : SL + 2, :SL] for p in qkv_parts])
-    gains = jnp.concatenate(
-        [lax.dynamic_index_in_dim(gains_parts, w ^ j, 0, keepdims=False) for j in range(WA)], axis=1
-    ).astype(f32)
-    gain_a, gain_m = gains[0:1], gains[1:2]
-
-    def ring_keys(kv, extras):
+
+    def ring_keys(kv, extras, held):
         if n != 8:
-            done = [e() for e in extras]
-            return ring_gather(kv, n, position), done
+            for e in extras:
+                held.update(e(held))
+            return ring_gather(kv, n, position)
         rows = BLK // 2
-        ahead, behind, done = [kv], [kv], []
+        ahead, behind = [kv], [kv]
         for step in range(4):
-            more = extras[step]()
+            more = extras[step](held)
             if step < 3:
                 f, b = ring_shift(ahead[-1], n, 1), ring_shift(behind[-1], n, -1)
             else:
                 f = ring_shift(ahead[-1][:rows], n, 1)
                 b = ring_shift(behind[-1][rows:], n, -1)
-            f, b, *more = bar(f, b, *more)
+            f, b, *values = bar(f, b, *more.values())
             ahead.append(f)
             behind.append(b)
-            done.append(more)
+            held.update(zip(more.keys(), values))
         far = jnp.concatenate([ahead[4], behind[4]], axis=0)
-        return jnp.stack(ahead[:4] + [far] + behind[3:0:-1]), done
-
-    def nothing():
-        return []
-
+        return jnp.stack(ahead[:4] + [far] + behind[3:0:-1])
+
+    def spread(dkv, extras, held):
+        if n != 8:
+            for e in extras:
+                held.update(e(held))
+            total = lax.psum_scatter(
+                by_distance(dkv, n, position), "ctx", scatter_dimension=0, tiled=False
+            )
+            return (total, jnp.zeros_like(total), jnp.zeros_like(total))
+        go = back = None
+        for step in range(4):
+            more = extras[step](held)
+            if step == 0:
+                go, back = ring_far(lambda k: dkv[k], n)
+            else:
+                go, back = ring_near(lambda k: dkv[k], n, 4 - step, go, back)
+            go, back, *values = bar(go, back, *more.values())
+            held.update(zip(more.keys(), values))
+        return (dkv[0], go, back)
+
+    gate_mine = swap(gate_half, 2)
+    x, a4, q3, kv, gains = project(scal, [first], tables, qkv_parts)
+    gain_a, gain_m = gains[0:1], gains[1:2]
+    kv, out_own = bar(kv, out_own)
+    held = dict(gate_mine=gate_mine)
     out_across = swap(out_own, 2)
-    gate_mine = swap(gate_half, 2)
-    x, a4, q3, kv = project(scal, [tokens[0]], tables, qkv_parts)
-    held = {}
-
-    def step1():
-        return [out_across]
-
-    def step2():
-        held["up_mine"] = swap(after(up_half, kv), 2)
-        return [swap(out_across, 1), swap(out_own, 1), gate_mine]
-
-    def step3():
-        held["gate_other"] = side_swap(gate_mine, n)
-        return []
-
-    def step4():
-        return [held["up_mine"], held["gate_other"]]
-
-    every, more = ring_keys(kv, [step1, step2, step3, step4])
-    out_across, (out_diag, out_side, gate_mine), (up_mine, gate_other) = more[0][0], more[1], more[3]
-    out_parts = [out_own, out_side, out_across, out_diag]
-    up_other = side_swap(up_mine, n)
+    up_mine = swap(after(up_half, kv), 2)
+
+    def gate_other(h):
+        return side_swap(h["gate_mine"], n)
+
+    extras = [
+        lambda h: dict(out_side=swap(out_own, 1), gate_mine=h["gate_mine"]),
+        lambda h: dict(out_across=out_across),
+        lambda h: dict(out_diag=swap(h["out_across"], 1)),
+        lambda h: dict(gate_other=gate_other(h), up_mine=up_mine),
+    ]
+    every = ring_keys(kv, extras, held)
+    out_parts = [out_own, held["out_side"], held["out_across"], held["out_diag"]]
+    up_other = side_swap(held["up_mine"], n)
     down_mine = swap(after(down_half, every), 2)
     *sl, o_t, lse, m, b = attend(scal, sched, qinfo, q3, every, x, a4, gain_m, out_parts)
     m, b, up_other, down_mine = bar(m, b, up_other, down_mine)
@@ -965,104 +1061,84 @@
         ],
         axis=0,
     )
-    ff_parts = [keep, core_part, gate_mine, up_mine, gate_other, up_other, down_own, down_far]
+    ff_parts = [
+        keep,
+        core_part,
+        held["gate_mine"],
+        held["up_mine"],
+        held["gate_other"],
+        up_other,
+        down_own,
+        down_far,
+    ]
     b_far = swap(b, 2)
     z, z_give, gu, y_own, y_side = mlp(scal, b, b_side, ff_parts)
     y_own, y_side, b_far, z_give = bar(y_own, y_side, b_far, z_give)
     kept0 = [x, q3, every, o_t, lse, m, gu, z]
 
-    y_got = swap(y_side, 1)
-    z_got0 = swap(z_give, 2)
-    x, a4, q3, kv = project(scal, [m, y_own, y_got], tables, qkv_parts)
-    top = cotangent[0]
-    b0, sl0 = b, sl
-
-    def step1():
-        return [z_got0, swap(b_far, 1)]
-
-    def step2():
-        return [swap(sl0[1], 1), swap(sl0[2], 2)]
-
-    def step3():
-        return [swap(sl0[3], 3), swap(after(top, kv), 2)]
-
-    def step4():
-        return [swap(top, 1)]
-
-    every, more = ring_keys(kv, [step1, step2, step3, step4])
-    (z_got0, b_diag), (s1, s2), (s3, top_far), (top_side,) = more
-    kept0 += [z_got0, [b0, b_side, b_far, b_diag], [sl0[0], s1, s2, s3]]
-    top_diag = swap(top_far, 1)
+    x, a4, q3, kv, _ = project(scal, [m, y_own, swap(y_side, 1)], tables, qkv_parts)
+    kv, z_give, b_far = bar(kv, z_give, b_far)
+    b0, b0_side, sl0 = b, b_side, sl
+    held = {}
+    extras = [
+        lambda h: dict(z_got=swap(z_give, 2), b_diag=swap(b_far, 1)),
+        lambda h: dict(s1=swap(sl0[1], 1), s2=swap(sl0[2], 2)),
+        lambda h: dict(s3=swap(sl0[3], 3), top_side=swap(top, 1)),
+        lambda h: dict(top_far=swap(top, 2)),
+    ]
+    every = ring_keys(kv, extras, held)
+    kept0 += [
+        held["z_got"],
+        [b0, b0_side, b_far, held["b_diag"]],
+        [sl0[0], held["s1"], held["s2"], held["s3"]],
+    ]
+    top_side, top_far = held["top_side"], held["top_far"]
     *sl, o_t, lse, m, b = attend(scal, sched, qinfo, q3, every, x, a4, gain_m, out_parts)
-    m, b, top_diag = bar(m, b, top_diag)
+    m, b = bar(m, b)
     b_side = swap(b, 1)
     b_far = swap(b, 2)
     z, z_give, gu, y_own, y_side = mlp(scal, b, b_side, ff_parts)
-    y_own, y_side, b_far, z_give, z = bar(y_own, y_side, b_far, z_give, z)
-    kept1 = [x, q3, every, o_t, lse, m, gu, z]
-
-    x, q3, every, o_t, lse, m, gu, z = kept1
+    y_own, y_side, b_far, z_give, z, top = bar(y_own, y_side, b_far, z_give, z, top)
+
     y_got = swap(y_side, 1)
     z_got = swap(z_give, 2)
-    b_diag = swap(b_far, 1)
-    keep_d, give_d, db_own, db_side = mlp_back(scal, after(top, y_side), top_side, gu, ff_parts)
-    db_own, db_side, give_d, z_got, b_diag, y_got = bar(
-        db_own, db_side, give_d, z_got, b_diag, y_got
-    )
+    keep_d, give_d, db_own, db_side = mlp_back(scal, top, top_side, gu, ff_parts)
+    db_own, db_side, give_d, z_got, y_got = bar(db_own, db_side, give_d, z_got, y_got)
     output = (m + y_own + y_got).astype(bf16)[None]
     db_got = swap(db_side, 1)
     got_d = swap(give_d, 2)
+    b_diag = swap(b_far, 1)
+    top_diag = swap(top_far, 1)
     dm, dml, gain_m_1, dq, dkv = attend_back(
         scal, sched, qinfo, top, db_own, db_got, m, gain_m, out_parts, q3, every, o_t, lse, tables
     )
-    dkv, dq, dml, got_d = bar(dkv, dq, dml, got_d)
-
-    def spread(dkv, extras):
-        if n != 8:
-            done = [e() for e in extras]
-            total = lax.psum_scatter(
-                by_distance(dkv, n, position), "ctx", scatter_dimension=0, tiled=False
-            )
-            return (total, jnp.zeros_like(total), jnp.zeros_like(total)), done
-        done = []
-        go = back = None
-        for step in range(4):
-            more = extras[step]()
-            if step == 0:
-                go, back = ring_far(lambda k: dkv[k], n)
-            else:
-                go, back = ring_near(lambda k: dkv[k], n, 4 - step, go, back)
-            go, back, *more = bar(go, back, *more)
-            done.append(more)
-        return (dkv[0], go, back), done
-
+    dkv, dq, dml, b_diag, top_diag = bar(dkv, dq, dml, b_diag, top_diag)
     lows = [top, top_side, top_far, top_diag]
-
-    def step1():
-        return [swap(sl[1], 1), swap(sl[2], 2), grad_down(scal, z, z_got, lows, None)]
-
-    def step2():
-        return [swap(sl[3], 3), swap(dq, 2), query_back(scal, after(dq, dkv), qkv_parts)]
-
-    def step3():
-        bs = [b, b_side, b_far, b_diag]
-        return [swap(after(dml, dq), 2), grad_ff(scal, bs, keep_d, got_d, None)]
-
-    def step4():
-        return [swap(dq, 1), swap(dml, 1)]
-
-
-    addends, more = spread(dkv, [step1, step2, step3, step4])
-    (s1, s2, down_1), (s3, dq_far, da), (dml_far, ff_1), (dq_side, dml_side) = more
-    dq_diag = swap(dq_far, 1)
-    dml_diag = swap(dml_far, 1)
-    dkv0, dx, low, gain_a_1 = project_back(scal, addends, tables, da, qkv_parts, x, dm, gain_a)
+    bs = [b, b_side, b_far, b_diag]
+    sl1, keep_d1, z1 = sl, keep_d, z
+    held = {}
+    extras = [
+        lambda h: dict(got_d=got_d, down_1=grad_down(scal, z1, z_got, lows, None)),
+        lambda h: dict(
+            s1=swap(sl1[1], 1), s2=swap(sl1[2], 2), da=query_back(scal, dq, qkv_parts)
+        ),
+        lambda h: dict(
+            s3=swap(sl1[3], 3), dq_far=swap(dq, 2), ff_1=grad_ff(scal, bs, keep_d1, h["got_d"], None)
+        ),
+        lambda h: dict(dq_side=swap(dq, 1), dml_side=swap(dml, 1), dml_far=swap(dml, 2)),
+    ]
+    addends = spread(dkv, extras, held)
+    down_1, ff_1 = held["down_1"], held["ff_1"]
+    dq_diag, dml_diag = swap(held["dq_far"], 1), swap(held["dml_far"], 1)
+    dkv0, dx, low = project_back(
+        scal, addends, tables, held["da"], qkv_parts, x, dm, gain_a, gain_m_1
+    )
     dx, low, dkv0, dq_diag, dml_diag = bar(dx, low, dkv0, dq_diag, dml_diag)
-    slices_1 = [sl[0], s1, s2, s3]
-    dqs_1 = [dq, dq_side, dq_far, dq_diag]
-    dmls_1 = [dml, dml_side, dml_far, dml_diag]
-
-    x, q3, every, o_t, lse, m, gu, z, z_got, bs, slices = kept0
+    slices_1 = [sl[0], held["s1"], held["s2"], held["s3"]]
+    dqs_1 = [dq, held["dq_side"], held["dq_far"], dq_diag]
+    dmls_1 = [dml, held["dml_side"], held["dml_far"], dml_diag]
+
+    x, q3, every, o_t, lse, m, gu, z, z_got, bs0, slices = kept0
     low_side = swap(low, 1)
     low_far = swap(low, 2)
     keep_d, give_d, db_own, db_side = mlp_back(scal, low, low_side, gu, ff_parts)
@@ -1074,68 +1150,64 @@
     db_got, down_grad = bar(db_got, down_grad)
     down_piece = at_position(down_grad.reshape(n, FFQ // n, D), n, position)
     got_d = swap(give_d, 2)
-    down_go = down_back = None
+    held = {}
     if n == 8:
-        down_go, down_back = ring_far(down_piece, n)
+        held["down"] = ring_far(down_piece, n)
     dm, dml, gain_m_0, dq, dkv = attend_back(
         scal, sched, qinfo, dx, db_own, db_got, m, gain_m, out_parts, q3, every, o_t, lse, tables
     )
     dkv, dq, dml, got_d, dkv_side, dkv_far = bar(dkv, dq, dml, got_d, dkv_side, dkv_far)
+    dkvs_1 = [dkv0, dkv_side, dkv_far]
 
     def ff_piece_of(ff):
         sub = n // 8
         pieces = ff.reshape(8, WA, sub, 64 // sub, FFQ).transpose(0, 2, 1, 3, 4)
         return pieces.reshape(n, WA, 64 // sub, FFQ)
 
-    def down_step(k):
-        nonlocal down_go, down_back
+    def down_step(k, h):
         if n != 8:
-            return []
-        down_go, down_back = ring_near(down_piece, n, k, down_go, down_back)
-        return [down_go, down_back]
-
-    def keep_down(pair):
-        nonlocal down_go, down_back
-        if n == 8:
-            down_go, down_back = pair
-
-    def step1():
-        ff = grad_ff(scal, bs, keep_d, got_d, ff_1)
-        return [ff, swap(dq, 2)] + down_step(3)
-
-    def step2():
-        return [swap(after(dml, dq), 2), query_back(scal, dq, qkv_parts)] + down_step(2)
-
-    def step3():
-        dkvs = [dkv0, dkv_side, dkv_far, swap(dkv_far, 1)]
-        return [grad_rows(scal, slices_1, dkvs, dqs_1, dmls_1, None)] + down_step(1)
-
-    def step4():
-        return [swap(dq, 1), swap(dml, 1)]
-
-    addends, more = spread(dkv, [step1, step2, step3, step4])
-    (ff_grad, dq_far, *_), (dml_far, da, *_), (rows_1, *_), (dq_side, dml_side) = more
-    dqs = [dq, dq_side, dq_far, swap(dq_far, 1)]
-    dmls = [dml, dml_side, dml_far, swap(dml_far, 1)]
-    dkv0, dx, low, gain_a_0 = project_back(scal, addends, tables, da, qkv_parts, x, dm, gain_a)
+            return {}
+        go, back = h.get("down_go"), h.get("down_back")
+        if go is None:
+            go, back = h["down"]
+        go, back = ring_near(down_piece, n, k, go, back)
+        return dict(down_go=go, down_back=back)
+
+    keep_d0, dq0, dml0 = keep_d, dq, dml
+    extras = [
+        lambda h: dict(
+            dq_far=swap(dq0, 2), ff=grad_ff(scal, bs0, keep_d0, got_d, ff_1), **down_step(3, h)
+        ),
+        lambda h: dict(dml_far=swap(dml0, 2), da=query_back(scal, dq0, qkv_parts), **down_step(2, h)),
+        lambda h: dict(dkv_diag=swap(dkv_far, 1), **down_step(1, h)),
+        lambda h: dict(dq_side=swap(dq0, 1), dml_side=swap(dml0, 1)),
+    ]
+    addends = spread(dkv, extras, held)
+    dkv0, dx, low = project_back(
+        scal, addends, tables, held["da"], qkv_parts, x, dm, gain_a, gain_m_0
+    )
     input_grad = low[None]
 
-    gain_sum = jnp.concatenate([gain_a_0 + gain_a_1, gain_m_0 + gain_m_1], axis=0)
-    gain_sum = lax.dynamic_slice_in_dim(all_sum(gain_sum, n), w * SL, SL, 1)
-    ff_pieces = ff_piece_of(ff_grad)
+    ff_pieces = ff_piece_of(held["ff"])
     if n == 8:
-        down_all = ring_gather(total_low(down_piece(0), down_go, down_back), n, position)
+        down_mine = total_low(down_piece(0), held["down_go"], held["down_back"])
+        down_all = ring_gather(down_mine, n, position)
         ff_mine = total_low(*ring_scatter(at_position(ff_pieces, n, position), n))
     else:
         down_all = ring_sum(down_grad.reshape(n, FFQ // n, D), n, position)
         ff_mine = lax.psum_scatter(ff_pieces, "ctx", scatter_dimension=0, tiled=False)
     ff_all = ring_gather(rows_home(ff_mine, w), n, position)
+    rows_1 = grad_rows(scal, slices_1, dkvs_1 + [held["dkv_diag"]], dqs_1, dmls_1, None)
+    dqs = [dq, held["dq_side"], held["dq_far"], swap(held["dq_far"], 1)]
+    dmls = [dml, held["dml_side"], held["dml_far"], swap(held["dml_far"], 1)]
     rows_grad = grad_rows(scal, slices, everyone(dkv0), dqs, dmls, rows_1)
     rows_all = ring_sum(rows_grad.reshape(n, 256 // n, QKV + D), n, position)
     if n == 8:
         down_total = finish_down(scal, down_all)
         gate_total, up_total = finish_ff(scal, ff_all)
-        key_total, value_total, query_total, out_total = finish_rows(scal, rows_all, [KV, KV, D, D])
+        key_total, value_total, query_total, out_total, gain_rows = finish_rows(
+            scal, rows_all, [KV, KV, D, D]
+        )
     else:
         sub = n // 8
         whole = placed(ff_all, n, position).reshape(2, 4, sub, WA, 64 // sub, FFQ)
@@ -1143,22 +1215,25 @@
         whole = jnp.take(whole, w ^ jnp.arange(WA, dtype=i32), axis=1).transpose(0, 2, 1, 3)
         gate_total, up_total = whole.reshape(2, SL, -1).astype(f32)
         down_total = placed(down_all, n, position).reshape(FFQ, D).astype(f32)
-        rows_total = placed(rows_all, n, position).reshape(256, QKV + D)[:SL].astype(f32)
+        rows_total = placed(rows_all, n, position).reshape(256, QKV + D).astype(f32)
+        gain_rows = rows_total[SL:, :D]
+        rows_total = rows_total[:SL]
         key_total, value_total, query_total, out_total = (
             rows_total[:, :KV],
             rows_total[:, KV : 2 * KV],
             rows_total[:, 2 * KV : QKV],
             rows_total[:, QKV:],
         )
+    gain_rows = lax.dynamic_slice_in_dim(gain_rows[:2], w * SL, SL, 1)
     return (
         output,
         input_grad,
-        gain_sum[0],
+        gain_rows[0],
         query_total,
         key_total,
         value_total,
         out_total,
-        gain_sum[1],
+        gain_rows[1],
         gate_total,
         up_total,
         down_total,

time: 486 us -> 444 us (0.914)
  waiting for transfers between devices: 178 us -> 142 us
  Pallas kernels: 91.8 us -> 122 us
  local copies, waits for them, and re-layouts: 69.3 us -> 46.5 us
  starting transfers between devices: 131 us -> 117 us
    ppermute x80, waiting for transfers between devices: 119 us -> 85.1 us  [ring_shift(): lax.ppermute(x, 'ctx', [(order[i], order[(i + step) % n]) for i in range(...]
    pallas_call x25, Pallas kernels: 91.8 us -> 122 us  [call(): pl.pallas_call(body, name=name, in_specs=[SMEM] * n_scalar + (specs or [V...]
    unnamed x326 -> x287, local copies, waits for them, and re-layouts: 56.6 us -> 39.5 us
    ppermute x80, starting transfers between devices: 91.7 us -> 82.6 us  [ring_shift(): lax.ppermute(x, 'ctx', [(order[i], order[(i + step) % n]) for i in range(...]
    ppermute x59 -> x57, starting transfers between devices: 31.6 us -> 28.7 us  [swap(): return lax.ppermute(x, 'wa', [(i, i ^ mask) for i in range(WA)])]
    ppermute x59 -> x57, waiting for transfers between devices: 45.6 us -> 43.6 us  [swap(): return lax.ppermute(x, 'wa', [(i, i ^ mask) for i in range(WA)])]
  transfers between devices with their start and end apart: 145 -> 140, of which waited for: 54 -> 48; matrix products, arithmetic and copies ran while one was open for 6% -> 5% of each run, Pallas kernels for 18% -> 24%
where the time goes in v4:
time: 444 us; the launch traced here: 438 us
  waiting for transfers between devices  142 us (32%)
  Pallas kernels  122 us (27%)
  starting transfers between devices  117 us (26%)
  local copies, waits for them, and re-layouts  46.5 us (10%)
  other arithmetic  8.2 us (2%)
    pallas_call x25, Pallas kernels, call(): pl.pallas_call(body, name=name, in_specs=[SMEM] * n_scalar + (specs or [V...  122 us
    ppermute x80, waiting for transfers between devices, ring_shift(): lax.ppermute(x, 'ctx', [(order[i], order[(i + step) % n]) for i in range(...  85.1 us
    ppermute x80, starting transfers between devices, ring_shift(): lax.ppermute(x, 'ctx', [(order[i], order[(i + step) % n]) for i in range(...  82.6 us
    ppermute x57, waiting for transfers between devices, swap(): return lax.ppermute(x, 'wa', [(i, i ^ mask) for i in range(WA)])  43.6 us
    unnamed x287, local copies, waits for them, and re-layouts  39.5 us
    ppermute x57, starting transfers between devices, swap(): return lax.ppermute(x, 'wa', [(i, i ^ mask) for i in range(WA)])  28.7 us
    ppermute x3, waiting for transfers between devices, side_swap(): return lax.ppermute(x, 'ctx', [(i, i ^ 1) for i in range(n)])  12.9 us
  transfers between devices with their start and end apart: 140, of which 48 were waited for; matrix products, arithmetic and copies ran while one was open for 5% of the time, Pallas kernels for 24%

profile of v4, /device:TPU:0, one launch (start us, length us, event | category | flops | bytes accessed | tf_op | source)
XLA Modules:
  0.0 438.1 jit_solution(16852002789245387924)
XLA Ops:
  24.7 3.9 collective-permute-done.refs_5_.refs_7_.p2
  38.9 7.0 %collective-permute-done.7.gm = bf16[2,240,640]{2,1,0:T(8,128)(2,1)S(1)} collective-permute-done((bf16[2,240,640]{2,1,0:T(8,128)(2,1)}, bf16[2,240,640]{2,1,0:T(8,128)(2,1)S(1)}, u32[]{:S(2)}, u32[]{:S(2)}) %collective-permute-start.7) | collective-permute-done | bytes 614432 | tf_op jit(solution)/shard_map/ppermute | solution.py:36
  51.3 5.1 %collective-permute-done.10.p2 = bf16[240,960]{1,0:T(8,128)(2,1)S(1)} collective-permute-done((bf16[240,960]{1,0:T(8,128)(2,1)S(1)}, bf16[240,960]{1,0:T(8,128)(2,1)S(1)}, u32[]{:S(2)}, u32[]{:S(2)}) %collective-permute-start.10) | collective-permute-done | bytes 460832 | tf_op jit(solution)/shard_map/ppermute | solution.py:36
  58.7 10.9 %collective-permute-done.11 = bf16[128,640]{1,0:T(8,128)(2,1)S(1)} collective-permute-done((bf16[128,640]{1,0:T(8,128)(2,1)S(1)}, bf16[128,640]{1,0:T(8,128)(2,1)S(1)}, u32[]{:S(2)}, u32[]{:S(2)}) %collective-permute-start.11) | collective-permute-done | bytes 163872 | tf_op jit(solution)/shard_map/ppermute | solution.py:49
  77.3 7.6 %attend.2 = (bf16[2,128,240]{2,1,0:T(8,128)(2,1)S(1)}, bf16[2,128,240]{2,1,0:T(8,128)(2,1)S(1)}, bf16[2,128,240]{2,1,0:T(8,128)(2,1)S(1)}, bf16[2,128,240]{2,1,0...) custom-call(s32[5]{0:T(128)S(1)} %stack.112.sc, ...), custom_call_target="tpu_custom_call" | custom-call | flops 11500000256 | bytes 65536 | tf_op jit(solution)/shard_map/attend/pallas_call | solution.py:163
  91.3 10.0 %collective-permute-done.21 = bf16[320,960]{1,0:T(8,128)(2,1)S(1)} collective-permute-done((bf16[320,960]{1,0:T(8,128)(2,1)S(1)}, bf16[320,960]{1,0:T(8,128)(2,1)S(1)}, u32[]{:S(2)}, u32[]{:S(2)}) %collective-permute-start.21) | collective-permute-done | bytes 614432 | tf_op jit(solution)/shard_map/ppermute | solution.py:40
  102.7 5.8 %mlp.2 = (bf16[256,640]{1,0:T(8,128)(2,1)S(1)}, bf16[256,640]{1,0:T(8,128)(2,1)S(1)}, f32[2,2,256,640]{3,2,1,0:T(8,128)S(1)}, f32[128,960]{1,0:T(8,128)S(1)}, f32[128,960]{1,0:T(8,128)S(1)}) custom-call(s32[5]{0:T(128)S(1)} %stack.112.sc, bf16[128,960]{1,0:T(8,128)(2,1)S(1)} %get-tuple-element.254.b_own.refs_0_, ...), custom_call_target="tpu_custom_call" | custom-call | flops 6325000192 | bytes 65536 | tf_op jit(solution)/shard_map/mlp/pallas_call | solution.py:163
  111.2 4.0 project.3
  116.1 3.7 collective-permute-start.24
  119.7 3.6 collective-permute-done.24
  146.6 7.3 %attend.3 = (bf16[2,128,240]{2,1,0:T(8,128)(2,1)S(1)}, bf16[2,128,240]{2,1,0:T(8,128)(2,1)S(1)}, bf16[2,128,240]{2,1,0:T(8,128)(2,1)S(1)}, bf16[2,128,240]{2,1,0...) custom-call(s32[5]{0:T(128)S(1)} %stack.112.sc, ...), custom_call_target="tpu_custom_call" | custom-call | flops 11500000256 | bytes 65536 | tf_op jit(solution)/shard_map/attend/pallas_call | solution.py:163
  155.6 5.8 %mlp.3 = (bf16[256,640]{1,0:T(8,128)(2,1)S(1)}, bf16[256,640]{1,0:T(8,128)(2,1)S(1)}, f32[2,2,256,640]{3,2,1,0:T(8,128)S(1)}, f32[128,960]{1,0:T(8,128)S(1)}, f32[128,960]{1,0:T(8,128)S(1)}) custom-call(s32[5]{0:T(128)S(1)} %stack.112.sc, bf16[128,960]{1,0:T(8,128)(2,1)S(1)} %get-tuple-element.288.b_own.refs_0_, ...), custom_call_target="tpu_custom_call" | custom-call | flops 6325000192 | bytes 65536 | tf_op jit(solution)/shard_map/mlp/pallas_call | solution.py:163
  163.1 7.0 %mlp_back.2 = (bf16[2,256,640]{2,1,0:T(8,128)(2,1)S(1)}, bf16[2,256,640]{2,1,0:T(8,128)(2,1)S(1)}, f32[128,960]{1,0:T(8,128)S(1)}, f32[128,960]{1,0:T(8,128)S(1)}) custom-call(s32[5]{0:T(128)S(1)} %stack.112.sc, bf16[128,960]{1,0:T(8,128)(2,1)S(1)} %bitcast.257, bf16[128,960]{1,0:T(8,128)(2,1)S(1)} %collective-permute-done.35.l_side.refs_3_, ...), custom_call_target="tpu_custom_call" | custom-call | flops 7704999936 | bytes 65536 | tf_op jit(solution)/shard_map/mlp_back/pallas_call | solution.py:163
  174.8 9.5 %attend_back.2 = (f32[128,960]{1,0:T(8,128)S(1)}, bf16[128,960]{1,0:T(8,128)(2,1)S(1)}, f32[1,960]{1,0:T(1,128)S(1)}, bf16[128,960]{1,0:T(8,128)(2,1)S(1)}, bf16[8,128,640]{2,1,0:T(8,128)(2,1)S(1)}) custom-call(s32[5]{0:T(128)S(1)} %stack.112.sc, s32[9]{0:T(128)S(1)} %pad_add_fusion.1.sched, s32[8,384]{1,0:T(8,128)S(1)} %pad.9.qinfo, ...), custom_call_target="tpu_custom_call" | custom-call | flops 13799999488 | bytes 65536 | tf_op jit(solution)/shard_map/attend_back/pallas_call | solution.py:163
  211.9 4.6 %collective-permute-done.61.refs_14_ = bf16[128,960]{1,0:T(8,128)(2,1)S(1)} collective-permute-done((bf16[128,960]{1,0:T(8,128)(2,1)S(1)}, bf16[128,960]{1,0:T(8,128)(2,1)S(1)}, u32[]{:S(2)}, u32[]{:S(2)}) %collective-permute-start.61) | collective-permute-done | bytes 245792 | tf_op jit(solution)/shard_map/ppermute | solution.py:36
  222.4 8.2 %mlp_back.3 = (bf16[2,256,640]{2,1,0:T(8,128)(2,1)S(1)}, bf16[2,256,640]{2,1,0:T(8,128)(2,1)S(1)}, f32[128,960]{1,0:T(8,128)S(1)}, f32[128,960]{1,0:T(8,128)}) custom-call(s32[5]{0:T(128)S(1)} %stack.112.sc, bf16[128,960]{1,0:T(8,128)(2,1)S(1)} %get-tuple-element.342.l_own.refs_2_, bf16[128,960]{1,0:T(8,128)(2,1)S(1)} %collective-permute-done.64.l_side.refs_3_, ...), custom_call_target="tpu_custom_call" | custom-call | flops 7704999936 | bytes 65536 | tf_op jit(solution)/shard_map/mlp_back/pallas_call | solution.py:163
  241.4 3.8 grad_down.3
  247.5 9.3 %attend_back.3 = (f32[128,960]{1,0:T(8,128)S(1)}, bf16[128,960]{1,0:T(8,128)(2,1)S(1)}, f32[1,960]{1,0:T(1,128)S(1)}, bf16[128,960]{1,0:T(8,128)(2,1)S(1)}, bf16[8,128,640]{2,1,0:T(8,128)(2,1)S(1)}) custom-call(s32[5]{0:T(128)S(1)} %stack.112.sc, s32[9]{0:T(128)S(1)} %pad_add_fusion.1.sched, s32[8,384]{1,0:T(8,128)S(1)} %pad.9.qinfo, ...), custom_call_target="tpu_custom_call" | custom-call | flops 13799999488 | bytes 65536 | tf_op jit(solution)/shard_map/attend_back/pallas_call | solution.py:163
  266.6 3.8 collective-permute-done.73.refs_10_
  287.7 4.3 collective-permute-done.86
  295.4 4.0 collective-permute-done.88.go
  301.5 4.3 project_back.3
  308.0 3.5 collective-permute-done.93.refs_6_
  311.7 4.3 grad_rows.2.refs_16_
  320.2 4.3 grad_rows.3
  327.3 4.6 %collective-permute-done.137.refs_6_ = bf16[80,960]{1,0:T(8,128)(2,1)S(1)} collective-permute-done((bf16[80,960]{1,0:T(8,128)(2,1)S(1)}, bf16[80,960]{1,0:T(8,128)(2,1)S(1)}, u32[]{:S(2)}, u32[]{:S(2)}) %collective-permute-start.137) | collective-permute-done | bytes 153632 | tf_op jit(solution)/shard_map/ppermute | solution.py:49
  334.5 9.2 %collective-permute-done.98 = bf16[32,2560]{1,0:T(8,128)(2,1)S(1)} collective-permute-done((bf16[32,2560]{1,0:T(8,128)(2,1)S(1)}, bf16[32,2560]{1,0:T(8,128)(2,1)S(1)}, u32[]{:S(2)}, u32[]{:S(2)}) %collective-permute-start.98) | collective-permute-done | bytes 163872 | tf_op jit(solution)/shard_map/ppermute | solution.py:49
  346.4 4.5 %collective-permute-done.102 = bf16[32,2560]{1,0:T(8,128)(2,1)S(1)} collective-permute-done((bf16[32,2560]{1,0:T(8,128)(2,1)S(1)}, bf16[32,2560]{1,0:T(8,128)(2,1)S(1)}, u32[]{:S(2)}, u32[]{:S(2)}) %collective-permute-start.102) | collective-permute-done | bytes 163872 | tf_op jit(solution)/shard_map/ppermute | solution.py:49
  353.0 4.9 %collective-permute-done.119 = bf16[4,64,640]{2,1,0:T(8,128)(2,1)S(1)} collective-permute-done((bf16[4,64,640]{2,1,0:T(8,128)(2,1)S(1)}, bf16[4,64,640]{2,1,0:T(8,128)(2,1)S(1)}, u32[]{:S(2)}, u32[]{:S(2)}) %collective-permute-start.119) | collective-permute-done | bytes 327712 | tf_op jit(solution)/shard_map/ppermute | solution.py:49
  413.6 6.5 %collective-permute-done.130.refs_5_ = bf16[4,64,640]{2,1,0:T(8,128)(2,1)S(1)} collective-permute-done((bf16[4,64,640]{2,1,0:T(8,128)(2,1)}, bf16[4,64,640]{2,1,0:T(8,128)(2,1)S(1)}, u32[]{:S(2)}, u32[]{:S(2)}) %collective-permute-start.130) | collective-permute-done | bytes 327712 | tf_op jit(solution)/shard_map/ppermute | solution.py:49
  425.9 4.4 %finish_rows.1 = (f32[240,320]{1,0:T(8,128)S(1)}, f32[240,320]{1,0:T(8,128)S(1)}, f32[240,960]{1,0:T(8,128)}, f32[240,960]{1,0:T(8,128)}, f32[8,960]{1,0:T(8,128)S(1)}) custom-call(s32[5]{0:T(128)S(1)} %stack.112.sc, bf16[32,2560]{1,0:T(8,128)(2,1)S(1)} %copy-done.9, bf16[32,2560]{1,0:T(8,128)(2,1)S(1)} %copy-done.84, bf16[32,2560]{1,0:T(8,128)(2,1)S(1)} %copy-done.88, ...), custom_call_target="tpu_custom_call" | custom-call | flops 2875000064 | bytes 65536 | tf_op jit(solution)/shard_map/finish_rows/pallas_call | solution.py:163
  432.8 5.0 %finish_ff.1 = (f32[240,2560]{1,0:T(8,128)}, f32[240,2560]{1,0:T(8,128)}) custom-call(s32[5]{0:T(128)S(1)} %stack.112.sc, bf16[4,64,640]{2,1,0:T(8,128)(2,1)S(1)} %copy-done.3, bf16[4,64,640]{2,1,0:T(8,128)(2,1)} %collective-permute-done.124.refs_1_, bf16[4,64,640]{2,1,0:T(8,128)(2,1)S(1)} %collective-permute-done.125.refs_2_, ...), custom_call_target="tpu_custom_call" | custom-call | flops 4600000000 | bytes 65536 | tf_op jit(solution)/shard_map/finish_ff/pallas_call | solution.py:163
  (649 shorter events, 250.1 us)
Async XLA Ops:
  6.9 21.7 %collective-permute-start = (bf16[248,1664]{1,0:T(8,128)(2,1)}, bf16[248,1664]{1,0:T(8,128)(2,1)}, u32[]{:S(2)}, u32[]{:S(2)}) collective-permute-start(bf16[248,1664]{1,0:T(8,128)(2,1)} %pack_qkv.1.refs_3_.refs_5_.p0), channel_id=1, source_target_pairs={{0,2},{1,3},{2,0},{3,1},{4,6},{5,7},{6,4},{7,5},{8,10},{9,11},{10,... | collective-permute-start | bytes 2476040 | tf_op jit(solution)/shard_map/ppermute | solution.py:36
  9.9 18.7 %collective-permute-start.1 = (bf16[248,1664]{1,0:T(8,128)(2,1)}, bf16[248,1664]{1,0:T(8,128)(2,1)}, u32[]{:S(2)}, u32[]{:S(2)}) collective-permute-start(bf16[248,1664]{1,0:T(8,128)(2,1)} %pack_qkv.1.refs_3_.refs_5_.p0), channel_id=1, source_target_pairs={{0,1},{1,0},{2,3},{3,2},{4,5},{5,4},{6,7},{7,6},{8,9},{9,8},{10,11... | collective-permute-start | bytes 2476040 | tf_op jit(solution)/shard_map/ppermute | solution.py:36
  29.0 16.9 %collective-permute-start.7 = (bf16[2,240,640]{2,1,0:T(8,128)(2,1)}, bf16[2,240,640]{2,1,0:T(8,128)(2,1)S(1)}, u32[]{:S(2)}, u32[]{:S(2)}) collective-permute-start(bf16[2,240,640]{2,1,0:T(8,128)(2,1)} %pad_maximum_fusion.1), channel_id=1, source_target_pairs={{0,2},{1,3},{2,0},{3,1},{4,6},{5,7},{6,4},{7,5},{8,10},{9,11},{10,... | collective-permute-start | bytes 1843208 | tf_op jit(solution)/shard_map/ppermute | solution.py:36
  34.9 12.7 %collective-permute-start.6 = (bf16[240,960]{1,0:T(8,128)(2,1)S(1)}, bf16[240,960]{1,0:T(8,128)(2,1)S(1)}, u32[]{:S(2)}, u32[]{:S(2)}) collective-permute-start(bf16[240,960]{1,0:T(8,128)(2,1)S(1)} %copy-done.33), channel_id=1, source_target_pairs={{0,1},{1,0},{2,3},{3,2},{4,5},{5,4},{6,7},{7,6},{8,9},{9,8},{10,11... | collective-permute-start | bytes 1382408 | tf_op jit(solution)/shard_map/ppermute | solution.py:36
  35.1 21.3 %collective-permute-start.10 = (bf16[240,960]{1,0:T(8,128)(2,1)S(1)}, bf16[240,960]{1,0:T(8,128)(2,1)S(1)}, u32[]{:S(2)}, u32[]{:S(2)}) collective-permute-start(bf16[240,960]{1,0:T(8,128)(2,1)S(1)} %copy-done.33), channel_id=1, source_target_pairs={{0,2},{1,3},{2,0},{3,1},{4,6},{5,7},{6,4},{7,5},{8,10},{9,11},{10,... | collective-permute-start | bytes 1382408 | tf_op jit(solution)/shard_map/ppermute | solution.py:36
  45.9 25.8 %collective-permute-start.17 = (bf16[2,240,640]{2,1,0:T(8,128)(2,1)S(1)}, bf16[2,240,640]{2,1,0:T(8,128)(2,1)S(1)}, u32[]{:S(2)}, u32[]{:S(2)}) collective-permute-start(bf16[2,240,640]{2,1,0:T(8,128)(2,1)S(1)} %copy-done.128), channel_id=1, source_target_pairs={{0,2},{1,3},{2,0},{3,1},{4,6},{5,7},{6,4},{7,5},{8,10},{9,11},{10,... | collective-permute-start | bytes 1843208 | tf_op jit(solution)/shard_map/ppermute | solution.py:36
  49.8 22.0 %collective-permute-start.16 = (bf16[2,240,640]{2,1,0:T(8,128)(2,1)S(1)}, bf16[2,240,640]{2,1,0:T(8,128)(2,1)S(1)}, u32[]{:S(2)}, u32[]{:S(2)}) collective-permute-start(bf16[2,240,640]{2,1,0:T(8,128)(2,1)S(1)} %collective-permute-done.7.gm), channel_id=1, source_target_pairs={{0,4},{4,0},{8,12},{12,8},{16,20},{20,16},{24,28},{28,24},{1,5},{5... | collective-permute-start | bytes 1843208 | tf_op jit(solution)/shard_map/ppermute | solution.py:40
  56.4 13.1 %collective-permute-start.13 = (bf16[240,960]{1,0:T(8,128)(2,1)S(1)}, bf16[240,960]{1,0:T(8,128)(2,1)S(1)}, u32[]{:S(2)}, u32[]{:S(2)}) collective-permute-start(bf16[240,960]{1,0:T(8,128)(2,1)S(1)} %collective-permute-done.10.p2), channel_id=1, source_target_pairs={{0,1},{1,0},{2,3},{3,2},{4,5},{5,4},{6,7},{7,6},{8,9},{9,8},{10,11... | collective-permute-start | bytes 1382408 | tf_op jit(solution)/shard_map/ppermute | solution.py:36
  56.6 13.0 %collective-permute-start.11 = (bf16[128,640]{1,0:T(8,128)(2,1)S(1)}, bf16[128,640]{1,0:T(8,128)(2,1)S(1)}, u32[]{:S(2)}, u32[]{:S(2)}) collective-permute-start(bf16[128,640]{1,0:T(8,128)(2,1)S(1)} %collective-permute-done.8), channel_id=1, source_target_pairs={{0,8},{8,16},{16,24},{24,28},{28,20},{20,12},{12,4},{4,0},{1,9},{9... | collective-permute-start | bytes 491528 | tf_op jit(solution)/shard_map/ppermute | solution.py:49
  74.4 14.1 %collective-permute-start.18 = (bf16[2,240,640]{2,1,0:T(8,128)(2,1)S(1)}, bf16[2,240,640]{2,1,0:T(8,128)(2,1)S(1)}, u32[]{:S(2)}, u32[]{:S(2)}) collective-permute-start(bf16[2,240,640]{2,1,0:T(8,128)(2,1)S(1)} %collective-permute-done.17.um), channel_id=1, source_target_pairs={{0,4},{4,0},{8,12},{12,8},{16,20},{20,16},{24,28},{28,24},{1,5},{5... | collective-permute-start | bytes 1843208 | tf_op jit(solution)/shard_map/ppermute | solution.py:40
  91.0 18.3 %collective-permute-start.22 = (bf16[128,960]{1,0:T(8,128)(2,1)S(1)}, bf16[128,960]{1,0:T(8,128)(2,1)S(1)}, u32[]{:S(2)}, u32[]{:S(2)}) collective-permute-start(bf16[128,960]{1,0:T(8,128)(2,1)S(1)} %get-tuple-element.254.b_own.refs_0_), channel_id=1, source_target_pairs={{0,2},{1,3},{2,0},{3,1},{4,6},{5,7},{6,4},{7,5},{8,10},{9,11},{10,... | collective-permute-start | bytes 737288 | tf_op jit(solution)/shard_map/ppermute | solution.py:36
  115.6 20.7 %collective-permute-start.35 = (bf16[128,960]{1,0:T(8,128)(2,1)S(1)}, bf16[128,960]{1,0:T(8,128)(2,1)S(1)}, u32[]{:S(2)}, u32[]{:S(2)}) collective-permute-start(bf16[128,960]{1,0:T(8,128)(2,1)S(1)} %bitcast.255), channel_id=1, source_target_pairs={{0,1},{1,0},{2,3},{3,2},{4,5},{5,4},{6,7},{7,6},{8,9},{9,8},{10,11... | collective-permute-start | bytes 737288 | tf_op jit(solution)/shard_map/ppermute | solution.py:36
  129.2 14.0 %collective-permute-start.38 = (bf16[128,960]{1,0:T(8,128)(2,1)S(1)}, bf16[128,960]{1,0:T(8,128)(2,1)S(1)}, u32[]{:S(2)}, u32[]{:S(2)}) collective-permute-start(bf16[128,960]{1,0:T(8,128)(2,1)S(1)} %bitcast.256), channel_id=1, source_target_pairs={{0,2},{1,3},{2,0},{3,1},{4,6},{5,7},{6,4},{7,5},{8,10},{9,11},{10,... | collective-permute-start | bytes 737288 | tf_op jit(solution)/shard_map/ppermute | solution.py:36
  172.6 25.7 %collective-permute-start.51 = (bf16[2,128,240]{2,1,0:T(8,128)(2,1)S(1)}, bf16[2,128,240]{2,1,0:T(8,128)(2,1)S(1)}, u32[]{:S(2)}, u32[]{:S(2)}) collective-permute-start(bf16[2,128,240]{2,1,0:T(8,128)(2,1)S(1)} %get-tuple-element.319), channel_id=1, source_target_pairs={{0,1},{1,0},{2,3},{3,2},{4,5},{5,4},{6,7},{7,6},{8,9},{9,8},{10,11... | collective-permute-start | bytes 368648 | tf_op jit(solution)/shard_map/ppermute | solution.py:36
  172.6 26.5 %collective-permute-start.52 = (bf16[2,128,240]{2,1,0:T(8,128)(2,1)S(1)}, bf16[2,128,240]{2,1,0:T(8,128)(2,1)S(1)}, u32[]{:S(2)}, u32[]{:S(2)}) collective-permute-start(bf16[2,128,240]{2,1,0:T(8,128)(2,1)S(1)} %get-tuple-element.320), channel_id=1, source_target_pairs={{0,2},{1,3},{2,0},{3,1},{4,6},{5,7},{6,4},{7,5},{8,10},{9,11},{10,... | collective-permute-start | bytes 368648 | tf_op jit(solution)/shard_map/ppermute | solution.py:36
  174.0 18.7 %collective-permute-start.48 = (bf16[2,256,640]{2,1,0:T(8,128)(2,1)S(1)}, bf16[2,256,640]{2,1,0:T(8,128)(2,1)S(1)}, u32[]{:S(2)}, u32[]{:S(2)}) collective-permute-start(bf16[2,256,640]{2,1,0:T(8,128)(2,1)S(1)} %get-tuple-element.313), channel_id=1, source_target_pairs={{0,2},{1,3},{2,0},{3,1},{4,6},{5,7},{6,4},{7,5},{8,10},{9,11},{10,... | collective-permute-start | bytes 1966088 | tf_op jit(solution)/shard_map/ppermute | solution.py:36
  189.3 18.2 %collective-permute-start.55 = (bf16[2,128,240]{2,1,0:T(8,128)(2,1)S(1)}, bf16[2,128,240]{2,1,0:T(8,128)(2,1)S(1)}, u32[]{:S(2)}, u32[]{:S(2)}) collective-permute-start(bf16[2,128,240]{2,1,0:T(8,128)(2,1)S(1)} %get-tuple-element.324), channel_id=1, source_target_pairs={{0,3},{1,2},{2,1},{3,0},{4,7},{5,6},{6,5},{7,4},{8,11},{9,10},{10,... | collective-permute-start | bytes 368648 | tf_op jit(solution)/shard_map/ppermute | solution.py:36
  233.7 25.3 %collective-permute-start.69 = (bf16[136,640]{1,0:T(8,128)(2,1)}, bf16[136,640]{1,0:T(8,128)(2,1)S(1)}, u32[]{:S(2)}, u32[]{:S(2)}) collective-permute-start(bf16[136,640]{1,0:T(8,128)(2,1)} %copy-done.73), channel_id=1, source_target_pairs={{0,1},{1,0},{2,3},{3,2},{4,5},{5,4},{6,7},{7,6},{8,9},{9,8},{10,11... | collective-permute-start | bytes 522248 | tf_op jit(solution)/shard_map/ppermute | solution.py:36
  233.7 25.3 %collective-permute-start.70 = (bf16[136,640]{1,0:T(8,128)(2,1)}, bf16[136,640]{1,0:T(8,128)(2,1)S(1)}, u32[]{:S(2)}, u32[]{:S(2)}) collective-permute-start(bf16[136,640]{1,0:T(8,128)(2,1)} %copy-done.73), channel_id=1, source_target_pairs={{0,2},{1,3},{2,0},{3,1},{4,6},{5,7},{6,4},{7,5},{8,10},{9,11},{10,... | collective-permute-start | bytes 522248 | tf_op jit(solution)/shard_map/ppermute | solution.py:36
  235.3 23.8 %collective-permute-start.68 = (bf16[2,256,640]{2,1,0:T(8,128)(2,1)}, bf16[2,256,640]{2,1,0:T(8,128)(2,1)S(1)}, u32[]{:S(2)}, u32[]{:S(2)}) collective-permute-start(bf16[2,256,640]{2,1,0:T(8,128)(2,1)} %copy-done.31), channel_id=1, source_target_pairs={{0,2},{1,3},{2,0},{3,1},{4,6},{5,7},{6,4},{7,5},{8,10},{9,11},{10,... | collective-permute-start | bytes 1966088 | tf_op jit(solution)/shard_map/ppermute | solution.py:36
  264.5 13.7 %collective-permute-start.80 = (bf16[128,960]{1,0:T(8,128)(2,1)S(1)}, bf16[128,960]{1,0:T(8,128)(2,1)S(1)}, u32[]{:S(2)}, u32[]{:S(2)}) collective-permute-start(bf16[128,960]{1,0:T(8,128)(2,1)S(1)} %get-tuple-element.370.refs_12_), channel_id=1, source_target_pairs={{0,2},{1,3},{2,0},{3,1},{4,6},{5,7},{6,4},{7,5},{8,10},{9,11},{10,... | collective-permute-start | bytes 737288 | tf_op jit(solution)/shard_map/ppermute | solution.py:36
  292.7 15.3 %collective-permute-start.95 = (bf16[128,960]{1,0:T(8,128)(2,1)S(1)}, bf16[128,960]{1,0:T(8,128)(2,1)S(1)}, u32[]{:S(2)}, u32[]{:S(2)}) collective-permute-start(bf16[128,960]{1,0:T(8,128)(2,1)S(1)} %collective-permute-done.73.refs_10_), channel_id=1, source_target_pairs={{0,1},{1,0},{2,3},{3,2},{4,5},{5,4},{6,7},{7,6},{8,9},{9,8},{10,11... | collective-permute-start | bytes 737288 | tf_op jit(solution)/shard_map/ppermute | solution.py:36
  295.1 20.9 %collective-permute-start.96 = (bf16[128,960]{1,0:T(8,128)(2,1)S(1)}, bf16[128,960]{1,0:T(8,128)(2,1)S(1)}, u32[]{:S(2)}, u32[]{:S(2)}) collective-permute-start(bf16[128,960]{1,0:T(8,128)(2,1)S(1)} %collective-permute-done.80.refs_14_), channel_id=1, source_target_pairs={{0,1},{1,0},{2,3},{3,2},{4,5},{5,4},{6,7},{7,6},{8,9},{9,8},{10,11... | collective-permute-start | bytes 737288 | tf_op jit(solution)/shard_map/ppermute | solution.py:36
  317.9 26.2 %collective-permute-start.118 = (bf16[4,64,640]{2,1,0:T(8,128)(2,1)S(1)}, bf16[4,64,640]{2,1,0:T(8,128)(2,1)S(1)}, u32[]{:S(2)}, u32[]{:S(2)}) collective-permute-start(bf16[4,64,640]{2,1,0:T(8,128)(2,1)S(1)} %pad_maximum_fusion.4), channel_id=1, source_target_pairs={{0,4},{8,0},{16,8},{24,16},{28,24},{20,28},{12,20},{4,12},{1,5},{9... | collective-permute-start | bytes 983048 | tf_op jit(solution)/shard_map/ppermute | solution.py:49
  318.2 52.9 %collective-permute-start.133 = (bf16[80,960]{1,0:T(8,128)(2,1)S(1)}, bf16[80,960]{1,0:T(8,128)(2,1)S(1)}, u32[]{:S(2)}, u32[]{:S(2)}) collective-permute-start(bf16[80,960]{1,0:T(8,128)(2,1)S(1)} %collective-permute-done.132.refs_1_), channel_id=1, source_target_pairs={{0,8},{8,16},{16,24},{24,28},{28,20},{20,12},{12,4},{4,0},{1,9},{9... | collective-permute-start | bytes 460808 | tf_op jit(solution)/shard_map/ppermute | solution.py:49
  331.9 13.9 %collective-permute-start.115 = (bf16[4,64,640]{2,1,0:T(8,128)(2,1)S(1)}, bf16[4,64,640]{2,1,0:T(8,128)(2,1)S(1)}, u32[]{:S(2)}, u32[]{:S(2)}) collective-permute-start(bf16[4,64,640]{2,1,0:T(8,128)(2,1)S(1)} %fusion.2), channel_id=1, source_target_pairs={{0,8},{8,16},{16,24},{24,28},{28,20},{20,12},{12,4},{4,0},{1,9},{9... | collective-permute-start | bytes 983048 | tf_op jit(solution)/shard_map/ppermute | solution.py:49
  332.4 39.4 %collective-permute-start.138 = (bf16[80,960]{1,0:T(8,128)(2,1)S(1)}, bf16[80,960]{1,0:T(8,128)(2,1)S(1)}, u32[]{:S(2)}, u32[]{:S(2)}) collective-permute-start(bf16[80,960]{1,0:T(8,128)(2,1)S(1)} %collective-permute-done.137.refs_6_), channel_id=1, source_target_pairs={{0,4},{8,0},{16,8},{24,16},{28,24},{20,28},{12,20},{4,12},{1,5},{9... | collective-permute-start | bytes 460808 | tf_op jit(solution)/shard_map/ppermute | solution.py:49
  392.6 18.1 %collective-permute-start.125 = (bf16[4,64,640]{2,1,0:T(8,128)(2,1)}, bf16[4,64,640]{2,1,0:T(8,128)(2,1)S(1)}, u32[]{:S(2)}, u32[]{:S(2)}) collective-permute-start(bf16[4,64,640]{2,1,0:T(8,128)(2,1)} %collective-permute-done.124.refs_1_), channel_id=1, source_target_pairs={{0,8},{8,16},{16,24},{24,28},{28,20},{20,12},{12,4},{4,0},{1,9},{9... | collective-permute-start | bytes 983048 | tf_op jit(solution)/shard_map/ppermute | solution.py:49
  392.8 18.8 %collective-permute-start.129 = (bf16[4,64,640]{2,1,0:T(8,128)(2,1)}, bf16[4,64,640]{2,1,0:T(8,128)(2,1)}, u32[]{:S(2)}, u32[]{:S(2)}) collective-permute-start(bf16[4,64,640]{2,1,0:T(8,128)(2,1)} %collective-permute-done.128.refs_7_), channel_id=1, source_target_pairs={{0,4},{8,0},{16,8},{24,16},{28,24},{20,28},{12,20},{4,12},{1,5},{9... | collective-permute-start | bytes 983048 | tf_op jit(solution)/shard_map/ppermute | solution.py:49
  396.9 15.7 %collective-permute-start.112 = (bf16[16,2560]{1,0:T(8,128)(2,1)}, bf16[16,2560]{1,0:T(8,128)(2,1)S(1)}, u32[]{:S(2)}, u32[]{:S(2)}) collective-permute-start(bf16[16,2560]{1,0:T(8,128)(2,1)} %slice.355), channel_id=1, source_target_pairs={{0,4},{8,0},{16,8},{24,16},{28,24},{20,28},{12,20},{4,12},{1,5},{9... | collective-permute-start | bytes 245768 | tf_op jit(solution)/shard_map/ppermute | solution.py:49
  398.6 14.0 %collective-permute-start.108 = (bf16[16,2560]{1,0:T(8,128)(2,1)}, bf16[16,2560]{1,0:T(8,128)(2,1)}, u32[]{:S(2)}, u32[]{:S(2)}) collective-permute-start(bf16[16,2560]{1,0:T(8,128)(2,1)} %slice.354), channel_id=1, source_target_pairs={{0,8},{8,16},{16,24},{24,28},{28,20},{20,12},{12,4},{4,0},{1,9},{9... | collective-permute-start | bytes 245768 | tf_op jit(solution)/shard_map/ppermute | solution.py:49
  420.1 12.6 %collective-permute-start.131 = (bf16[2,64,640]{2,1,0:T(8,128)(2,1)S(1)}, bf16[2,64,640]{2,1,0:T(8,128)(2,1)S(1)}, u32[]{:S(2)}, u32[]{:S(2)}) collective-permute-start(bf16[2,64,640]{2,1,0:T(8,128)(2,1)S(1)} %slice.357), channel_id=1, source_target_pairs={{0,4},{8,0},{16,8},{24,16},{28,24},{20,28},{12,20},{4,12},{1,5},{9... | collective-permute-start | bytes 491528 | tf_op jit(solution)/shard_map/ppermute | solution.py:49
  (241 other events, 2572.2 us)

commit v5 on v4

--- a/solution.py
+++ b/solution.py
@@ -156,14 +156,20 @@
 SMEM = pl.BlockSpec(memory_space=pltpu.SMEM)
 
 
+ANY = pl.BlockSpec(memory_space=pl.ANY)
 HBM = pl.BlockSpec(memory_space=pltpu.HBM)
 
 
 def call(body, name, n_scalar, ins, outs, scratch=(), us=2.0, limit=10, specs=None, out_specs=None):
+    specs = specs or [VMEM] * (len(ins) - n_scalar)
+    ins = list(ins[:n_scalar]) + [
+        pltpu.with_memory_space_constraint(x, pltpu.HBM) if spec is HBM else x
+        for x, spec in zip(ins[n_scalar:], specs)
+    ]
     return pl.pallas_call(
         body,
         name=name,
-        in_specs=[SMEM] * n_scalar + (specs or [VMEM] * (len(ins) - n_scalar)),
+        in_specs=[SMEM] * n_scalar + specs,
         out_specs=out_specs or [VMEM] * len(outs),
         out_shape=list(outs),
         scratch_shapes=list(scratch),
@@ -182,7 +188,7 @@
 
 def call_fetched(body, name, scal, ins, outs, us, limit, scratch=(), far=None, far_out=False):
     count, n_out = len(ins), len(outs)
-    far = [True] * count if far is None else far
+    far = far or [False] * count
 
     def whole(sc, *refs):
         sources, results = refs[:count], refs[count : count + n_out]
@@ -206,8 +212,8 @@
         bufs + [pltpu.SemaphoreType.DMA((max(count, n_out),)), *held, *scratch],
         us=us,
         limit=limit,
-        specs=[HBM if f else pl.BlockSpec(memory_space=pl.ANY) for f in far],
-        out_specs=[HBM] * n_out if far_out else None,
+        specs=[HBM if f else ANY for f in far],
+        out_specs=[ANY] * n_out if far_out else None,
     )
 
 
@@ -257,7 +263,7 @@
 def pack_qkv(scal, wq, wk, wv, gains):
     ins = [wq, wk.T, wv.T, gains]
     outs = [shape((SL + 8, QKVP), bf16)]
-    return call_fetched(pack_qkv_body, "pack_qkv", scal, ins, outs, us=3, limit=8)[0]
+    return call_fetched(pack_qkv_body, "pack_qkv", scal, ins, outs, us=3, limit=8, far=[True] * 3 + [False])[0]
 
 
 def pack_rest_body(sc, w_out, w_gate, w_up, w_down, out_ref, keep, give, down):
@@ -276,7 +282,7 @@
     quarters = shape((2, 2, SL, FFQ), bf16)
     outs = [shape((SL, D), bf16), quarters, quarters, shape((FFQ, D), bf16)]
     ins = [w_out, w_gate, w_up, w_down.T]
-    return call_fetched(pack_rest_body, "pack_rest", scal, ins, outs, us=6, limit=24)
+    return call_fetched(pack_rest_body, "pack_rest", scal, ins, outs, us=6, limit=24, far=[True] * 4)
 
 
 def head_only(tables):
@@ -348,8 +354,8 @@
             pltpu.SemaphoreType.DMA((WA,)),
         ],
         us=3,
-        limit=16,
-        specs=[VMEM] * (len(xs) + 2) + [HBM] * WA,
+        limit=10,
+        specs=[VMEM] * (len(xs) + 2) + [ANY] * WA,
     )
 
 
@@ -496,7 +502,7 @@
             pltpu.VMEM((2, 2, 2 * BLK, FFQ), f32),
             pltpu.SemaphoreType.DMA((5,)),
         ],
-        out_specs=[HBM, VMEM, HBM, VMEM, VMEM],
+        out_specs=[ANY, VMEM, ANY, VMEM, VMEM],
         limit=12,
         us=5.5,
     )
@@ -560,7 +566,7 @@
             pltpu.VMEM((2, 2, 2 * BLK, FFQ), f32),
             pltpu.SemaphoreType.DMA((4,)),
         ],
-        specs=[VMEM, VMEM, HBM] + [VMEM] * 8,
+        specs=[VMEM, VMEM, ANY] + [VMEM] * 8,
         limit=12,
         us=6.7,
     )
@@ -575,8 +581,21 @@
     return out, gain_grad
 
 
-def attend_back_body(n, sc, sched, qinfo, dy, db_own, db_got, m, gain, p0, p1, p2, p3, q3, kv, o_t, lse, cos_ref, sin_ref, *refs):
-    dm_ref, dml_ref, gg, dq_ref, dkv_ref, lst, do3, d_scr, dq_scr, dq_t = refs
+def attend_back_body(n, far, sc, sched, qinfo, dy, db_own, db_got, gain, lse, cos_ref, sin_ref, *refs):
+    (m, *parts, q3, kv, o_t), refs = refs[:8], refs[8:]
+    dm_ref, dml_ref, gg, dq_ref, dkv_ref, lst, do3, d_scr, dq_scr, dq_t = refs[:10]
+    waits = []
+    if far:
+        bufs, sem = refs[10:18], refs[18]
+        copies = [
+            pltpu.make_async_copy(a, b, sem.at[i])
+            for i, (a, b) in enumerate(zip((m, *parts, q3, kv, o_t), bufs))
+        ]
+        for c in copies:
+            c.start()
+        m, *parts, q3, kv, o_t = bufs
+        copies[0].wait()
+        waits = copies[1:]
     count = list_blocks(sched, lst, n)
     part, gain_grad = norm_back(db_own[...] + db_got[...], m[...], gain[...])
     gg[...] = gain_grad
@@ -584,7 +603,9 @@
     dm_ref[...] = dm
     dml = dm.astype(bf16)
     dml_ref[...] = dml
-    for k, p in enumerate((p0, p1, p2, p3)):
+    for c in waits:
+        c.wait()
+    for k, p in enumerate(parts):
         d_scr[sc[0] ^ k] = nt(dml, p[...]).astype(bf16).astype(f32)
     whole = jnp.concatenate([d_scr[j] for j in range(WA)], axis=1)
     for j in range(QH):
@@ -631,13 +652,15 @@
             dq_ref[:, 128 * i :] = u[:, :HS]
 
 
-def attend_back(scal, sched, qinfo, dy, db_own, db_got, m, gain, parts, q3, kv, o_t, lse, tables):
+def attend_back(far, scal, sched, qinfo, dy, db_own, db_got, m, gain, parts, q3, kv, o_t, lse, tables):
     n = kv.shape[0]
+    kept = [m, *parts, q3, kv, o_t]
+    bufs = [pltpu.VMEM(x.shape, x.dtype) for x in kept] + [pltpu.SemaphoreType.DMA((8,))]
     return call(
-        functools.partial(attend_back_body, n),
+        functools.partial(attend_back_body, n, far),
         "attend_back",
         2,
-        [scal, sched, qinfo, dy, db_own, db_got, m, gain, *parts, q3, kv, o_t, lse, *tables],
+        [scal, sched, qinfo, dy, db_own, db_got, gain, lse, *tables, *kept],
         [
             shape((BLK, D), f32),
             shape((BLK, D), bf16),
@@ -651,8 +674,10 @@
             pltpu.VMEM((WA, BLK, SL), f32),
             pltpu.VMEM((BLK, D + 64), f32),
             pltpu.VMEM((KVH, HS, R3), f32),
+            *(bufs if far else []),
         ],
-        limit=8,
+        specs=[VMEM] * 8 + [HBM if far else VMEM] * 8,
+        limit=(16 if n == 8 else 40) if far else 8,
         us=12,
     )
 
@@ -676,7 +701,7 @@
         [scal, dq, *parts],
         [shape((WA, BLK, SL), f32)],
         [pltpu.VMEM((WA, SL + 8, QKVP), bf16), pltpu.SemaphoreType.DMA((WA,))],
-        specs=[VMEM] + [HBM] * WA,
+        specs=[VMEM] + [ANY] * WA,
         us=2,
     )[0]
 
@@ -723,7 +748,7 @@
             pltpu.SemaphoreType.DMA((WA,)),
         ],
         us=2.5,
-        specs=[VMEM] * 10 + [HBM] * WA,
+        specs=[VMEM] * 10 + [ANY] * WA,
     )
 
 
@@ -731,8 +756,7 @@
     out = refs[-1]
     slices = refs[:WA]
     lo = 0
-    for t, kind in enumerate((0, 0, 1)):
-        lows = refs[WA * (t + 1) : WA * (t + 2)]
+    for kind, lows in ((0, refs[WA : 2 * WA]), (0, refs[2 * WA : 3 * WA]), (1, refs[3 * WA : 4 * WA])):
         acc = None
         for sl, low in zip(slices, lows):
             part = tn(sl[kind], low[:BLK])
@@ -759,24 +783,31 @@
     out[SL : SL + 2, :D] = whole.astype(out.dtype)
 
 
-def grad_rows(scal, slices, dkvs, dqs, dms, prev, far=None):
+def grad_rows(scal, slices, dkvs, dqs, dmls, prev):
     has_prev = prev is not None
     cols = QKV + D
     return call_fetched(
         functools.partial(grad_rows_body, has_prev),
         "grad_rows",
         scal,
-        [*slices, *dkvs, *dqs, *dms] + ([prev] if has_prev else []),
+        [*slices, *dkvs, *dqs, *dmls] + ([prev] if has_prev else []),
         [shape((256, cols), bf16 if has_prev else f32)],
         us=4,
-        limit=24,
-        far=far,
+        limit=12,
+        far=[True] * WA + [not has_prev] * (3 * WA) + [True] * has_prev,
         far_out=not has_prev,
     )[0]
 
 
-def grad_ff_body(has_prev, sc, b0, b1, b2, b3, keep, got, *refs):
+def grad_ffd_body(has_prev, sc, b0, b1, b2, b3, keep, got, z, zg, l0, l1, l2, l3, *refs):
     out, bt = refs[-2:]
+
+    def put(piece, block, lo, part):
+        rows, cols = part.shape
+        if has_prev:
+            part = part + refs[0][piece, block, lo : lo + rows, :cols]
+        out[piece, block, lo : lo + rows, :] = part.astype(out.dtype)
+
     for m, b in enumerate((b0, b1, b2, b3)):
         bt[:, BLK * m : BLK * (m + 1)] = b[...].astype(f32).T.astype(bf16)
     for gu in range(2):
@@ -785,56 +816,37 @@
             acc = mm(lhs[:, : 2 * BLK], keep[gu]) + mm(lhs[:, 2 * BLK :], got[gu])
             for i in range(4):
                 rows = min(64, SL - 64 * i)
-                part = acc[64 * i : 64 * i + rows]
-                if has_prev:
-                    part = part + refs[0][4 * gu + i, j, :rows]
-                out[4 * gu + i, j, :rows] = part.astype(out.dtype)
+                put(4 * gu + i, j, 0, acc[64 * i : 64 * i + rows])
                 if rows < 64:
                     out[4 * gu + i, j, rows:] = jnp.zeros((64 - rows, FFQ), out.dtype)
-
-
-def grad_ff(scal, bs, keep, got, prev):
+    acc = tn(z[:BLK], l0[...]) + tn(z[BLK:], l1[...])
+    acc = acc + tn(zg[:BLK], l2[...]) + tn(zg[BLK:], l3[...])
+    for p in range(8):
+        d = acc[80 * p : 80 * (p + 1)]
+        put(p, 4, 0, d[:64, :FFQ])
+        put(p, 5, 0, d[64:, :FFQ])
+        put(p, 5, 16, jnp.concatenate([d[:40, FFQ:], d[40:, FFQ:]], axis=1))
+        out[p, 5, 56:] = jnp.zeros((8, FFQ), out.dtype)
+
+
+def grad_ffd(scal, bs, keep, got, z, z_got, lows, prev):
     has_prev = prev is not None
     return call_fetched(
-        functools.partial(grad_ff_body, has_prev),
-        "grad_ff",
+        functools.partial(grad_ffd_body, has_prev),
+        "grad_ffd",
         scal,
-        [*bs, keep, got] + ([prev] if has_prev else []),
-        [shape((8, WA, 64, FFQ), bf16 if has_prev else f32)],
-        us=5,
-        limit=32,
+        [*bs, keep, got, z, z_got, *lows] + ([prev] if has_prev else []),
+        [shape((8, WA + 2, 64, FFQ), bf16 if has_prev else f32)],
+        us=7,
+        limit=24,
         scratch=[pltpu.VMEM((D, WA * BLK), bf16)],
-        far=[False] * 6 + [True] * has_prev,
+        far=[has_prev] * 4 + [False, False] + [has_prev] * 2 + [False] * WA + [True] * has_prev,
         far_out=not has_prev,
     )[0]
 
 
-def grad_down_body(has_prev, sc, z, zg, l0, l1, l2, l3, *refs):
-    out = refs[-1]
-    acc = tn(z[:BLK], l0[...]) + tn(z[BLK:], l1[...])
-    acc = acc + tn(zg[:BLK], l2[...]) + tn(zg[BLK:], l3[...])
-    if has_prev:
-        acc = acc + refs[0][...]
-    out[...] = acc.astype(out.dtype)
-
-
-def grad_down(scal, z, z_got, lows, prev):
-    has_prev = prev is not None
-    return call_fetched(
-        functools.partial(grad_down_body, has_prev),
-        "grad_down",
-        scal,
-        [z, z_got, *lows] + ([prev] if has_prev else []),
-        [shape((FFQ, D), bf16 if has_prev else f32)],
-        us=3,
-        limit=20,
-        far=[True, True] + [False] * 4 + [True] * has_prev,
-        far_out=not has_prev,
-    )[0]
-
-
 def finish_ff_body(n, sc, *refs):
-    gate, up = refs[n:]
+    gate, up, down, whole = refs[n:]
     position, w = sc[3], sc[0]
     for k in range(n):
         p = (position - k + n) % n
@@ -848,76 +860,68 @@
                         lo = pl.multiple_of(FFQ * (w ^ m), 128)
                         out[pl.ds(first, rows), pl.ds(lo, FFQ)] = refs[k][m, :rows].astype(f32)
 
+        at = pl.multiple_of(80 * p, 8)
+        whole[pl.ds(at, 64), :FFQ] = refs[k][4].astype(f32)
+        whole[pl.ds(at + 64, 16), :FFQ] = refs[k][5, :16].astype(f32)
+        for i in range(2):
+            part = refs[k][5, 16:56, 320 * i : 320 * (i + 1)]
+            whole[pl.ds(at + 40 * i, 40), FFQ:] = part.astype(f32)
+    down[...] = whole[...].T
+
 
 def finish_ff(scal, gathered):
-    return call_fetched(
+    gate, up, down = call_fetched(
         functools.partial(finish_ff_body, len(gathered)),
         "finish_ff",
         scal,
         list(gathered),
-        [shape((SL, 4 * FFQ), f32)] * 2,
-        us=4,
-        limit=20,
-        far=[False] * len(gathered),
-    )
-
-
-def finish_down_body(n, sc, *refs):
-    out = refs[n]
-    for k in range(n):
-        p = (sc[3] - k + n) % n
-        rows = refs[k].shape[0]
-        out[pl.ds(pl.multiple_of(p * rows, 8), rows), :] = refs[k][...].astype(f32)
-
-
-def finish_down(scal, gathered):
-    return call_fetched(
-        functools.partial(finish_down_body, len(gathered)),
-        "finish_down",
-        scal,
-        list(gathered),
-        [shape((FFQ, D), f32)],
-        us=2.5,
-        limit=20,
-        far=[False] * len(gathered),
-    )[0]
-
-
-def finish_rows_body(n, widths, sc, *refs):
-    *outs, gains = refs[n:]
+        [shape((SL, 4 * FFQ), f32), shape((SL, 4 * FFQ), f32), shape((D, FFQ), f32)],
+        us=6,
+        limit=32,
+        far=[True] * len(gathered),
+        scratch=[pltpu.VMEM((FFQ, D), f32)],
+    )
+    return gate, up, down.T
+
+
+def finish_rows_body(n, sc, *refs):
+    keys, values, query, rows_out, gains, whole = refs[n:]
     for k in range(n):
         p = (sc[3] - k + n) % n
         rows = refs[k].shape[0]
         tail = SL - rows * (n - 1)
         first = pl.multiple_of(p * rows, 8)
+        whole[pl.ds(first, rows), :] = refs[k][:, : 2 * KV].astype(f32)
 
         @pl.when(p < n - 1)
         def _():
-            lo = 0
-            for out, width in zip(outs, widths):
-                out[pl.ds(first, rows), :] = refs[k][:, lo : lo + width].astype(f32)
-                lo += width
+            query[pl.ds(first, rows), :] = refs[k][:, 2 * KV : QKV].astype(f32)
+            rows_out[pl.ds(first, rows), :] = refs[k][:, QKV:].astype(f32)
 
         @pl.when(p == n - 1)
         def _():
-            lo = 0
-            for out, width in zip(outs, widths):
-                out[rows * (n - 1) :, :] = refs[k][:tail, lo : lo + width].astype(f32)
-                lo += width
+            query[rows * (n - 1) :, :] = refs[k][:tail, 2 * KV : QKV].astype(f32)
+            rows_out[rows * (n - 1) :, :] = refs[k][:tail, QKV:].astype(f32)
             gains[...] = refs[k][tail : tail + 8, :D].astype(f32)
 
-
-def finish_rows(scal, gathered, widths):
-    return call_fetched(
-        functools.partial(finish_rows_body, len(gathered), tuple(widths)),
+    keys[...] = whole[:SL, :KV].T
+    values[...] = whole[:SL, KV:].T
+
+
+def finish_rows(scal, gathered):
+    wide = shape((SL, D), f32)
+    keys, values, query, rows_out, gains = call_fetched(
+        functools.partial(finish_rows_body, len(gathered)),
         "finish_rows",
         scal,
         list(gathered),
-        [shape((SL, width), f32) for width in widths] + [shape((8, D), f32)],
-        us=2.5,
+        [shape((KV, SL), f32), shape((KV, SL), f32), wide, wide, shape((8, D), f32)],
+        us=4,
         limit=20,
-        far=[False] * len(gathered),
-    )
+        far=[True] * len(gathered),
+        scratch=[pltpu.VMEM((256, 2 * KV), f32)],
+    )
+    return keys.T, values.T, query, rows_out, gains
 
 
 def body(
@@ -1110,7 +1114,7 @@
     b_diag = swap(b_far, 1)
     top_diag = swap(top_far, 1)
     dm, dml, gain_m_1, dq, dkv = attend_back(
-        scal, sched, qinfo, top, db_own, db_got, m, gain_m, out_parts, q3, every, o_t, lse, tables
+        False, scal, sched, qinfo, top, db_own, db_got, m, gain_m, out_parts, q3, every, o_t, lse, tables
     )
     dkv, dq, dml, b_diag, top_diag = bar(dkv, dq, dml, b_diag, top_diag)
     lows = [top, top_side, top_far, top_diag]
@@ -1118,17 +1122,19 @@
     sl1, keep_d1, z1 = sl, keep_d, z
     held = {}
     extras = [
-        lambda h: dict(got_d=got_d, down_1=grad_down(scal, z1, z_got, lows, None)),
+        lambda h: dict(got_d=got_d),
         lambda h: dict(
             s1=swap(sl1[1], 1), s2=swap(sl1[2], 2), da=query_back(scal, dq, qkv_parts)
         ),
         lambda h: dict(
-            s3=swap(sl1[3], 3), dq_far=swap(dq, 2), ff_1=grad_ff(scal, bs, keep_d1, h["got_d"], None)
+            s3=swap(sl1[3], 3),
+            dq_far=swap(dq, 2),
+            ff_1=grad_ffd(scal, bs, keep_d1, h["got_d"], z1, z_got, lows, None),
         ),
         lambda h: dict(dq_side=swap(dq, 1), dml_side=swap(dml, 1), dml_far=swap(dml, 2)),
     ]
     addends = spread(dkv, extras, held)
-    down_1, ff_1 = held["down_1"], held["ff_1"]
+    ff_1 = held["ff_1"]
     dq_diag, dml_diag = swap(held["dq_far"], 1), swap(held["dml_far"], 1)
     dkv0, dx, low = project_back(
         scal, addends, tables, held["da"], qkv_parts, x, dm, gain_a, gain_m_1
@@ -1144,77 +1150,120 @@
     keep_d, give_d, db_own, db_side = mlp_back(scal, low, low_side, gu, ff_parts)
     db_own, db_side, give_d, low_far = bar(db_own, db_side, give_d, low_far)
     db_got = swap(db_side, 1)
+    got_d = swap(give_d, 2)
     low_diag = swap(low_far, 1)
     dkv_side, dkv_far = swap(dkv0, 1), swap(dkv0, 2)
-    down_grad = grad_down(scal, z, z_got, [low, low_side, low_far, low_diag], down_1)
-    db_got, down_grad = bar(db_got, down_grad)
-    down_piece = at_position(down_grad.reshape(n, FFQ // n, D), n, position)
-    got_d = swap(give_d, 2)
-    held = {}
-    if n == 8:
-        held["down"] = ring_far(down_piece, n)
     dm, dml, gain_m_0, dq, dkv = attend_back(
-        scal, sched, qinfo, dx, db_own, db_got, m, gain_m, out_parts, q3, every, o_t, lse, tables
-    )
-    dkv, dq, dml, got_d, dkv_side, dkv_far = bar(dkv, dq, dml, got_d, dkv_side, dkv_far)
+        True, scal, sched, qinfo, dx, db_own, db_got, m, gain_m, out_parts, q3, every, o_t, lse, tables
+    )
+    dkv, dq, dml, got_d, dkv_side, dkv_far, low_diag = bar(
+        dkv, dq, dml, got_d, dkv_side, dkv_far, low_diag
+    )
     dkvs_1 = [dkv0, dkv_side, dkv_far]
+    lows_0 = [low, low_side, low_far, low_diag]
 
     def ff_piece_of(ff):
         sub = n // 8
-        pieces = ff.reshape(8, WA, sub, 64 // sub, FFQ).transpose(0, 2, 1, 3, 4)
-        return pieces.reshape(n, WA, 64 // sub, FFQ)
-
-    def down_step(k, h):
+        pieces = ff.reshape(8, WA + 2, sub, 64 // sub, FFQ).transpose(0, 2, 1, 3, 4)
+        return pieces.reshape(n, WA + 2, 64 // sub, FFQ)
+
+    keep_d0, dq0, dml0 = keep_d, dq, dml
+    held = {}
+
+    def ff_ring(h, k):
         if n != 8:
             return {}
-        go, back = h.get("down_go"), h.get("down_back")
-        if go is None:
-            go, back = h["down"]
-        go, back = ring_near(down_piece, n, k, go, back)
-        return dict(down_go=go, down_back=back)
-
-    keep_d0, dq0, dml0 = keep_d, dq, dml
+        if k == 4:
+            h["ff_piece"] = at_position(ff_piece_of(h["ff"]), n, position)
+            go, back = ring_far(h["ff_piece"], n)
+        else:
+            go, back = ring_near(h["ff_piece"], n, k, h["ff_go"], h["ff_back"])
+        return dict(ff_go=go, ff_back=back)
+
     extras = [
-        lambda h: dict(
-            dq_far=swap(dq0, 2), ff=grad_ff(scal, bs0, keep_d0, got_d, ff_1), **down_step(3, h)
-        ),
-        lambda h: dict(dml_far=swap(dml0, 2), da=query_back(scal, dq0, qkv_parts), **down_step(2, h)),
-        lambda h: dict(dkv_diag=swap(dkv_far, 1), **down_step(1, h)),
-        lambda h: dict(dq_side=swap(dq0, 1), dml_side=swap(dml0, 1)),
+        lambda h: dict(dq_far=swap(dq0, 2), ff=grad_ffd(scal, bs0, keep_d0, got_d, z, z_got, lows_0, ff_1)),
+        lambda h: dict(dml_far=swap(dml0, 2), **ff_ring(h, 4)),
+        lambda h: dict(da=query_back(scal, dq0, qkv_parts), dkv_diag=swap(dkv_far, 1)),
+        lambda h: dict(dq_side=swap(dq0, 1), dml_side=swap(dml0, 1), **ff_ring(h, 3)),
     ]
     addends = spread(dkv, extras, held)
     dkv0, dx, low = project_back(
         scal, addends, tables, held["da"], qkv_parts, x, dm, gain_a, gain_m_0
     )
-    input_grad = low[None]
-
-    ff_pieces = ff_piece_of(held["ff"])
+    rows_0 = [held["dq_far"], held["dml_far"]]
+
     if n == 8:
-        down_mine = total_low(down_piece(0), held["down_go"], held["down_back"])
-        down_all = ring_gather(down_mine, n, position)
-        ff_mine = total_low(*ring_scatter(at_position(ff_pieces, n, position), n))
+        ff_piece = held["ff_piece"]
+        ff_go, ff_back = ring_near(ff_piece, n, 2, held["ff_go"], held["ff_back"])
+        dkv_sent = dkv0
+        dkv_side, dkv_far_0 = swap(dkv0, 1), swap(dkv0, 2)
+        dq_diag, dml_diag = swap(rows_0[0], 1), swap(rows_0[1], 1)
+        rows_1 = grad_rows(scal, slices_1, dkvs_1 + [held["dkv_diag"]], dqs_1, dmls_1, None)
+        dkv_side, dkv_far_0, dq_diag, dml_diag, rows_1, ff_go, ff_back, low = bar(
+            dkv_side, dkv_far_0, dq_diag, dml_diag, rows_1, ff_go, ff_back, low
+        )
+        ff_go, ff_back = ring_near(ff_piece, n, 1, ff_go, ff_back)
+        dkvs = [dkv_sent, dkv_side, dkv_far_0, swap(dkv_far_0, 1)]
+        dqs = [dq, held["dq_side"], rows_0[0], dq_diag]
+        dmls = [dml, held["dml_side"], rows_0[1], dml_diag]
+        rows_grad = grad_rows(scal, slices, dkvs, dqs, dmls, rows_1)
+        rows_grad, ff_go, ff_back = bar(rows_grad, ff_go, ff_back)
+        piece = at_position(rows_grad.reshape(n, 256 // n, QKV + D), n, position)
+        go, back = ring_far(piece, n)
+        ff_mine = total_low(ff_piece(0), ff_go, ff_back)
+        home = rows_home(ff_mine[:WA], w)
+        go, back, home, down_mine = bar(go, back, home, ff_mine[WA:])
+        ff_ahead = [jnp.concatenate([home, down_mine], axis=0)]
+        ff_behind = list(ff_ahead)
+        for k in (3, 2, 1):
+            go, back = ring_near(piece, n, k, go, back)
+            f, g = ring_shift(ff_ahead[-1], n, 1), ring_shift(ff_behind[-1], n, -1)
+            go, back, f, g = bar(go, back, f, g)
+            ff_ahead.append(f)
+            ff_behind.append(g)
+        mine = total_low(piece(0), go, back)
+        f, g = ring_shift(ff_ahead[-1][:3], n, 1), ring_shift(ff_behind[-1][3:], n, -1)
+        ahead, behind = [mine], [mine]
+        a, c = ring_shift(mine, n, 1), ring_shift(mine, n, -1)
+        a, c, f, g = bar(a, c, f, g)
+        ahead.append(a)
+        behind.append(c)
+        ff_far = jnp.concatenate([f, g], axis=0)
+        ff_all = ff_ahead + [ff_far] + ff_behind[:0:-1]
+        gate_total, up_total, down_total = finish_ff(scal, ff_all)
+        for _ in range(2):
+            a, c = ring_shift(ahead[-1], n, 1), ring_shift(behind[-1], n, -1)
+            a, c, gate_total, up_total, down_total = bar(a, c, gate_total, up_total, down_total)
+            ahead.append(a)
+            behind.append(c)
+        half = mine.shape[0] // 2
+        far = jnp.concatenate(
+            [ring_shift(ahead[-1][:half], n, 1), ring_shift(behind[-1][half:], n, -1)], axis=0
+        )
+        rows_all = ahead + [far] + behind[:0:-1]
+        key_total, value_total, query_total, out_total, gain_rows = finish_rows(scal, rows_all)
     else:
-        down_all = ring_sum(down_grad.reshape(n, FFQ // n, D), n, position)
-        ff_mine = lax.psum_scatter(ff_pieces, "ctx", scatter_dimension=0, tiled=False)
-    ff_all = ring_gather(rows_home(ff_mine, w), n, position)
-    rows_1 = grad_rows(scal, slices_1, dkvs_1 + [held["dkv_diag"]], dqs_1, dmls_1, None)
-    dqs = [dq, held["dq_side"], held["dq_far"], swap(held["dq_far"], 1)]
-    dmls = [dml, held["dml_side"], held["dml_far"], swap(held["dml_far"], 1)]
-    rows_grad = grad_rows(scal, slices, everyone(dkv0), dqs, dmls, rows_1)
-    rows_all = ring_sum(rows_grad.reshape(n, 256 // n, QKV + D), n, position)
-    if n == 8:
-        down_total = finish_down(scal, down_all)
-        gate_total, up_total = finish_ff(scal, ff_all)
-        key_total, value_total, query_total, out_total, gain_rows = finish_rows(
-            scal, rows_all, [KV, KV, D, D]
+        ff_mine = lax.psum_scatter(
+            ff_piece_of(held["ff"]), "ctx", scatter_dimension=0, tiled=False
         )
-    else:
+        ff_home = jnp.concatenate([rows_home(ff_mine[:WA], w), ff_mine[WA:]], axis=0)
+        ff_all = ring_gather(ff_home, n, position)
+        rows_1 = grad_rows(scal, slices_1, dkvs_1 + [held["dkv_diag"]], dqs_1, dmls_1, None)
+        dqs = [dq, held["dq_side"], held["dq_far"], swap(held["dq_far"], 1)]
+        dmls = [dml, held["dml_side"], held["dml_far"], swap(held["dml_far"], 1)]
+        rows_grad = grad_rows(scal, slices, everyone(dkv0), dqs, dmls, rows_1)
+        rows_all = ring_sum(rows_grad.reshape(n, 256 // n, QKV + D), n, position)
         sub = n // 8
-        whole = placed(ff_all, n, position).reshape(2, 4, sub, WA, 64 // sub, FFQ)
-        whole = whole.transpose(0, 3, 1, 2, 4, 5).reshape(2, WA, 256, FFQ)[:, :, :SL]
+        whole = placed(ff_all, n, position).reshape(8, sub, WA + 2, 64 // sub, FFQ)
+        whole = whole.transpose(0, 2, 1, 3, 4).reshape(8, WA + 2, 64, FFQ)
+        down = whole[:, WA:].reshape(8, 128, FFQ)
+        right = down[:, 80:120].reshape(8, 40, 2, FFQ // 2).transpose(0, 2, 1, 3)
+        down = jnp.concatenate([down[:, :80], right.reshape(8, 80, FFQ // 2)], axis=2)
+        down_total = down.reshape(FFQ, D).astype(f32)
+        whole = whole[:, :WA].reshape(2, 4, WA, 64, FFQ).transpose(0, 2, 1, 3, 4)
+        whole = whole.reshape(2, WA, 256, FFQ)[:, :, :SL]
         whole = jnp.take(whole, w ^ jnp.arange(WA, dtype=i32), axis=1).transpose(0, 2, 1, 3)
         gate_total, up_total = whole.reshape(2, SL, -1).astype(f32)
-        down_total = placed(down_all, n, position).reshape(FFQ, D).astype(f32)
         rows_total = placed(rows_all, n, position).reshape(256, QKV + D).astype(f32)
         gain_rows = rows_total[SL:, :D]
         rows_total = rows_total[:SL]
@@ -1224,6 +1273,7 @@
             rows_total[:, 2 * KV : QKV],
             rows_total[:, QKV:],
         )
+    input_grad = low[None]
     gain_rows = lax.dynamic_slice_in_dim(gain_rows[:2], w * SL, SL, 1)
     return (
         output,

time: 444 us -> 428 us (0.964)
  local copies, waits for them, and re-layouts: 46.5 us -> 27.5 us
  Pallas kernels: 122 us -> 109 us
  waiting for transfers between devices: 142 us -> 150 us
  other arithmetic: 8.2 us -> 14 us
    unnamed x287 -> x225, local copies, waits for them, and re-layouts: 39.5 us -> 22.1 us
    ppermute x80 -> x64, waiting for transfers between devices: 85.1 us -> 98 us  [ring_shift(): lax.ppermute(x, 'ctx', [(order[i], order[(i + step) % n]) for i in range(...]
    pallas_call x25 -> x22, Pallas kernels: 122 us -> 109 us  [call(): pl.pallas_call(body, name=name, in_specs=[SMEM] * n_scalar + specs, out_s...]
    ppermute x80 -> x64, starting transfers between devices: 82.6 us -> 73 us  [ring_shift(): lax.ppermute(x, 'ctx', [(order[i], order[(i + step) % n]) for i in range(...]
    ppermute x57, waiting for transfers between devices: 43.6 us -> 34.2 us  [swap(): return lax.ppermute(x, 'wa', [(i, i ^ mask) for i in range(WA)])]
    ppermute x57, starting transfers between devices: 28.7 us -> 37.5 us  [swap(): return lax.ppermute(x, 'wa', [(i, i ^ mask) for i in range(WA)])]
    ppermute x3, waiting for transfers between devices: 12.9 us -> 17.8 us  [side_swap(): return lax.ppermute(x, 'ctx', [(i, i ^ 1) for i in range(n)])]
  transfers between devices with their start and end apart: 140 -> 124, of which waited for: 48 -> 48; matrix products, arithmetic and copies ran while one was open for 5% -> 4% of each run, Pallas kernels for 24% -> 22%
where the time goes in v5:
time: 428 us; the launch traced here: 420 us
  waiting for transfers between devices  150 us (35%)
  starting transfers between devices  116 us (27%)
  Pallas kernels  109 us (25%)
  local copies, waits for them, and re-layouts  27.5 us (6%)
  other arithmetic  14 us (3%)
    pallas_call x22, Pallas kernels, call(): pl.pallas_call(body, name=name, in_specs=[SMEM] * n_scalar + specs, out_s...  109 us
    ppermute x64, waiting for transfers between devices, ring_shift(): lax.ppermute(x, 'ctx', [(order[i], order[(i + step) % n]) for i in range(...  98 us
    ppermute x64, starting transfers between devices, ring_shift(): lax.ppermute(x, 'ctx', [(order[i], order[(i + step) % n]) for i in range(...  73 us
    ppermute x57, starting transfers between devices, swap(): return lax.ppermute(x, 'wa', [(i, i ^ mask) for i in range(WA)])  37.5 us
    ppermute x57, waiting for transfers between devices, swap(): return lax.ppermute(x, 'wa', [(i, i ^ mask) for i in range(WA)])  34.2 us
    unnamed x225, local copies, waits for them, and re-layouts  22.1 us
    ppermute x3, waiting for transfers between devices, side_swap(): return lax.ppermute(x, 'ctx', [(i, i ^ 1) for i in range(n)])  17.8 us
  transfers between devices with their start and end apart: 124, of which 48 were waited for; matrix products, arithmetic and copies ran while one was open for 4% of the time, Pallas kernels for 22%

profile of v5, /device:TPU:0, one launch (start us, length us, event | category | flops | bytes accessed | tf_op | source)
XLA Modules:
  0.0 420.2 jit_solution(12266695680931961930)
XLA Ops:
  7.6 5.8 %pack_rest.1 = (bf16[240,960]{1,0:T(8,128)(2,1)S(1)}, bf16[2,2,240,640]{3,2,1,0:T(8,128)(2,1)S(1)}, bf16[2,2,240,640]{3,2,1,0:T(8,128)(2,1)}, bf16[640,960]{1,0:T(8,128)(2,1)S(1)}) custom-call(s32[5]{0:T(128)S(1)} %stack.112.sc, f32[240,960]{1,0:T(8,128)} %refs_0_.2, f32[240,2560]{1,0:T(8,128)} %refs_1_.1, f32[240,2560]{1,0:T(8,128)} %refs_2_.1, ...), custom_call_target="tpu_custom_call" | custom-call | flops 6899999744 | bytes 65536 | tf_op jit(solution)/shard_map/pack_rest/pallas_call | solution.py:169
  36.6 7.0 %collective-permute-done.7.gm = bf16[2,240,640]{2,1,0:T(8,128)(2,1)S(1)} collective-permute-done((bf16[2,240,640]{2,1,0:T(8,128)(2,1)}, bf16[2,240,640]{2,1,0:T(8,128)(2,1)S(1)}, u32[]{:S(2)}, u32[]{:S(2)}) %collective-permute-start.7) | collective-permute-done | bytes 614432 | tf_op jit(solution)/shard_map/ppermute | solution.py:36
  49.0 5.1 %collective-permute-done.10.p2.refs_3_ = bf16[240,960]{1,0:T(8,128)(2,1)S(1)} collective-permute-done((bf16[240,960]{1,0:T(8,128)(2,1)S(1)}, bf16[240,960]{1,0:T(8,128)(2,1)S(1)}, u32[]{:S(2)}, u32[]{:S(2)}) %collective-permute-start.10) | collective-permute-done | bytes 460832 | tf_op jit(solution)/shard_map/ppermute | solution.py:36
  56.3 10.9 %collective-permute-done.11 = bf16[128,640]{1,0:T(8,128)(2,1)S(1)} collective-permute-done((bf16[128,640]{1,0:T(8,128)(2,1)S(1)}, bf16[128,640]{1,0:T(8,128)(2,1)S(1)}, u32[]{:S(2)}, u32[]{:S(2)}) %collective-permute-start.11) | collective-permute-done | bytes 163872 | tf_op jit(solution)/shard_map/ppermute | solution.py:49
  78.3 7.8 %collective-permute-done.18.uo = bf16[2,240,640]{2,1,0:T(8,128)(2,1)S(1)} collective-permute-done((bf16[2,240,640]{2,1,0:T(8,128)(2,1)S(1)}, bf16[2,240,640]{2,1,0:T(8,128)(2,1)S(1)}, u32[]{:S(2)}, u32[]{:S(2)}) %collective-permute-start.18) | collective-permute-done | bytes 614432 | tf_op jit(solution)/shard_map/ppermute | solution.py:40
  89.0 10.0 %collective-permute-done.21 = bf16[320,960]{1,0:T(8,128)(2,1)S(1)} collective-permute-done((bf16[320,960]{1,0:T(8,128)(2,1)S(1)}, bf16[320,960]{1,0:T(8,128)(2,1)S(1)}, u32[]{:S(2)}, u32[]{:S(2)}) %collective-permute-start.21) | collective-permute-done | bytes 614432 | tf_op jit(solution)/shard_map/ppermute | solution.py:40
  100.4 5.8 %mlp.2 = (bf16[256,640]{1,0:T(8,128)(2,1)S(1)}, bf16[256,640]{1,0:T(8,128)(2,1)S(1)}, f32[2,2,256,640]{3,2,1,0:T(8,128)S(1)}, f32[128,960]{1,0:T(8,128)S(1)}, f32[128,960]{1,0:T(8,128)S(1)}) custom-call(s32[5]{0:T(128)S(1)} %stack.112.sc, bf16[128,960]{1,0:T(8,128)(2,1)S(1)} %get-tuple-element.292.b_own.refs_0_, ...), custom_call_target="tpu_custom_call" | custom-call | flops 6325000192 | bytes 65536 | tf_op jit(solution)/shard_map/mlp/pallas_call | solution.py:169
  108.2 4.0 project.3
  113.1 3.7 collective-permute-start.24
  147.7 4.8 %collective-permute-start.40 = (bf16[128,960]{1,0:T(8,128)(2,1)S(1)}, bf16[128,960]{1,0:T(8,128)(2,1)S(1)}, u32[]{:S(2)}, u32[]{:S(2)}) collective-permute-start(bf16[128,960]{1,0:T(8,128)(2,1)S(1)} %get-tuple-element.326.b_own.refs_0_), channel_id=1, source_target_pairs={{0,2},{1,3},{2,0},{3,1},{4,6},{5,7},{6,4},{7,5},{8,10},{9,11},{10,... | collective-permute-start | bytes 737288 | tf_op jit(solution)/shard_map/ppermute | solution.py:36
  152.4 5.8 %mlp.3 = (bf16[256,640]{1,0:T(8,128)(2,1)S(1)}, bf16[256,640]{1,0:T(8,128)(2,1)S(1)}, f32[2,2,256,640]{3,2,1,0:T(8,128)S(1)}, f32[128,960]{1,0:T(8,128)S(1)}, f32[128,960]{1,0:T(8,128)S(1)}) custom-call(s32[5]{0:T(128)S(1)} %stack.112.sc, bf16[128,960]{1,0:T(8,128)(2,1)S(1)} %get-tuple-element.326.b_own.refs_0_, ...), custom_call_target="tpu_custom_call" | custom-call | flops 6325000192 | bytes 65536 | tf_op jit(solution)/shard_map/mlp/pallas_call | solution.py:169
  160.7 7.2 %mlp_back.2 = (bf16[2,256,640]{2,1,0:T(8,128)(2,1)S(1)}, bf16[2,256,640]{2,1,0:T(8,128)(2,1)S(1)}, f32[128,960]{1,0:T(8,128)S(1)}, f32[128,960]{1,0:T(8,128)S(1)}) custom-call(s32[5]{0:T(128)S(1)} %stack.112.sc, bf16[128,960]{1,0:T(8,128)(2,1)S(1)} %bitcast.220, bf16[128,960]{1,0:T(8,128)(2,1)S(1)} %collective-permute-done.35.l_side.refs_9_, ...), custom_call_target="tpu_custom_call" | custom-call | flops 7704999936 | bytes 65536 | tf_op jit(solution)/shard_map/mlp_back/pallas_call | solution.py:169
  170.2 4.8 %attend_back.2 = (f32[128,960]{1,0:T(8,128)S(1)}, bf16[128,960]{1,0:T(8,128)(2,1)S(1)}, f32[1,960]{1,0:T(1,128)S(1)}, bf16[128,960]{1,0:T(8,128)(2,1)S(1)}, bf16[8,128,640]{2,1,0:T(8,128)(2,1)S(1)}) custom-call(s32[5]{0:T(128)S(1)} %stack.112.sc, s32[9]{0:T(128)S(1)} %pad_add_fusion.1.sched, s32[8,384]{1,0:T(8,128)S(1)} %pad.9.qinfo, ...), custom_call_target="tpu_custom_call" | custom-call | flops 13799999488 | bytes 65536 | tf_op jit(solution)/shard_map/attend_back/pallas_call | solution.py:169
  175.1 6.8 %collective-permute-start.46 = (bf16[64,640]{1,0:T(8,128)(2,1)S(1)}, bf16[64,640]{1,0:T(8,128)(2,1)S(1)}, u32[]{:S(2)}, u32[]{:S(2)}) collective-permute-start(bf16[64,640]{1,0:T(8,128)(2,1)S(1)} %get-tuple-element.561), channel_id=1, source_target_pairs={{0,8},{8,16},{16,24},{24,28},{28,20},{20,12},{12,4},{4,0},{1,9},{9... | collective-permute-start | bytes 245768 | tf_op jit(solution)/shard_map/ppermute | solution.py:49
  196.1 5.2 %grad_ffd.2.refs_12_ = f32[8,6,64,640]{3,2,1,0:T(8,128)S(1)} custom-call(s32[5]{0:T(128)S(1)} %stack.112.sc, bf16[128,960]{1,0:T(8,128)(2,1)S(1)} %get-tuple-element.326.b_own.refs_0_, bf16[128,960]{1,0:T(8,128)(2,1)S(1)} %collective-permute-done.39.b_side.refs_1_, bf16[128,960]{1,0:T(8,128)(2,1)S(1)} %collective-permute-done.40.refs_2_, ...), custom_call_target="tpu_custom_call" | custom-call | flops 8049999872 | bytes 65536 | tf_op jit(solution)/shard_map/grad_ffd/pallas_call | solution.py:169
  204.8 5.5 %collective-permute-done.61.refs_14_ = bf16[128,960]{1,0:T(8,128)(2,1)S(1)} collective-permute-done((bf16[128,960]{1,0:T(8,128)(2,1)S(1)}, bf16[128,960]{1,0:T(8,128)(2,1)S(1)}, u32[]{:S(2)}, u32[]{:S(2)}) %collective-permute-start.61) | collective-permute-done | bytes 245792 | tf_op jit(solution)/shard_map/ppermute | solution.py:36
  216.5 8.2 %mlp_back.3 = (bf16[2,256,640]{2,1,0:T(8,128)(2,1)S(1)}, bf16[2,256,640]{2,1,0:T(8,128)(2,1)S(1)}, f32[128,960]{1,0:T(8,128)S(1)}, f32[128,960]{1,0:T(8,128)}) custom-call(s32[5]{0:T(128)S(1)} %stack.112.sc, bf16[128,960]{1,0:T(8,128)(2,1)S(1)} %get-tuple-element.380.l_own.refs_8_, bf16[128,960]{1,0:T(8,128)(2,1)S(1)} %collective-permute-done.64.l_side.refs_9_, ...), custom_call_target="tpu_custom_call" | custom-call | flops 7704999936 | bytes 65536 | tf_op jit(solution)/shard_map/mlp_back/pallas_call | solution.py:169
  236.1 6.7 %attend_back.3 = (f32[128,960]{1,0:T(8,128)S(1)}, bf16[128,960]{1,0:T(8,128)(2,1)S(1)}, f32[1,960]{1,0:T(1,128)S(1)}, bf16[128,960]{1,0:T(8,128)(2,1)S(1)}, bf16[8,128,640]{2,1,0:T(8,128)(2,1)S(1)}) custom-call(s32[5]{0:T(128)S(1)} %stack.112.sc, s32[9]{0:T(128)S(1)} %pad_add_fusion.1.sched, s32[8,384]{1,0:T(8,128)S(1)} %pad.9.qinfo, ...), custom_call_target="tpu_custom_call" | custom-call | flops 13799999488 | bytes 65536 | tf_op jit(solution)/shard_map/attend_back/pallas_call | solution.py:169
  243.6 5.8 %collective-permute-done.67.refs_5_ = bf16[2,256,640]{2,1,0:T(8,128)(2,1)S(1)} collective-permute-done((bf16[2,256,640]{2,1,0:T(8,128)(2,1)}, bf16[2,256,640]{2,1,0:T(8,128)(2,1)S(1)}, u32[]{:S(2)}, u32[]{:S(2)}) %collective-permute-start.67) | collective-permute-done | bytes 655392 | tf_op jit(solution)/shard_map/ppermute | solution.py:36
  253.5 7.8 %grad_ffd.3 = bf16[8,6,64,640]{3,2,1,0:T(8,128)(2,1)S(1)} custom-call(s32[5]{0:T(128)S(1)} %stack.112.sc, bf16[128,960]{1,0:T(8,128)(2,1)} %copy-done.25, bf16[128,960]{1,0:T(8,128)(2,1)} %copy-done.26, bf16[128,960]{1,0:T(8,128)(2,1)} %copy-done.84, bf16[128,960]{1,0:T(8,128)(2,1)} %copy-done.87, bf16[2,256,640]{2,1,0:T(8,128)(2,1)S(1)} %copy-done.55, ...), custom_call_target="tpu_custom_call" | custom-call | flops 8049999872 | bytes 65536 | tf_op jit(solution)/shard_map/grad_ffd/pallas_call | solution.py:169
  269.4 6.3 %collective-permute-done.75 = bf16[128,640]{1,0:T(8,128)(2,1)} collective-permute-done((bf16[128,640]{1,0:T(8,128)(2,1)}, bf16[128,640]{1,0:T(8,128)(2,1)}, u32[]{:S(2)}, u32[]{:S(2)}) %collective-permute-start.75) | collective-permute-done | bytes 163872 | tf_op jit(solution)/shard_map/ppermute | solution.py:49
  290.5 5.9 %collective-permute-done.82.go = bf16[128,640]{1,0:T(8,128)(2,1)S(1)} collective-permute-done((bf16[128,640]{1,0:T(8,128)(2,1)S(1)}, bf16[128,640]{1,0:T(8,128)(2,1)S(1)}, u32[]{:S(2)}, u32[]{:S(2)}) %collective-permute-start.82) | collective-permute-done | bytes 163872 | tf_op jit(solution)/shard_map/ppermute | solution.py:49
  299.3 4.2 project_back.3
  305.3 4.5 %grad_rows.2.refs_16_ = f32[256,2560]{1,0:T(8,128)S(1)} custom-call(s32[5]{0:T(128)S(1)} %stack.112.sc, bf16[2,128,240]{2,1,0:T(8,128)(2,1)} %copy-done.60, bf16[2,128,240]{2,1,0:T(8,128)(2,1)} %copy-done.99, bf16[2,128,240]{2,1,0:T(8,128)(2,1)} %copy-done.100, bf16[2,128,240]{2,1,0:T(8,128)(2,1)} %copy-done.101, bf16[136,640]{1,0:T(8,128)(2,1)} %copy-done.43, ...), custom_call_target="tpu_custom_call" | custom-call | flops 4600000000 | bytes 65536 | tf_op jit(solution)/shard_map/grad_rows/pallas_call | solution.py:169
  315.9 4.8 %grad_rows.3 = bf16[256,2560]{1,0:T(8,128)(2,1)S(1)} custom-call(s32[5]{0:T(128)S(1)} %stack.112.sc, bf16[2,128,240]{2,1,0:T(8,128)(2,1)} %copy-done.59, bf16[2,128,240]{2,1,0:T(8,128)(2,1)} %collective-permute-done.30.refs_1_, bf16[2,128,240]{2,1,0:T(8,128)(2,1)} %copy-done.97, bf16[2,128,240]{2,1,0:T(8,128)(2,1)} %copy-done.98, ...), custom_call_target="tpu_custom_call" | custom-call | flops 4600000000 | bytes 65536 | tf_op jit(solution)/shard_map/grad_rows/pallas_call | solution.py:169
  320.8 5.9 %collective-permute-done.95 = bf16[6,64,640]{2,1,0:T(8,128)(2,1)} collective-permute-done((bf16[6,64,640]{2,1,0:T(8,128)(2,1)}, bf16[6,64,640]{2,1,0:T(8,128)(2,1)}, u32[]{:S(2)}, u32[]{:S(2)}) %collective-permute-start.95) | collective-permute-done | bytes 491552 | tf_op jit(solution)/shard_map/ppermute | solution.py:49
  339.5 12.0 %collective-permute-done.102 = bf16[32,2560]{1,0:T(8,128)(2,1)S(1)} collective-permute-done((bf16[32,2560]{1,0:T(8,128)(2,1)S(1)}, bf16[32,2560]{1,0:T(8,128)(2,1)S(1)}, u32[]{:S(2)}, u32[]{:S(2)}) %collective-permute-start.102) | collective-permute-done | bytes 163872 | tf_op jit(solution)/shard_map/ppermute | solution.py:49
  356.2 10.8 %collective-permute-done.106 = bf16[32,2560]{1,0:T(8,128)(2,1)S(1)} collective-permute-done((bf16[32,2560]{1,0:T(8,128)(2,1)S(1)}, bf16[32,2560]{1,0:T(8,128)(2,1)S(1)}, u32[]{:S(2)}, u32[]{:S(2)}) %collective-permute-start.106) | collective-permute-done | bytes 163872 | tf_op jit(solution)/shard_map/ppermute | solution.py:49
  371.6 10.3 %collective-permute-done.110 = bf16[32,2560]{1,0:T(8,128)(2,1)S(1)} collective-permute-done((bf16[32,2560]{1,0:T(8,128)(2,1)S(1)}, bf16[32,2560]{1,0:T(8,128)(2,1)S(1)}, u32[]{:S(2)}, u32[]{:S(2)}) %collective-permute-start.110) | collective-permute-done | bytes 163872 | tf_op jit(solution)/shard_map/ppermute | solution.py:49
  386.3 5.3 %collective-permute-done.114.refs_1_ = bf16[32,2560]{1,0:T(8,128)(2,1)S(1)} collective-permute-done((bf16[32,2560]{1,0:T(8,128)(2,1)S(1)}, bf16[32,2560]{1,0:T(8,128)(2,1)S(1)}, u32[]{:S(2)}, u32[]{:S(2)}) %collective-permute-start.114) | collective-permute-done | bytes 163872 | tf_op jit(solution)/shard_map/ppermute | solution.py:49
  395.6 6.7 %finish_ff.1 = (f32[240,2560]{1,0:T(8,128)}, f32[240,2560]{1,0:T(8,128)}, f32[960,640]{1,0:T(8,128)}) custom-call(s32[5]{0:T(128)S(1)} %stack.112.sc, bf16[6,64,640]{2,1,0:T(8,128)(2,1)} %copy-done.71, bf16[6,64,640]{2,1,0:T(8,128)(2,1)} %copy-done.78, bf16[6,64,640]{2,1,0:T(8,128)(2,1)} %copy-done.80, bf16[6,64,640]{2,1,0:T(8,128)(2,1)} %copy-done.73, ...), custom_call_target="tpu_custom_call" | custom-call | flops 6899999744 | bytes 65536 | tf_op jit(solution)/shard_map/finish_ff/pallas_call | solution.py:169
  414.9 4.2 %finish_rows.1 = (f32[320,240]{1,0:T(8,128)}, f32[320,240]{1,0:T(8,128)}, f32[240,960]{1,0:T(8,128)}, f32[240,960]{1,0:T(8,128)}, f32[8,960]{1,0:T(8,128)S(1)}) custom-call(s32[5]{0:T(128)S(1)} %stack.112.sc, bf16[32,2560]{1,0:T(8,128)(2,1)} %copy-done.72, bf16[32,2560]{1,0:T(8,128)(2,1)} %copy-done.93, bf16[32,2560]{1,0:T(8,128)(2,1)} %copy-done.95, ...), custom_call_target="tpu_custom_call" | custom-call | flops 4600000000 | bytes 65536 | tf_op jit(solution)/shard_map/finish_rows/pallas_call | solution.py:169
  (542 shorter events, 207.8 us)
Async XLA Ops:
  4.6 21.7 %collective-permute-start = (bf16[248,1664]{1,0:T(8,128)(2,1)}, bf16[248,1664]{1,0:T(8,128)(2,1)}, u32[]{:S(2)}, u32[]{:S(2)}) collective-permute-start(bf16[248,1664]{1,0:T(8,128)(2,1)} %pack_qkv.1.refs_3_.refs_5_.p0), channel_id=1, source_target_pairs={{0,2},{1,3},{2,0},{3,1},{4,6},{5,7},{6,4},{7,5},{8,10},{9,11},{10,... | collective-permute-start | bytes 2476040 | tf_op jit(solution)/shard_map/ppermute | solution.py:36
  7.6 18.7 %collective-permute-start.1 = (bf16[248,1664]{1,0:T(8,128)(2,1)}, bf16[248,1664]{1,0:T(8,128)(2,1)}, u32[]{:S(2)}, u32[]{:S(2)}) collective-permute-start(bf16[248,1664]{1,0:T(8,128)(2,1)} %pack_qkv.1.refs_3_.refs_5_.p0), channel_id=1, source_target_pairs={{0,1},{1,0},{2,3},{3,2},{4,5},{5,4},{6,7},{7,6},{8,9},{9,8},{10,11... | collective-permute-start | bytes 2476040 | tf_op jit(solution)/shard_map/ppermute | solution.py:36
  26.7 16.9 %collective-permute-start.7 = (bf16[2,240,640]{2,1,0:T(8,128)(2,1)}, bf16[2,240,640]{2,1,0:T(8,128)(2,1)S(1)}, u32[]{:S(2)}, u32[]{:S(2)}) collective-permute-start(bf16[2,240,640]{2,1,0:T(8,128)(2,1)} %pad_maximum_fusion.1), channel_id=1, source_target_pairs={{0,2},{1,3},{2,0},{3,1},{4,6},{5,7},{6,4},{7,5},{8,10},{9,11},{10,... | collective-permute-start | bytes 1843208 | tf_op jit(solution)/shard_map/ppermute | solution.py:36
  32.8 21.3 %collective-permute-start.10 = (bf16[240,960]{1,0:T(8,128)(2,1)S(1)}, bf16[240,960]{1,0:T(8,128)(2,1)S(1)}, u32[]{:S(2)}, u32[]{:S(2)}) collective-permute-start(bf16[240,960]{1,0:T(8,128)(2,1)S(1)} %copy-done.19), channel_id=1, source_target_pairs={{0,2},{1,3},{2,0},{3,1},{4,6},{5,7},{6,4},{7,5},{8,10},{9,11},{10,... | collective-permute-start | bytes 1382408 | tf_op jit(solution)/shard_map/ppermute | solution.py:36
  43.6 25.8 %collective-permute-start.17 = (bf16[2,240,640]{2,1,0:T(8,128)(2,1)S(1)}, bf16[2,240,640]{2,1,0:T(8,128)(2,1)S(1)}, u32[]{:S(2)}, u32[]{:S(2)}) collective-permute-start(bf16[2,240,640]{2,1,0:T(8,128)(2,1)S(1)} %copy-done.65), channel_id=1, source_target_pairs={{0,2},{1,3},{2,0},{3,1},{4,6},{5,7},{6,4},{7,5},{8,10},{9,11},{10,... | collective-permute-start | bytes 1843208 | tf_op jit(solution)/shard_map/ppermute | solution.py:36
  47.4 22.0 %collective-permute-start.16 = (bf16[2,240,640]{2,1,0:T(8,128)(2,1)S(1)}, bf16[2,240,640]{2,1,0:T(8,128)(2,1)S(1)}, u32[]{:S(2)}, u32[]{:S(2)}) collective-permute-start(bf16[2,240,640]{2,1,0:T(8,128)(2,1)S(1)} %collective-permute-done.7.gm), channel_id=1, source_target_pairs={{0,4},{4,0},{8,12},{12,8},{16,20},{20,16},{24,28},{28,24},{1,5},{5... | collective-permute-start | bytes 1843208 | tf_op jit(solution)/shard_map/ppermute | solution.py:40
  54.1 13.1 %collective-permute-start.13 = (bf16[240,960]{1,0:T(8,128)(2,1)S(1)}, bf16[240,960]{1,0:T(8,128)(2,1)S(1)}, u32[]{:S(2)}, u32[]{:S(2)}) collective-permute-start(bf16[240,960]{1,0:T(8,128)(2,1)S(1)} %collective-permute-done.10.p2.refs_3_), channel_id=1, source_target_pairs={{0,1},{1,0},{2,3},{3,2},{4,5},{5,4},{6,7},{7,6},{8,9},{9,8},{10,11... | collective-permute-start | bytes 1382408 | tf_op jit(solution)/shard_map/ppermute | solution.py:36
  72.1 14.1 %collective-permute-start.18 = (bf16[2,240,640]{2,1,0:T(8,128)(2,1)S(1)}, bf16[2,240,640]{2,1,0:T(8,128)(2,1)S(1)}, u32[]{:S(2)}, u32[]{:S(2)}) collective-permute-start(bf16[2,240,640]{2,1,0:T(8,128)(2,1)S(1)} %collective-permute-done.17.um), channel_id=1, source_target_pairs={{0,4},{4,0},{8,12},{12,8},{16,20},{20,16},{24,28},{28,24},{1,5},{5... | collective-permute-start | bytes 1843208 | tf_op jit(solution)/shard_map/ppermute | solution.py:40
  88.7 17.5 %collective-permute-start.22 = (bf16[128,960]{1,0:T(8,128)(2,1)S(1)}, bf16[128,960]{1,0:T(8,128)(2,1)S(1)}, u32[]{:S(2)}, u32[]{:S(2)}) collective-permute-start(bf16[128,960]{1,0:T(8,128)(2,1)S(1)} %get-tuple-element.292.b_own.refs_0_), channel_id=1, source_target_pairs={{0,2},{1,3},{2,0},{3,1},{4,6},{5,7},{6,4},{7,5},{8,10},{9,11},{10,... | collective-permute-start | bytes 737288 | tf_op jit(solution)/shard_map/ppermute | solution.py:36
  112.6 21.3 %collective-permute-start.35 = (bf16[128,960]{1,0:T(8,128)(2,1)S(1)}, bf16[128,960]{1,0:T(8,128)(2,1)S(1)}, u32[]{:S(2)}, u32[]{:S(2)}) collective-permute-start(bf16[128,960]{1,0:T(8,128)(2,1)S(1)} %bitcast.218), channel_id=1, source_target_pairs={{0,1},{1,0},{2,3},{3,2},{4,5},{5,4},{6,7},{7,6},{8,9},{9,8},{10,11... | collective-permute-start | bytes 737288 | tf_op jit(solution)/shard_map/ppermute | solution.py:36
  126.9 13.6 %collective-permute-start.38 = (bf16[128,960]{1,0:T(8,128)(2,1)S(1)}, bf16[128,960]{1,0:T(8,128)(2,1)S(1)}, u32[]{:S(2)}, u32[]{:S(2)}) collective-permute-start(bf16[128,960]{1,0:T(8,128)(2,1)S(1)} %bitcast.219), channel_id=1, source_target_pairs={{0,2},{1,3},{2,0},{3,1},{4,6},{5,7},{6,4},{7,5},{8,10},{9,11},{10,... | collective-permute-start | bytes 737288 | tf_op jit(solution)/shard_map/ppermute | solution.py:36
  169.0 17.4 %collective-permute-start.48 = (bf16[2,256,640]{2,1,0:T(8,128)(2,1)S(1)}, bf16[2,256,640]{2,1,0:T(8,128)(2,1)S(1)}, u32[]{:S(2)}, u32[]{:S(2)}) collective-permute-start(bf16[2,256,640]{2,1,0:T(8,128)(2,1)S(1)} %get-tuple-element.351), channel_id=1, source_target_pairs={{0,2},{1,3},{2,0},{3,1},{4,6},{5,7},{6,4},{7,5},{8,10},{9,11},{10,... | collective-permute-start | bytes 1966088 | tf_op jit(solution)/shard_map/ppermute | solution.py:36
  184.3 17.1 %collective-permute-start.55 = (bf16[2,128,240]{2,1,0:T(8,128)(2,1)S(1)}, bf16[2,128,240]{2,1,0:T(8,128)(2,1)S(1)}, u32[]{:S(2)}, u32[]{:S(2)}) collective-permute-start(bf16[2,128,240]{2,1,0:T(8,128)(2,1)S(1)} %get-tuple-element.359), channel_id=1, source_target_pairs={{0,3},{1,2},{2,1},{3,0},{4,7},{5,6},{6,5},{7,4},{8,11},{9,10},{10,... | collective-permute-start | bytes 368648 | tf_op jit(solution)/shard_map/ppermute | solution.py:36
  228.3 15.3 %collective-permute-start.68 = (bf16[136,640]{1,0:T(8,128)(2,1)}, bf16[136,640]{1,0:T(8,128)(2,1)S(1)}, u32[]{:S(2)}, u32[]{:S(2)}) collective-permute-start(bf16[136,640]{1,0:T(8,128)(2,1)} %copy-done.43), channel_id=1, source_target_pairs={{0,1},{1,0},{2,3},{3,2},{4,5},{5,4},{6,7},{7,6},{8,9},{9,8},{10,11... | collective-permute-start | bytes 522248 | tf_op jit(solution)/shard_map/ppermute | solution.py:36
  228.4 15.1 %collective-permute-start.69 = (bf16[136,640]{1,0:T(8,128)(2,1)}, bf16[136,640]{1,0:T(8,128)(2,1)S(1)}, u32[]{:S(2)}, u32[]{:S(2)}) collective-permute-start(bf16[136,640]{1,0:T(8,128)(2,1)} %copy-done.43), channel_id=1, source_target_pairs={{0,2},{1,3},{2,0},{3,1},{4,6},{5,7},{6,4},{7,5},{8,10},{9,11},{10,... | collective-permute-start | bytes 522248 | tf_op jit(solution)/shard_map/ppermute | solution.py:36
  229.3 20.1 %collective-permute-start.67 = (bf16[2,256,640]{2,1,0:T(8,128)(2,1)}, bf16[2,256,640]{2,1,0:T(8,128)(2,1)S(1)}, u32[]{:S(2)}, u32[]{:S(2)}) collective-permute-start(bf16[2,256,640]{2,1,0:T(8,128)(2,1)} %copy-done.15), channel_id=1, source_target_pairs={{0,2},{1,3},{2,0},{3,1},{4,6},{5,7},{6,4},{7,5},{8,10},{9,11},{10,... | collective-permute-start | bytes 1966088 | tf_op jit(solution)/shard_map/ppermute | solution.py:36
  230.5 13.1 %collective-permute-start.70 = (bf16[128,960]{1,0:T(8,128)(2,1)}, bf16[128,960]{1,0:T(8,128)(2,1)S(1)}, u32[]{:S(2)}, u32[]{:S(2)}) collective-permute-start(bf16[128,960]{1,0:T(8,128)(2,1)} %copy-done.39), channel_id=1, source_target_pairs={{0,1},{1,0},{2,3},{3,2},{4,5},{5,4},{6,7},{7,6},{8,9},{9,8},{10,11... | collective-permute-start | bytes 737288 | tf_op jit(solution)/shard_map/ppermute | solution.py:36
  252.1 15.7 %collective-permute-start.76 = (bf16[128,960]{1,0:T(8,128)(2,1)S(1)}, bf16[128,960]{1,0:T(8,128)(2,1)}, u32[]{:S(2)}, u32[]{:S(2)}) collective-permute-start(bf16[128,960]{1,0:T(8,128)(2,1)S(1)} %get-tuple-element.406.refs_12_), channel_id=1, source_target_pairs={{0,2},{1,3},{2,0},{3,1},{4,6},{5,7},{6,4},{7,5},{8,10},{9,11},{10,... | collective-permute-start | bytes 737288 | tf_op jit(solution)/shard_map/ppermute | solution.py:36
  267.9 20.0 %collective-permute-start.84 = (bf16[128,960]{1,0:T(8,128)(2,1)S(1)}, bf16[128,960]{1,0:T(8,128)(2,1)S(1)}, u32[]{:S(2)}, u32[]{:S(2)}) collective-permute-start(bf16[128,960]{1,0:T(8,128)(2,1)S(1)} %copy-done.28), channel_id=1, source_target_pairs={{0,1},{1,0},{2,3},{3,2},{4,5},{5,4},{6,7},{7,6},{8,9},{9,8},{10,11... | collective-permute-start | bytes 737288 | tf_op jit(solution)/shard_map/ppermute | solution.py:36
  281.5 15.2 %collective-permute-start.86 = (bf16[6,64,640]{2,1,0:T(8,128)(2,1)S(1)}, bf16[6,64,640]{2,1,0:T(8,128)(2,1)S(1)}, u32[]{:S(2)}, u32[]{:S(2)}) collective-permute-start(bf16[6,64,640]{2,1,0:T(8,128)(2,1)S(1)} %pad_maximum_fusion.3), channel_id=1, source_target_pairs={{0,8},{8,16},{16,24},{24,28},{28,20},{20,12},{12,4},{4,0},{1,9},{9... | collective-permute-start | bytes 1474568 | tf_op jit(solution)/shard_map/ppermute | solution.py:49
  281.9 14.8 %collective-permute-start.87 = (bf16[6,64,640]{2,1,0:T(8,128)(2,1)S(1)}, bf16[6,64,640]{2,1,0:T(8,128)(2,1)S(1)}, u32[]{:S(2)}, u32[]{:S(2)}) collective-permute-start(bf16[6,64,640]{2,1,0:T(8,128)(2,1)S(1)} %pad_maximum_fusion.4), channel_id=1, source_target_pairs={{0,4},{8,0},{16,8},{24,16},{28,24},{20,28},{12,20},{4,12},{1,5},{9... | collective-permute-start | bytes 1474568 | tf_op jit(solution)/shard_map/ppermute | solution.py:49
  296.4 15.0 %collective-permute-start.91 = (bf16[128,960]{1,0:T(8,128)(2,1)}, bf16[128,960]{1,0:T(8,128)(2,1)S(1)}, u32[]{:S(2)}, u32[]{:S(2)}) collective-permute-start(bf16[128,960]{1,0:T(8,128)(2,1)} %collective-permute-done.76.refs_14_), channel_id=1, source_target_pairs={{0,1},{1,0},{2,3},{3,2},{4,5},{5,4},{6,7},{7,6},{8,9},{9,8},{10,11... | collective-permute-start | bytes 737288 | tf_op jit(solution)/shard_map/ppermute | solution.py:36
  297.0 14.5 %collective-permute-start.92 = (bf16[6,64,640]{2,1,0:T(8,128)(2,1)S(1)}, bf16[6,64,640]{2,1,0:T(8,128)(2,1)S(1)}, u32[]{:S(2)}, u32[]{:S(2)}) collective-permute-start(bf16[6,64,640]{2,1,0:T(8,128)(2,1)S(1)} %get-tuple-element.527), channel_id=1, source_target_pairs={{0,8},{8,16},{16,24},{24,28},{28,20},{20,12},{12,4},{4,0},{1,9},{9... | collective-permute-start | bytes 1474568 | tf_op jit(solution)/shard_map/ppermute | solution.py:49
  297.1 14.3 %collective-permute-start.93 = (bf16[6,64,640]{2,1,0:T(8,128)(2,1)S(1)}, bf16[6,64,640]{2,1,0:T(8,128)(2,1)S(1)}, u32[]{:S(2)}, u32[]{:S(2)}) collective-permute-start(bf16[6,64,640]{2,1,0:T(8,128)(2,1)S(1)} %get-tuple-element.526), channel_id=1, source_target_pairs={{0,4},{8,0},{16,8},{24,16},{28,24},{20,28},{12,20},{4,12},{1,5},{9... | collective-permute-start | bytes 1474568 | tf_op jit(solution)/shard_map/ppermute | solution.py:49
  312.9 13.7 %collective-permute-start.95 = (bf16[6,64,640]{2,1,0:T(8,128)(2,1)}, bf16[6,64,640]{2,1,0:T(8,128)(2,1)}, u32[]{:S(2)}, u32[]{:S(2)}) collective-permute-start(bf16[6,64,640]{2,1,0:T(8,128)(2,1)} %get-tuple-element.525), channel_id=1, source_target_pairs={{0,8},{8,16},{16,24},{24,28},{28,20},{20,12},{12,4},{4,0},{1,9},{9... | collective-permute-start | bytes 1474568 | tf_op jit(solution)/shard_map/ppermute | solution.py:49
  313.0 13.7 %collective-permute-start.96 = (bf16[6,64,640]{2,1,0:T(8,128)(2,1)}, bf16[6,64,640]{2,1,0:T(8,128)(2,1)}, u32[]{:S(2)}, u32[]{:S(2)}) collective-permute-start(bf16[6,64,640]{2,1,0:T(8,128)(2,1)} %get-tuple-element.524), channel_id=1, source_target_pairs={{0,4},{8,0},{16,8},{24,16},{28,24},{20,28},{12,20},{4,12},{1,5},{9... | collective-permute-start | bytes 1474568 | tf_op jit(solution)/shard_map/ppermute | solution.py:49
  335.2 16.7 %collective-permute-start.104 = (bf16[6,64,640]{2,1,0:T(8,128)(2,1)S(1)}, bf16[6,64,640]{2,1,0:T(8,128)(2,1)S(1)}, u32[]{:S(2)}, u32[]{:S(2)}) collective-permute-start(bf16[6,64,640]{2,1,0:T(8,128)(2,1)S(1)} %constant_dynamic-update-slice_fusion.refs_0_), channel_id=1, source_target_pairs={{0,8},{8,16},{16,24},{24,28},{28,20},{20,12},{12,4},{4,0},{1,9},{9... | collective-permute-start | bytes 1474568 | tf_op jit(solution)/shard_map/ppermute | solution.py:49
  337.0 14.9 %collective-permute-start.105 = (bf16[6,64,640]{2,1,0:T(8,128)(2,1)S(1)}, bf16[6,64,640]{2,1,0:T(8,128)(2,1)S(1)}, u32[]{:S(2)}, u32[]{:S(2)}) collective-permute-start(bf16[6,64,640]{2,1,0:T(8,128)(2,1)S(1)} %constant_dynamic-update-slice_fusion.refs_0_), channel_id=1, source_target_pairs={{0,4},{8,0},{16,8},{24,16},{28,24},{20,28},{12,20},{4,12},{1,5},{9... | collective-permute-start | bytes 1474568 | tf_op jit(solution)/shard_map/ppermute | solution.py:49
  337.4 14.1 %collective-permute-start.102 = (bf16[32,2560]{1,0:T(8,128)(2,1)S(1)}, bf16[32,2560]{1,0:T(8,128)(2,1)S(1)}, u32[]{:S(2)}, u32[]{:S(2)}) collective-permute-start(bf16[32,2560]{1,0:T(8,128)(2,1)S(1)} %pad_maximum_fusion.11), channel_id=1, source_target_pairs={{0,8},{8,16},{16,24},{24,28},{28,20},{20,12},{12,4},{4,0},{1,9},{9... | collective-permute-start | bytes 491528 | tf_op jit(solution)/shard_map/ppermute | solution.py:49
  351.9 15.4 %collective-permute-start.108 = (bf16[6,64,640]{2,1,0:T(8,128)(2,1)S(1)}, bf16[6,64,640]{2,1,0:T(8,128)(2,1)S(1)}, u32[]{:S(2)}, u32[]{:S(2)}) collective-permute-start(bf16[6,64,640]{2,1,0:T(8,128)(2,1)S(1)} %collective-permute-done.104.refs_1_), channel_id=1, source_target_pairs={{0,8},{8,16},{16,24},{24,28},{28,20},{20,12},{12,4},{4,0},{1,9},{9... | collective-permute-start | bytes 1474568 | tf_op jit(solution)/shard_map/ppermute | solution.py:49
  353.5 13.8 %collective-permute-start.109 = (bf16[6,64,640]{2,1,0:T(8,128)(2,1)S(1)}, bf16[6,64,640]{2,1,0:T(8,128)(2,1)S(1)}, u32[]{:S(2)}, u32[]{:S(2)}) collective-permute-start(bf16[6,64,640]{2,1,0:T(8,128)(2,1)S(1)} %collective-permute-done.105.refs_7_), channel_id=1, source_target_pairs={{0,4},{8,0},{16,8},{24,16},{28,24},{20,28},{12,20},{4,12},{1,5},{9... | collective-permute-start | bytes 1474568 | tf_op jit(solution)/shard_map/ppermute | solution.py:49
  367.3 14.6 %collective-permute-start.112 = (bf16[6,64,640]{2,1,0:T(8,128)(2,1)S(1)}, bf16[6,64,640]{2,1,0:T(8,128)(2,1)S(1)}, u32[]{:S(2)}, u32[]{:S(2)}) collective-permute-start(bf16[6,64,640]{2,1,0:T(8,128)(2,1)S(1)} %collective-permute-done.108.refs_2_), channel_id=1, source_target_pairs={{0,8},{8,16},{16,24},{24,28},{28,20},{20,12},{12,4},{4,0},{1,9},{9... | collective-permute-start | bytes 1474568 | tf_op jit(solution)/shard_map/ppermute | solution.py:49
  (195 other events, 2264.5 us)

commit v6 on v5

--- a/solution.py
+++ b/solution.py
@@ -766,7 +766,7 @@
             acc = acc + refs[4 * WA][:SL, lo : lo + width]
             out[:SL, lo : lo + width] = acc.astype(bf16)
         else:
-            out[:SL, lo : lo + width] = acc
+            out[:SL, lo : lo + width] = acc.astype(bf16)
         lo += width
     gains = sum(low[BLK:, :].astype(f32) for low in refs[WA : 2 * WA])
     rest = D - 2 * KV
@@ -778,7 +778,7 @@
         axis=0,
     )
     if has_prev:
-        whole = whole + refs[4 * WA][SL : SL + 2, :D]
+        whole = whole + refs[4 * WA][SL : SL + 2, :D].astype(f32)
     out[SL:, :] = jnp.zeros((256 - SL, lo), out.dtype)
     out[SL : SL + 2, :D] = whole.astype(out.dtype)
 
@@ -791,7 +791,7 @@
         "grad_rows",
         scal,
         [*slices, *dkvs, *dqs, *dmls] + ([prev] if has_prev else []),
-        [shape((256, cols), bf16 if has_prev else f32)],
+        [shape((256, cols), bf16)],
         us=4,
         limit=12,
         far=[True] * WA + [not has_prev] * (3 * WA) + [True] * has_prev,
@@ -836,7 +836,7 @@
         "grad_ffd",
         scal,
         [*bs, keep, got, z, z_got, *lows] + ([prev] if has_prev else []),
-        [shape((8, WA + 2, 64, FFQ), bf16 if has_prev else f32)],
+        [shape((8, WA + 2, 64, FFQ), bf16)],
         us=7,
         limit=24,
         scratch=[pltpu.VMEM((D, WA * BLK), bf16)],
@@ -1195,6 +1195,7 @@
     if n == 8:
         ff_piece = held["ff_piece"]
         ff_go, ff_back = ring_near(ff_piece, n, 2, held["ff_go"], held["ff_back"])
+        dkv0, rows_0[0], rows_0[1] = bar(dkv0, rows_0[0], rows_0[1])
         dkv_sent = dkv0
         dkv_side, dkv_far_0 = swap(dkv0, 1), swap(dkv0, 2)
         dq_diag, dml_diag = swap(rows_0[0], 1), swap(rows_0[1], 1)

time: 428 us -> 438 us (1.023)
  waiting for transfers between devices: 150 us -> 162 us
    ppermute x64, waiting for transfers between devices: 98 us -> 107 us  [ring_shift(): lax.ppermute(x, 'ctx', [(order[i], order[(i + step) % n]) for i in range(...]
    unnamed x225 -> x219, local copies, waits for them, and re-layouts: 22.1 us -> 21.8 us
  transfers between devices with their start and end apart: 124 -> 124, of which waited for: 48 -> 52; matrix products, arithmetic and copies ran while one was open for 4% -> 5% of each run, Pallas kernels for 22% -> 20%
where the time goes in v6:
time: 438 us; the launch traced here: 432 us
  waiting for transfers between devices  162 us (37%)
  starting transfers between devices  115 us (26%)
  Pallas kernels  107 us (24%)
  local copies, waits for them, and re-layouts  27.1 us (6%)
  other arithmetic  17.7 us (4%)
    pallas_call x22, Pallas kernels, call(): pl.pallas_call(body, name=name, in_specs=[SMEM] * n_scalar + specs, out_s...  107 us
    ppermute x64, waiting for transfers between devices, ring_shift(): lax.ppermute(x, 'ctx', [(order[i], order[(i + step) % n]) for i in range(...  107 us
    ppermute x64, starting transfers between devices, ring_shift(): lax.ppermute(x, 'ctx', [(order[i], order[(i + step) % n]) for i in range(...  75.2 us
    ppermute x57, waiting for transfers between devices, swap(): return lax.ppermute(x, 'wa', [(i, i ^ mask) for i in range(WA)])  37.1 us
    ppermute x57, starting transfers between devices, swap(): return lax.ppermute(x, 'wa', [(i, i ^ mask) for i in range(WA)])  33.6 us
    unnamed x219, local copies, waits for them, and re-layouts  21.8 us
    ppermute x3, waiting for transfers between devices, side_swap(): return lax.ppermute(x, 'ctx', [(i, i ^ 1) for i in range(n)])  17.8 us
  transfers between devices with their start and end apart: 124, of which 52 were waited for; matrix products, arithmetic and copies ran while one was open for 5% of the time, Pallas kernels for 20%

profile of v6, /device:TPU:0, one launch (start us, length us, event | category | flops | bytes accessed | tf_op | source)
XLA Modules:
  0.0 431.7 jit_solution(13816864311254356225)
XLA Ops:
  7.6 5.8 %pack_rest.1 = (bf16[240,960]{1,0:T(8,128)(2,1)S(1)}, bf16[2,2,240,640]{3,2,1,0:T(8,128)(2,1)S(1)}, bf16[2,2,240,640]{3,2,1,0:T(8,128)(2,1)}, bf16[640,960]{1,0:T(8,128)(2,1)S(1)}) custom-call(s32[5]{0:T(128)S(1)} %stack.112.sc, f32[240,960]{1,0:T(8,128)} %refs_0_.2, f32[240,2560]{1,0:T(8,128)} %refs_1_.1, f32[240,2560]{1,0:T(8,128)} %refs_2_.1, ...), custom_call_target="tpu_custom_call" | custom-call | flops 6899999744 | bytes 65536 | tf_op jit(solution)/shard_map/pack_rest/pallas_call | solution.py:169
  36.6 7.0 %collective-permute-done.7.gm = bf16[2,240,640]{2,1,0:T(8,128)(2,1)S(1)} collective-permute-done((bf16[2,240,640]{2,1,0:T(8,128)(2,1)}, bf16[2,240,640]{2,1,0:T(8,128)(2,1)S(1)}, u32[]{:S(2)}, u32[]{:S(2)}) %collective-permute-start.7) | collective-permute-done | bytes 614432 | tf_op jit(solution)/shard_map/ppermute | solution.py:36
  49.0 5.1 %collective-permute-done.10.p2.refs_3_ = bf16[240,960]{1,0:T(8,128)(2,1)S(1)} collective-permute-done((bf16[240,960]{1,0:T(8,128)(2,1)S(1)}, bf16[240,960]{1,0:T(8,128)(2,1)S(1)}, u32[]{:S(2)}, u32[]{:S(2)}) %collective-permute-start.10) | collective-permute-done | bytes 460832 | tf_op jit(solution)/shard_map/ppermute | solution.py:36
  56.3 10.9 %collective-permute-done.11 = bf16[128,640]{1,0:T(8,128)(2,1)S(1)} collective-permute-done((bf16[128,640]{1,0:T(8,128)(2,1)S(1)}, bf16[128,640]{1,0:T(8,128)(2,1)S(1)}, u32[]{:S(2)}, u32[]{:S(2)}) %collective-permute-start.11) | collective-permute-done | bytes 163872 | tf_op jit(solution)/shard_map/ppermute | solution.py:49
  78.3 7.8 %collective-permute-done.18.uo = bf16[2,240,640]{2,1,0:T(8,128)(2,1)S(1)} collective-permute-done((bf16[2,240,640]{2,1,0:T(8,128)(2,1)S(1)}, bf16[2,240,640]{2,1,0:T(8,128)(2,1)S(1)}, u32[]{:S(2)}, u32[]{:S(2)}) %collective-permute-start.18) | collective-permute-done | bytes 614432 | tf_op jit(solution)/shard_map/ppermute | solution.py:40
  89.0 10.0 %collective-permute-done.21 = bf16[320,960]{1,0:T(8,128)(2,1)S(1)} collective-permute-done((bf16[320,960]{1,0:T(8,128)(2,1)S(1)}, bf16[320,960]{1,0:T(8,128)(2,1)S(1)}, u32[]{:S(2)}, u32[]{:S(2)}) %collective-permute-start.21) | collective-permute-done | bytes 614432 | tf_op jit(solution)/shard_map/ppermute | solution.py:40
  100.4 5.8 %mlp.2 = (bf16[256,640]{1,0:T(8,128)(2,1)S(1)}, bf16[256,640]{1,0:T(8,128)(2,1)S(1)}, f32[2,2,256,640]{3,2,1,0:T(8,128)S(1)}, f32[128,960]{1,0:T(8,128)S(1)}, f32[128,960]{1,0:T(8,128)S(1)}) custom-call(s32[5]{0:T(128)S(1)} %stack.112.sc, bf16[128,960]{1,0:T(8,128)(2,1)S(1)} %get-tuple-element.295.b_own.refs_0_, ...), custom_call_target="tpu_custom_call" | custom-call | flops 6325000192 | bytes 65536 | tf_op jit(solution)/shard_map/mlp/pallas_call | solution.py:169
  108.2 4.0 project.3
  113.1 3.7 collective-permute-start.24
  151.0 5.8 %mlp.3 = (bf16[256,640]{1,0:T(8,128)(2,1)S(1)}, bf16[256,640]{1,0:T(8,128)(2,1)S(1)}, f32[2,2,256,640]{3,2,1,0:T(8,128)S(1)}, f32[128,960]{1,0:T(8,128)S(1)}, f32[128,960]{1,0:T(8,128)S(1)}) custom-call(s32[5]{0:T(128)S(1)} %stack.112.sc, bf16[128,960]{1,0:T(8,128)(2,1)S(1)} %get-tuple-element.329.b_own.refs_0_, ...), custom_call_target="tpu_custom_call" | custom-call | flops 6325000192 | bytes 65536 | tf_op jit(solution)/shard_map/mlp/pallas_call | solution.py:169
  158.4 7.2 %mlp_back.2 = (bf16[2,256,640]{2,1,0:T(8,128)(2,1)S(1)}, bf16[2,256,640]{2,1,0:T(8,128)(2,1)S(1)}, f32[128,960]{1,0:T(8,128)S(1)}, f32[128,960]{1,0:T(8,128)S(1)}) custom-call(s32[5]{0:T(128)S(1)} %stack.112.sc, bf16[128,960]{1,0:T(8,128)(2,1)S(1)} %bitcast.220, bf16[128,960]{1,0:T(8,128)(2,1)S(1)} %collective-permute-done.35.l_side.refs_9_, ...), custom_call_target="tpu_custom_call" | custom-call | flops 7704999936 | bytes 65536 | tf_op jit(solution)/shard_map/mlp_back/pallas_call | solution.py:169
  168.9 4.8 %attend_back.2 = (f32[128,960]{1,0:T(8,128)S(1)}, bf16[128,960]{1,0:T(8,128)(2,1)S(1)}, f32[1,960]{1,0:T(1,128)S(1)}, bf16[128,960]{1,0:T(8,128)(2,1)S(1)}, bf16[8,128,640]{2,1,0:T(8,128)(2,1)S(1)}) custom-call(s32[5]{0:T(128)S(1)} %stack.112.sc, s32[9]{0:T(128)S(1)} %pad_add_fusion.1.sched, s32[8,384]{1,0:T(8,128)S(1)} %pad.9.qinfo, ...), custom_call_target="tpu_custom_call" | custom-call | flops 13799999488 | bytes 65536 | tf_op jit(solution)/shard_map/attend_back/pallas_call | solution.py:169
  176.1 5.1 %collective-permute-start.47 = (bf16[64,640]{1,0:T(8,128)(2,1)S(1)}, bf16[64,640]{1,0:T(8,128)(2,1)S(1)}, u32[]{:S(2)}, u32[]{:S(2)}) collective-permute-start(bf16[64,640]{1,0:T(8,128)(2,1)S(1)} %get-tuple-element.566), channel_id=1, source_target_pairs={{0,4},{8,0},{16,8},{24,16},{28,24},{20,28},{12,20},{4,12},{1,5},{9... | collective-permute-start | bytes 245768 | tf_op jit(solution)/shard_map/ppermute | solution.py:49
  196.7 4.9 %grad_ffd.2.refs_12_ = bf16[8,6,64,640]{3,2,1,0:T(8,128)(2,1)S(1)} custom-call(s32[5]{0:T(128)S(1)} %stack.112.sc, bf16[128,960]{1,0:T(8,128)(2,1)S(1)} %get-tuple-element.329.b_own.refs_0_, bf16[128,960]{1,0:T(8,128)(2,1)S(1)} %collective-permute-done.39.b_side.refs_1_, bf16[128,960]{1,0:T(8,128)(2,1)S(1)} %collective-permute-done.40.refs_2_, ...), custom_call_target="tpu_custom_call" | custom-call | flops 8049999872 | bytes 65536 | tf_op jit(solution)/shard_map/grad_ffd/pallas_call | solution.py:169
  205.1 5.5 %collective-permute-done.61.refs_14_ = bf16[128,960]{1,0:T(8,128)(2,1)S(1)} collective-permute-done((bf16[128,960]{1,0:T(8,128)(2,1)S(1)}, bf16[128,960]{1,0:T(8,128)(2,1)S(1)}, u32[]{:S(2)}, u32[]{:S(2)}) %collective-permute-start.61) | collective-permute-done | bytes 245792 | tf_op jit(solution)/shard_map/ppermute | solution.py:36
  217.3 8.2 %mlp_back.3 = (bf16[2,256,640]{2,1,0:T(8,128)(2,1)S(1)}, bf16[2,256,640]{2,1,0:T(8,128)(2,1)S(1)}, f32[128,960]{1,0:T(8,128)S(1)}, f32[128,960]{1,0:T(8,128)}) custom-call(s32[5]{0:T(128)S(1)} %stack.112.sc, bf16[128,960]{1,0:T(8,128)(2,1)S(1)} %get-tuple-element.383.l_own.refs_8_, bf16[128,960]{1,0:T(8,128)(2,1)S(1)} %collective-permute-done.64.l_side.refs_9_, ...), custom_call_target="tpu_custom_call" | custom-call | flops 7704999936 | bytes 65536 | tf_op jit(solution)/shard_map/mlp_back/pallas_call | solution.py:169
  236.9 6.7 %attend_back.3 = (f32[128,960]{1,0:T(8,128)S(1)}, bf16[128,960]{1,0:T(8,128)(2,1)S(1)}, f32[1,960]{1,0:T(1,128)S(1)}, bf16[128,960]{1,0:T(8,128)(2,1)S(1)}, bf16[8,128,640]{2,1,0:T(8,128)(2,1)S(1)}) custom-call(s32[5]{0:T(128)S(1)} %stack.112.sc, s32[9]{0:T(128)S(1)} %pad_add_fusion.1.sched, s32[8,384]{1,0:T(8,128)S(1)} %pad.9.qinfo, ...), custom_call_target="tpu_custom_call" | custom-call | flops 13799999488 | bytes 65536 | tf_op jit(solution)/shard_map/attend_back/pallas_call | solution.py:169
  244.4 5.8 %collective-permute-done.67.refs_5_ = bf16[2,256,640]{2,1,0:T(8,128)(2,1)S(1)} collective-permute-done((bf16[2,256,640]{2,1,0:T(8,128)(2,1)}, bf16[2,256,640]{2,1,0:T(8,128)(2,1)S(1)}, u32[]{:S(2)}, u32[]{:S(2)}) %collective-permute-start.67) | collective-permute-done | bytes 655392 | tf_op jit(solution)/shard_map/ppermute | solution.py:36
  254.3 6.7 %grad_ffd.3 = bf16[8,6,64,640]{3,2,1,0:T(8,128)(2,1)S(1)} custom-call(s32[5]{0:T(128)S(1)} %stack.112.sc, bf16[128,960]{1,0:T(8,128)(2,1)} %copy-done.24, bf16[128,960]{1,0:T(8,128)(2,1)} %copy-done.25, bf16[128,960]{1,0:T(8,128)(2,1)} %copy-done.82, bf16[128,960]{1,0:T(8,128)(2,1)} %copy-done.85, bf16[2,256,640]{2,1,0:T(8,128)(2,1)S(1)} %copy-done.52, ...), custom_call_target="tpu_custom_call" | custom-call | flops 8049999872 | bytes 65536 | tf_op jit(solution)/shard_map/grad_ffd/pallas_call | solution.py:169
  269.6 6.2 %collective-permute-done.75 = bf16[128,640]{1,0:T(8,128)(2,1)} collective-permute-done((bf16[128,640]{1,0:T(8,128)(2,1)}, bf16[128,640]{1,0:T(8,128)(2,1)}, u32[]{:S(2)}, u32[]{:S(2)}) %collective-permute-start.75) | collective-permute-done | bytes 163872 | tf_op jit(solution)/shard_map/ppermute | solution.py:49
  290.6 6.4 %collective-permute-done.82.go = bf16[128,640]{1,0:T(8,128)(2,1)S(1)} collective-permute-done((bf16[128,640]{1,0:T(8,128)(2,1)S(1)}, bf16[128,640]{1,0:T(8,128)(2,1)S(1)}, u32[]{:S(2)}, u32[]{:S(2)}) %collective-permute-start.82) | collective-permute-done | bytes 163872 | tf_op jit(solution)/shard_map/ppermute | solution.py:49
  297.1 4.2 project_back.3
  307.2 4.4 %grad_rows.2.refs_16_ = bf16[256,2560]{1,0:T(8,128)(2,1)S(1)} custom-call(s32[5]{0:T(128)S(1)} %stack.112.sc, bf16[2,128,240]{2,1,0:T(8,128)(2,1)} %copy-done.57, bf16[2,128,240]{2,1,0:T(8,128)(2,1)} %copy-done.96, bf16[2,128,240]{2,1,0:T(8,128)(2,1)} %copy-done.97, bf16[2,128,240]{2,1,0:T(8,128)(2,1)} %copy-done.98, bf16[136,640]{1,0:T(8,128)(2,1)} %copy-done.40, ...), custom_call_target="tpu_custom_call" | custom-call | flops 4600000000 | bytes 65536 | tf_op jit(solution)/shard_map/grad_rows/pallas_call | solution.py:169
  312.6 5.0 %collective-permute-done.92 = bf16[6,64,640]{2,1,0:T(8,128)(2,1)S(1)} collective-permute-done((bf16[6,64,640]{2,1,0:T(8,128)(2,1)}, bf16[6,64,640]{2,1,0:T(8,128)(2,1)S(1)}, u32[]{:S(2)}, u32[]{:S(2)}) %collective-permute-start.92) | collective-permute-done | bytes 491552 | tf_op jit(solution)/shard_map/ppermute | solution.py:49
  323.2 4.4 %grad_rows.3 = bf16[256,2560]{1,0:T(8,128)(2,1)S(1)} custom-call(s32[5]{0:T(128)S(1)} %stack.112.sc, bf16[2,128,240]{2,1,0:T(8,128)(2,1)} %copy-done.56, bf16[2,128,240]{2,1,0:T(8,128)(2,1)} %collective-permute-done.30.refs_1_, bf16[2,128,240]{2,1,0:T(8,128)(2,1)} %copy-done.94, bf16[2,128,240]{2,1,0:T(8,128)(2,1)} %copy-done.95, ...), custom_call_target="tpu_custom_call" | custom-call | flops 4600000000 | bytes 65536 | tf_op jit(solution)/shard_map/grad_rows/pallas_call | solution.py:169
  327.6 7.4 %collective-permute-done.95 = bf16[6,64,640]{2,1,0:T(8,128)(2,1)} collective-permute-done((bf16[6,64,640]{2,1,0:T(8,128)(2,1)}, bf16[6,64,640]{2,1,0:T(8,128)(2,1)}, u32[]{:S(2)}, u32[]{:S(2)}) %collective-permute-start.95) | collective-permute-done | bytes 491552 | tf_op jit(solution)/shard_map/ppermute | solution.py:49
  350.3 11.0 %collective-permute-done.102 = bf16[32,2560]{1,0:T(8,128)(2,1)S(1)} collective-permute-done((bf16[32,2560]{1,0:T(8,128)(2,1)S(1)}, bf16[32,2560]{1,0:T(8,128)(2,1)S(1)}, u32[]{:S(2)}, u32[]{:S(2)}) %collective-permute-start.102) | collective-permute-done | bytes 163872 | tf_op jit(solution)/shard_map/ppermute | solution.py:49
  366.7 9.8 %collective-permute-done.106 = bf16[32,2560]{1,0:T(8,128)(2,1)S(1)} collective-permute-done((bf16[32,2560]{1,0:T(8,128)(2,1)S(1)}, bf16[32,2560]{1,0:T(8,128)(2,1)S(1)}, u32[]{:S(2)}, u32[]{:S(2)}) %collective-permute-start.106) | collective-permute-done | bytes 163872 | tf_op jit(solution)/shard_map/ppermute | solution.py:49
  382.2 9.1 %collective-permute-done.110 = bf16[32,2560]{1,0:T(8,128)(2,1)S(1)} collective-permute-done((bf16[32,2560]{1,0:T(8,128)(2,1)S(1)}, bf16[32,2560]{1,0:T(8,128)(2,1)S(1)}, u32[]{:S(2)}, u32[]{:S(2)}) %collective-permute-start.110) | collective-permute-done | bytes 163872 | tf_op jit(solution)/shard_map/ppermute | solution.py:49
  396.8 4.4 %collective-permute-done.114.refs_1_ = bf16[32,2560]{1,0:T(8,128)(2,1)S(1)} collective-permute-done((bf16[32,2560]{1,0:T(8,128)(2,1)S(1)}, bf16[32,2560]{1,0:T(8,128)(2,1)S(1)}, u32[]{:S(2)}, u32[]{:S(2)}) %collective-permute-start.114) | collective-permute-done | bytes 163872 | tf_op jit(solution)/shard_map/ppermute | solution.py:49
  407.1 6.7 %finish_ff.1 = (f32[240,2560]{1,0:T(8,128)}, f32[240,2560]{1,0:T(8,128)}, f32[960,640]{1,0:T(8,128)}) custom-call(s32[5]{0:T(128)S(1)} %stack.112.sc, bf16[6,64,640]{2,1,0:T(8,128)(2,1)} %copy-done.69, bf16[6,64,640]{2,1,0:T(8,128)(2,1)} %copy-done.76, bf16[6,64,640]{2,1,0:T(8,128)(2,1)} %copy-done.78, bf16[6,64,640]{2,1,0:T(8,128)(2,1)} %copy-done.71, ...), custom_call_target="tpu_custom_call" | custom-call | flops 6899999744 | bytes 65536 | tf_op jit(solution)/shard_map/finish_ff/pallas_call | solution.py:169
  426.4 4.2 finish_rows.1
  (536 shorter events, 224.9 us)
Async XLA Ops:
  4.6 21.7 %collective-permute-start = (bf16[248,1664]{1,0:T(8,128)(2,1)}, bf16[248,1664]{1,0:T(8,128)(2,1)}, u32[]{:S(2)}, u32[]{:S(2)}) collective-permute-start(bf16[248,1664]{1,0:T(8,128)(2,1)} %pack_qkv.1.refs_3_.refs_5_.p0), channel_id=1, source_target_pairs={{0,2},{1,3},{2,0},{3,1},{4,6},{5,7},{6,4},{7,5},{8,10},{9,11},{10,... | collective-permute-start | bytes 2476040 | tf_op jit(solution)/shard_map/ppermute | solution.py:36
  7.6 18.7 %collective-permute-start.1 = (bf16[248,1664]{1,0:T(8,128)(2,1)}, bf16[248,1664]{1,0:T(8,128)(2,1)}, u32[]{:S(2)}, u32[]{:S(2)}) collective-permute-start(bf16[248,1664]{1,0:T(8,128)(2,1)} %pack_qkv.1.refs_3_.refs_5_.p0), channel_id=1, source_target_pairs={{0,1},{1,0},{2,3},{3,2},{4,5},{5,4},{6,7},{7,6},{8,9},{9,8},{10,11... | collective-permute-start | bytes 2476040 | tf_op jit(solution)/shard_map/ppermute | solution.py:36
  26.7 16.9 %collective-permute-start.7 = (bf16[2,240,640]{2,1,0:T(8,128)(2,1)}, bf16[2,240,640]{2,1,0:T(8,128)(2,1)S(1)}, u32[]{:S(2)}, u32[]{:S(2)}) collective-permute-start(bf16[2,240,640]{2,1,0:T(8,128)(2,1)} %pad_maximum_fusion.1), channel_id=1, source_target_pairs={{0,2},{1,3},{2,0},{3,1},{4,6},{5,7},{6,4},{7,5},{8,10},{9,11},{10,... | collective-permute-start | bytes 1843208 | tf_op jit(solution)/shard_map/ppermute | solution.py:36
  32.8 21.3 %collective-permute-start.10 = (bf16[240,960]{1,0:T(8,128)(2,1)S(1)}, bf16[240,960]{1,0:T(8,128)(2,1)S(1)}, u32[]{:S(2)}, u32[]{:S(2)}) collective-permute-start(bf16[240,960]{1,0:T(8,128)(2,1)S(1)} %copy-done.18), channel_id=1, source_target_pairs={{0,2},{1,3},{2,0},{3,1},{4,6},{5,7},{6,4},{7,5},{8,10},{9,11},{10,... | collective-permute-start | bytes 1382408 | tf_op jit(solution)/shard_map/ppermute | solution.py:36
  43.6 25.8 %collective-permute-start.17 = (bf16[2,240,640]{2,1,0:T(8,128)(2,1)S(1)}, bf16[2,240,640]{2,1,0:T(8,128)(2,1)S(1)}, u32[]{:S(2)}, u32[]{:S(2)}) collective-permute-start(bf16[2,240,640]{2,1,0:T(8,128)(2,1)S(1)} %copy-done.62), channel_id=1, source_target_pairs={{0,2},{1,3},{2,0},{3,1},{4,6},{5,7},{6,4},{7,5},{8,10},{9,11},{10,... | collective-permute-start | bytes 1843208 | tf_op jit(solution)/shard_map/ppermute | solution.py:36
  47.4 22.0 %collective-permute-start.16 = (bf16[2,240,640]{2,1,0:T(8,128)(2,1)S(1)}, bf16[2,240,640]{2,1,0:T(8,128)(2,1)S(1)}, u32[]{:S(2)}, u32[]{:S(2)}) collective-permute-start(bf16[2,240,640]{2,1,0:T(8,128)(2,1)S(1)} %collective-permute-done.7.gm), channel_id=1, source_target_pairs={{0,4},{4,0},{8,12},{12,8},{16,20},{20,16},{24,28},{28,24},{1,5},{5... | collective-permute-start | bytes 1843208 | tf_op jit(solution)/shard_map/ppermute | solution.py:40
  54.1 13.1 %collective-permute-start.13 = (bf16[240,960]{1,0:T(8,128)(2,1)S(1)}, bf16[240,960]{1,0:T(8,128)(2,1)S(1)}, u32[]{:S(2)}, u32[]{:S(2)}) collective-permute-start(bf16[240,960]{1,0:T(8,128)(2,1)S(1)} %collective-permute-done.10.p2.refs_3_), channel_id=1, source_target_pairs={{0,1},{1,0},{2,3},{3,2},{4,5},{5,4},{6,7},{7,6},{8,9},{9,8},{10,11... | collective-permute-start | bytes 1382408 | tf_op jit(solution)/shard_map/ppermute | solution.py:36
  72.1 14.1 %collective-permute-start.18 = (bf16[2,240,640]{2,1,0:T(8,128)(2,1)S(1)}, bf16[2,240,640]{2,1,0:T(8,128)(2,1)S(1)}, u32[]{:S(2)}, u32[]{:S(2)}) collective-permute-start(bf16[2,240,640]{2,1,0:T(8,128)(2,1)S(1)} %collective-permute-done.17.um), channel_id=1, source_target_pairs={{0,4},{4,0},{8,12},{12,8},{16,20},{20,16},{24,28},{28,24},{1,5},{5... | collective-permute-start | bytes 1843208 | tf_op jit(solution)/shard_map/ppermute | solution.py:40
  88.7 17.5 %collective-permute-start.22 = (bf16[128,960]{1,0:T(8,128)(2,1)S(1)}, bf16[128,960]{1,0:T(8,128)(2,1)S(1)}, u32[]{:S(2)}, u32[]{:S(2)}) collective-permute-start(bf16[128,960]{1,0:T(8,128)(2,1)S(1)} %get-tuple-element.295.b_own.refs_0_), channel_id=1, source_target_pairs={{0,2},{1,3},{2,0},{3,1},{4,6},{5,7},{6,4},{7,5},{8,10},{9,11},{10,... | collective-permute-start | bytes 737288 | tf_op jit(solution)/shard_map/ppermute | solution.py:36
  112.6 21.4 %collective-permute-start.35 = (bf16[128,960]{1,0:T(8,128)(2,1)S(1)}, bf16[128,960]{1,0:T(8,128)(2,1)S(1)}, u32[]{:S(2)}, u32[]{:S(2)}) collective-permute-start(bf16[128,960]{1,0:T(8,128)(2,1)S(1)} %bitcast.218), channel_id=1, source_target_pairs={{0,1},{1,0},{2,3},{3,2},{4,5},{5,4},{6,7},{7,6},{8,9},{9,8},{10,11... | collective-permute-start | bytes 737288 | tf_op jit(solution)/shard_map/ppermute | solution.py:36
  126.9 13.6 %collective-permute-start.38 = (bf16[128,960]{1,0:T(8,128)(2,1)S(1)}, bf16[128,960]{1,0:T(8,128)(2,1)S(1)}, u32[]{:S(2)}, u32[]{:S(2)}) collective-permute-start(bf16[128,960]{1,0:T(8,128)(2,1)S(1)} %bitcast.219), channel_id=1, source_target_pairs={{0,2},{1,3},{2,0},{3,1},{4,6},{5,7},{6,4},{7,5},{8,10},{9,11},{10,... | collective-permute-start | bytes 737288 | tf_op jit(solution)/shard_map/ppermute | solution.py:36
  167.5 18.3 %collective-permute-start.48 = (bf16[2,256,640]{2,1,0:T(8,128)(2,1)S(1)}, bf16[2,256,640]{2,1,0:T(8,128)(2,1)S(1)}, u32[]{:S(2)}, u32[]{:S(2)}) collective-permute-start(bf16[2,256,640]{2,1,0:T(8,128)(2,1)S(1)} %get-tuple-element.354), channel_id=1, source_target_pairs={{0,2},{1,3},{2,0},{3,1},{4,6},{5,7},{6,4},{7,5},{8,10},{9,11},{10,... | collective-permute-start | bytes 1966088 | tf_op jit(solution)/shard_map/ppermute | solution.py:36
  185.7 15.9 %collective-permute-start.55 = (bf16[2,128,240]{2,1,0:T(8,128)(2,1)S(1)}, bf16[2,128,240]{2,1,0:T(8,128)(2,1)S(1)}, u32[]{:S(2)}, u32[]{:S(2)}) collective-permute-start(bf16[2,128,240]{2,1,0:T(8,128)(2,1)S(1)} %get-tuple-element.362), channel_id=1, source_target_pairs={{0,3},{1,2},{2,1},{3,0},{4,7},{5,6},{6,5},{7,4},{8,11},{9,10},{10,... | collective-permute-start | bytes 368648 | tf_op jit(solution)/shard_map/ppermute | solution.py:36
  229.1 15.3 %collective-permute-start.68 = (bf16[136,640]{1,0:T(8,128)(2,1)}, bf16[136,640]{1,0:T(8,128)(2,1)S(1)}, u32[]{:S(2)}, u32[]{:S(2)}) collective-permute-start(bf16[136,640]{1,0:T(8,128)(2,1)} %copy-done.40), channel_id=1, source_target_pairs={{0,1},{1,0},{2,3},{3,2},{4,5},{5,4},{6,7},{7,6},{8,9},{9,8},{10,11... | collective-permute-start | bytes 522248 | tf_op jit(solution)/shard_map/ppermute | solution.py:36
  229.2 15.2 %collective-permute-start.69 = (bf16[136,640]{1,0:T(8,128)(2,1)}, bf16[136,640]{1,0:T(8,128)(2,1)S(1)}, u32[]{:S(2)}, u32[]{:S(2)}) collective-permute-start(bf16[136,640]{1,0:T(8,128)(2,1)} %copy-done.40), channel_id=1, source_target_pairs={{0,2},{1,3},{2,0},{3,1},{4,6},{5,7},{6,4},{7,5},{8,10},{9,11},{10,... | collective-permute-start | bytes 522248 | tf_op jit(solution)/shard_map/ppermute | solution.py:36
  230.1 20.0 %collective-permute-start.67 = (bf16[2,256,640]{2,1,0:T(8,128)(2,1)}, bf16[2,256,640]{2,1,0:T(8,128)(2,1)S(1)}, u32[]{:S(2)}, u32[]{:S(2)}) collective-permute-start(bf16[2,256,640]{2,1,0:T(8,128)(2,1)} %copy-done.14), channel_id=1, source_target_pairs={{0,2},{1,3},{2,0},{3,1},{4,6},{5,7},{6,4},{7,5},{8,10},{9,11},{10,... | collective-permute-start | bytes 1966088 | tf_op jit(solution)/shard_map/ppermute | solution.py:36
  231.3 13.1 %collective-permute-start.70 = (bf16[128,960]{1,0:T(8,128)(2,1)}, bf16[128,960]{1,0:T(8,128)(2,1)S(1)}, u32[]{:S(2)}, u32[]{:S(2)}) collective-permute-start(bf16[128,960]{1,0:T(8,128)(2,1)} %copy-done.38), channel_id=1, source_target_pairs={{0,1},{1,0},{2,3},{3,2},{4,5},{5,4},{6,7},{7,6},{8,9},{9,8},{10,11... | collective-permute-start | bytes 737288 | tf_op jit(solution)/shard_map/ppermute | solution.py:36
  253.6 15.0 %collective-permute-start.76 = (bf16[128,960]{1,0:T(8,128)(2,1)S(1)}, bf16[128,960]{1,0:T(8,128)(2,1)}, u32[]{:S(2)}, u32[]{:S(2)}) collective-permute-start(bf16[128,960]{1,0:T(8,128)(2,1)S(1)} %get-tuple-element.409.refs_12_), channel_id=1, source_target_pairs={{0,2},{1,3},{2,0},{3,1},{4,6},{5,7},{6,4},{7,5},{8,10},{9,11},{10,... | collective-permute-start | bytes 737288 | tf_op jit(solution)/shard_map/ppermute | solution.py:36
  268.7 19.0 %collective-permute-start.84 = (bf16[128,960]{1,0:T(8,128)(2,1)S(1)}, bf16[128,960]{1,0:T(8,128)(2,1)S(1)}, u32[]{:S(2)}, u32[]{:S(2)}) collective-permute-start(bf16[128,960]{1,0:T(8,128)(2,1)S(1)} %copy-done.27), channel_id=1, source_target_pairs={{0,1},{1,0},{2,3},{3,2},{4,5},{5,4},{6,7},{7,6},{8,9},{9,8},{10,11... | collective-permute-start | bytes 737288 | tf_op jit(solution)/shard_map/ppermute | solution.py:36
  281.7 15.4 %collective-permute-start.86 = (bf16[6,64,640]{2,1,0:T(8,128)(2,1)S(1)}, bf16[6,64,640]{2,1,0:T(8,128)(2,1)S(1)}, u32[]{:S(2)}, u32[]{:S(2)}) collective-permute-start(bf16[6,64,640]{2,1,0:T(8,128)(2,1)S(1)} %pad_maximum_fusion.3), channel_id=1, source_target_pairs={{0,8},{8,16},{16,24},{24,28},{28,20},{20,12},{12,4},{4,0},{1,9},{9... | collective-permute-start | bytes 1474568 | tf_op jit(solution)/shard_map/ppermute | solution.py:49
  281.9 15.2 %collective-permute-start.87 = (bf16[6,64,640]{2,1,0:T(8,128)(2,1)S(1)}, bf16[6,64,640]{2,1,0:T(8,128)(2,1)S(1)}, u32[]{:S(2)}, u32[]{:S(2)}) collective-permute-start(bf16[6,64,640]{2,1,0:T(8,128)(2,1)S(1)} %pad_maximum_fusion.4), channel_id=1, source_target_pairs={{0,4},{8,0},{16,8},{24,16},{28,24},{20,28},{12,20},{4,12},{1,5},{9... | collective-permute-start | bytes 1474568 | tf_op jit(solution)/shard_map/ppermute | solution.py:49
  303.8 13.8 %collective-permute-start.92 = (bf16[6,64,640]{2,1,0:T(8,128)(2,1)}, bf16[6,64,640]{2,1,0:T(8,128)(2,1)S(1)}, u32[]{:S(2)}, u32[]{:S(2)}) collective-permute-start(bf16[6,64,640]{2,1,0:T(8,128)(2,1)} %get-tuple-element.533), channel_id=1, source_target_pairs={{0,8},{8,16},{16,24},{24,28},{28,20},{20,12},{12,4},{4,0},{1,9},{9... | collective-permute-start | bytes 1474568 | tf_op jit(solution)/shard_map/ppermute | solution.py:49
  304.4 13.7 %collective-permute-start.93 = (bf16[6,64,640]{2,1,0:T(8,128)(2,1)}, bf16[6,64,640]{2,1,0:T(8,128)(2,1)}, u32[]{:S(2)}, u32[]{:S(2)}) collective-permute-start(bf16[6,64,640]{2,1,0:T(8,128)(2,1)} %get-tuple-element.532), channel_id=1, source_target_pairs={{0,4},{8,0},{16,8},{24,16},{28,24},{20,28},{12,20},{4,12},{1,5},{9... | collective-permute-start | bytes 1474568 | tf_op jit(solution)/shard_map/ppermute | solution.py:49
  321.2 13.9 %collective-permute-start.95 = (bf16[6,64,640]{2,1,0:T(8,128)(2,1)}, bf16[6,64,640]{2,1,0:T(8,128)(2,1)}, u32[]{:S(2)}, u32[]{:S(2)}) collective-permute-start(bf16[6,64,640]{2,1,0:T(8,128)(2,1)} %get-tuple-element.531), channel_id=1, source_target_pairs={{0,8},{8,16},{16,24},{24,28},{28,20},{20,12},{12,4},{4,0},{1,9},{9... | collective-permute-start | bytes 1474568 | tf_op jit(solution)/shard_map/ppermute | solution.py:49
  322.5 13.6 %collective-permute-start.96 = (bf16[6,64,640]{2,1,0:T(8,128)(2,1)}, bf16[6,64,640]{2,1,0:T(8,128)(2,1)}, u32[]{:S(2)}, u32[]{:S(2)}) collective-permute-start(bf16[6,64,640]{2,1,0:T(8,128)(2,1)} %get-tuple-element.530), channel_id=1, source_target_pairs={{0,4},{8,0},{16,8},{24,16},{28,24},{20,28},{12,20},{4,12},{1,5},{9... | collective-permute-start | bytes 1474568 | tf_op jit(solution)/shard_map/ppermute | solution.py:49
  346.0 16.5 %collective-permute-start.104 = (bf16[6,64,640]{2,1,0:T(8,128)(2,1)S(1)}, bf16[6,64,640]{2,1,0:T(8,128)(2,1)S(1)}, u32[]{:S(2)}, u32[]{:S(2)}) collective-permute-start(bf16[6,64,640]{2,1,0:T(8,128)(2,1)S(1)} %constant_dynamic-update-slice_fusion.refs_0_), channel_id=1, source_target_pairs={{0,8},{8,16},{16,24},{24,28},{28,20},{20,12},{12,4},{4,0},{1,9},{9... | collective-permute-start | bytes 1474568 | tf_op jit(solution)/shard_map/ppermute | solution.py:49
  347.5 14.9 %collective-permute-start.105 = (bf16[6,64,640]{2,1,0:T(8,128)(2,1)S(1)}, bf16[6,64,640]{2,1,0:T(8,128)(2,1)S(1)}, u32[]{:S(2)}, u32[]{:S(2)}) collective-permute-start(bf16[6,64,640]{2,1,0:T(8,128)(2,1)S(1)} %constant_dynamic-update-slice_fusion.refs_0_), channel_id=1, source_target_pairs={{0,4},{8,0},{16,8},{24,16},{28,24},{20,28},{12,20},{4,12},{1,5},{9... | collective-permute-start | bytes 1474568 | tf_op jit(solution)/shard_map/ppermute | solution.py:49
  348.1 13.1 %collective-permute-start.102 = (bf16[32,2560]{1,0:T(8,128)(2,1)S(1)}, bf16[32,2560]{1,0:T(8,128)(2,1)S(1)}, u32[]{:S(2)}, u32[]{:S(2)}) collective-permute-start(bf16[32,2560]{1,0:T(8,128)(2,1)S(1)} %pad_maximum_fusion.11), channel_id=1, source_target_pairs={{0,8},{8,16},{16,24},{24,28},{28,20},{20,12},{12,4},{4,0},{1,9},{9... | collective-permute-start | bytes 491528 | tf_op jit(solution)/shard_map/ppermute | solution.py:49
  362.5 15.4 %collective-permute-start.108 = (bf16[6,64,640]{2,1,0:T(8,128)(2,1)S(1)}, bf16[6,64,640]{2,1,0:T(8,128)(2,1)S(1)}, u32[]{:S(2)}, u32[]{:S(2)}) collective-permute-start(bf16[6,64,640]{2,1,0:T(8,128)(2,1)S(1)} %collective-permute-done.104.refs_1_), channel_id=1, source_target_pairs={{0,8},{8,16},{16,24},{24,28},{28,20},{20,12},{12,4},{4,0},{1,9},{9... | collective-permute-start | bytes 1474568 | tf_op jit(solution)/shard_map/ppermute | solution.py:49
  364.1 13.8 %collective-permute-start.109 = (bf16[6,64,640]{2,1,0:T(8,128)(2,1)S(1)}, bf16[6,64,640]{2,1,0:T(8,128)(2,1)S(1)}, u32[]{:S(2)}, u32[]{:S(2)}) collective-permute-start(bf16[6,64,640]{2,1,0:T(8,128)(2,1)S(1)} %collective-permute-done.105.refs_7_), channel_id=1, source_target_pairs={{0,4},{8,0},{16,8},{24,16},{28,24},{20,28},{12,20},{4,12},{1,5},{9... | collective-permute-start | bytes 1474568 | tf_op jit(solution)/shard_map/ppermute | solution.py:49
  377.9 14.4 %collective-permute-start.112 = (bf16[6,64,640]{2,1,0:T(8,128)(2,1)S(1)}, bf16[6,64,640]{2,1,0:T(8,128)(2,1)S(1)}, u32[]{:S(2)}, u32[]{:S(2)}) collective-permute-start(bf16[6,64,640]{2,1,0:T(8,128)(2,1)S(1)} %collective-permute-done.108.refs_2_), channel_id=1, source_target_pairs={{0,8},{8,16},{16,24},{24,28},{28,20},{20,12},{12,4},{4,0},{1,9},{9... | collective-permute-start | bytes 1474568 | tf_op jit(solution)/shard_map/ppermute | solution.py:49
  379.3 13.0 %collective-permute-start.113 = (bf16[6,64,640]{2,1,0:T(8,128)(2,1)S(1)}, bf16[6,64,640]{2,1,0:T(8,128)(2,1)S(1)}, u32[]{:S(2)}, u32[]{:S(2)}) collective-permute-start(bf16[6,64,640]{2,1,0:T(8,128)(2,1)S(1)} %collective-permute-done.109.refs_6_), channel_id=1, source_target_pairs={{0,4},{8,0},{16,8},{24,16},{28,24},{20,28},{12,20},{4,12},{1,5},{9... | collective-permute-start | bytes 1474568 | tf_op jit(solution)/shard_map/ppermute | solution.py:49
  (192 other events, 2261.4 us)
